TPU v7x, 32 devices: a whole 2x2x4 slice. The times are simulated.
32 devices in a mesh: fsdp: 8 (over z, core), rows: 4 (over y, x).
Axes of the slice: x: 2, y: 2, z: 4, core: 2. Of those that a mesh axis runs over, the one named last changes fastest.
Arguments:
- query_rows: bfloat16 [8, 1024, 1536], P('fsdp', 'rows'), may hold values from -6 to 6
- key_rows: bfloat16 [8, 1024, 1536], P('fsdp', 'rows'), may hold values from -6 to 6
- value_rows: bfloat16 [8, 1024, 1536], P('fsdp', 'rows'), may hold values from -6 to 6
- grad_out: bfloat16 [8, 1024, 3072], P('fsdp', 'rows'), may hold values from -6 to 6
- w_out: bfloat16 [1536, 3072], P('fsdp'), may hold values from -0.15625 to 0.15625
Outputs:
- grad_query: bfloat16 [8, 1024, 1536], P('fsdp', 'rows')
- grad_key: bfloat16 [8, 1024, 1536], P('fsdp', 'rows')
- grad_value: bfloat16 [8, 1024, 1536], P('fsdp', 'rows')
- grad_w_out: float32 [1536, 3072], P('fsdp')
All inputs are finite; a program needn't handle non-finite values.
Results may differ from a plain program's by a relative error of at most 0.02.
Values may be sent and summed in bfloat16 or wider, within the bound.
No kernel may reach another device: no remote copies, remote signals or barrier semaphores. Data moves between devices by JAX's collectives and lax.ppermute only.
A program may use at most 192 MiB of HBM per device.

v0:
```python
import functools
import math

import jax
import jax.numpy as jnp
from jax import lax
from jax.experimental import pallas as pl
from jax.experimental.pallas import tpu as pltpu
from jax.sharding import PartitionSpec as P


HDIM = 128


NT = (((1,), (1,)), ((), ()))
NN = (((1,), (0,)), ((), ()))


def dot(a, b, dims=NN):
    return lax.dot_general(a, b, dims, preferred_element_type=jnp.float32)


def whole(shape):
    return pl.BlockSpec(shape, lambda *_: (0,) * len(shape))


def cost(flops, moved, exps=0):
    return pl.CostEstimate(flops=flops, bytes_accessed=moved, transcendentals=exps)


def pack(place, query, key, value, rows):
    tokens, width = query.shape[1], query.shape[2] // rows

    def body(place_ref, q_ref, k_ref, v_ref, *out):
        for slot in range(rows):

            @pl.when(pl.program_id(0) == slot)
            def _():
                out[slot][0] = q_ref[0]
                out[slot][1] = k_ref[0]
                out[slot][2] = v_ref[0]

    part = pl.BlockSpec((1, tokens, width), lambda j, place_ref: (0, 0, place_ref[0] ^ j))
    shape = (3, tokens, width)
    return pl.pallas_call(
        body,
        grid_spec=pltpu.PrefetchScalarGridSpec(
            num_scalar_prefetch=1,
            grid=(rows,),
            in_specs=[part] * 3,
            out_specs=[whole(shape)] * rows,
        ),
        out_shape=[jax.ShapeDtypeStruct(shape, query.dtype)] * rows,
        cost_estimate=cost(0, 12 * query.size),
        name="pack",
    )(place, query, key, value)


def unpack(place, parts):
    heads, rows = len(parts), len(parts[0])
    _, tokens, width = parts[0][0].shape

    def body(place_ref, *refs):
        ins, outs = refs[:-3], refs[-3:]
        for slot in range(rows):

            @pl.when(pl.program_id(0) == slot)
            def _():
                for head in range(heads):
                    for at in range(3):
                        outs[at][0, :, head * width : (head + 1) * width] = ins[
                            head * rows + slot
                        ][at]

    part = pl.BlockSpec(
        (1, tokens, width * heads), lambda j, place_ref: (0, 0, place_ref[0] ^ j)
    )
    full = jax.ShapeDtypeStruct((1, tokens, width * heads * rows), parts[0][0].dtype)
    return pl.pallas_call(
        body,
        grid_spec=pltpu.PrefetchScalarGridSpec(
            num_scalar_prefetch=1,
            grid=(rows,),
            in_specs=[whole(parts[0][0].shape)] * (rows * heads),
            out_specs=[part] * 3,
        ),
        out_shape=[full] * 3,
        cost_estimate=cost(0, 12 * tokens * width * heads * rows),
        name="unpack",
    )(place, *(block for head in parts for block in head))


def forward(parts):
    rows = len(parts)
    _, tokens, width = parts[0].shape
    length, heads = rows * tokens, width // HDIM
    scale = math.log2(math.e) / math.sqrt(HDIM)

    def body(*refs):
        ins, (probs_ref, attended_ref) = refs[:rows], refs[rows:]
        keys = jnp.concatenate([ref[1] for ref in ins], axis=0)
        values = jnp.concatenate([ref[2] for ref in ins], axis=0).T
        for slot in range(rows):
            across = slice(slot * tokens, (slot + 1) * tokens)
            scores = dot(keys, ins[slot][0], NT)
            top = jnp.max(scores, axis=0, keepdims=True)
            powers = jnp.exp2((scores - top) * scale)
            total = jnp.sum(powers, axis=0, keepdims=True)
            probs = (powers * (1.0 / total)).astype(jnp.bfloat16)
            probs_ref[0, :, across] = probs
            attended_ref[:, across] = dot(values, probs).astype(jnp.bfloat16)

    part = pl.BlockSpec((3, tokens, HDIM), lambda h: (0, 0, h))
    return pl.pallas_call(
        body,
        grid=(heads,),
        in_specs=[part] * rows,
        out_specs=[
            pl.BlockSpec((1, length, length), lambda h: (h, 0, 0)),
            pl.BlockSpec((HDIM, length), lambda h: (h, 0)),
        ],
        out_shape=[
            jax.ShapeDtypeStruct((heads, length, length), jnp.bfloat16),
            jax.ShapeDtypeStruct((width, length), jnp.bfloat16),
        ],
        cost_estimate=cost(
            8 * heads * length * length * HDIM, 2 * heads * length * length, heads * length * length
        ),
        name="forward",
    )(*parts)


def backward(parts, probs, grad_attn, head):
    rows = len(parts)
    tokens = parts[0].shape[1]
    length = rows * tokens
    factor = 1.0 / math.sqrt(HDIM)

    def body(*refs):
        ins, (probs_ref, grad_ref), outs = refs[:rows], refs[rows : rows + 2], refs[rows + 2 :]
        keys = jnp.concatenate([ref[1] for ref in ins], axis=0).T
        values = jnp.concatenate([ref[2] for ref in ins], axis=0)
        grad_key = jnp.zeros((length, HDIM), jnp.float32)
        grad_value = jnp.zeros((length, HDIM), jnp.float32)
        for slot in range(rows):
            across = slice(slot * tokens, (slot + 1) * tokens)
            grad = grad_ref[:, across]
            low = probs_ref[0, :, across]
            high = low.astype(jnp.float32)
            grad_probs = dot(values, grad)
            centre = jnp.sum(high * grad_probs, axis=0, keepdims=True)
            grad_scores = (high * (grad_probs - centre)).astype(jnp.bfloat16)
            outs[slot][0] = (dot(keys, grad_scores) * factor).T.astype(jnp.bfloat16)
            grad_key += dot(grad_scores, ins[slot][0])
            grad_value += dot(low, grad, NT)
        grad_key *= factor
        for slot in range(rows):
            down = slice(slot * tokens, (slot + 1) * tokens)
            outs[slot][1] = grad_key[down].astype(jnp.bfloat16)
            outs[slot][2] = grad_value[down].astype(jnp.bfloat16)

    part = pl.BlockSpec((3, tokens, HDIM), lambda i: (0, 0, head))
    shape = (3, tokens, HDIM)
    return pl.pallas_call(
        body,
        grid=(1,),
        in_specs=[part] * rows
        + [
            pl.BlockSpec((1, length, length), lambda i: (head, 0, 0)),
            pl.BlockSpec((HDIM, length), lambda i: (head, 0)),
        ],
        out_specs=[whole(shape)] * rows,
        out_shape=[jax.ShapeDtypeStruct(shape, jnp.bfloat16)] * rows,
        cost_estimate=cost(8 * length * length * HDIM, 2 * length * length),
        name="backward",
    )(*parts, probs, grad_attn)


def project(weights, grads):
    chunks, rows = len(grads), len(grads[0])
    half, depth = weights[0].shape
    tokens, wide = grads[0][0].shape
    steps = 2
    step = wide // steps

    def body(*refs):
        first, second = refs[:2]
        ins, out, total = refs[2:-2], refs[-2], refs[-1]
        at = pl.program_id(0)
        lines = jnp.concatenate([first[...], second[...]], axis=0)
        for chunk in range(chunks):

            @pl.when(at // steps == chunk)
            def _():
                columns = jnp.concatenate(
                    [ins[chunk * rows + slot][...] for slot in range(rows)], axis=0
                )
                term = dot(lines, columns, NT)
                if chunk:
                    total[...] += term
                else:
                    total[...] = jnp.where(at == 0, 0.0, total[...]) + term

        @pl.when(at == chunks * steps - 1)
        def _():
            out[...] = total[...].astype(out.dtype)

    def block_of(chunk):
        return pl.BlockSpec(
            (tokens, step), lambda i: (0, jnp.clip(i - chunk * steps, 0, steps - 1))
        )

    shape = (2 * half, rows * tokens)
    return pl.pallas_call(
        body,
        grid=(chunks * steps,),
        in_specs=[pl.BlockSpec((half, step), lambda i: (0, i))] * 2
        + [block_of(chunk) for chunk in range(chunks) for _ in range(rows)],
        out_specs=whole(shape),
        out_shape=jax.ShapeDtypeStruct(shape, jnp.bfloat16),
        scratch_shapes=[pltpu.VMEM(shape, jnp.float32)],
        cost_estimate=cost(2 * shape[0] * shape[1] * depth, 2 * depth * (shape[0] + shape[1])),
        name="project",
    )(*weights, *(block for chunk in grads for block in chunk))


def weight_terms(place, attended, grads, planes):
    rows = len(grads)
    width, length = attended.shape
    tokens, wide = grads[0].shape
    piece = width // 2 // planes
    step = wide // 2

    def body(place_ref, attended_ref, *refs):
        ins, (keep, give) = refs[:rows], refs[rows:]
        columns = jnp.concatenate([ref[...] for ref in ins], axis=0)
        term = dot(attended_ref[...], columns).astype(jnp.bfloat16)
        plane, core = place_ref[1], place_ref[2]
        for side in range(2):
            for out, mine in ((keep, core == side), (give, core != side)):

                @pl.when(mine)
                def _():
                    for at in range(planes):
                        start = (side * planes + at) * piece
                        out[(at - plane) & (planes - 1)] = term[start : start + piece]

    shape = jax.ShapeDtypeStruct((planes, piece, wide), jnp.bfloat16)
    spec = pl.BlockSpec((planes, piece, step), lambda i, place_ref: (0, 0, i))
    return pl.pallas_call(
        body,
        grid_spec=pltpu.PrefetchScalarGridSpec(
            num_scalar_prefetch=1,
            grid=(wide // step,),
            in_specs=[whole((width, length))]
            + [pl.BlockSpec((tokens, step), lambda i, place_ref: (0, i))] * rows,
            out_specs=[spec] * 2,
        ),
        out_shape=[shape] * 2,
        cost_estimate=cost(2 * width * length * wide, 2 * (width * length + length * wide)),
        name="weight_terms",
    )(place, attended, *grads)


def assemble(place, pieces, planes):
    chunks = len(pieces)
    piece, wide = pieces[0][0].shape

    def body(place_ref, *refs):
        ins, out = refs[:-1], refs[-1]
        for chunk in range(chunks):
            for back in range(planes):
                start = ((place_ref[1] + planes - back) & (planes - 1)) * piece
                out[pl.ds(pl.multiple_of(start, 16), piece), chunk * wide : (chunk + 1) * wide] = (
                    ins[chunk * planes + back][...].astype(out.dtype)
                )

    shape = (planes * piece, chunks * wide)
    return pl.pallas_call(
        body,
        grid_spec=pltpu.PrefetchScalarGridSpec(
            num_scalar_prefetch=1,
            grid=(1,),
            in_specs=[whole((piece, wide))] * (chunks * planes),
            out_specs=whole(shape),
        ),
        out_shape=jax.ShapeDtypeStruct(shape, jnp.float32),
        cost_estimate=cost(0, 6 * shape[0] * shape[1]),
        name="assemble",
    )(place, *(block for chunk in pieces for block in chunk))


def after(value, *done):
    return lax.optimization_barrier((value, done))[0]


def onward(planes, hop, z, c, r):
    to = z + 1 if z > r else z - 1
    return (to, c, r) if abs(z - r) == hop and 0 <= to < planes else None


def by_heads(fsdp, rows, query_rows, key_rows, value_rows, grad_out, w_out):
    planes = fsdp // 2
    row = lax.axis_index("rows")
    member = lax.axis_index("fsdp")
    plane, core = member // 2, member % 2
    place = jnp.stack([row, plane, core]).astype(jnp.int32)

    def send(array, target):
        pairs = []
        for z in range(planes):
            for c in range(2):
                for r in range(rows):
                    to = target(z, c, r)
                    if to is not None:
                        pairs.append(((z * 2 + c) * rows + r, (to[0] * 2 + to[1]) * rows + to[2]))
        return lax.ppermute(array, ("fsdp", "rows"), pairs)

    def to_row(array, slot):
        return send(array, lambda z, c, r: (z, c, r ^ slot))

    def to_core(array):
        return send(array, lambda z, c, r: (z, 1 - c, r))

    def to_plane(array, ahead):
        return send(array, lambda z, c, r: ((z + ahead) % planes, c, r))

    grad_flat = grad_out[0]
    wide = grad_flat.shape[1] // 2
    own = [grad_flat[:, :wide], grad_flat[:, wide:]]
    by_x, by_y = [to_row(own[0], 1)], [to_row(own[0], 2)]

    packed = pack(place, query_rows, key_rows, value_rows, rows)
    parts = [packed[0]] + [to_row(packed[slot], slot) for slot in range(1, rows)]

    here = []
    away = jnp.abs(plane - row)
    cut = w_out.shape[0] // 2
    for half in (w_out[:cut], w_out[cut:]):
        half = after(half, packed[0])
        above = send(half, lambda z, c, r: (z + 1, c, r) if z == r and z + 1 < planes else None)
        below = send(half, lambda z, c, r: (z - 1, c, r) if z == r and z > 0 else None)
        got = half
        stage = jnp.where(plane > row, above, below)
        for hop in range(1, planes):
            got = jnp.where(away == hop, stage, got)
            if hop + 1 < planes:
                stage = send(stage, functools.partial(onward, planes, hop))
        here.append(got)
    here = jnp.concatenate(here, axis=0)
    other = to_core(here)
    weights = [jnp.where(core == 0, here, other), jnp.where(core == 0, other, here)]

    probs, attended = forward(parts)

    across = [to_row(by_x[0], 2)]
    second = after(own[1], by_x[0], by_y[0])
    by_x.append(to_row(second, 1))
    by_y.append(to_row(second, 2))
    across.append(to_row(by_y[1], 1))
    grads = [[own[at], by_x[at], by_y[at], across[at]] for at in range(2)]

    def reduce_cores(attended, chunk):
        keep, give = weight_terms(place, attended, chunk, planes)
        got = to_core(give)
        return [
            (keep[at].astype(jnp.float32) + got[at].astype(jnp.float32)).astype(jnp.bfloat16)
            for at in range(planes)
        ]

    def reduce_planes(both, *done):
        got = [to_plane(both[ahead], ahead) for ahead in range(1, planes)]
        got = after(got, *done)
        total = both[0].astype(jnp.float32)
        for part in got:
            total = total + part.astype(jnp.float32)
        return total.astype(jnp.bfloat16)

    def gather_rows(total):
        return [total] + [to_row(total, slot) for slot in range(1, rows)]

    def to_owners(blocks):
        stack = jnp.stack(blocks)
        pieces = []
        for ahead in range(planes):
            block = lax.dynamic_index_in_dim(stack, ((plane + ahead) % planes) ^ row, 0, False)
            pieces.append(to_plane(block, ahead) if ahead else block)
        return pieces

    first = reduce_planes(reduce_cores(attended, grads[0]))
    blocks = gather_rows(first)
    both = reduce_cores(after(attended, first), grads[1])
    grad_attn = project(after(weights, both[0]), grads)
    back = []
    for head in range(probs.shape[0]):
        sent = backward(parts, probs, grad_attn, head)
        back.append([sent[0]] + [to_row(sent[slot], slot) for slot in range(1, rows)])
    grad_query, grad_key, grad_value = unpack(place, back)
    last = gather_rows(reduce_planes(both, back[0][0]))
    pieces = [to_owners(blocks), to_owners(after(last, back[-1][0]))]
    grad_w_out = assemble(place, pieces, planes)
    return grad_query, grad_key, grad_value, grad_w_out


def by_tokens(query_rows, key_rows, value_rows, grad_out, w_out):
    tokens, width = query_rows.shape[1:]
    heads = width // HDIM
    factor = 1.0 / math.sqrt(HDIM)
    grad_flat = grad_out[0]
    groups = math.gcd(heads, 3)

    def split(array, count):
        return jnp.moveaxis(array.reshape(count, groups, heads // groups, HDIM), 1, 0)

    def join(array, count):
        return jnp.moveaxis(array, 0, 1).reshape(count, width)

    grad_attn = lax.dot_general(
        grad_flat,
        lax.all_gather(w_out, "fsdp", axis=0, tiled=True),
        NT,
        preferred_element_type=jnp.float32,
    ).astype(jnp.bfloat16)
    all_keys = lax.all_gather(key_rows, "rows", axis=1, tiled=True)
    all_values = lax.all_gather(value_rows, "rows", axis=1, tiled=True)
    length = all_keys.shape[1]

    def product(spec, a, b):
        return jnp.einsum(spec, a, b, preferred_element_type=jnp.float32)

    def attend(inputs):
        queries, keys, values, grads = inputs
        probs = jax.nn.softmax(product("qhd,khd->hqk", queries, keys) * factor, axis=-1)
        low = probs.astype(jnp.bfloat16)
        attended = product("hqk,khd->qhd", low, values)
        value_part = product("hqk,qhd->khd", low, grads)
        grad_probs = product("qhd,khd->hqk", grads, values)
        centre = jnp.sum(probs * grad_probs, axis=-1, keepdims=True)
        grad_scores = (probs * (grad_probs - centre)).astype(jnp.bfloat16)
        grad_query = product("hqk,khd->qhd", grad_scores, keys) * factor
        key_part = product("hqk,qhd->khd", grad_scores, queries) * factor
        return (
            attended.astype(jnp.bfloat16),
            grad_query.astype(jnp.bfloat16),
            key_part.astype(jnp.bfloat16),
            value_part.astype(jnp.bfloat16),
        )

    attended, grad_query, key_part, value_part = lax.map(
        attend,
        (
            split(query_rows[0], tokens),
            split(all_keys[0], length),
            split(all_values[0], length),
            split(grad_attn, tokens),
        ),
    )

    def scatter(part):
        part = join(part, length).reshape(1, length, width)
        return lax.psum_scatter(part, "rows", scatter_dimension=1, tiled=True)

    term = lax.dot_general(
        join(attended, tokens),
        grad_flat,
        (((0,), (0,)), ((), ())),
        preferred_element_type=jnp.float32,
    ).astype(jnp.bfloat16)
    share = lax.psum_scatter(term, "fsdp", scatter_dimension=0, tiled=True)
    grad_w_out = lax.psum(share, "rows").astype(jnp.float32)
    return (
        join(grad_query, tokens).reshape(1, tokens, width),
        scatter(key_part),
        scatter(value_part),
        grad_w_out,
    )


def solution(mesh):
    fsdp, rows = mesh.shape["fsdp"], mesh.shape["rows"]

    def local(query_rows, key_rows, value_rows, grad_out, w_out):
        heads = query_rows.shape[2] // HDIM
        if rows == 4 and fsdp == 2 * rows and heads % rows == 0:
            plan = functools.partial(by_heads, fsdp, rows)
        else:
            plan = by_tokens
        return plan(query_rows, key_rows, value_rows, grad_out, w_out)

    tokens = P("fsdp", "rows", None)
    return jax.shard_map(
        local,
        mesh=mesh,
        in_specs=(tokens, tokens, tokens, tokens, P("fsdp", None)),
        out_specs=(tokens, tokens, tokens, P("fsdp", None)),
        check_vma=False,
    )
```

profile of v0, /device:TPU:0, one launch (start us, length us, event | category | flops | bytes accessed | tf_op | source)
XLA Modules:
  0.0 215.4 jit_solution(1886079166454488632)
XLA Ops:
  0.6 2.1 fusion.12
  3.4 4.6 %pack.1 = (bf16[3,256,384]{2,1,0:T(8,128)(2,1)}, bf16[3,256,384]{2,1,0:T(8,128)(2,1)}, bf16[3,256,384]{2,1,0:T(8,128)(2,1)}, bf16[3,256,384]{2,1,0:T(8,128)(2,1)}) custom-call(s32[3]{0:T(128)} %pad_add_fusion.place_ref, bf16[1,256,1536]{2,1,0:T(8,128)(2,1)} %q_ref.1, bf16[1,256,1536]{2,1,0:T(8,128)(2,1)} %k_ref.1, bf16[1,256,1536]{2,1,0:T(8,128)(2,1)} %v_ref.1), custom_call_target="tpu_custom_call" | custom-call | bytes 4718592 | tf_op jit(solution)/shard_map/pack/pallas_call | solution.py:45
  8.1 5.0 %collective-permute-start.7 = (bf16[96,3072]{1,0:T(8,128)(2,1)S(1)}, bf16[96,3072]{1,0:T(8,128)(2,1)S(1)}, u32[]{:S(2)}, u32[]{:S(2)}) collective-permute-start(bf16[96,3072]{1,0:T(8,128)(2,1)S(1)} %get-tuple-element.51), channel_id=1, source_target_pairs={{0,8},{4,12},{9,17},{13,21},{18,26},{22,30}} | collective-permute-start | bytes 1769480 | tf_op jit(solution)/shard_map/ppermute | solution.py:317
  13.1 0.7 collective-permute-start.8
  13.8 1.5 fusion.11
  15.6 6.2 %collective-permute-start.3 = (bf16[96,3072]{1,0:T(8,128)(2,1)}, bf16[96,3072]{1,0:T(8,128)(2,1)}, u32[]{:S(2)}, u32[]{:S(2)}) collective-permute-start(bf16[96,3072]{1,0:T(8,128)(2,1)} %get-tuple-element.50), channel_id=1, source_target_pairs={{0,8},{4,12},{9,17},{13,21},{18,26},{22,30}} | collective-permute-start | bytes 1769480 | tf_op jit(solution)/shard_map/ppermute | solution.py:317
  21.8 5.0 %collective-permute-done.7 = bf16[96,3072]{1,0:T(8,128)(2,1)S(1)} collective-permute-done((bf16[96,3072]{1,0:T(8,128)(2,1)S(1)}, bf16[96,3072]{1,0:T(8,128)(2,1)S(1)}, u32[]{:S(2)}, u32[]{:S(2)}) %collective-permute-start.7) | collective-permute-done | bytes 589856 | tf_op jit(solution)/shard_map/ppermute | solution.py:317
  26.7 0.7 collective-permute-start.4
  27.4 3.5 %collective-permute-start = (bf16[3,256,384]{2,1,0:T(8,128)(2,1)}, bf16[3,256,384]{2,1,0:T(8,128)(2,1)S(1)}, u32[]{:S(2)}, u32[]{:S(2)}) collective-permute-start(bf16[3,256,384]{2,1,0:T(8,128)(2,1)} %get-tuple-element.46), channel_id=1, source_target_pairs={{0,1},{1,0},{2,3},{3,2},{4,5},{5,4},{6,7},{7,6},{8,9},{9,8},{10,11... | collective-permute-start | bytes 1769480 | tf_op jit(solution)/shard_map/ppermute | solution.py:317
  31.0 4.8 %collective-permute-done.12.refs_1_.refs_3_ = bf16[256,1536]{1,0:T(8,128)(2,1)} collective-permute-done((bf16[256,1536]{1,0:T(8,128)(2,1)S(1)}, bf16[256,1536]{1,0:T(8,128)(2,1)}, u32[]{:S(2)}, u32[]{:S(2)}) %collective-permute-start.12) | collective-permute-done | bytes 786464 | tf_op jit(solution)/shard_map/ppermute | solution.py:317
  35.9 1.5 collective-permute-start.2
  37.4 11.1 %collective-permute-done.refs_1_ = bf16[3,256,384]{2,1,0:T(8,128)(2,1)S(1)} collective-permute-done((bf16[3,256,384]{2,1,0:T(8,128)(2,1)}, bf16[3,256,384]{2,1,0:T(8,128)(2,1)S(1)}, u32[]{:S(2)}, u32[]{:S(2)}) %collective-permute-start) | collective-permute-done | bytes 589856 | tf_op jit(solution)/shard_map/ppermute | solution.py:317
  48.4 1.5 collective-permute-start.9
  49.9 2.0 collective-permute-start.14
  51.9 0.9 broadcast_select_fusion.3
  52.8 11.1 %collective-permute-done.1.refs_2_ = bf16[3,256,384]{2,1,0:T(8,128)(2,1)S(1)} collective-permute-done((bf16[3,256,384]{2,1,0:T(8,128)(2,1)S(1)}, bf16[3,256,384]{2,1,0:T(8,128)(2,1)S(1)}, u32[]{:S(2)}, u32[]{:S(2)}) %collective-permute-start.1) | collective-permute-done | bytes 589856 | tf_op jit(solution)/shard_map/ppermute | solution.py:317
  63.9 1.5 collective-permute-start.5
  65.4 1.5 collective-permute-start.10
  66.9 0.8 copy-done.2
  67.7 12.6 %forward.1 = (bf16[3,1024,1024]{2,1,0:T(8,128)(2,1)}, bf16[384,1024]{1,0:T(8,128)(2,1)}) custom-call(bf16[3,256,384]{2,1,0:T(8,128)(2,1)} %get-tuple-element.45.refs_0_, bf16[3,256,384]{2,1,0:T(8,128)(2,1)} %copy-done, bf16[3,256,384]{2,1,0:T(8,128)(2,1)} %copy-done.1, bf16[3,256,384]{2,1,0:T(8,128)(2,1)} %copy-done.2), custom_call_target="tpu_custom_call" | custom-call | flops 3221225472 | bytes 6291456 | tf_op jit(solution)/shard_map/forward/pallas_call | solution.py:114
  80.4 1.5 collective-permute-start.6
  81.9 13.0 %collective-permute-done.14.refs_3_.refs_5_ = bf16[256,1536]{1,0:T(8,128)(2,1)} collective-permute-done((bf16[256,1536]{1,0:T(8,128)(2,1)}, bf16[256,1536]{1,0:T(8,128)(2,1)}, u32[]{:S(2)}, u32[]{:S(2)}) %collective-permute-start.14) | collective-permute-done | bytes 786464 | tf_op jit(solution)/shard_map/ppermute | solution.py:317
  94.9 5.3 %weight_terms.2 = (bf16[4,48,1536]{2,1,0:T(8,128)(2,1)}, bf16[4,48,1536]{2,1,0:T(8,128)(2,1)}) custom-call(s32[3]{0:T(128)} %pad_add_fusion.place_ref, bf16[384,1024]{1,0:T(8,128)(2,1)} %get-tuple-element.58.attended_ref, bf16[256,1536]{1,0:T(8,128)(2,1)} %copy-done.4, bf16[256,1536]{1,0:T(8,128)(2,1)} %collective-permute-done.12.refs_1_.refs_3_, ...), custom_call_target="tpu_custom_call" | custom-call | flops 1207959552 | bytes 3932160 | tf_op jit(solution)/shard_map/weight_terms/pallas_call | solution.py:250
  100.9 1.3 select_select_fusion.1
  102.4 3.1 %collective-permute-start.16 = (bf16[48,1536]{1,0:T(8,128)(2,1)S(1)}, bf16[48,1536]{1,0:T(8,128)(2,1)S(1)}, u32[]{:S(2)}, u32[]{:S(2)}) collective-permute-start(bf16[48,1536]{1,0:T(8,128)(2,1)S(1)} %get-tuple-element.96), channel_id=1, source_target_pairs={{0,8},{1,9},{2,10},{3,11},{4,12},{5,13},{6,14},{7,15},{8,16},{9,17... | collective-permute-start | bytes 442376 | tf_op jit(solution)/shard_map/ppermute | solution.py:317
  105.5 1.8 collective-permute-start.17
  107.3 2.2 %collective-permute-start.18 = (bf16[48,1536]{1,0:T(8,128)(2,1)S(1)}, bf16[48,1536]{1,0:T(8,128)(2,1)S(1)}, u32[]{:S(2)}, u32[]{:S(2)}) collective-permute-start(bf16[48,1536]{1,0:T(8,128)(2,1)S(1)} %get-tuple-element.94), channel_id=1, source_target_pairs={{0,24},{1,25},{2,26},{3,27},{4,28},{5,29},{6,30},{7,31},{8,0},{9,1... | collective-permute-start | bytes 442376 | tf_op jit(solution)/shard_map/ppermute | solution.py:317
  109.5 1.1 pad_maximum_fusion
  110.6 1.0 collective-permute-done.16
  111.6 5.8 %collective-permute-done.17 = bf16[48,1536]{1,0:T(8,128)(2,1)S(1)} collective-permute-done((bf16[48,1536]{1,0:T(8,128)(2,1)S(1)}, bf16[48,1536]{1,0:T(8,128)(2,1)S(1)}, u32[]{:S(2)}, u32[]{:S(2)}) %collective-permute-start.17) | collective-permute-done | bytes 147488 | tf_op jit(solution)/shard_map/ppermute | solution.py:317
  117.5 1.6 collective-permute-start.34
  119.6 1.4 collective-permute-start.32
  121.0 5.1 %weight_terms.3 = (bf16[4,48,1536]{2,1,0:T(8,128)(2,1)}, bf16[4,48,1536]{2,1,0:T(8,128)(2,1)}) custom-call(s32[3]{0:T(128)} %pad_add_fusion.place_ref, bf16[384,1024]{1,0:T(8,128)(2,1)} %get-tuple-element.58.attended_ref, bf16[256,1536]{1,0:T(8,128)(2,1)} %copy-done.3, bf16[256,1536]{1,0:T(8,128)(2,1)} %copy-done.9, ...), custom_call_target="tpu_custom_call" | custom-call | flops 1207959552 | bytes 3932160 | tf_op jit(solution)/shard_map/weight_terms/pallas_call | solution.py:250
  126.1 1.1 collective-permute-done.33
  127.3 0.7 dynamic-slice_bitcast_fusion.4
  128.1 3.8 %collective-permute-start.35 = (bf16[48,1536]{1,0:T(8,128)(2,1)S(1)}, bf16[48,1536]{1,0:T(8,128)(2,1)S(1)}, u32[]{:S(2)}, u32[]{:S(2)}) collective-permute-start(bf16[48,1536]{1,0:T(8,128)(2,1)S(1)} %get-tuple-element.105), channel_id=1, source_target_pairs={{0,8},{1,9},{2,10},{3,11},{4,12},{5,13},{6,14},{7,15},{8,16},{9,17... | collective-permute-start | bytes 442376 | tf_op jit(solution)/shard_map/ppermute | solution.py:317
  131.9 3.3 %broadcast_select_fusion = (bf16[192,3072]{1,0:T(8,128)(2,1)}, bf16[192,3072]{1,0:T(8,128)(2,1)}) fusion(bf16[192,3072]{1,0:T(8,128)(2,1)} %collective-permute-done.11, pred[]{:T(512)S(6)} %eq.26, bf16[96,3072]{1,0:T(8,128)(2,1)S(1)} %select_select_fusion, bf16[96,3072]{1,0:T(8,128)(2,1)S(1)} %select_select_fusion.1), kind=kLoop, calls=%fused_computation.1 | loop fusion | flops 3538944 | bytes 4718593 | tf_op jit(solution)/shard_map/jit(_where)/select_n | solution.py:352
  135.4 1.7 collective-permute-start.39
  137.1 2.8 %collective-permute-start.40 = (bf16[48,1536]{1,0:T(8,128)(2,1)S(1)}, bf16[48,1536]{1,0:T(8,128)(2,1)S(1)}, u32[]{:S(2)}, u32[]{:S(2)}) collective-permute-start(bf16[48,1536]{1,0:T(8,128)(2,1)S(1)} %get-tuple-element.90), channel_id=1, source_target_pairs={{0,24},{1,25},{2,26},{3,27},{4,28},{5,29},{6,30},{7,31},{8,0},{9,1... | collective-permute-start | bytes 442376 | tf_op jit(solution)/shard_map/ppermute | solution.py:317
  139.9 7.2 %project.1.refs_5_ = bf16[384,1024]{1,0:T(8,128)(2,1)} custom-call(bf16[192,3072]{1,0:T(8,128)(2,1)} %get-tuple-element.62.refs_0_, bf16[192,3072]{1,0:T(8,128)(2,1)} %get-tuple-element.63.refs_1_, bf16[256,1536]{1,0:T(8,128)(2,1)} %copy-done.4, bf16[256,1536]{1,0:T(8,128)(2,1)} %collective-permute-done.12.refs_1_.refs_3_, ...), custom_call_target="tpu_custom_call" | custom-call | flops 2415919104 | bytes 8650752 | tf_op jit(solution)/shard_map/project/pallas_call | solution.py:214
  147.1 6.6 %backward.3 = (bf16[3,256,128]{2,1,0:T(8,128)(2,1)}, bf16[3,256,128]{2,1,0:T(8,128)(2,1)}, bf16[3,256,128]{2,1,0:T(8,128)(2,1)}, bf16[3,256,128]{2,1,0:T(8,128)(2,1)}) custom-call(bf16[3,256,384]{2,1,0:T(8,128)(2,1)} %get-tuple-element.45.refs_0_, bf16[3,256,384]{2,1,0:T(8,128)(2,1)} %copy-done, bf16[3,256,384]{2,1,0:T(8,128)(2,1)} %copy-done.1, ...), custom_call_target="tpu_custom_call" | custom-call | flops 1073741824 | bytes 2097152 | tf_op jit(solution)/shard_map/backward/pallas_call | solution.py:164
  154.3 1.6 collective-permute-start.41
  156.5 1.4 collective-permute-start.43
  157.9 6.6 %backward.4 = (bf16[3,256,128]{2,1,0:T(8,128)(2,1)}, bf16[3,256,128]{2,1,0:T(8,128)(2,1)}, bf16[3,256,128]{2,1,0:T(8,128)(2,1)}, bf16[3,256,128]{2,1,0:T(8,128)(2,1)}) custom-call(bf16[3,256,384]{2,1,0:T(8,128)(2,1)} %get-tuple-element.45.refs_0_, bf16[3,256,384]{2,1,0:T(8,128)(2,1)} %copy-done, bf16[3,256,384]{2,1,0:T(8,128)(2,1)} %copy-done.1, ...), custom_call_target="tpu_custom_call" | custom-call | flops 1073741824 | bytes 2097152 | tf_op jit(solution)/shard_map/backward/pallas_call | solution.py:164
  164.5 6.6 %backward.5 = (bf16[3,256,128]{2,1,0:T(8,128)(2,1)}, bf16[3,256,128]{2,1,0:T(8,128)(2,1)}, bf16[3,256,128]{2,1,0:T(8,128)(2,1)}, bf16[3,256,128]{2,1,0:T(8,128)(2,1)}) custom-call(bf16[3,256,384]{2,1,0:T(8,128)(2,1)} %get-tuple-element.45.refs_0_, bf16[3,256,384]{2,1,0:T(8,128)(2,1)} %copy-done, bf16[3,256,384]{2,1,0:T(8,128)(2,1)} %copy-done.1, ...), custom_call_target="tpu_custom_call" | custom-call | flops 1073741824 | bytes 2097152 | tf_op jit(solution)/shard_map/backward/pallas_call | solution.py:164
  171.2 1.5 collective-permute-start.24
  172.7 1.5 collective-permute-start.25
  174.9 1.5 collective-permute-start.27
  176.4 1.6 collective-permute-start.28
  178.0 6.4 %collective-permute-done.24.refs_2_ = bf16[3,256,128]{2,1,0:T(8,128)(2,1)S(1)} collective-permute-done((bf16[3,256,128]{2,1,0:T(8,128)(2,1)S(1)}, bf16[3,256,128]{2,1,0:T(8,128)(2,1)S(1)}, u32[]{:S(2)}, u32[]{:S(2)}) %collective-permute-start.24) | collective-permute-done | bytes 196640 | tf_op jit(solution)/shard_map/ppermute | solution.py:317
  184.3 0.9 collective-permute-start.29
  185.3 1.2 collective-permute-start.30
  186.5 1.5 collective-permute-start.31
  188.0 0.7 dynamic-slice_bitcast_fusion
  188.7 4.1 %collective-permute-done.27.refs_6_ = bf16[3,256,128]{2,1,0:T(8,128)(2,1)S(1)} collective-permute-done((bf16[3,256,128]{2,1,0:T(8,128)(2,1)S(1)}, bf16[3,256,128]{2,1,0:T(8,128)(2,1)S(1)}, u32[]{:S(2)}, u32[]{:S(2)}) %collective-permute-start.27) | collective-permute-done | bytes 196640 | tf_op jit(solution)/shard_map/ppermute | solution.py:317
  192.8 1.3 collective-permute-start.36
  194.1 1.2 collective-permute-start.37
  195.3 0.8 collective-permute-start.44
  196.1 1.2 collective-permute-done.30.refs_10_
  197.3 1.0 collective-permute-start.45
  198.3 1.2 collective-permute-start.46
  199.6 4.5 %unpack.1 = (bf16[1,256,1536]{2,1,0:T(8,128)(2,1)}, bf16[1,256,1536]{2,1,0:T(8,128)(2,1)}, bf16[1,256,1536]{2,1,0:T(8,128)(2,1)}) custom-call(s32[3]{0:T(128)} %pad_add_fusion.place_ref, bf16[3,256,128]{2,1,0:T(8,128)(2,1)} %get-tuple-element.64.refs_0_, bf16[3,256,128]{2,1,0:T(8,128)(2,1)} %copy-done.12, bf16[3,256,128]{2,1,0:T(8,128)(2,1)} %copy-done.13, ...), custom_call_target="tpu_custom_call" | custom-call | bytes 4718592 | tf_op jit(solution)/shard_map/unpack/pallas_call | solution.py:79
  204.8 6.3 %collective-permute-done.45.refs_6_ = bf16[48,1536]{1,0:T(8,128)(2,1)S(1)} collective-permute-done((bf16[48,1536]{1,0:T(8,128)(2,1)S(1)}, bf16[48,1536]{1,0:T(8,128)(2,1)S(1)}, u32[]{:S(2)}, u32[]{:S(2)}) %collective-permute-start.45) | collective-permute-done | bytes 147488 | tf_op jit(solution)/shard_map/ppermute | solution.py:317
  211.8 3.6 %assemble.1 = f32[192,3072]{1,0:T(8,128)} custom-call(s32[3]{0:T(128)} %pad_add_fusion.place_ref, bf16[48,1536]{1,0:T(8,128)(2,1)} %get-tuple-element.106.refs_0_, bf16[48,1536]{1,0:T(8,128)(2,1)} %copy-done.21, bf16[48,1536]{1,0:T(8,128)(2,1)} %copy-done.22, bf16[48,1536]{1,0:T(8,128)(2,1)} %copy-done.23, bf16[48,1536]{1,0:T(8,128)(2,1)} %get-tuple-element.102.refs_4_, ...), custom_call_target="tpu_custom_call" | custom-call | bytes 3538944 | tf_op jit(solution)/shard_map/assemble/pallas_call | solution.py:279
  (129 shorter events, 6.4 us)
Async XLA Ops:
  2.8 10.3 %copy-start.5 = (bf16[96,3072]{1,0:T(8,128)(2,1)}, bf16[96,3072]{1,0:T(8,128)(2,1)S(1)}, u32[]{:S(2)}) copy-start(bf16[96,3072]{1,0:T(8,128)(2,1)S(1)} %get-tuple-element.51) | copy-start | bytes 1769476
  8.1 18.7 %collective-permute-start.7 = (bf16[96,3072]{1,0:T(8,128)(2,1)S(1)}, bf16[96,3072]{1,0:T(8,128)(2,1)S(1)}, u32[]{:S(2)}, u32[]{:S(2)}) collective-permute-start(bf16[96,3072]{1,0:T(8,128)(2,1)S(1)} %get-tuple-element.51), channel_id=1, source_target_pairs={{0,8},{4,12},{9,17},{13,21},{18,26},{22,30}} | collective-permute-start | bytes 1769480 | tf_op jit(solution)/shard_map/ppermute | solution.py:317
  13.1 14.3 %collective-permute-start.8 = (bf16[96,3072]{1,0:T(8,128)(2,1)S(1)}, bf16[96,3072]{1,0:T(8,128)(2,1)S(1)}, u32[]{:S(2)}, u32[]{:S(2)}) collective-permute-start(bf16[96,3072]{1,0:T(8,128)(2,1)S(1)} %get-tuple-element.51), channel_id=1, source_target_pairs={{9,1},{13,5},{18,10},{22,14},{27,19},{31,23}} | collective-permute-start | bytes 1769480 | tf_op jit(solution)/shard_map/ppermute | solution.py:317
  15.3 37.6 %copy-start.4 = (bf16[256,1536]{1,0:T(8,128)(2,1)}, bf16[256,1536]{1,0:T(8,128)(2,1)S(1)}, u32[]{:S(2)}) copy-start(bf16[256,1536]{1,0:T(8,128)(2,1)S(1)} %get-tuple-element.89.refs_0_.refs_2_) | copy-start | bytes 2359300
  15.3 65.0 %copy-start.3 = (bf16[256,1536]{1,0:T(8,128)(2,1)}, bf16[256,1536]{1,0:T(8,128)(2,1)S(1)}, u32[]{:S(2)}) copy-start(bf16[256,1536]{1,0:T(8,128)(2,1)S(1)} %get-tuple-element.59.refs_0_.refs_6_) | copy-start | bytes 2359300
  15.3 20.6 %collective-permute-start.12 = (bf16[256,1536]{1,0:T(8,128)(2,1)S(1)}, bf16[256,1536]{1,0:T(8,128)(2,1)}, u32[]{:S(2)}, u32[]{:S(2)}) collective-permute-start(bf16[256,1536]{1,0:T(8,128)(2,1)S(1)} %get-tuple-element.89.refs_0_.refs_2_), channel_id=1, source_target_pairs={{0,1},{1,0},{2,3},{3,2},{4,5},{5,4},{6,7},{7,6},{8,9},{9,8},{10,11... | collective-permute-start | bytes 2359304 | tf_op jit(solution)/shard_map/ppermute | solution.py:317
  15.4 20.5 %collective-permute-start.13 = (bf16[256,1536]{1,0:T(8,128)(2,1)S(1)}, bf16[256,1536]{1,0:T(8,128)(2,1)}, u32[]{:S(2)}, u32[]{:S(2)}) collective-permute-start(bf16[256,1536]{1,0:T(8,128)(2,1)S(1)} %get-tuple-element.89.refs_0_.refs_2_), channel_id=1, source_target_pairs={{0,2},{1,3},{2,0},{3,1},{4,6},{5,7},{6,4},{7,5},{8,10},{9,11},{10,... | collective-permute-start | bytes 2359304 | tf_op jit(solution)/shard_map/ppermute | solution.py:317
  15.6 34.4 %collective-permute-start.3 = (bf16[96,3072]{1,0:T(8,128)(2,1)}, bf16[96,3072]{1,0:T(8,128)(2,1)}, u32[]{:S(2)}, u32[]{:S(2)}) collective-permute-start(bf16[96,3072]{1,0:T(8,128)(2,1)} %get-tuple-element.50), channel_id=1, source_target_pairs={{0,8},{4,12},{9,17},{13,21},{18,26},{22,30}} | collective-permute-start | bytes 1769480 | tf_op jit(solution)/shard_map/ppermute | solution.py:317
  21.8 14.1 %copy-start.27 = (bf16[3,256,384]{2,1,0:T(8,128)(2,1)S(1)}, bf16[3,256,384]{2,1,0:T(8,128)(2,1)}, u32[]{:S(2)}) copy-start(bf16[3,256,384]{2,1,0:T(8,128)(2,1)} %get-tuple-element.47) | copy-start | bytes 1769476
  26.7 23.2 %collective-permute-start.4 = (bf16[96,3072]{1,0:T(8,128)(2,1)}, bf16[96,3072]{1,0:T(8,128)(2,1)S(1)}, u32[]{:S(2)}, u32[]{:S(2)}) collective-permute-start(bf16[96,3072]{1,0:T(8,128)(2,1)} %get-tuple-element.50), channel_id=1, source_target_pairs={{9,1},{13,5},{18,10},{22,14},{27,19},{31,23}} | collective-permute-start | bytes 1769480 | tf_op jit(solution)/shard_map/ppermute | solution.py:317
  27.4 21.0 %collective-permute-start = (bf16[3,256,384]{2,1,0:T(8,128)(2,1)}, bf16[3,256,384]{2,1,0:T(8,128)(2,1)S(1)}, u32[]{:S(2)}, u32[]{:S(2)}) collective-permute-start(bf16[3,256,384]{2,1,0:T(8,128)(2,1)} %get-tuple-element.46), channel_id=1, source_target_pairs={{0,1},{1,0},{2,3},{3,2},{4,5},{5,4},{6,7},{7,6},{8,9},{9,8},{10,11... | collective-permute-start | bytes 1769480 | tf_op jit(solution)/shard_map/ppermute | solution.py:317
  31.0 32.9 %copy-start.7 = (bf16[96,3072]{1,0:T(8,128)(2,1)}, bf16[96,3072]{1,0:T(8,128)(2,1)S(1)}, u32[]{:S(2)}) copy-start(bf16[96,3072]{1,0:T(8,128)(2,1)S(1)} %broadcast_select_fusion.2) | copy-start | bytes 1769476
  35.9 28.0 %collective-permute-start.1 = (bf16[3,256,384]{2,1,0:T(8,128)(2,1)S(1)}, bf16[3,256,384]{2,1,0:T(8,128)(2,1)S(1)}, u32[]{:S(2)}, u32[]{:S(2)}) collective-permute-start(bf16[3,256,384]{2,1,0:T(8,128)(2,1)S(1)} %copy-done.27), channel_id=1, source_target_pairs={{0,2},{1,3},{2,0},{3,1},{4,6},{5,7},{6,4},{7,5},{8,10},{9,11},{10,... | collective-permute-start | bytes 1769480 | tf_op jit(solution)/shard_map/ppermute | solution.py:317
  35.9 31.0 %collective-permute-start.2 = (bf16[3,256,384]{2,1,0:T(8,128)(2,1)}, bf16[3,256,384]{2,1,0:T(8,128)(2,1)S(1)}, u32[]{:S(2)}, u32[]{:S(2)}) collective-permute-start(bf16[3,256,384]{2,1,0:T(8,128)(2,1)} %get-tuple-element.48), channel_id=1, source_target_pairs={{0,3},{1,2},{2,1},{3,0},{4,7},{5,6},{6,5},{7,4},{8,11},{9,10},{10,... | collective-permute-start | bytes 1769480 | tf_op jit(solution)/shard_map/ppermute | solution.py:317
  48.4 18.5 %copy-start = (bf16[3,256,384]{2,1,0:T(8,128)(2,1)}, bf16[3,256,384]{2,1,0:T(8,128)(2,1)S(1)}, u32[]{:S(2)}) copy-start(bf16[3,256,384]{2,1,0:T(8,128)(2,1)S(1)} %collective-permute-done.refs_1_) | copy-start | bytes 1769476
  48.4 17.0 %collective-permute-start.9 = (bf16[96,3072]{1,0:T(8,128)(2,1)S(1)}, bf16[96,3072]{1,0:T(8,128)(2,1)}, u32[]{:S(2)}, u32[]{:S(2)}) collective-permute-start(bf16[96,3072]{1,0:T(8,128)(2,1)S(1)} %broadcast_select_fusion.2), channel_id=1, source_target_pairs={{8,16},{10,2},{12,20},{14,6},{17,25},{19,11},{21,29},{23,15}} | collective-permute-start | bytes 1769480 | tf_op jit(solution)/shard_map/ppermute | solution.py:317
  49.9 50.2 %collective-permute-start.20 = (bf16[256,1536]{1,0:T(8,128)(2,1)S(1)}, bf16[256,1536]{1,0:T(8,128)(2,1)}, u32[]{:S(2)}, u32[]{:S(2)}) collective-permute-start(bf16[256,1536]{1,0:T(8,128)(2,1)S(1)} %get-tuple-element.59.refs_0_.refs_6_), channel_id=1, source_target_pairs={{0,2},{1,3},{2,0},{3,1},{4,6},{5,7},{6,4},{7,5},{8,10},{9,11},{10,... | collective-permute-start | bytes 2359304 | tf_op jit(solution)/shard_map/ppermute | solution.py:317
  49.9 44.9 %collective-permute-start.14 = (bf16[256,1536]{1,0:T(8,128)(2,1)}, bf16[256,1536]{1,0:T(8,128)(2,1)}, u32[]{:S(2)}, u32[]{:S(2)}) collective-permute-start(bf16[256,1536]{1,0:T(8,128)(2,1)} %collective-permute-done.12.refs_1_.refs_3_), channel_id=1, source_target_pairs={{0,2},{1,3},{2,0},{3,1},{4,6},{5,7},{6,4},{7,5},{8,10},{9,11},{10,... | collective-permute-start | bytes 2359304 | tf_op jit(solution)/shard_map/ppermute | solution.py:317
  63.9 16.4 %collective-permute-start.5 = (bf16[96,3072]{1,0:T(8,128)(2,1)}, bf16[96,3072]{1,0:T(8,128)(2,1)}, u32[]{:S(2)}, u32[]{:S(2)}) collective-permute-start(bf16[96,3072]{1,0:T(8,128)(2,1)} %broadcast_select_fusion.3), channel_id=1, source_target_pairs={{8,16},{10,2},{12,20},{14,6},{17,25},{19,11},{21,29},{23,15}} | collective-permute-start | bytes 1769480 | tf_op jit(solution)/shard_map/ppermute | solution.py:317
  65.4 35.4 %collective-permute-start.10 = (bf16[96,3072]{1,0:T(8,128)(2,1)}, bf16[96,3072]{1,0:T(8,128)(2,1)}, u32[]{:S(2)}, u32[]{:S(2)}) collective-permute-start(bf16[96,3072]{1,0:T(8,128)(2,1)} %collective-permute-done.9), channel_id=1, source_target_pairs={{11,3},{15,7},{16,24},{20,28}} | collective-permute-start | bytes 1769480 | tf_op jit(solution)/shard_map/ppermute | solution.py:317
  80.3 39.3 %collective-permute-start.19 = (bf16[256,1536]{1,0:T(8,128)(2,1)S(1)}, bf16[256,1536]{1,0:T(8,128)(2,1)S(1)}, u32[]{:S(2)}, u32[]{:S(2)}) collective-permute-start(bf16[256,1536]{1,0:T(8,128)(2,1)S(1)} %get-tuple-element.59.refs_0_.refs_6_), channel_id=1, source_target_pairs={{0,1},{1,0},{2,3},{3,2},{4,5},{5,4},{6,7},{7,6},{8,9},{9,8},{10,11... | collective-permute-start | bytes 2359304 | tf_op jit(solution)/shard_map/ppermute | solution.py:317
  80.4 20.5 %collective-permute-start.6 = (bf16[96,3072]{1,0:T(8,128)(2,1)}, bf16[96,3072]{1,0:T(8,128)(2,1)}, u32[]{:S(2)}, u32[]{:S(2)}) collective-permute-start(bf16[96,3072]{1,0:T(8,128)(2,1)} %collective-permute-done.5), channel_id=1, source_target_pairs={{11,3},{15,7},{16,24},{20,28}} | collective-permute-start | bytes 1769480 | tf_op jit(solution)/shard_map/ppermute | solution.py:317
  100.1 2.2 %collective-permute-start.15 = (bf16[4,48,1536]{2,1,0:T(8,128)(2,1)}, bf16[4,48,1536]{2,1,0:T(8,128)(2,1)S(1)}, u32[]{:S(2)}, u32[]{:S(2)}) collective-permute-start(bf16[4,48,1536]{2,1,0:T(8,128)(2,1)} %get-tuple-element.54), channel_id=1, source_target_pairs={{0,4},{1,5},{2,6},{3,7},{4,0},{5,1},{6,2},{7,3},{8,12},{9,13},{10,... | collective-permute-start | bytes 1769480 | tf_op jit(solution)/shard_map/ppermute | solution.py:317
  100.1 20.9 %collective-permute-start.21 = (bf16[256,1536]{1,0:T(8,128)(2,1)}, bf16[256,1536]{1,0:T(8,128)(2,1)}, u32[]{:S(2)}, u32[]{:S(2)}) collective-permute-start(bf16[256,1536]{1,0:T(8,128)(2,1)} %collective-permute-done.20.refs_2_.refs_8_), channel_id=1, source_target_pairs={{0,1},{1,0},{2,3},{3,2},{4,5},{5,4},{6,7},{7,6},{8,9},{9,8},{10,11... | collective-permute-start | bytes 2359304 | tf_op jit(solution)/shard_map/ppermute | solution.py:317
  102.4 9.1 %collective-permute-start.16 = (bf16[48,1536]{1,0:T(8,128)(2,1)S(1)}, bf16[48,1536]{1,0:T(8,128)(2,1)S(1)}, u32[]{:S(2)}, u32[]{:S(2)}) collective-permute-start(bf16[48,1536]{1,0:T(8,128)(2,1)S(1)} %get-tuple-element.96), channel_id=1, source_target_pairs={{0,8},{1,9},{2,10},{3,11},{4,12},{5,13},{6,14},{7,15},{8,16},{9,17... | collective-permute-start | bytes 442376 | tf_op jit(solution)/shard_map/ppermute | solution.py:317
  105.5 11.8 %collective-permute-start.17 = (bf16[48,1536]{1,0:T(8,128)(2,1)S(1)}, bf16[48,1536]{1,0:T(8,128)(2,1)S(1)}, u32[]{:S(2)}, u32[]{:S(2)}) collective-permute-start(bf16[48,1536]{1,0:T(8,128)(2,1)S(1)} %get-tuple-element.95), channel_id=1, source_target_pairs={{0,16},{1,17},{2,18},{3,19},{4,20},{5,21},{6,22},{7,23},{8,24},{9,... | collective-permute-start | bytes 442376 | tf_op jit(solution)/shard_map/ppermute | solution.py:317
  107.3 10.0 %collective-permute-start.18 = (bf16[48,1536]{1,0:T(8,128)(2,1)S(1)}, bf16[48,1536]{1,0:T(8,128)(2,1)S(1)}, u32[]{:S(2)}, u32[]{:S(2)}) collective-permute-start(bf16[48,1536]{1,0:T(8,128)(2,1)S(1)} %get-tuple-element.94), channel_id=1, source_target_pairs={{0,24},{1,25},{2,26},{3,27},{4,28},{5,29},{6,30},{7,31},{8,0},{9,1... | collective-permute-start | bytes 442376 | tf_op jit(solution)/shard_map/ppermute | solution.py:317
  111.6 20.3 %collective-permute-start.11 = (bf16[192,3072]{1,0:T(8,128)(2,1)}, bf16[192,3072]{1,0:T(8,128)(2,1)}, u32[]{:S(2)}, u32[]{:S(2)}) collective-permute-start(bf16[192,3072]{1,0:T(8,128)(2,1)} %pad_maximum_fusion), channel_id=1, source_target_pairs={{0,4},{1,5},{2,6},{3,7},{4,0},{5,1},{6,2},{7,3},{8,12},{9,13},{10,... | collective-permute-start | bytes 3538952 | tf_op jit(solution)/shard_map/ppermute | solution.py:317
  117.5 8.7 %collective-permute-start.34 = (bf16[48,1536]{1,0:T(8,128)(2,1)S(1)}, bf16[48,1536]{1,0:T(8,128)(2,1)S(1)}, u32[]{:S(2)}, u32[]{:S(2)}) collective-permute-start(bf16[48,1536]{1,0:T(8,128)(2,1)S(1)} %fusion.2), channel_id=1, source_target_pairs={{0,3},{1,2},{2,1},{3,0},{4,7},{5,6},{6,5},{7,4},{8,11},{9,10},{10,... | collective-permute-start | bytes 442376 | tf_op jit(solution)/shard_map/ppermute | solution.py:317
  119.1 8.2 %collective-permute-start.33 = (bf16[48,1536]{1,0:T(8,128)(2,1)S(1)}, bf16[48,1536]{1,0:T(8,128)(2,1)S(1)}, u32[]{:S(2)}, u32[]{:S(2)}) collective-permute-start(bf16[48,1536]{1,0:T(8,128)(2,1)S(1)} %fusion.2), channel_id=1, source_target_pairs={{0,2},{1,3},{2,0},{3,1},{4,6},{5,7},{6,4},{7,5},{8,10},{9,11},{10,... | collective-permute-start | bytes 442376 | tf_op jit(solution)/shard_map/ppermute | solution.py:317
  119.6 7.7 %collective-permute-start.32 = (bf16[48,1536]{1,0:T(8,128)(2,1)S(1)}, bf16[48,1536]{1,0:T(8,128)(2,1)S(1)}, u32[]{:S(2)}, u32[]{:S(2)}) collective-permute-start(bf16[48,1536]{1,0:T(8,128)(2,1)S(1)} %fusion.2), channel_id=1, source_target_pairs={{0,1},{1,0},{2,3},{3,2},{4,5},{5,4},{6,7},{7,6},{8,9},{9,8},{10,11... | collective-permute-start | bytes 442376 | tf_op jit(solution)/shard_map/ppermute | solution.py:317
  126.1 9.0 %collective-permute-start.22 = (bf16[4,48,1536]{2,1,0:T(8,128)(2,1)}, bf16[4,48,1536]{2,1,0:T(8,128)(2,1)S(1)}, u32[]{:S(2)}, u32[]{:S(2)}) collective-permute-start(bf16[4,48,1536]{2,1,0:T(8,128)(2,1)} %get-tuple-element.61), channel_id=1, source_target_pairs={{0,4},{1,5},{2,6},{3,7},{4,0},{5,1},{6,2},{7,3},{8,12},{9,13},{10,... | collective-permute-start | bytes 1769480 | tf_op jit(solution)/shard_map/ppermute | solution.py:317
  128.0 7.1 %copy-start.10 = (bf16[4,48,1536]{2,1,0:T(8,128)(2,1)S(1)}, bf16[4,48,1536]{2,1,0:T(8,128)(2,1)}, u32[]{:S(2)}) copy-start(bf16[4,48,1536]{2,1,0:T(8,128)(2,1)} %get-tuple-element.60) | copy-start | bytes 1769476
  128.1 46.8 %collective-permute-start.35 = (bf16[48,1536]{1,0:T(8,128)(2,1)S(1)}, bf16[48,1536]{1,0:T(8,128)(2,1)S(1)}, u32[]{:S(2)}, u32[]{:S(2)}) collective-permute-start(bf16[48,1536]{1,0:T(8,128)(2,1)S(1)} %get-tuple-element.105), channel_id=1, source_target_pairs={{0,8},{1,9},{2,10},{3,11},{4,12},{5,13},{6,14},{7,15},{8,16},{9,17... | collective-permute-start | bytes 442376 | tf_op jit(solution)/shard_map/ppermute | solution.py:317
  135.3 18.9 %collective-permute-start.38 = (bf16[48,1536]{1,0:T(8,128)(2,1)S(1)}, bf16[48,1536]{1,0:T(8,128)(2,1)S(1)}, u32[]{:S(2)}, u32[]{:S(2)}) collective-permute-start(bf16[48,1536]{1,0:T(8,128)(2,1)S(1)} %get-tuple-element.92), channel_id=1, source_target_pairs={{0,8},{1,9},{2,10},{3,11},{4,12},{5,13},{6,14},{7,15},{8,16},{9,17... | collective-permute-start | bytes 442376 | tf_op jit(solution)/shard_map/ppermute | solution.py:317
  135.4 18.8 %collective-permute-start.39 = (bf16[48,1536]{1,0:T(8,128)(2,1)S(1)}, bf16[48,1536]{1,0:T(8,128)(2,1)S(1)}, u32[]{:S(2)}, u32[]{:S(2)}) collective-permute-start(bf16[48,1536]{1,0:T(8,128)(2,1)S(1)} %get-tuple-element.91), channel_id=1, source_target_pairs={{0,16},{1,17},{2,18},{3,19},{4,20},{5,21},{6,22},{7,23},{8,24},{9,... | collective-permute-start | bytes 442376 | tf_op jit(solution)/shard_map/ppermute | solution.py:317
  137.1 17.2 %collective-permute-start.40 = (bf16[48,1536]{1,0:T(8,128)(2,1)S(1)}, bf16[48,1536]{1,0:T(8,128)(2,1)S(1)}, u32[]{:S(2)}, u32[]{:S(2)}) collective-permute-start(bf16[48,1536]{1,0:T(8,128)(2,1)S(1)} %get-tuple-element.90), channel_id=1, source_target_pairs={{0,24},{1,25},{2,26},{3,27},{4,28},{5,29},{6,30},{7,31},{8,0},{9,1... | collective-permute-start | bytes 442376 | tf_op jit(solution)/shard_map/ppermute | solution.py:317
  153.7 22.7 %collective-permute-start.23 = (bf16[3,256,128]{2,1,0:T(8,128)(2,1)}, bf16[3,256,128]{2,1,0:T(8,128)(2,1)S(1)}, u32[]{:S(2)}, u32[]{:S(2)}) collective-permute-start(bf16[3,256,128]{2,1,0:T(8,128)(2,1)} %get-tuple-element.65), channel_id=1, source_target_pairs={{0,1},{1,0},{2,3},{3,2},{4,5},{5,4},{6,7},{7,6},{8,9},{9,8},{10,11... | collective-permute-start | bytes 589832 | tf_op jit(solution)/shard_map/ppermute | solution.py:317
  154.3 16.9 %collective-permute-start.41 = (bf16[48,1536]{1,0:T(8,128)(2,1)S(1)}, bf16[48,1536]{1,0:T(8,128)(2,1)S(1)}, u32[]{:S(2)}, u32[]{:S(2)}) collective-permute-start(bf16[48,1536]{1,0:T(8,128)(2,1)S(1)} %add_convert_fusion), channel_id=1, source_target_pairs={{0,1},{1,0},{2,3},{3,2},{4,5},{5,4},{6,7},{7,6},{8,9},{9,8},{10,11... | collective-permute-start | bytes 442376 | tf_op jit(solution)/shard_map/ppermute | solution.py:317
  155.9 16.8 %collective-permute-start.42 = (bf16[48,1536]{1,0:T(8,128)(2,1)S(1)}, bf16[48,1536]{1,0:T(8,128)(2,1)S(1)}, u32[]{:S(2)}, u32[]{:S(2)}) collective-permute-start(bf16[48,1536]{1,0:T(8,128)(2,1)S(1)} %add_convert_fusion), channel_id=1, source_target_pairs={{0,2},{1,3},{2,0},{3,1},{4,6},{5,7},{6,4},{7,5},{8,10},{9,11},{10,... | collective-permute-start | bytes 442376 | tf_op jit(solution)/shard_map/ppermute | solution.py:317
  156.5 17.8 %collective-permute-start.43 = (bf16[48,1536]{1,0:T(8,128)(2,1)S(1)}, bf16[48,1536]{1,0:T(8,128)(2,1)S(1)}, u32[]{:S(2)}, u32[]{:S(2)}) collective-permute-start(bf16[48,1536]{1,0:T(8,128)(2,1)S(1)} %add_convert_fusion), channel_id=1, source_target_pairs={{0,3},{1,2},{2,1},{3,0},{4,7},{5,6},{6,5},{7,4},{8,11},{9,10},{10,... | collective-permute-start | bytes 442376 | tf_op jit(solution)/shard_map/ppermute | solution.py:317
  164.5 8.3 %copy-start.31 = (bf16[3,256,128]{2,1,0:T(8,128)(2,1)S(1)}, bf16[3,256,128]{2,1,0:T(8,128)(2,1)}, u32[]{:S(2)}) copy-start(bf16[3,256,128]{2,1,0:T(8,128)(2,1)} %get-tuple-element.67) | copy-start | bytes 589828
  164.5 9.8 %copy-start.35 = (bf16[3,256,128]{2,1,0:T(8,128)(2,1)S(1)}, bf16[3,256,128]{2,1,0:T(8,128)(2,1)}, u32[]{:S(2)}) copy-start(bf16[3,256,128]{2,1,0:T(8,128)(2,1)} %get-tuple-element.69) | copy-start | bytes 589828
  171.1 13.2 %copy-start.30 = (bf16[3,256,128]{2,1,0:T(8,128)(2,1)S(1)}, bf16[3,256,128]{2,1,0:T(8,128)(2,1)}, u32[]{:S(2)}) copy-start(bf16[3,256,128]{2,1,0:T(8,128)(2,1)} %get-tuple-element.73) | copy-start | bytes 589828
  171.2 14.1 %copy-start.29 = (bf16[3,256,128]{2,1,0:T(8,128)(2,1)S(1)}, bf16[3,256,128]{2,1,0:T(8,128)(2,1)}, u32[]{:S(2)}) copy-start(bf16[3,256,128]{2,1,0:T(8,128)(2,1)} %get-tuple-element.74) | copy-start | bytes 589828
  171.2 15.3 %copy-start.28 = (bf16[3,256,128]{2,1,0:T(8,128)(2,1)S(1)}, bf16[3,256,128]{2,1,0:T(8,128)(2,1)}, u32[]{:S(2)}) copy-start(bf16[3,256,128]{2,1,0:T(8,128)(2,1)} %get-tuple-element.75) | copy-start | bytes 589828
  171.2 13.1 %collective-permute-start.24 = (bf16[3,256,128]{2,1,0:T(8,128)(2,1)S(1)}, bf16[3,256,128]{2,1,0:T(8,128)(2,1)S(1)}, u32[]{:S(2)}, u32[]{:S(2)}) collective-permute-start(bf16[3,256,128]{2,1,0:T(8,128)(2,1)S(1)} %copy-done.33), channel_id=1, source_target_pairs={{0,2},{1,3},{2,0},{3,1},{4,6},{5,7},{6,4},{7,5},{8,10},{9,11},{10,... | collective-permute-start | bytes 589832 | tf_op jit(solution)/shard_map/ppermute | solution.py:317
  172.7 12.5 %collective-permute-start.25 = (bf16[3,256,128]{2,1,0:T(8,128)(2,1)S(1)}, bf16[3,256,128]{2,1,0:T(8,128)(2,1)S(1)}, u32[]{:S(2)}, u32[]{:S(2)}) collective-permute-start(bf16[3,256,128]{2,1,0:T(8,128)(2,1)S(1)} %copy-done.31), channel_id=1, source_target_pairs={{0,3},{1,2},{2,1},{3,0},{4,7},{5,6},{6,5},{7,4},{8,11},{9,10},{10,... | collective-permute-start | bytes 589832 | tf_op jit(solution)/shard_map/ppermute | solution.py:317
  174.3 12.2 %collective-permute-start.26 = (bf16[3,256,128]{2,1,0:T(8,128)(2,1)S(1)}, bf16[3,256,128]{2,1,0:T(8,128)(2,1)S(1)}, u32[]{:S(2)}, u32[]{:S(2)}) collective-permute-start(bf16[3,256,128]{2,1,0:T(8,128)(2,1)S(1)} %copy-done.35), channel_id=1, source_target_pairs={{0,1},{1,0},{2,3},{3,2},{4,5},{5,4},{6,7},{7,6},{8,9},{9,8},{10,11... | collective-permute-start | bytes 589832 | tf_op jit(solution)/shard_map/ppermute | solution.py:317
  174.9 29.2 %copy-start.21 = (bf16[48,1536]{1,0:T(8,128)(2,1)}, bf16[48,1536]{1,0:T(8,128)(2,1)S(1)}, u32[]{:S(2)}) copy-start(bf16[48,1536]{1,0:T(8,128)(2,1)S(1)} %collective-permute-done.35.refs_1_) | copy-start | bytes 442372
  174.9 17.9 %collective-permute-start.27 = (bf16[3,256,128]{2,1,0:T(8,128)(2,1)S(1)}, bf16[3,256,128]{2,1,0:T(8,128)(2,1)S(1)}, u32[]{:S(2)}, u32[]{:S(2)}) collective-permute-start(bf16[3,256,128]{2,1,0:T(8,128)(2,1)S(1)} %copy-done.34), channel_id=1, source_target_pairs={{0,2},{1,3},{2,0},{3,1},{4,6},{5,7},{6,4},{7,5},{8,10},{9,11},{10,... | collective-permute-start | bytes 589832 | tf_op jit(solution)/shard_map/ppermute | solution.py:317
  176.4 23.1 %copy-start.12 = (bf16[3,256,128]{2,1,0:T(8,128)(2,1)}, bf16[3,256,128]{2,1,0:T(8,128)(2,1)S(1)}, u32[]{:S(2)}) copy-start(bf16[3,256,128]{2,1,0:T(8,128)(2,1)S(1)} %collective-permute-done.23.refs_1_) | copy-start | bytes 589828
  176.4 17.7 %collective-permute-start.28 = (bf16[3,256,128]{2,1,0:T(8,128)(2,1)S(1)}, bf16[3,256,128]{2,1,0:T(8,128)(2,1)S(1)}, u32[]{:S(2)}, u32[]{:S(2)}) collective-permute-start(bf16[3,256,128]{2,1,0:T(8,128)(2,1)S(1)} %copy-done.32), channel_id=1, source_target_pairs={{0,3},{1,2},{2,1},{3,0},{4,7},{5,6},{6,5},{7,4},{8,11},{9,10},{10,... | collective-permute-start | bytes 589832 | tf_op jit(solution)/shard_map/ppermute | solution.py:317
  184.3 15.2 %copy-start.13 = (bf16[3,256,128]{2,1,0:T(8,128)(2,1)}, bf16[3,256,128]{2,1,0:T(8,128)(2,1)S(1)}, u32[]{:S(2)}) copy-start(bf16[3,256,128]{2,1,0:T(8,128)(2,1)S(1)} %collective-permute-done.24.refs_2_) | copy-start | bytes 589828
  184.3 11.0 %collective-permute-start.29 = (bf16[3,256,128]{2,1,0:T(8,128)(2,1)S(1)}, bf16[3,256,128]{2,1,0:T(8,128)(2,1)S(1)}, u32[]{:S(2)}, u32[]{:S(2)}) collective-permute-start(bf16[3,256,128]{2,1,0:T(8,128)(2,1)S(1)} %copy-done.30), channel_id=1, source_target_pairs={{0,1},{1,0},{2,3},{3,2},{4,5},{5,4},{6,7},{7,6},{8,9},{9,8},{10,11... | collective-permute-start | bytes 589832 | tf_op jit(solution)/shard_map/ppermute | solution.py:317
  185.3 14.3 %copy-start.14 = (bf16[3,256,128]{2,1,0:T(8,128)(2,1)}, bf16[3,256,128]{2,1,0:T(8,128)(2,1)S(1)}, u32[]{:S(2)}) copy-start(bf16[3,256,128]{2,1,0:T(8,128)(2,1)S(1)} %collective-permute-done.25.refs_3_) | copy-start | bytes 589828
  185.3 12.0 %collective-permute-start.30 = (bf16[3,256,128]{2,1,0:T(8,128)(2,1)S(1)}, bf16[3,256,128]{2,1,0:T(8,128)(2,1)S(1)}, u32[]{:S(2)}, u32[]{:S(2)}) collective-permute-start(bf16[3,256,128]{2,1,0:T(8,128)(2,1)S(1)} %copy-done.29), channel_id=1, source_target_pairs={{0,2},{1,3},{2,0},{3,1},{4,6},{5,7},{6,4},{7,5},{8,10},{9,11},{10,... | collective-permute-start | bytes 589832 | tf_op jit(solution)/shard_map/ppermute | solution.py:317
  186.5 13.0 %copy-start.15 = (bf16[3,256,128]{2,1,0:T(8,128)(2,1)}, bf16[3,256,128]{2,1,0:T(8,128)(2,1)S(1)}, u32[]{:S(2)}) copy-start(bf16[3,256,128]{2,1,0:T(8,128)(2,1)S(1)} %collective-permute-done.26.refs_5_) | copy-start | bytes 589828
  186.5 11.8 %collective-permute-start.31 = (bf16[3,256,128]{2,1,0:T(8,128)(2,1)S(1)}, bf16[3,256,128]{2,1,0:T(8,128)(2,1)S(1)}, u32[]{:S(2)}, u32[]{:S(2)}) collective-permute-start(bf16[3,256,128]{2,1,0:T(8,128)(2,1)S(1)} %copy-done.28), channel_id=1, source_target_pairs={{0,3},{1,2},{2,1},{3,0},{4,7},{5,6},{6,5},{7,4},{8,11},{9,10},{10,... | collective-permute-start | bytes 589832 | tf_op jit(solution)/shard_map/ppermute | solution.py:317
  192.8 11.4 %collective-permute-start.36 = (bf16[48,1536]{1,0:T(8,128)(2,1)S(1)}, bf16[48,1536]{1,0:T(8,128)(2,1)S(1)}, u32[]{:S(2)}, u32[]{:S(2)}) collective-permute-start(bf16[48,1536]{1,0:T(8,128)(2,1)S(1)} %get-tuple-element.104), channel_id=1, source_target_pairs={{0,16},{1,17},{2,18},{3,19},{4,20},{5,21},{6,22},{7,23},{8,24},{9,... | collective-permute-start | bytes 442376 | tf_op jit(solution)/shard_map/ppermute | solution.py:317
  194.1 10.1 %collective-permute-start.37 = (bf16[48,1536]{1,0:T(8,128)(2,1)S(1)}, bf16[48,1536]{1,0:T(8,128)(2,1)S(1)}, u32[]{:S(2)}, u32[]{:S(2)}) collective-permute-start(bf16[48,1536]{1,0:T(8,128)(2,1)S(1)} %get-tuple-element.103), channel_id=1, source_target_pairs={{0,24},{1,25},{2,26},{3,27},{4,28},{5,29},{6,30},{7,31},{8,0},{9,1... | collective-permute-start | bytes 442376 | tf_op jit(solution)/shard_map/ppermute | solution.py:317
  195.3 9.5 %collective-permute-start.44 = (bf16[48,1536]{1,0:T(8,128)(2,1)S(1)}, bf16[48,1536]{1,0:T(8,128)(2,1)S(1)}, u32[]{:S(2)}, u32[]{:S(2)}) collective-permute-start(bf16[48,1536]{1,0:T(8,128)(2,1)S(1)} %get-tuple-element.101), channel_id=1, source_target_pairs={{0,8},{1,9},{2,10},{3,11},{4,12},{5,13},{6,14},{7,15},{8,16},{9,17... | collective-permute-start | bytes 442376 | tf_op jit(solution)/shard_map/ppermute | solution.py:317
  197.3 13.8 %collective-permute-start.45 = (bf16[48,1536]{1,0:T(8,128)(2,1)S(1)}, bf16[48,1536]{1,0:T(8,128)(2,1)S(1)}, u32[]{:S(2)}, u32[]{:S(2)}) collective-permute-start(bf16[48,1536]{1,0:T(8,128)(2,1)S(1)} %get-tuple-element.100), channel_id=1, source_target_pairs={{0,16},{1,17},{2,18},{3,19},{4,20},{5,21},{6,22},{7,23},{8,24},{9,... | collective-permute-start | bytes 442376 | tf_op jit(solution)/shard_map/ppermute | solution.py:317
  198.3 12.8 %collective-permute-start.46 = (bf16[48,1536]{1,0:T(8,128)(2,1)S(1)}, bf16[48,1536]{1,0:T(8,128)(2,1)S(1)}, u32[]{:S(2)}, u32[]{:S(2)}) collective-permute-start(bf16[48,1536]{1,0:T(8,128)(2,1)S(1)} %get-tuple-element.99), channel_id=1, source_target_pairs={{0,24},{1,25},{2,26},{3,27},{4,28},{5,29},{6,30},{7,31},{8,0},{9,1... | collective-permute-start | bytes 442376 | tf_op jit(solution)/shard_map/ppermute | solution.py:317
  (19 other events, 75.8 us)
where the time goes:
time: 216 us; the launch traced here: 215 us
  waiting for transfers between devices  71.6 us (33%)
  starting transfers between devices  65.5 us (30%)
  Pallas kernels  62.6 us (29%)
  other arithmetic  7.91 us (4%)
  local copies, waits for them, and re-layouts  6.65 us (3%)
    ppermute x47, waiting for transfers between devices, send(): return lax.ppermute(array, ('fsdp', 'rows'), pairs)  71.6 us
    ppermute x47, starting transfers between devices, send(): return lax.ppermute(array, ('fsdp', 'rows'), pairs)  65.5 us
    pallas_call x3, Pallas kernels, backward(): pl.pallas_call(body, grid=(1,), in_specs=[part] * rows + [pl.BlockSpec((1...  19.8 us
    pallas_call x1, Pallas kernels, forward(): pl.pallas_call(body, grid=(heads,), in_specs=[part] * rows, out_specs=[pl...  12.6 us
    pallas_call x2, Pallas kernels, weight_terms(): pl.pallas_call(body, grid_spec=pltpu.PrefetchScalarGridSpec(num_scalar_pr...  10.4 us
    pallas_call x1, Pallas kernels, project(): pl.pallas_call(body, grid=(chunks * steps,), in_specs=[pl.BlockSpec((half...  7.23 us
    pallas_call x1, Pallas kernels, pack(): pl.pallas_call(body, grid_spec=pltpu.PrefetchScalarGridSpec(num_scalar_pr...  4.64 us
    pallas_call x1, Pallas kernels, unpack(): pl.pallas_call(body, grid_spec=pltpu.PrefetchScalarGridSpec(num_scalar_pr...  4.47 us
  transfers between devices with their start and end apart: 47, of which 15 were waited for; matrix products, arithmetic and copies ran while one was open for 5% of the time, Pallas kernels for 25%

commit v1 on v0

--- a/solution.py
+++ b/solution.py
@@ -57,8 +57,10 @@
 
 
 def unpack(place, parts):
-    heads, rows = len(parts), len(parts[0])
-    _, tokens, width = parts[0][0].shape
+    calls, rows = len(parts), len(parts[0])
+    tokens = parts[0][0].shape[1]
+    widths = [part[0].shape[2] for part in parts]
+    starts = [sum(widths[:at]) for at in range(calls + 1)]
 
     def body(place_ref, *refs):
         ins, outs = refs[:-3], refs[-3:]
@@ -66,28 +68,26 @@
 
             @pl.when(pl.program_id(0) == slot)
             def _():
-                for head in range(heads):
+                for call in range(calls):
                     for at in range(3):
-                        outs[at][0, :, head * width : (head + 1) * width] = ins[
-                            head * rows + slot
+                        outs[at][0, :, starts[call] : starts[call + 1]] = ins[
+                            call * rows + slot
                         ][at]
 
-    part = pl.BlockSpec(
-        (1, tokens, width * heads), lambda j, place_ref: (0, 0, place_ref[0] ^ j)
-    )
-    full = jax.ShapeDtypeStruct((1, tokens, width * heads * rows), parts[0][0].dtype)
+    part = pl.BlockSpec((1, tokens, starts[-1]), lambda j, place_ref: (0, 0, place_ref[0] ^ j))
+    full = jax.ShapeDtypeStruct((1, tokens, starts[-1] * rows), parts[0][0].dtype)
     return pl.pallas_call(
         body,
         grid_spec=pltpu.PrefetchScalarGridSpec(
             num_scalar_prefetch=1,
             grid=(rows,),
-            in_specs=[whole(parts[0][0].shape)] * (rows * heads),
+            in_specs=[whole(block.shape) for part in parts for block in part],
             out_specs=[part] * 3,
         ),
         out_shape=[full] * 3,
-        cost_estimate=cost(0, 12 * tokens * width * heads * rows),
+        cost_estimate=cost(0, 12 * tokens * starts[-1] * rows),
         name="unpack",
-    )(place, *(block for head in parts for block in head))
+    )(place, *(block for part in parts for block in part))
 
 
 def forward(parts):
@@ -130,7 +130,7 @@
     )(*parts)
 
 
-def backward(parts, probs, grad_attn, head):
+def backward(parts, probs, grad_attn, first, count):
     rows = len(parts)
     tokens = parts[0].shape[1]
     length = rows * tokens
@@ -159,31 +159,31 @@
             outs[slot][1] = grad_key[down].astype(jnp.bfloat16)
             outs[slot][2] = grad_value[down].astype(jnp.bfloat16)
 
-    part = pl.BlockSpec((3, tokens, HDIM), lambda i: (0, 0, head))
-    shape = (3, tokens, HDIM)
-    return pl.pallas_call(
-        body,
-        grid=(1,),
+    part = pl.BlockSpec((3, tokens, HDIM), lambda i: (0, 0, first + i))
+    shape = (3, tokens, count * HDIM)
+    return pl.pallas_call(
+        body,
+        grid=(count,),
         in_specs=[part] * rows
         + [
-            pl.BlockSpec((1, length, length), lambda i: (head, 0, 0)),
-            pl.BlockSpec((HDIM, length), lambda i: (head, 0)),
+            pl.BlockSpec((1, length, length), lambda i: (first + i, 0, 0)),
+            pl.BlockSpec((HDIM, length), lambda i: (first + i, 0)),
         ],
-        out_specs=[whole(shape)] * rows,
+        out_specs=[pl.BlockSpec((3, tokens, HDIM), lambda i: (0, 0, i))] * rows,
         out_shape=[jax.ShapeDtypeStruct(shape, jnp.bfloat16)] * rows,
-        cost_estimate=cost(8 * length * length * HDIM, 2 * length * length),
+        cost_estimate=cost(8 * count * length * length * HDIM, 2 * count * length * length),
         name="backward",
     )(*parts, probs, grad_attn)
 
 
-def project(weights, grads):
+def project(place, weights, grads):
     chunks, rows = len(grads), len(grads[0])
     half, depth = weights[0].shape
     tokens, wide = grads[0][0].shape
     steps = 2
     step = wide // steps
 
-    def body(*refs):
+    def body(place_ref, *refs):
         first, second = refs[:2]
         ins, out, total = refs[2:-2], refs[-2], refs[-1]
         at = pl.program_id(0)
@@ -203,25 +203,33 @@
 
         @pl.when(at == chunks * steps - 1)
         def _():
-            out[...] = total[...].astype(out.dtype)
+            for core in range(2):
+
+                @pl.when(place_ref[2] == core)
+                def _():
+                    out[core * half : (core + 1) * half] = total[:half].astype(out.dtype)
+                    out[(1 - core) * half : (2 - core) * half] = total[half:].astype(out.dtype)
 
     def block_of(chunk):
         return pl.BlockSpec(
-            (tokens, step), lambda i: (0, jnp.clip(i - chunk * steps, 0, steps - 1))
+            (tokens, step), lambda i, place_ref: (0, jnp.clip(i - chunk * steps, 0, steps - 1))
         )
 
     shape = (2 * half, rows * tokens)
     return pl.pallas_call(
         body,
-        grid=(chunks * steps,),
-        in_specs=[pl.BlockSpec((half, step), lambda i: (0, i))] * 2
-        + [block_of(chunk) for chunk in range(chunks) for _ in range(rows)],
-        out_specs=whole(shape),
+        grid_spec=pltpu.PrefetchScalarGridSpec(
+            num_scalar_prefetch=1,
+            grid=(chunks * steps,),
+            in_specs=[pl.BlockSpec((half, step), lambda i, place_ref: (0, i))] * 2
+            + [block_of(chunk) for chunk in range(chunks) for _ in range(rows)],
+            out_specs=whole(shape),
+            scratch_shapes=[pltpu.VMEM(shape, jnp.float32)],
+        ),
         out_shape=jax.ShapeDtypeStruct(shape, jnp.bfloat16),
-        scratch_shapes=[pltpu.VMEM(shape, jnp.float32)],
         cost_estimate=cost(2 * shape[0] * shape[1] * depth, 2 * depth * (shape[0] + shape[1])),
         name="project",
-    )(*weights, *(block for chunk in grads for block in chunk))
+    )(place, *weights, *(block for chunk in grads for block in chunk))
 
 
 def weight_terms(place, attended, grads, planes):
@@ -269,10 +277,10 @@
     def body(place_ref, *refs):
         ins, out = refs[:-1], refs[-1]
         for chunk in range(chunks):
-            for back in range(planes):
-                start = ((place_ref[1] + planes - back) & (planes - 1)) * piece
+            for turn in range(planes):
+                start = (((place_ref[1] ^ place_ref[0]) - turn) & (planes - 1)) * piece
                 out[pl.ds(pl.multiple_of(start, 16), piece), chunk * wide : (chunk + 1) * wide] = (
-                    ins[chunk * planes + back][...].astype(out.dtype)
+                    ins[chunk * planes + turn][...].astype(out.dtype)
                 )
 
     shape = (planes * piece, chunks * wide)
@@ -292,11 +300,6 @@
 
 def after(value, *done):
     return lax.optimization_barrier((value, done))[0]
-
-
-def onward(planes, hop, z, c, r):
-    to = z + 1 if z > r else z - 1
-    return (to, c, r) if abs(z - r) == hop and 0 <= to < planes else None
 
 
 def by_heads(fsdp, rows, query_rows, key_rows, value_rows, grad_out, w_out):
@@ -327,38 +330,24 @@
 
     grad_flat = grad_out[0]
     wide = grad_flat.shape[1] // 2
-    own = [grad_flat[:, :wide], grad_flat[:, wide:]]
-    by_x, by_y = [to_row(own[0], 1)], [to_row(own[0], 2)]
+    left, right = grad_flat[:, :wide], grad_flat[:, wide:]
+    left_x, right_y = to_row(left, 1), to_row(right, 2)
 
     packed = pack(place, query_rows, key_rows, value_rows, rows)
     parts = [packed[0]] + [to_row(packed[slot], slot) for slot in range(1, rows)]
 
-    here = []
-    away = jnp.abs(plane - row)
-    cut = w_out.shape[0] // 2
-    for half in (w_out[:cut], w_out[cut:]):
-        half = after(half, packed[0])
-        above = send(half, lambda z, c, r: (z + 1, c, r) if z == r and z + 1 < planes else None)
-        below = send(half, lambda z, c, r: (z - 1, c, r) if z == r and z > 0 else None)
-        got = half
-        stage = jnp.where(plane > row, above, below)
-        for hop in range(1, planes):
-            got = jnp.where(away == hop, stage, got)
-            if hop + 1 < planes:
-                stage = send(stage, functools.partial(onward, planes, hop))
-        here.append(got)
-    here = jnp.concatenate(here, axis=0)
-    other = to_core(here)
-    weights = [jnp.where(core == 0, here, other), jnp.where(core == 0, other, here)]
+    here = w_out
+    for ahead in range(1, planes):
+        got = send(w_out, lambda z, c, r: ((z + ahead) % planes, c, r) if z == r else None)
+        here = jnp.where((plane - row) % planes == ahead, got, here)
+    weights = [here, to_core(here)]
+
+    hand_y, hand_x = to_row(left_x, 2), to_row(right_y, 1)
+    left, right = after((left, right), left_x, right_y)
+    left_y, right_x = to_row(left, 2), to_row(right, 1)
+    grads = [[left, left_x, left_y, hand_y], [right, right_x, right_y, hand_x]]
 
     probs, attended = forward(parts)
-
-    across = [to_row(by_x[0], 2)]
-    second = after(own[1], by_x[0], by_y[0])
-    by_x.append(to_row(second, 1))
-    by_y.append(to_row(second, 2))
-    across.append(to_row(by_y[1], 1))
-    grads = [[own[at], by_x[at], by_y[at], across[at]] for at in range(2)]
 
     def reduce_cores(attended, chunk):
         keep, give = weight_terms(place, attended, chunk, planes)
@@ -376,28 +365,26 @@
             total = total + part.astype(jnp.float32)
         return total.astype(jnp.bfloat16)
 
-    def gather_rows(total):
-        return [total] + [to_row(total, slot) for slot in range(1, rows)]
-
-    def to_owners(blocks):
-        stack = jnp.stack(blocks)
-        pieces = []
-        for ahead in range(planes):
-            block = lax.dynamic_index_in_dim(stack, ((plane + ahead) % planes) ^ row, 0, False)
-            pieces.append(to_plane(block, ahead) if ahead else block)
-        return pieces
-
-    first = reduce_planes(reduce_cores(attended, grads[0]))
-    blocks = gather_rows(first)
-    both = reduce_cores(after(attended, first), grads[1])
-    grad_attn = project(after(weights, both[0]), grads)
-    back = []
-    for head in range(probs.shape[0]):
-        sent = backward(parts, probs, grad_attn, head)
-        back.append([sent[0]] + [to_row(sent[slot], slot) for slot in range(1, rows)])
+    def deliver(total):
+        return [
+            send(total, lambda z, c, r: (r, c, r ^ ((z + turn) % planes)))
+            for turn in range(planes)
+        ]
+
+    both = [reduce_cores(attended, grads[0])]
+    both.append(reduce_cores(after(attended, both[0]), grads[1]))
+    grad_attn = project(place, after(weights, both[1]), grads)
+    heads = probs.shape[0]
+    back, sent = [], []
+    for first, count in ((0, 1), (1, heads - 1)):
+        sent.append(backward(parts, probs, grad_attn, first, count))
+        back.append([sent[-1][0]] + [to_row(sent[-1][slot], slot) for slot in range(1, rows)])
+        if not first:
+            early = reduce_planes(both[0], sent[0][0])
+            probs = after(probs, early)
+    late = reduce_planes(both[1], sent[1][0])
+    pieces = [deliver(early), deliver(late)]
     grad_query, grad_key, grad_value = unpack(place, back)
-    last = gather_rows(reduce_planes(both, back[0][0]))
-    pieces = [to_owners(blocks), to_owners(after(last, back[-1][0]))]
     grad_w_out = assemble(place, pieces, planes)
     return grad_query, grad_key, grad_value, grad_w_out
 

time: 216 us -> 260 us (1.20)
  waiting for transfers between devices: 71.6 us -> 105 us
  starting transfers between devices: 65.5 us -> 80.7 us
  other arithmetic: 7.91 us -> 5.08 us
    ppermute x47 -> x35, waiting for transfers between devices: 71.6 us -> 105 us  [send(): return lax.ppermute(array, ('fsdp', 'rows'), pairs)]
    ppermute x47 -> x35, starting transfers between devices: 65.5 us -> 80.7 us  [send(): return lax.ppermute(array, ('fsdp', 'rows'), pairs)]
    select_n x5 -> x1, other arithmetic: 5.57 us -> 0.21 us  [by_heads(): here = jnp.where((plane - row) % planes == ahead, got, here)]
    convert_element_type x2, other arithmetic: 0.25 us -> 3.01 us  [reduce_cores(): (keep[at].astype(jnp.float32) + got[at].astype(jnp.float32)).astype(jnp.b...]
    pallas_call x4 -> x3, Pallas kernels: 27 us -> 25 us  [the longest x2 17.1 us: backward(): pl.pallas_call(body, grid=(count,), in_specs=[part] * rows + [pl.BlockSpe...]
  transfers between devices with their start and end apart: 47 -> 35, of which waited for: 15 -> 12; matrix products, arithmetic and copies ran while one was open for 5% -> 2% of each run, Pallas kernels for 25% -> 22%
where the time goes in v1:
time: 260 us; the launch traced here: 258 us
  waiting for transfers between devices  105 us (40%)
  starting transfers between devices  80.7 us (31%)
  Pallas kernels  60.6 us (23%)
  local copies, waits for them, and re-layouts  5.1 us (2%)
  other arithmetic  5.08 us (2%)
    ppermute x35, waiting for transfers between devices, send(): return lax.ppermute(array, ('fsdp', 'rows'), pairs)  105 us
    ppermute x35, starting transfers between devices, send(): return lax.ppermute(array, ('fsdp', 'rows'), pairs)  80.7 us
    pallas_call x2, Pallas kernels, backward(): pl.pallas_call(body, grid=(count,), in_specs=[part] * rows + [pl.BlockSpe...  17.1 us
    pallas_call x1, Pallas kernels, forward(): pl.pallas_call(body, grid=(heads,), in_specs=[part] * rows, out_specs=[pl...  12.6 us
    pallas_call x2, Pallas kernels, weight_terms(): pl.pallas_call(body, grid_spec=pltpu.PrefetchScalarGridSpec(num_scalar_pr...  10.5 us
    pallas_call x1, Pallas kernels, project(): pl.pallas_call(body, grid_spec=pltpu.PrefetchScalarGridSpec(num_scalar_pr...  7.88 us
  transfers between devices with their start and end apart: 35, of which 12 were waited for; matrix products, arithmetic and copies ran while one was open for 2% of the time, Pallas kernels for 22%

profile of v1, /device:TPU:0, one launch (start us, length us, event | category | flops | bytes accessed | tf_op | source)
XLA Modules:
  0.0 257.9 jit_solution(4827753577240577966)
XLA Ops:
  0.6 1.5 fusion.8
  2.1 3.0 %collective-permute-start.7 = (bf16[256,1536]{1,0:T(8,128)(2,1)S(1)}, bf16[256,1536]{1,0:T(8,128)(2,1)}, u32[]{:S(2)}, u32[]{:S(2)}) collective-permute-start(bf16[256,1536]{1,0:T(8,128)(2,1)S(1)} %get-tuple-element.43.refs_0_.refs_2_), channel_id=1, source_target_pairs={{0,1},{1,0},{2,3},{3,2},{4,5},{5,4},{6,7},{7,6},{8,9},{9,8},{10,11... | collective-permute-start | bytes 2359304 | tf_op jit(solution)/shard_map/ppermute | solution.py:320
  5.2 1.5 collective-permute-start.8
  6.7 0.7 pad_add_fusion.place_ref
  7.3 4.7 %pack.1 = (bf16[3,256,384]{2,1,0:T(8,128)(2,1)}, bf16[3,256,384]{2,1,0:T(8,128)(2,1)}, bf16[3,256,384]{2,1,0:T(8,128)(2,1)}, bf16[3,256,384]{2,1,0:T(8,128)(2,1)}) custom-call(s32[3]{0:T(128)} %pad_add_fusion.place_ref, bf16[1,256,1536]{2,1,0:T(8,128)(2,1)} %q_ref.1, bf16[1,256,1536]{2,1,0:T(8,128)(2,1)} %k_ref.1, bf16[1,256,1536]{2,1,0:T(8,128)(2,1)} %v_ref.1), custom_call_target="tpu_custom_call" | custom-call | bytes 4718592 | tf_op jit(solution)/shard_map/pack/pallas_call | solution.py:45
  12.0 0.5 collective-permute-start
  12.6 2.9 %collective-permute-start.2 = (bf16[3,256,384]{2,1,0:T(8,128)(2,1)}, bf16[3,256,384]{2,1,0:T(8,128)(2,1)S(1)}, u32[]{:S(2)}, u32[]{:S(2)}) collective-permute-start(bf16[3,256,384]{2,1,0:T(8,128)(2,1)} %get-tuple-element.40), channel_id=1, source_target_pairs={{0,3},{1,2},{2,1},{3,0},{4,7},{5,6},{6,5},{7,4},{8,11},{9,10},{10,... | collective-permute-start | bytes 1769480 | tf_op jit(solution)/shard_map/ppermute | solution.py:320
  15.5 20.7 %collective-permute-done.refs_1_ = bf16[3,256,384]{2,1,0:T(8,128)(2,1)S(1)} collective-permute-done((bf16[3,256,384]{2,1,0:T(8,128)(2,1)}, bf16[3,256,384]{2,1,0:T(8,128)(2,1)S(1)}, u32[]{:S(2)}, u32[]{:S(2)}) %collective-permute-start) | collective-permute-done | bytes 589856 | tf_op jit(solution)/shard_map/ppermute | solution.py:320
  36.2 7.1 %collective-permute-start.3 = (bf16[192,3072]{1,0:T(8,128)(2,1)}, bf16[192,3072]{1,0:T(8,128)(2,1)}, u32[]{:S(2)}, u32[]{:S(2)}) collective-permute-start(bf16[192,3072]{1,0:T(8,128)(2,1)} %param.9), channel_id=1, source_target_pairs={{0,24},{4,28},{9,1},{13,5},{18,10},{22,14},{27,19},{31,23}} | collective-permute-start | bytes 3538952 | tf_op jit(solution)/shard_map/ppermute | solution.py:320
  43.3 2.4 collective-permute-start.4
  45.7 2.3 collective-permute-start.5
  48.0 1.9 collective-permute-done.1.refs_2_
  50.0 2.4 collective-permute-start.9
  52.4 0.1 collective-permute-start.10
  52.5 0.7 copy-done.5
  53.2 12.6 %forward.1 = (bf16[3,1024,1024]{2,1,0:T(8,128)(2,1)}, bf16[384,1024]{1,0:T(8,128)(2,1)}) custom-call(bf16[3,256,384]{2,1,0:T(8,128)(2,1)} %get-tuple-element.37.refs_0_, bf16[3,256,384]{2,1,0:T(8,128)(2,1)} %copy-done.3, bf16[3,256,384]{2,1,0:T(8,128)(2,1)} %copy-done.4, bf16[3,256,384]{2,1,0:T(8,128)(2,1)} %copy-done.5), custom_call_target="tpu_custom_call" | custom-call | flops 3221225472 | bytes 6291456 | tf_op jit(solution)/shard_map/forward/pallas_call | solution.py:114
  65.8 5.1 %collective-permute-done.9.refs_2_.refs_4_ = bf16[256,1536]{1,0:T(8,128)(2,1)} collective-permute-done((bf16[256,1536]{1,0:T(8,128)(2,1)S(1)}, bf16[256,1536]{1,0:T(8,128)(2,1)}, u32[]{:S(2)}, u32[]{:S(2)}) %collective-permute-start.9) | collective-permute-done | bytes 786464 | tf_op jit(solution)/shard_map/ppermute | solution.py:320
  70.9 12.4 %collective-permute-done.10.refs_3_.refs_5_ = bf16[256,1536]{1,0:T(8,128)(2,1)} collective-permute-done((bf16[256,1536]{1,0:T(8,128)(2,1)}, bf16[256,1536]{1,0:T(8,128)(2,1)}, u32[]{:S(2)}, u32[]{:S(2)}) %collective-permute-start.10) | collective-permute-done | bytes 786464 | tf_op jit(solution)/shard_map/ppermute | solution.py:320
  83.3 1.2 collective-permute-start.13
  84.5 5.4 %weight_terms.2 = (bf16[4,48,1536]{2,1,0:T(8,128)(2,1)}, bf16[4,48,1536]{2,1,0:T(8,128)(2,1)}) custom-call(s32[3]{0:T(128)} %pad_add_fusion.place_ref, bf16[384,1024]{1,0:T(8,128)(2,1)} %get-tuple-element.46.attended_ref, bf16[256,1536]{1,0:T(8,128)(2,1)} %copy-done.2, bf16[256,1536]{1,0:T(8,128)(2,1)} %collective-permute-done.7.refs_1_.refs_3_, ...), custom_call_target="tpu_custom_call" | custom-call | flops 1207959552 | bytes 3932160 | tf_op jit(solution)/shard_map/weight_terms/pallas_call | solution.py:258
  89.9 0.1 collective-permute-start.11
  89.9 4.2 %collective-permute-done.4 = bf16[192,3072]{1,0:T(8,128)(2,1)} collective-permute-done((bf16[192,3072]{1,0:T(8,128)(2,1)}, bf16[192,3072]{1,0:T(8,128)(2,1)}, u32[]{:S(2)}, u32[]{:S(2)}) %collective-permute-start.4) | collective-permute-done | bytes 1179680 | tf_op jit(solution)/shard_map/ppermute | solution.py:320
  94.2 22.2 %collective-permute-done.5 = bf16[192,3072]{1,0:T(8,128)(2,1)} collective-permute-done((bf16[192,3072]{1,0:T(8,128)(2,1)}, bf16[192,3072]{1,0:T(8,128)(2,1)}, u32[]{:S(2)}, u32[]{:S(2)}) %collective-permute-start.5) | collective-permute-done | bytes 1179680 | tf_op jit(solution)/shard_map/ppermute | solution.py:320
  116.3 0.2 select_select_fusion.refs_0_
  116.6 0.1 collective-permute-start.6
  116.7 1.0 fusion.3
  117.7 5.1 %weight_terms.3 = (bf16[4,48,1536]{2,1,0:T(8,128)(2,1)}, bf16[4,48,1536]{2,1,0:T(8,128)(2,1)}) custom-call(s32[3]{0:T(128)} %pad_add_fusion.place_ref, bf16[384,1024]{1,0:T(8,128)(2,1)} %get-tuple-element.46.attended_ref, bf16[256,1536]{1,0:T(8,128)(2,1)} %copy-done.1, bf16[256,1536]{1,0:T(8,128)(2,1)} %collective-permute-done.12.refs_1_.refs_7_, ...), custom_call_target="tpu_custom_call" | custom-call | flops 1207959552 | bytes 3932160 | tf_op jit(solution)/shard_map/weight_terms/pallas_call | solution.py:258
  122.8 0.4 collective-permute-start.14
  123.2 3.7 %collective-permute-start.18 = (bf16[48,1536]{1,0:T(8,128)(2,1)}, bf16[48,1536]{1,0:T(8,128)(2,1)}, u32[]{:S(2)}, u32[]{:S(2)}) collective-permute-start(bf16[48,1536]{1,0:T(8,128)(2,1)} %get-tuple-element.78), channel_id=1, source_target_pairs={{0,8},{1,9},{2,10},{3,11},{4,12},{5,13},{6,14},{7,15},{8,16},{9,17... | collective-permute-start | bytes 442376 | tf_op jit(solution)/shard_map/ppermute | solution.py:320
  127.0 2.4 collective-permute-start.20
  129.3 2.0 fusion.7
  131.3 1.1 copy-done.6
  132.4 7.9 %project.1.refs_5_ = bf16[384,1024]{1,0:T(8,128)(2,1)} custom-call(s32[3]{0:T(128)} %pad_add_fusion.place_ref, bf16[192,3072]{1,0:T(8,128)(2,1)} %copy-done, bf16[192,3072]{1,0:T(8,128)(2,1)} %copy-done.6, bf16[256,1536]{1,0:T(8,128)(2,1)} %copy-done.2, bf16[256,1536]{1,0:T(8,128)(2,1)} %collective-permute-done.7.refs_1_.refs_3_, ...), custom_call_target="tpu_custom_call" | custom-call | flops 2415919104 | bytes 8650752 | tf_op jit(solution)/shard_map/project/pallas_call | solution.py:219
  140.3 6.7 %backward.2 = (bf16[3,256,128]{2,1,0:T(8,128)(2,1)}, bf16[3,256,128]{2,1,0:T(8,128)(2,1)}, bf16[3,256,128]{2,1,0:T(8,128)(2,1)}, bf16[3,256,128]{2,1,0:T(8,128)(2,1)}) custom-call(bf16[3,256,384]{2,1,0:T(8,128)(2,1)} %get-tuple-element.37.refs_0_, bf16[3,256,384]{2,1,0:T(8,128)(2,1)} %copy-done.3, bf16[3,256,384]{2,1,0:T(8,128)(2,1)} %copy-done.4, ...), custom_call_target="tpu_custom_call" | custom-call | flops 1073741824 | bytes 2097152 | tf_op jit(solution)/shard_map/backward/pallas_call | solution.py:164
  147.0 1.1 add_convert_fusion.1
  148.2 0.8 collective-permute-start.24
  149.0 1.9 collective-permute-start.25
  150.9 1.0 collective-permute-start.28
  151.9 6.5 %collective-permute-start.29 = (bf16[48,1536]{1,0:T(8,128)(2,1)S(1)}, bf16[48,1536]{1,0:T(8,128)(2,1)S(1)}, u32[]{:S(2)}, u32[]{:S(2)}) collective-permute-start(bf16[48,1536]{1,0:T(8,128)(2,1)S(1)} %copy-done.15), channel_id=1, source_target_pairs={{0,16},{1,17},{2,18},{3,19},{4,20},{5,21},{6,22},{7,23},{8,24},{9,... | collective-permute-start | bytes 442376 | tf_op jit(solution)/shard_map/ppermute | solution.py:320
  158.4 2.0 collective-permute-start.30
  160.4 10.5 %backward.3 = (bf16[3,256,256]{2,1,0:T(8,128)(2,1)}, bf16[3,256,256]{2,1,0:T(8,128)(2,1)}, bf16[3,256,256]{2,1,0:T(8,128)(2,1)}, bf16[3,256,256]{2,1,0:T(8,128)(2,1)}) custom-call(bf16[3,256,384]{2,1,0:T(8,128)(2,1)} %get-tuple-element.37.refs_0_, bf16[3,256,384]{2,1,0:T(8,128)(2,1)} %copy-done.3, bf16[3,256,384]{2,1,0:T(8,128)(2,1)} %copy-done.4, ...), custom_call_target="tpu_custom_call" | custom-call | flops 2147483648 | bytes 4194304 | tf_op jit(solution)/shard_map/backward/pallas_call | solution.py:164
  170.9 2.5 collective-permute-start.26
  173.3 1.8 collective-permute-done.29
  175.1 2.8 %collective-permute-start.27 = (bf16[48,1536]{1,0:T(8,128)(2,1)S(1)}, bf16[48,1536]{1,0:T(8,128)(2,1)S(1)}, u32[]{:S(2)}, u32[]{:S(2)}) collective-permute-start(bf16[48,1536]{1,0:T(8,128)(2,1)S(1)} %add_convert_fusion.1), channel_id=1, source_target_pairs={{0,3},{1,10},{2,17},{3,24},{4,7},{5,14},{6,21},{7,28},{8,0},{9,9},... | collective-permute-start | bytes 442376 | tf_op jit(solution)/shard_map/ppermute | solution.py:320
  178.0 20.8 %collective-permute-done.30 = bf16[48,1536]{1,0:T(8,128)(2,1)S(1)} collective-permute-done((bf16[48,1536]{1,0:T(8,128)(2,1)S(1)}, bf16[48,1536]{1,0:T(8,128)(2,1)S(1)}, u32[]{:S(2)}, u32[]{:S(2)}) %collective-permute-start.30) | collective-permute-done | bytes 147488 | tf_op jit(solution)/shard_map/ppermute | solution.py:320
  198.8 0.1 add_convert_fusion
  198.9 0.7 collective-permute-start.31
  199.6 5.2 %collective-permute-start.32 = (bf16[48,1536]{1,0:T(8,128)(2,1)S(1)}, bf16[48,1536]{1,0:T(8,128)(2,1)S(1)}, u32[]{:S(2)}, u32[]{:S(2)}) collective-permute-start(bf16[48,1536]{1,0:T(8,128)(2,1)S(1)} %add_convert_fusion), channel_id=1, source_target_pairs={{0,1},{1,8},{2,19},{3,26},{4,5},{5,12},{6,23},{7,30},{8,2},{9,11},... | collective-permute-start | bytes 442376 | tf_op jit(solution)/shard_map/ppermute | solution.py:320
  204.8 3.0 %collective-permute-start.21 = (bf16[3,256,256]{2,1,0:T(8,128)(2,1)}, bf16[3,256,256]{2,1,0:T(8,128)(2,1)S(1)}, u32[]{:S(2)}, u32[]{:S(2)}) collective-permute-start(bf16[3,256,256]{2,1,0:T(8,128)(2,1)} %get-tuple-element.61), channel_id=1, source_target_pairs={{0,1},{1,0},{2,3},{3,2},{4,5},{5,4},{6,7},{7,6},{8,9},{9,8},{10,11... | collective-permute-start | bytes 1179656 | tf_op jit(solution)/shard_map/ppermute | solution.py:320
  207.8 3.7 %collective-permute-done.27.refs_3_ = bf16[48,1536]{1,0:T(8,128)(2,1)S(1)} collective-permute-done((bf16[48,1536]{1,0:T(8,128)(2,1)S(1)}, bf16[48,1536]{1,0:T(8,128)(2,1)S(1)}, u32[]{:S(2)}, u32[]{:S(2)}) %collective-permute-start.27) | collective-permute-done | bytes 147488 | tf_op jit(solution)/shard_map/ppermute | solution.py:320
  211.5 0.1 collective-permute-start.23
  211.6 3.8 %collective-permute-start.33 = (bf16[48,1536]{1,0:T(8,128)(2,1)S(1)}, bf16[48,1536]{1,0:T(8,128)(2,1)S(1)}, u32[]{:S(2)}, u32[]{:S(2)}) collective-permute-start(bf16[48,1536]{1,0:T(8,128)(2,1)S(1)} %add_convert_fusion), channel_id=1, source_target_pairs={{0,2},{1,11},{2,16},{3,25},{4,6},{5,15},{6,20},{7,29},{8,3},{9,10}... | collective-permute-start | bytes 442376 | tf_op jit(solution)/shard_map/ppermute | solution.py:320
  215.5 14.3 %collective-permute-start.34 = (bf16[48,1536]{1,0:T(8,128)(2,1)S(1)}, bf16[48,1536]{1,0:T(8,128)(2,1)S(1)}, u32[]{:S(2)}, u32[]{:S(2)}) collective-permute-start(bf16[48,1536]{1,0:T(8,128)(2,1)S(1)} %add_convert_fusion), channel_id=1, source_target_pairs={{0,3},{1,10},{2,17},{3,24},{4,7},{5,14},{6,21},{7,28},{8,0},{9,9},... | collective-permute-start | bytes 442376 | tf_op jit(solution)/shard_map/ppermute | solution.py:320
  229.7 7.7 %collective-permute-done.33.refs_6_ = bf16[48,1536]{1,0:T(8,128)(2,1)S(1)} collective-permute-done((bf16[48,1536]{1,0:T(8,128)(2,1)S(1)}, bf16[48,1536]{1,0:T(8,128)(2,1)S(1)}, u32[]{:S(2)}, u32[]{:S(2)}) %collective-permute-start.33) | collective-permute-done | bytes 147488 | tf_op jit(solution)/shard_map/ppermute | solution.py:320
  237.4 2.5 collective-permute-start.16
  239.9 3.7 %collective-permute-done.34.refs_7_ = bf16[48,1536]{1,0:T(8,128)(2,1)S(1)} collective-permute-done((bf16[48,1536]{1,0:T(8,128)(2,1)S(1)}, bf16[48,1536]{1,0:T(8,128)(2,1)S(1)}, u32[]{:S(2)}, u32[]{:S(2)}) %collective-permute-start.34) | collective-permute-done | bytes 147488 | tf_op jit(solution)/shard_map/ppermute | solution.py:320
  243.7 3.4 %collective-permute-start.17 = (bf16[3,256,128]{2,1,0:T(8,128)(2,1)S(1)}, bf16[3,256,128]{2,1,0:T(8,128)(2,1)S(1)}, u32[]{:S(2)}, u32[]{:S(2)}) collective-permute-start(bf16[3,256,128]{2,1,0:T(8,128)(2,1)S(1)} %copy-done.25), channel_id=1, source_target_pairs={{0,3},{1,2},{2,1},{3,0},{4,7},{5,6},{6,5},{7,4},{8,11},{9,10},{10,... | collective-permute-start | bytes 589832 | tf_op jit(solution)/shard_map/ppermute | solution.py:320
  247.2 3.6 %assemble.1 = f32[192,3072]{1,0:T(8,128)} custom-call(s32[3]{0:T(128)} %pad_add_fusion.place_ref, bf16[48,1536]{1,0:T(8,128)(2,1)} %copy-done.17, bf16[48,1536]{1,0:T(8,128)(2,1)} %copy-done.18, bf16[48,1536]{1,0:T(8,128)(2,1)} %copy-done.19, bf16[48,1536]{1,0:T(8,128)(2,1)} %copy-done.20, bf16[48,1536]{1,0:T(8,128)(2,1)} %copy-done.21, ...), custom_call_target="tpu_custom_call" | custom-call | bytes 3538944 | tf_op jit(solution)/shard_map/assemble/pallas_call | solution.py:287
  250.7 1.1 collective-permute-done.17.refs_3_
  251.9 0.6 copy-done.14
  252.5 0.2 copy-done.9
  252.7 0.1 copy-done.10
  252.8 0.8 copy-done.11
  253.6 4.3 %unpack.1 = (bf16[1,256,1536]{2,1,0:T(8,128)(2,1)}, bf16[1,256,1536]{2,1,0:T(8,128)(2,1)}, bf16[1,256,1536]{2,1,0:T(8,128)(2,1)}) custom-call(s32[3]{0:T(128)} %pad_add_fusion.place_ref, bf16[3,256,128]{2,1,0:T(8,128)(2,1)} %get-tuple-element.52.refs_0_, bf16[3,256,128]{2,1,0:T(8,128)(2,1)} %copy-done.12, bf16[3,256,128]{2,1,0:T(8,128)(2,1)} %copy-done.13, ...), custom_call_target="tpu_custom_call" | custom-call | bytes 4718592 | tf_op jit(solution)/shard_map/unpack/pallas_call | solution.py:79
  (78 shorter events, 0.2 us)
Async XLA Ops:
  2.1 47.9 %copy-start.2 = (bf16[256,1536]{1,0:T(8,128)(2,1)}, bf16[256,1536]{1,0:T(8,128)(2,1)S(1)}, u32[]{:S(2)}) copy-start(bf16[256,1536]{1,0:T(8,128)(2,1)S(1)} %get-tuple-element.43.refs_0_.refs_2_) | copy-start | bytes 2359300
  2.1 68.8 %copy-start.1 = (bf16[256,1536]{1,0:T(8,128)(2,1)}, bf16[256,1536]{1,0:T(8,128)(2,1)S(1)}, u32[]{:S(2)}) copy-start(bf16[256,1536]{1,0:T(8,128)(2,1)S(1)} %get-tuple-element.47.refs_0_.refs_6_) | copy-start | bytes 2359300
  2.1 41.2 %collective-permute-start.7 = (bf16[256,1536]{1,0:T(8,128)(2,1)S(1)}, bf16[256,1536]{1,0:T(8,128)(2,1)}, u32[]{:S(2)}, u32[]{:S(2)}) collective-permute-start(bf16[256,1536]{1,0:T(8,128)(2,1)S(1)} %get-tuple-element.43.refs_0_.refs_2_), channel_id=1, source_target_pairs={{0,1},{1,0},{2,3},{3,2},{4,5},{5,4},{6,7},{7,6},{8,9},{9,8},{10,11... | collective-permute-start | bytes 2359304 | tf_op jit(solution)/shard_map/ppermute | solution.py:320
  5.2 40.5 %collective-permute-start.8 = (bf16[256,1536]{1,0:T(8,128)(2,1)S(1)}, bf16[256,1536]{1,0:T(8,128)(2,1)}, u32[]{:S(2)}, u32[]{:S(2)}) collective-permute-start(bf16[256,1536]{1,0:T(8,128)(2,1)S(1)} %get-tuple-element.47.refs_0_.refs_6_), channel_id=1, source_target_pairs={{0,2},{1,3},{2,0},{3,1},{4,6},{5,7},{6,4},{7,5},{8,10},{9,11},{10,... | collective-permute-start | bytes 2359304 | tf_op jit(solution)/shard_map/ppermute | solution.py:320
  12.0 24.2 %collective-permute-start = (bf16[3,256,384]{2,1,0:T(8,128)(2,1)}, bf16[3,256,384]{2,1,0:T(8,128)(2,1)S(1)}, u32[]{:S(2)}, u32[]{:S(2)}) collective-permute-start(bf16[3,256,384]{2,1,0:T(8,128)(2,1)} %get-tuple-element.38), channel_id=1, source_target_pairs={{0,1},{1,0},{2,3},{3,2},{4,5},{5,4},{6,7},{7,6},{8,9},{9,8},{10,11... | collective-permute-start | bytes 1769480 | tf_op jit(solution)/shard_map/ppermute | solution.py:320
  12.5 37.5 %collective-permute-start.1 = (bf16[3,256,384]{2,1,0:T(8,128)(2,1)}, bf16[3,256,384]{2,1,0:T(8,128)(2,1)S(1)}, u32[]{:S(2)}, u32[]{:S(2)}) collective-permute-start(bf16[3,256,384]{2,1,0:T(8,128)(2,1)} %get-tuple-element.39), channel_id=1, source_target_pairs={{0,2},{1,3},{2,0},{3,1},{4,6},{5,7},{6,4},{7,5},{8,10},{9,11},{10,... | collective-permute-start | bytes 1769480 | tf_op jit(solution)/shard_map/ppermute | solution.py:320
  12.6 39.8 %collective-permute-start.2 = (bf16[3,256,384]{2,1,0:T(8,128)(2,1)}, bf16[3,256,384]{2,1,0:T(8,128)(2,1)S(1)}, u32[]{:S(2)}, u32[]{:S(2)}) collective-permute-start(bf16[3,256,384]{2,1,0:T(8,128)(2,1)} %get-tuple-element.40), channel_id=1, source_target_pairs={{0,3},{1,2},{2,1},{3,0},{4,7},{5,6},{6,5},{7,4},{8,11},{9,10},{10,... | collective-permute-start | bytes 1769480 | tf_op jit(solution)/shard_map/ppermute | solution.py:320
  36.2 16.3 %copy-start.3 = (bf16[3,256,384]{2,1,0:T(8,128)(2,1)}, bf16[3,256,384]{2,1,0:T(8,128)(2,1)S(1)}, u32[]{:S(2)}) copy-start(bf16[3,256,384]{2,1,0:T(8,128)(2,1)S(1)} %collective-permute-done.refs_1_) | copy-start | bytes 1769476
  36.2 53.7 %collective-permute-start.3 = (bf16[192,3072]{1,0:T(8,128)(2,1)}, bf16[192,3072]{1,0:T(8,128)(2,1)}, u32[]{:S(2)}, u32[]{:S(2)}) collective-permute-start(bf16[192,3072]{1,0:T(8,128)(2,1)} %param.9), channel_id=1, source_target_pairs={{0,24},{4,28},{9,1},{13,5},{18,10},{22,14},{27,19},{31,23}} | collective-permute-start | bytes 3538952 | tf_op jit(solution)/shard_map/ppermute | solution.py:320
  43.3 50.8 %collective-permute-start.4 = (bf16[192,3072]{1,0:T(8,128)(2,1)}, bf16[192,3072]{1,0:T(8,128)(2,1)}, u32[]{:S(2)}, u32[]{:S(2)}) collective-permute-start(bf16[192,3072]{1,0:T(8,128)(2,1)} %param.9), channel_id=1, source_target_pairs={{0,16},{4,20},{9,25},{13,29},{18,2},{22,6},{27,11},{31,15}} | collective-permute-start | bytes 3538952 | tf_op jit(solution)/shard_map/ppermute | solution.py:320
  45.7 70.6 %collective-permute-start.5 = (bf16[192,3072]{1,0:T(8,128)(2,1)}, bf16[192,3072]{1,0:T(8,128)(2,1)}, u32[]{:S(2)}, u32[]{:S(2)}) collective-permute-start(bf16[192,3072]{1,0:T(8,128)(2,1)} %param.9), channel_id=1, source_target_pairs={{0,8},{4,12},{9,17},{13,21},{18,26},{22,30},{27,3},{31,7}} | collective-permute-start | bytes 3538952 | tf_op jit(solution)/shard_map/ppermute | solution.py:320
  50.0 2.5 copy-start.4
  50.0 20.9 %collective-permute-start.9 = (bf16[256,1536]{1,0:T(8,128)(2,1)S(1)}, bf16[256,1536]{1,0:T(8,128)(2,1)}, u32[]{:S(2)}, u32[]{:S(2)}) collective-permute-start(bf16[256,1536]{1,0:T(8,128)(2,1)S(1)} %get-tuple-element.43.refs_0_.refs_2_), channel_id=1, source_target_pairs={{0,2},{1,3},{2,0},{3,1},{4,6},{5,7},{6,4},{7,5},{8,10},{9,11},{10,... | collective-permute-start | bytes 2359304 | tf_op jit(solution)/shard_map/ppermute | solution.py:320
  52.4 0.8 copy-start.5
  52.4 30.9 %collective-permute-start.10 = (bf16[256,1536]{1,0:T(8,128)(2,1)}, bf16[256,1536]{1,0:T(8,128)(2,1)}, u32[]{:S(2)}, u32[]{:S(2)}) collective-permute-start(bf16[256,1536]{1,0:T(8,128)(2,1)} %collective-permute-done.7.refs_1_.refs_3_), channel_id=1, source_target_pairs={{0,2},{1,3},{2,0},{3,1},{4,6},{5,7},{6,4},{7,5},{8,10},{9,11},{10,... | collective-permute-start | bytes 2359304 | tf_op jit(solution)/shard_map/ppermute | solution.py:320
  70.9 46.8 %collective-permute-start.12 = (bf16[256,1536]{1,0:T(8,128)(2,1)S(1)}, bf16[256,1536]{1,0:T(8,128)(2,1)}, u32[]{:S(2)}, u32[]{:S(2)}) collective-permute-start(bf16[256,1536]{1,0:T(8,128)(2,1)S(1)} %get-tuple-element.47.refs_0_.refs_6_), channel_id=1, source_target_pairs={{0,1},{1,0},{2,3},{3,2},{4,5},{5,4},{6,7},{7,6},{8,9},{9,8},{10,11... | collective-permute-start | bytes 2359304 | tf_op jit(solution)/shard_map/ppermute | solution.py:320
  83.3 34.5 %collective-permute-start.13 = (bf16[256,1536]{1,0:T(8,128)(2,1)}, bf16[256,1536]{1,0:T(8,128)(2,1)}, u32[]{:S(2)}, u32[]{:S(2)}) collective-permute-start(bf16[256,1536]{1,0:T(8,128)(2,1)} %collective-permute-done.8.refs_2_.refs_8_), channel_id=1, source_target_pairs={{0,1},{1,0},{2,3},{3,2},{4,5},{5,4},{6,7},{7,6},{8,9},{9,8},{10,11... | collective-permute-start | bytes 2359304 | tf_op jit(solution)/shard_map/ppermute | solution.py:320
  84.5 31.8 %copy-start.7 = (bf16[192,3072]{1,0:T(8,128)(2,1)S(1)}, bf16[192,3072]{1,0:T(8,128)(2,1)}, u32[]{:S(2)}) copy-start(bf16[192,3072]{1,0:T(8,128)(2,1)} %param.9) | copy-start | bytes 3538948
  89.9 26.8 %copy-start.8 = (bf16[4,48,1536]{2,1,0:T(8,128)(2,1)S(1)}, bf16[4,48,1536]{2,1,0:T(8,128)(2,1)}, u32[]{:S(2)}) copy-start(bf16[4,48,1536]{2,1,0:T(8,128)(2,1)} %get-tuple-element.44) | copy-start | bytes 1769476
  89.9 26.8 %collective-permute-start.11 = (bf16[4,48,1536]{2,1,0:T(8,128)(2,1)}, bf16[4,48,1536]{2,1,0:T(8,128)(2,1)S(1)}, u32[]{:S(2)}, u32[]{:S(2)}) collective-permute-start(bf16[4,48,1536]{2,1,0:T(8,128)(2,1)} %get-tuple-element.45), channel_id=1, source_target_pairs={{0,4},{1,5},{2,6},{3,7},{4,0},{5,1},{6,2},{7,3},{8,12},{9,13},{10,... | collective-permute-start | bytes 1769480 | tf_op jit(solution)/shard_map/ppermute | solution.py:320
  116.5 6.3 %copy-start = (bf16[192,3072]{1,0:T(8,128)(2,1)}, bf16[192,3072]{1,0:T(8,128)(2,1)S(1)}, u32[]{:S(2)}) copy-start(bf16[192,3072]{1,0:T(8,128)(2,1)S(1)} %select_select_fusion.refs_0_) | copy-start | bytes 3538948
  116.6 14.8 %collective-permute-start.6 = (bf16[192,3072]{1,0:T(8,128)(2,1)S(1)}, bf16[192,3072]{1,0:T(8,128)(2,1)S(1)}, u32[]{:S(2)}, u32[]{:S(2)}) collective-permute-start(bf16[192,3072]{1,0:T(8,128)(2,1)S(1)} %select_select_fusion.refs_0_), channel_id=1, source_target_pairs={{0,4},{1,5},{2,6},{3,7},{4,0},{5,1},{6,2},{7,3},{8,12},{9,13},{10,... | collective-permute-start | bytes 3538952 | tf_op jit(solution)/shard_map/ppermute | solution.py:320
  122.8 6.5 %collective-permute-start.14 = (bf16[4,48,1536]{2,1,0:T(8,128)(2,1)}, bf16[4,48,1536]{2,1,0:T(8,128)(2,1)S(1)}, u32[]{:S(2)}, u32[]{:S(2)}) collective-permute-start(bf16[4,48,1536]{2,1,0:T(8,128)(2,1)} %get-tuple-element.49), channel_id=1, source_target_pairs={{0,4},{1,5},{2,6},{3,7},{4,0},{5,1},{6,2},{7,3},{8,12},{9,13},{10,... | collective-permute-start | bytes 1769480 | tf_op jit(solution)/shard_map/ppermute | solution.py:320
  123.2 23.7 %collective-permute-start.18 = (bf16[48,1536]{1,0:T(8,128)(2,1)}, bf16[48,1536]{1,0:T(8,128)(2,1)}, u32[]{:S(2)}, u32[]{:S(2)}) collective-permute-start(bf16[48,1536]{1,0:T(8,128)(2,1)} %get-tuple-element.78), channel_id=1, source_target_pairs={{0,8},{1,9},{2,10},{3,11},{4,12},{5,13},{6,14},{7,15},{8,16},{9,17... | collective-permute-start | bytes 442376 | tf_op jit(solution)/shard_map/ppermute | solution.py:320
  127.0 20.0 %collective-permute-start.19 = (bf16[48,1536]{1,0:T(8,128)(2,1)}, bf16[48,1536]{1,0:T(8,128)(2,1)}, u32[]{:S(2)}, u32[]{:S(2)}) collective-permute-start(bf16[48,1536]{1,0:T(8,128)(2,1)} %get-tuple-element.77), channel_id=1, source_target_pairs={{0,16},{1,17},{2,18},{3,19},{4,20},{5,21},{6,22},{7,23},{8,24},{9,... | collective-permute-start | bytes 442376 | tf_op jit(solution)/shard_map/ppermute | solution.py:320
  127.0 20.0 %collective-permute-start.20 = (bf16[48,1536]{1,0:T(8,128)(2,1)}, bf16[48,1536]{1,0:T(8,128)(2,1)}, u32[]{:S(2)}, u32[]{:S(2)}) collective-permute-start(bf16[48,1536]{1,0:T(8,128)(2,1)} %get-tuple-element.76), channel_id=1, source_target_pairs={{0,24},{1,25},{2,26},{3,27},{4,28},{5,29},{6,30},{7,31},{8,0},{9,1... | collective-permute-start | bytes 442376 | tf_op jit(solution)/shard_map/ppermute | solution.py:320
  131.3 1.1 copy-start.6
  140.3 10.6 %copy-start.16 = (bf16[48,1536]{1,0:T(8,128)(2,1)S(1)}, bf16[48,1536]{1,0:T(8,128)(2,1)}, u32[]{:S(2)}) copy-start(bf16[48,1536]{1,0:T(8,128)(2,1)} %get-tuple-element.74) | copy-start | bytes 442372
  140.3 11.6 %copy-start.15 = (bf16[48,1536]{1,0:T(8,128)(2,1)S(1)}, bf16[48,1536]{1,0:T(8,128)(2,1)}, u32[]{:S(2)}) copy-start(bf16[48,1536]{1,0:T(8,128)(2,1)} %get-tuple-element.73) | copy-start | bytes 442372
  148.1 50.6 %copy-start.27 = (bf16[3,256,128]{2,1,0:T(8,128)(2,1)S(1)}, bf16[3,256,128]{2,1,0:T(8,128)(2,1)}, u32[]{:S(2)}) copy-start(bf16[3,256,128]{2,1,0:T(8,128)(2,1)} %get-tuple-element.53) | copy-start | bytes 589828
  148.1 89.3 %copy-start.26 = (bf16[3,256,128]{2,1,0:T(8,128)(2,1)S(1)}, bf16[3,256,128]{2,1,0:T(8,128)(2,1)}, u32[]{:S(2)}) copy-start(bf16[3,256,128]{2,1,0:T(8,128)(2,1)} %get-tuple-element.54) | copy-start | bytes 589828
  148.1 95.5 %copy-start.25 = (bf16[3,256,128]{2,1,0:T(8,128)(2,1)S(1)}, bf16[3,256,128]{2,1,0:T(8,128)(2,1)}, u32[]{:S(2)}) copy-start(bf16[3,256,128]{2,1,0:T(8,128)(2,1)} %get-tuple-element.55) | copy-start | bytes 589828
  148.2 50.7 %collective-permute-start.24 = (bf16[48,1536]{1,0:T(8,128)(2,1)S(1)}, bf16[48,1536]{1,0:T(8,128)(2,1)S(1)}, u32[]{:S(2)}, u32[]{:S(2)}) collective-permute-start(bf16[48,1536]{1,0:T(8,128)(2,1)S(1)} %add_convert_fusion.1), channel_id=1, source_target_pairs={{0,0},{1,9},{2,18},{3,27},{4,4},{5,13},{6,22},{7,31},{8,1},{9,8},{... | collective-permute-start | bytes 442376 | tf_op jit(solution)/shard_map/ppermute | solution.py:320
  149.0 50.6 %collective-permute-start.25 = (bf16[48,1536]{1,0:T(8,128)(2,1)S(1)}, bf16[48,1536]{1,0:T(8,128)(2,1)S(1)}, u32[]{:S(2)}, u32[]{:S(2)}) collective-permute-start(bf16[48,1536]{1,0:T(8,128)(2,1)S(1)} %add_convert_fusion.1), channel_id=1, source_target_pairs={{0,1},{1,8},{2,19},{3,26},{4,5},{5,12},{6,23},{7,30},{8,2},{9,11},... | collective-permute-start | bytes 442376 | tf_op jit(solution)/shard_map/ppermute | solution.py:320
  150.9 19.9 %collective-permute-start.28 = (bf16[48,1536]{1,0:T(8,128)(2,1)S(1)}, bf16[48,1536]{1,0:T(8,128)(2,1)S(1)}, u32[]{:S(2)}, u32[]{:S(2)}) collective-permute-start(bf16[48,1536]{1,0:T(8,128)(2,1)S(1)} %copy-done.16), channel_id=1, source_target_pairs={{0,8},{1,9},{2,10},{3,11},{4,12},{5,13},{6,14},{7,15},{8,16},{9,17... | collective-permute-start | bytes 442376 | tf_op jit(solution)/shard_map/ppermute | solution.py:320
  151.9 23.2 %collective-permute-start.29 = (bf16[48,1536]{1,0:T(8,128)(2,1)S(1)}, bf16[48,1536]{1,0:T(8,128)(2,1)S(1)}, u32[]{:S(2)}, u32[]{:S(2)}) collective-permute-start(bf16[48,1536]{1,0:T(8,128)(2,1)S(1)} %copy-done.15), channel_id=1, source_target_pairs={{0,16},{1,17},{2,18},{3,19},{4,20},{5,21},{6,22},{7,23},{8,24},{9,... | collective-permute-start | bytes 442376 | tf_op jit(solution)/shard_map/ppermute | solution.py:320
  158.4 40.4 %collective-permute-start.30 = (bf16[48,1536]{1,0:T(8,128)(2,1)S(1)}, bf16[48,1536]{1,0:T(8,128)(2,1)S(1)}, u32[]{:S(2)}, u32[]{:S(2)}) collective-permute-start(bf16[48,1536]{1,0:T(8,128)(2,1)S(1)} %get-tuple-element.72), channel_id=1, source_target_pairs={{0,24},{1,25},{2,26},{3,27},{4,28},{5,29},{6,30},{7,31},{8,0},{9,1... | collective-permute-start | bytes 442376 | tf_op jit(solution)/shard_map/ppermute | solution.py:320
  170.9 33.9 %collective-permute-start.26 = (bf16[48,1536]{1,0:T(8,128)(2,1)S(1)}, bf16[48,1536]{1,0:T(8,128)(2,1)S(1)}, u32[]{:S(2)}, u32[]{:S(2)}) collective-permute-start(bf16[48,1536]{1,0:T(8,128)(2,1)S(1)} %add_convert_fusion.1), channel_id=1, source_target_pairs={{0,2},{1,11},{2,16},{3,25},{4,6},{5,15},{6,20},{7,29},{8,3},{9,10}... | collective-permute-start | bytes 442376 | tf_op jit(solution)/shard_map/ppermute | solution.py:320
  175.1 36.3 %collective-permute-start.27 = (bf16[48,1536]{1,0:T(8,128)(2,1)S(1)}, bf16[48,1536]{1,0:T(8,128)(2,1)S(1)}, u32[]{:S(2)}, u32[]{:S(2)}) collective-permute-start(bf16[48,1536]{1,0:T(8,128)(2,1)S(1)} %add_convert_fusion.1), channel_id=1, source_target_pairs={{0,3},{1,10},{2,17},{3,24},{4,7},{5,14},{6,21},{7,28},{8,0},{9,9},... | collective-permute-start | bytes 442376 | tf_op jit(solution)/shard_map/ppermute | solution.py:320
  198.8 12.7 %collective-permute-start.15 = (bf16[3,256,128]{2,1,0:T(8,128)(2,1)S(1)}, bf16[3,256,128]{2,1,0:T(8,128)(2,1)S(1)}, u32[]{:S(2)}, u32[]{:S(2)}) collective-permute-start(bf16[3,256,128]{2,1,0:T(8,128)(2,1)S(1)} %copy-done.27), channel_id=1, source_target_pairs={{0,1},{1,0},{2,3},{3,2},{4,5},{5,4},{6,7},{7,6},{8,9},{9,8},{10,11... | collective-permute-start | bytes 589832 | tf_op jit(solution)/shard_map/ppermute | solution.py:320
  198.9 48.2 %copy-start.17 = (bf16[48,1536]{1,0:T(8,128)(2,1)}, bf16[48,1536]{1,0:T(8,128)(2,1)S(1)}, u32[]{:S(2)}) copy-start(bf16[48,1536]{1,0:T(8,128)(2,1)S(1)} %collective-permute-done.24.refs_0_) | copy-start | bytes 442372
  198.9 12.7 %collective-permute-start.31 = (bf16[48,1536]{1,0:T(8,128)(2,1)S(1)}, bf16[48,1536]{1,0:T(8,128)(2,1)S(1)}, u32[]{:S(2)}, u32[]{:S(2)}) collective-permute-start(bf16[48,1536]{1,0:T(8,128)(2,1)S(1)} %add_convert_fusion), channel_id=1, source_target_pairs={{0,0},{1,9},{2,18},{3,27},{4,4},{5,13},{6,22},{7,31},{8,1},{9,8},{... | collective-permute-start | bytes 442376 | tf_op jit(solution)/shard_map/ppermute | solution.py:320
  199.6 47.5 %copy-start.18 = (bf16[48,1536]{1,0:T(8,128)(2,1)}, bf16[48,1536]{1,0:T(8,128)(2,1)S(1)}, u32[]{:S(2)}) copy-start(bf16[48,1536]{1,0:T(8,128)(2,1)S(1)} %collective-permute-done.25.refs_1_) | copy-start | bytes 442372
  199.6 15.9 %collective-permute-start.32 = (bf16[48,1536]{1,0:T(8,128)(2,1)S(1)}, bf16[48,1536]{1,0:T(8,128)(2,1)S(1)}, u32[]{:S(2)}, u32[]{:S(2)}) collective-permute-start(bf16[48,1536]{1,0:T(8,128)(2,1)S(1)} %add_convert_fusion), channel_id=1, source_target_pairs={{0,1},{1,8},{2,19},{3,26},{4,5},{5,12},{6,23},{7,30},{8,2},{9,11},... | collective-permute-start | bytes 442376 | tf_op jit(solution)/shard_map/ppermute | solution.py:320
  204.8 42.3 %copy-start.19 = (bf16[48,1536]{1,0:T(8,128)(2,1)}, bf16[48,1536]{1,0:T(8,128)(2,1)S(1)}, u32[]{:S(2)}) copy-start(bf16[48,1536]{1,0:T(8,128)(2,1)S(1)} %collective-permute-done.26.refs_2_) | copy-start | bytes 442372
  204.8 47.1 %collective-permute-start.21 = (bf16[3,256,256]{2,1,0:T(8,128)(2,1)}, bf16[3,256,256]{2,1,0:T(8,128)(2,1)S(1)}, u32[]{:S(2)}, u32[]{:S(2)}) collective-permute-start(bf16[3,256,256]{2,1,0:T(8,128)(2,1)} %get-tuple-element.61), channel_id=1, source_target_pairs={{0,1},{1,0},{2,3},{3,2},{4,5},{5,4},{6,7},{7,6},{8,9},{9,8},{10,11... | collective-permute-start | bytes 1179656 | tf_op jit(solution)/shard_map/ppermute | solution.py:320
  211.5 35.7 %copy-start.20 = (bf16[48,1536]{1,0:T(8,128)(2,1)}, bf16[48,1536]{1,0:T(8,128)(2,1)S(1)}, u32[]{:S(2)}) copy-start(bf16[48,1536]{1,0:T(8,128)(2,1)S(1)} %collective-permute-done.27.refs_3_) | copy-start | bytes 442372
  211.5 40.4 %collective-permute-start.22 = (bf16[3,256,256]{2,1,0:T(8,128)(2,1)}, bf16[3,256,256]{2,1,0:T(8,128)(2,1)S(1)}, u32[]{:S(2)}, u32[]{:S(2)}) collective-permute-start(bf16[3,256,256]{2,1,0:T(8,128)(2,1)} %get-tuple-element.62), channel_id=1, source_target_pairs={{0,2},{1,3},{2,0},{3,1},{4,6},{5,7},{6,4},{7,5},{8,10},{9,11},{10,... | collective-permute-start | bytes 1179656 | tf_op jit(solution)/shard_map/ppermute | solution.py:320
  211.5 39.3 %copy-start.12 = (bf16[3,256,128]{2,1,0:T(8,128)(2,1)}, bf16[3,256,128]{2,1,0:T(8,128)(2,1)S(1)}, u32[]{:S(2)}) copy-start(bf16[3,256,128]{2,1,0:T(8,128)(2,1)S(1)} %collective-permute-done.15.refs_1_) | copy-start | bytes 589828
  211.5 40.4 %collective-permute-start.23 = (bf16[3,256,256]{2,1,0:T(8,128)(2,1)}, bf16[3,256,256]{2,1,0:T(8,128)(2,1)S(1)}, u32[]{:S(2)}, u32[]{:S(2)}) collective-permute-start(bf16[3,256,256]{2,1,0:T(8,128)(2,1)} %get-tuple-element.63), channel_id=1, source_target_pairs={{0,3},{1,2},{2,1},{3,0},{4,7},{5,6},{6,5},{7,4},{8,11},{9,10},{10,... | collective-permute-start | bytes 1179656 | tf_op jit(solution)/shard_map/ppermute | solution.py:320
  211.6 35.5 %copy-start.21 = (bf16[48,1536]{1,0:T(8,128)(2,1)}, bf16[48,1536]{1,0:T(8,128)(2,1)S(1)}, u32[]{:S(2)}) copy-start(bf16[48,1536]{1,0:T(8,128)(2,1)S(1)} %collective-permute-done.31.refs_4_) | copy-start | bytes 442372
  211.6 25.9 %collective-permute-start.33 = (bf16[48,1536]{1,0:T(8,128)(2,1)S(1)}, bf16[48,1536]{1,0:T(8,128)(2,1)S(1)}, u32[]{:S(2)}, u32[]{:S(2)}) collective-permute-start(bf16[48,1536]{1,0:T(8,128)(2,1)S(1)} %add_convert_fusion), channel_id=1, source_target_pairs={{0,2},{1,11},{2,16},{3,25},{4,6},{5,15},{6,20},{7,29},{8,3},{9,10}... | collective-permute-start | bytes 442376 | tf_op jit(solution)/shard_map/ppermute | solution.py:320
  215.4 31.7 %copy-start.22 = (bf16[48,1536]{1,0:T(8,128)(2,1)}, bf16[48,1536]{1,0:T(8,128)(2,1)S(1)}, u32[]{:S(2)}) copy-start(bf16[48,1536]{1,0:T(8,128)(2,1)S(1)} %collective-permute-done.32.refs_5_) | copy-start | bytes 442372
  215.5 28.2 %collective-permute-start.34 = (bf16[48,1536]{1,0:T(8,128)(2,1)S(1)}, bf16[48,1536]{1,0:T(8,128)(2,1)S(1)}, u32[]{:S(2)}, u32[]{:S(2)}) collective-permute-start(bf16[48,1536]{1,0:T(8,128)(2,1)S(1)} %add_convert_fusion), channel_id=1, source_target_pairs={{0,3},{1,10},{2,17},{3,24},{4,7},{5,14},{6,21},{7,28},{8,0},{9,9},... | collective-permute-start | bytes 442376 | tf_op jit(solution)/shard_map/ppermute | solution.py:320
  237.4 9.7 %copy-start.23 = (bf16[48,1536]{1,0:T(8,128)(2,1)}, bf16[48,1536]{1,0:T(8,128)(2,1)S(1)}, u32[]{:S(2)}) copy-start(bf16[48,1536]{1,0:T(8,128)(2,1)S(1)} %collective-permute-done.33.refs_6_) | copy-start | bytes 442372
  237.4 13.3 %collective-permute-start.16 = (bf16[3,256,128]{2,1,0:T(8,128)(2,1)S(1)}, bf16[3,256,128]{2,1,0:T(8,128)(2,1)S(1)}, u32[]{:S(2)}, u32[]{:S(2)}) collective-permute-start(bf16[3,256,128]{2,1,0:T(8,128)(2,1)S(1)} %copy-done.26), channel_id=1, source_target_pairs={{0,2},{1,3},{2,0},{3,1},{4,6},{5,7},{6,4},{7,5},{8,10},{9,11},{10,... | collective-permute-start | bytes 589832 | tf_op jit(solution)/shard_map/ppermute | solution.py:320
  243.7 3.5 %copy-start.24 = (bf16[48,1536]{1,0:T(8,128)(2,1)}, bf16[48,1536]{1,0:T(8,128)(2,1)S(1)}, u32[]{:S(2)}) copy-start(bf16[48,1536]{1,0:T(8,128)(2,1)S(1)} %collective-permute-done.34.refs_7_) | copy-start | bytes 442372
  243.7 8.2 %collective-permute-start.17 = (bf16[3,256,128]{2,1,0:T(8,128)(2,1)S(1)}, bf16[3,256,128]{2,1,0:T(8,128)(2,1)S(1)}, u32[]{:S(2)}, u32[]{:S(2)}) collective-permute-start(bf16[3,256,128]{2,1,0:T(8,128)(2,1)S(1)} %copy-done.25), channel_id=1, source_target_pairs={{0,3},{1,2},{2,1},{3,0},{4,7},{5,6},{6,5},{7,4},{8,11},{9,10},{10,... | collective-permute-start | bytes 589832 | tf_op jit(solution)/shard_map/ppermute | solution.py:320
  250.7 1.1 copy-start.13
  251.8 0.7 copy-start.14
  251.8 0.8 copy-start.9
  251.8 1.0 copy-start.10
  252.8 0.8 copy-start.11

commit v2 on v1

--- a/solution.py
+++ b/solution.py
@@ -31,29 +31,50 @@
 def pack(place, query, key, value, rows):
     tokens, width = query.shape[1], query.shape[2] // rows
 
-    def body(place_ref, q_ref, k_ref, v_ref, *out):
-        for slot in range(rows):
-
-            @pl.when(pl.program_id(0) == slot)
-            def _():
-                out[slot][0] = q_ref[0]
-                out[slot][1] = k_ref[0]
-                out[slot][2] = v_ref[0]
-
-    part = pl.BlockSpec((1, tokens, width), lambda j, place_ref: (0, 0, place_ref[0] ^ j))
+    def body(place_ref, *refs):
+        ins, outs, (held, sems) = refs[:3], refs[3:-2], refs[-2:]
+        moves = []
+        for slot in (*range(1, rows), 0):
+            start = pl.multiple_of((place_ref[0] ^ slot) * width, HDIM)
+            for at in range(3):
+                box = held.at[slot, at]
+                moves.append(
+                    (
+                        pltpu.make_async_copy(
+                            ins[at].at[0, :, pl.ds(start, width)], box, sems.at[0, slot, at]
+                        ),
+                        pltpu.make_async_copy(box, outs[slot].at[at], sems.at[1, slot, at]),
+                    )
+                )
+        run(moves)
+
     shape = (3, tokens, width)
     return pl.pallas_call(
         body,
         grid_spec=pltpu.PrefetchScalarGridSpec(
             num_scalar_prefetch=1,
-            grid=(rows,),
-            in_specs=[part] * 3,
-            out_specs=[whole(shape)] * rows,
+            grid=(1,),
+            in_specs=[pl.BlockSpec(memory_space=pl.ANY)] * 3,
+            out_specs=[pl.BlockSpec(memory_space=pl.ANY)] * rows,
+            scratch_shapes=[
+                pltpu.VMEM((rows, *shape), query.dtype),
+                pltpu.SemaphoreType.DMA((2, rows, 3)),
+            ],
         ),
         out_shape=[jax.ShapeDtypeStruct(shape, query.dtype)] * rows,
         cost_estimate=cost(0, 12 * query.size),
         name="pack",
     )(place, query, key, value)
+
+
+def run(moves):
+    for fetch, _ in moves:
+        fetch.start()
+    for fetch, store in moves:
+        fetch.wait()
+        store.start()
+    for _, store in moves:
+        store.wait()
 
 
 def unpack(place, parts):
@@ -61,31 +82,46 @@
     tokens = parts[0][0].shape[1]
     widths = [part[0].shape[2] for part in parts]
     starts = [sum(widths[:at]) for at in range(calls + 1)]
+    width = starts[-1]
 
     def body(place_ref, *refs):
-        ins, outs = refs[:-3], refs[-3:]
-        for slot in range(rows):
-
-            @pl.when(pl.program_id(0) == slot)
-            def _():
-                for call in range(calls):
-                    for at in range(3):
-                        outs[at][0, :, starts[call] : starts[call + 1]] = ins[
-                            call * rows + slot
-                        ][at]
-
-    part = pl.BlockSpec((1, tokens, starts[-1]), lambda j, place_ref: (0, 0, place_ref[0] ^ j))
-    full = jax.ShapeDtypeStruct((1, tokens, starts[-1] * rows), parts[0][0].dtype)
+        ins, outs, held, sems = refs[: calls * rows], refs[calls * rows : -2], refs[-2], refs[-1]
+        moves = []
+        for call in range(calls):
+            for slot in range(rows):
+                start = (place_ref[0] ^ slot) * width + starts[call]
+                start = pl.multiple_of(start, HDIM)
+                for at in range(3):
+                    box = held.at[slot, at, :, starts[call] : starts[call + 1]]
+                    moves.append(
+                        (
+                            pltpu.make_async_copy(
+                                ins[call * rows + slot].at[at], box, sems.at[0, call, slot, at]
+                            ),
+                            pltpu.make_async_copy(
+                                box,
+                                outs[at].at[0, :, pl.ds(start, widths[call])],
+                                sems.at[1, call, slot, at],
+                            ),
+                        )
+                    )
+        run(moves)
+
+    full = jax.ShapeDtypeStruct((1, tokens, width * rows), parts[0][0].dtype)
     return pl.pallas_call(
         body,
         grid_spec=pltpu.PrefetchScalarGridSpec(
             num_scalar_prefetch=1,
-            grid=(rows,),
-            in_specs=[whole(block.shape) for part in parts for block in part],
-            out_specs=[part] * 3,
+            grid=(1,),
+            in_specs=[pl.BlockSpec(memory_space=pl.ANY)] * (calls * rows),
+            out_specs=[pl.BlockSpec(memory_space=pl.ANY)] * 3,
+            scratch_shapes=[
+                pltpu.VMEM((rows, 3, tokens, width), parts[0][0].dtype),
+                pltpu.SemaphoreType.DMA((2, calls, rows, 3)),
+            ],
         ),
         out_shape=[full] * 3,
-        cost_estimate=cost(0, 12 * tokens * starts[-1] * rows),
+        cost_estimate=cost(0, 12 * tokens * width * rows),
         name="unpack",
     )(place, *(block for part in parts for block in part))
 
@@ -137,25 +173,24 @@
     factor = 1.0 / math.sqrt(HDIM)
 
     def body(*refs):
-        ins, (probs_ref, grad_ref), outs = refs[:rows], refs[rows : rows + 2], refs[rows + 2 :]
+        ins, (probs_ref, grad_ref) = refs[:rows], refs[rows : rows + 2]
+        outs, scores_ref = refs[rows + 2 : -1], refs[-1]
+        queries = jnp.concatenate([ref[0] for ref in ins], axis=0)
         keys = jnp.concatenate([ref[1] for ref in ins], axis=0).T
         values = jnp.concatenate([ref[2] for ref in ins], axis=0)
-        grad_key = jnp.zeros((length, HDIM), jnp.float32)
-        grad_value = jnp.zeros((length, HDIM), jnp.float32)
         for slot in range(rows):
             across = slice(slot * tokens, (slot + 1) * tokens)
-            grad = grad_ref[:, across]
-            low = probs_ref[0, :, across]
-            high = low.astype(jnp.float32)
-            grad_probs = dot(values, grad)
-            centre = jnp.sum(high * grad_probs, axis=0, keepdims=True)
-            grad_scores = (high * (grad_probs - centre)).astype(jnp.bfloat16)
-            outs[slot][0] = (dot(keys, grad_scores) * factor).T.astype(jnp.bfloat16)
-            grad_key += dot(grad_scores, ins[slot][0])
-            grad_value += dot(low, grad, NT)
-        grad_key *= factor
+            probs = probs_ref[0, :, across].astype(jnp.float32)
+            terms = probs * dot(values, grad_ref[:, across])
+            centre = jnp.sum(terms, axis=0, keepdims=True)
+            scores_ref[:, across] = (terms - probs * centre).astype(jnp.bfloat16)
+        scores = scores_ref[...]
+        grad_query = (dot(keys, scores) * factor).T
+        grad_key = dot(scores, queries) * factor
+        grad_value = dot(probs_ref[0], grad_ref[...], NT)
         for slot in range(rows):
             down = slice(slot * tokens, (slot + 1) * tokens)
+            outs[slot][0] = grad_query[down].astype(jnp.bfloat16)
             outs[slot][1] = grad_key[down].astype(jnp.bfloat16)
             outs[slot][2] = grad_value[down].astype(jnp.bfloat16)
 
@@ -171,17 +206,22 @@
         ],
         out_specs=[pl.BlockSpec((3, tokens, HDIM), lambda i: (0, 0, i))] * rows,
         out_shape=[jax.ShapeDtypeStruct(shape, jnp.bfloat16)] * rows,
+        scratch_shapes=[pltpu.VMEM((length, length), jnp.bfloat16)],
         cost_estimate=cost(8 * count * length * length * HDIM, 2 * count * length * length),
         name="backward",
     )(*parts, probs, grad_attn)
 
 
+def columns_of(blocks, odd):
+    return jnp.concatenate(
+        [ref[...] for ref in blocks[:-2]] + [jnp.where(odd, blocks[-1][...], blocks[-2][...])], axis=0
+    )
+
+
 def project(place, weights, grads):
-    chunks, rows = len(grads), len(grads[0])
+    chunks, count = len(grads), len(grads[0])
     half, depth = weights[0].shape
-    tokens, wide = grads[0][0].shape
-    steps = 2
-    step = wide // steps
+    tokens, step = grads[0][-1].shape
 
     def body(place_ref, *refs):
         first, second = refs[:2]
@@ -190,18 +230,16 @@
         lines = jnp.concatenate([first[...], second[...]], axis=0)
         for chunk in range(chunks):
 
-            @pl.when(at // steps == chunk)
+            @pl.when(at // 2 == chunk)
             def _():
-                columns = jnp.concatenate(
-                    [ins[chunk * rows + slot][...] for slot in range(rows)], axis=0
-                )
+                columns = columns_of(ins[chunk * count : (chunk + 1) * count], at % 2 == 1)
                 term = dot(lines, columns, NT)
                 if chunk:
                     total[...] += term
                 else:
                     total[...] = jnp.where(at == 0, 0.0, total[...]) + term
 
-        @pl.when(at == chunks * steps - 1)
+        @pl.when(at == chunks * 2 - 1)
         def _():
             for core in range(2):
 
@@ -212,17 +250,21 @@
 
     def block_of(chunk):
         return pl.BlockSpec(
-            (tokens, step), lambda i, place_ref: (0, jnp.clip(i - chunk * steps, 0, steps - 1))
+            (tokens, step), lambda i, place_ref: (0, jnp.clip(i - chunk * 2, 0, 1))
         )
 
-    shape = (2 * half, rows * tokens)
+    shape = (2 * half, (count - 1) * tokens)
     return pl.pallas_call(
         body,
         grid_spec=pltpu.PrefetchScalarGridSpec(
             num_scalar_prefetch=1,
-            grid=(chunks * steps,),
+            grid=(chunks * 2,),
             in_specs=[pl.BlockSpec((half, step), lambda i, place_ref: (0, i))] * 2
-            + [block_of(chunk) for chunk in range(chunks) for _ in range(rows)],
+            + [
+                spec
+                for chunk in range(chunks)
+                for spec in [block_of(chunk)] * (count - 2) + [whole((tokens, step))] * 2
+            ],
             out_specs=whole(shape),
             scratch_shapes=[pltpu.VMEM(shape, jnp.float32)],
         ),
@@ -232,65 +274,72 @@
     )(place, *weights, *(block for chunk in grads for block in chunk))
 
 
-def weight_terms(place, attended, grads, planes):
-    rows = len(grads)
+def weight_terms(place, attended, grads):
+    rows = len(grads) - 1
     width, length = attended.shape
-    tokens, wide = grads[0].shape
-    piece = width // 2 // planes
-    step = wide // 2
+    tokens, step = grads[-1].shape
+    piece = width // 2 // rows
 
     def body(place_ref, attended_ref, *refs):
-        ins, (keep, give) = refs[:rows], refs[rows:]
-        columns = jnp.concatenate([ref[...] for ref in ins], axis=0)
+        ins, (keep, give) = refs[:-2], refs[-2:]
+        columns = columns_of(ins, pl.program_id(0) == 1)
         term = dot(attended_ref[...], columns).astype(jnp.bfloat16)
-        plane, core = place_ref[1], place_ref[2]
+        row, core = place_ref[0], place_ref[2]
         for side in range(2):
             for out, mine in ((keep, core == side), (give, core != side)):
 
                 @pl.when(mine)
                 def _():
-                    for at in range(planes):
-                        start = (side * planes + at) * piece
-                        out[(at - plane) & (planes - 1)] = term[start : start + piece]
-
-    shape = jax.ShapeDtypeStruct((planes, piece, wide), jnp.bfloat16)
-    spec = pl.BlockSpec((planes, piece, step), lambda i, place_ref: (0, 0, i))
+                    for at in range(rows):
+                        start = (side * rows + at) * piece
+                        out[at ^ row] = term[start : start + piece]
+
+    shape = jax.ShapeDtypeStruct((rows, piece, 2 * step), jnp.bfloat16)
+    spec = pl.BlockSpec((rows, piece, step), lambda i, place_ref: (0, 0, i))
     return pl.pallas_call(
         body,
         grid_spec=pltpu.PrefetchScalarGridSpec(
             num_scalar_prefetch=1,
-            grid=(wide // step,),
+            grid=(2,),
             in_specs=[whole((width, length))]
-            + [pl.BlockSpec((tokens, step), lambda i, place_ref: (0, i))] * rows,
+            + [pl.BlockSpec((tokens, step), lambda i, place_ref: (0, i))] * (rows - 1)
+            + [whole((tokens, step))] * 2,
             out_specs=[spec] * 2,
         ),
         out_shape=[shape] * 2,
-        cost_estimate=cost(2 * width * length * wide, 2 * (width * length + length * wide)),
+        cost_estimate=cost(4 * width * length * step, 2 * (width * length + 2 * length * step)),
         name="weight_terms",
     )(place, attended, *grads)
 
 
-def assemble(place, pieces, planes):
-    chunks = len(pieces)
+def assemble(place, pieces):
+    chunks, rows = len(pieces), len(pieces[0])
     piece, wide = pieces[0][0].shape
+    step = wide // 2
 
     def body(place_ref, *refs):
         ins, out = refs[:-1], refs[-1]
         for chunk in range(chunks):
-            for turn in range(planes):
-                start = (((place_ref[1] ^ place_ref[0]) - turn) & (planes - 1)) * piece
-                out[pl.ds(pl.multiple_of(start, 16), piece), chunk * wide : (chunk + 1) * wide] = (
-                    ins[chunk * planes + turn][...].astype(out.dtype)
-                )
-
-    shape = (planes * piece, chunks * wide)
+
+            @pl.when(pl.program_id(0) // 2 == chunk)
+            def _():
+                for slot in range(rows):
+                    start = (place_ref[0] ^ slot) * piece
+                    out[pl.ds(pl.multiple_of(start, 16), piece), :] = ins[chunk * rows + slot][
+                        ...
+                    ].astype(out.dtype)
+
+    def block_of(chunk):
+        return pl.BlockSpec((piece, step), lambda i, place_ref: (0, jnp.clip(i - 2 * chunk, 0, 1)))
+
+    shape = (rows * piece, chunks * wide)
     return pl.pallas_call(
         body,
         grid_spec=pltpu.PrefetchScalarGridSpec(
             num_scalar_prefetch=1,
-            grid=(1,),
-            in_specs=[whole((piece, wide))] * (chunks * planes),
-            out_specs=whole(shape),
+            grid=(2 * chunks,),
+            in_specs=[block_of(chunk) for chunk in range(chunks) for _ in range(rows)],
+            out_specs=pl.BlockSpec((rows * piece, step), lambda i, place_ref: (0, i)),
         ),
         out_shape=jax.ShapeDtypeStruct(shape, jnp.float32),
         cost_estimate=cost(0, 6 * shape[0] * shape[1]),
@@ -330,62 +379,71 @@
 
     grad_flat = grad_out[0]
     wide = grad_flat.shape[1] // 2
-    left, right = grad_flat[:, :wide], grad_flat[:, wide:]
-    left_x, right_y = to_row(left, 1), to_row(right, 2)
+
+    def gather(chunk):
+        by_x, by_y = to_row(chunk, 1), to_row(chunk, 2)
+        even = to_row(by_x[:, : wide // 2], 2)
+        odd = to_row(by_y[:, wide // 2 :], 1)
+        return [chunk, by_x, by_y, even, odd]
+
+    grads = [gather(grad_flat[:, :wide])]
+
+    lines = [w_out] + [
+        send(w_out, lambda z, c, r: ((z + ahead) % planes, c, r) if z == r else None)
+        for ahead in range(1, planes)
+    ]
 
     packed = pack(place, query_rows, key_rows, value_rows, rows)
     parts = [packed[0]] + [to_row(packed[slot], slot) for slot in range(1, rows)]
-
-    here = w_out
+    probs, attended = forward(parts)
+    grads.append(gather(after(grad_flat[:, wide:], parts)))
+
+    def reduce_cores(attended, chunk):
+        keep, give = weight_terms(place, attended, chunk)
+        return keep, to_core(give)
+
+    def spread(keep, got):
+        both = [
+            (keep[slot].astype(jnp.float32) + got[slot].astype(jnp.float32)).astype(jnp.bfloat16)
+            for slot in range(rows)
+        ]
+        return [both[0]] + [to_row(both[slot], slot) for slot in range(1, rows)]
+
+    def reduce_planes(blocks):
+        stack = jnp.stack(blocks)
+
+        def block_of(ahead):
+            return lax.dynamic_index_in_dim(stack, ((plane + ahead) % planes) ^ row, 0, False)
+
+        return block_of(0), [to_plane(block_of(ahead), ahead) for ahead in range(1, planes)]
+
+    def collect(total, got):
+        for part in got:
+            total = total.astype(jnp.float32) + part.astype(jnp.float32)
+        total = total.astype(jnp.bfloat16)
+        return [total] + [to_row(total, slot) for slot in range(1, rows)]
+
+    early = reduce_planes(spread(*reduce_cores(attended, grads[0])))
+    late = reduce_cores(after(attended, early[0]), grads[1])
+    lines = after(lines, late[0])
+    here = lines[0]
     for ahead in range(1, planes):
-        got = send(w_out, lambda z, c, r: ((z + ahead) % planes, c, r) if z == r else None)
-        here = jnp.where((plane - row) % planes == ahead, got, here)
-    weights = [here, to_core(here)]
-
-    hand_y, hand_x = to_row(left_x, 2), to_row(right_y, 1)
-    left, right = after((left, right), left_x, right_y)
-    left_y, right_x = to_row(left, 2), to_row(right, 1)
-    grads = [[left, left_x, left_y, hand_y], [right, right_x, right_y, hand_x]]
-
-    probs, attended = forward(parts)
-
-    def reduce_cores(attended, chunk):
-        keep, give = weight_terms(place, attended, chunk, planes)
-        got = to_core(give)
-        return [
-            (keep[at].astype(jnp.float32) + got[at].astype(jnp.float32)).astype(jnp.bfloat16)
-            for at in range(planes)
-        ]
-
-    def reduce_planes(both, *done):
-        got = [to_plane(both[ahead], ahead) for ahead in range(1, planes)]
-        got = after(got, *done)
-        total = both[0].astype(jnp.float32)
-        for part in got:
-            total = total + part.astype(jnp.float32)
-        return total.astype(jnp.bfloat16)
-
-    def deliver(total):
-        return [
-            send(total, lambda z, c, r: (r, c, r ^ ((z + turn) % planes)))
-            for turn in range(planes)
-        ]
-
-    both = [reduce_cores(attended, grads[0])]
-    both.append(reduce_cores(after(attended, both[0]), grads[1]))
-    grad_attn = project(place, after(weights, both[1]), grads)
+        here = jnp.where((plane - row) % planes == ahead, lines[ahead], here)
+    other = to_core(here)
+    grad_attn = project(place, [here, other], grads)
     heads = probs.shape[0]
-    back, sent = [], []
-    for first, count in ((0, 1), (1, heads - 1)):
-        sent.append(backward(parts, probs, grad_attn, first, count))
-        back.append([sent[-1][0]] + [to_row(sent[-1][slot], slot) for slot in range(1, rows)])
-        if not first:
-            early = reduce_planes(both[0], sent[0][0])
-            probs = after(probs, early)
-    late = reduce_planes(both[1], sent[1][0])
-    pieces = [deliver(early), deliver(late)]
+    sent = [backward(parts, probs, grad_attn, 0, 1)]
+    blocks = after(spread(*late), sent[0][0])
+    late = reduce_planes(blocks)
+    sent.append(backward(parts, after(probs, late[0]), grad_attn, 1, heads - 1))
+    back = [
+        [message[0]]
+        + [to_row(message[slot], slot) for slot in range(1, rows)]
+        for message in sent
+    ]
+    pieces = [collect(*early), collect(*after(late, sent[1][0]))]
     grad_query, grad_key, grad_value = unpack(place, back)
-    grad_w_out = assemble(place, pieces, planes)
+    grad_w_out = assemble(place, pieces)
     return grad_query, grad_key, grad_value, grad_w_out
 
 

time: 260 us -> 281 us (1.081)
  waiting for transfers between devices: 105 us -> 153 us
  starting transfers between devices: 80.7 us -> 53.4 us
  local copies, waits for them, and re-layouts: 5.1 us -> 10.3 us
  Pallas kernels: 60.6 us -> 56.7 us
    ppermute x35 -> x41, waiting for transfers between devices: 105 us -> 153 us  [send(): return lax.ppermute(array, ('fsdp', 'rows'), pairs)]
    ppermute x35 -> x41, starting transfers between devices: 80.7 us -> 53.4 us  [send(): return lax.ppermute(array, ('fsdp', 'rows'), pairs)]
    pallas_call x2, Pallas kernels: 17.1 us -> 14.2 us  [backward(): pl.pallas_call(body, grid=(count,), in_specs=[part] * rows + [pl.BlockSpe...]
    slice x1 -> x5, local copies, waits for them, and re-layouts: 1.47 us -> 4.33 us  [the longest x2 1.81 us: gather(): even = to_row(by_x[:, :wide // 2], 2)]
  transfers between devices with their start and end apart: 35 -> 41, of which waited for: 12 -> 16; matrix products, arithmetic and copies ran while one was open for 2% -> 3% of each run, Pallas kernels for 22% -> 17%
where the time goes in v2:
time: 281 us; the launch traced here: 280 us
  waiting for transfers between devices  153 us (54%)
  Pallas kernels  56.7 us (20%)
  starting transfers between devices  53.4 us (19%)
  local copies, waits for them, and re-layouts  10.3 us (4%)
  other arithmetic  5.61 us (2%)
    ppermute x41, waiting for transfers between devices, send(): return lax.ppermute(array, ('fsdp', 'rows'), pairs)  153 us
    ppermute x41, starting transfers between devices, send(): return lax.ppermute(array, ('fsdp', 'rows'), pairs)  53.4 us
    pallas_call x2, Pallas kernels, backward(): pl.pallas_call(body, grid=(count,), in_specs=[part] * rows + [pl.BlockSpe...  14.2 us
    pallas_call x1, Pallas kernels, forward(): pl.pallas_call(body, grid=(heads,), in_specs=[part] * rows, out_specs=[pl...  12.6 us
    pallas_call x2, Pallas kernels, weight_terms(): pl.pallas_call(body, grid_spec=pltpu.PrefetchScalarGridSpec(num_scalar_pr...  10.2 us
    pallas_call x1, Pallas kernels, project(): pl.pallas_call(body, grid_spec=pltpu.PrefetchScalarGridSpec(num_scalar_pr...  8.24 us
  transfers between devices with their start and end apart: 41, of which 16 were waited for; matrix products, arithmetic and copies ran while one was open for 3% of the time, Pallas kernels for 17%

profile of v2, /device:TPU:0, one launch (start us, length us, event | category | flops | bytes accessed | tf_op | source)
XLA Modules:
  0.0 280.3 jit_solution(4045791528271576343)
XLA Ops:
  0.6 1.5 fusion.7
  2.1 3.0 %collective-permute-start.6 = (bf16[256,1536]{1,0:T(8,128)(2,1)S(1)}, bf16[256,1536]{1,0:T(8,128)(2,1)}, u32[]{:S(2)}, u32[]{:S(2)}) collective-permute-start(bf16[256,1536]{1,0:T(8,128)(2,1)S(1)} %get-tuple-element.79.refs_0_.refs_2_), channel_id=1, source_target_pairs={{0,1},{1,0},{2,3},{3,2},{4,5},{5,4},{6,7},{7,6},{8,9},{9,8},{10,11... | collective-permute-start | bytes 2359304 | tf_op jit(solution)/shard_map/ppermute | solution.py:369
  5.2 1.5 collective-permute-start.7
  6.7 0.7 pad_add_fusion.place_ref
  7.4 3.3 %pack.1 = (bf16[3,256,384]{2,1,0:T(8,128)(2,1)}, bf16[3,256,384]{2,1,0:T(8,128)(2,1)}, bf16[3,256,384]{2,1,0:T(8,128)(2,1)}, bf16[3,256,384]{2,1,0:T(8,128)(2,1)}) custom-call(s32[3]{0:T(128)} %pad_add_fusion.place_ref, bf16[1,256,1536]{2,1,0:T(8,128)(2,1)} %refs_0_.1, bf16[1,256,1536]{2,1,0:T(8,128)(2,1)} %refs_1_.1, bf16[1,256,1536]{2,1,0:T(8,128)(2,1)} %refs_2_.1), custom_call_target="tpu_custom_call" | custom-call | bytes 4718592 | tf_op jit(solution)/shard_map/pack/pallas_call | solution.py:52
  10.7 0.6 collective-permute-start
  11.3 2.9 %collective-permute-start.2 = (bf16[3,256,384]{2,1,0:T(8,128)(2,1)}, bf16[3,256,384]{2,1,0:T(8,128)(2,1)S(1)}, u32[]{:S(2)}, u32[]{:S(2)}) collective-permute-start(bf16[3,256,384]{2,1,0:T(8,128)(2,1)} %get-tuple-element.43), channel_id=1, source_target_pairs={{0,3},{1,2},{2,1},{3,0},{4,7},{5,6},{6,5},{7,4},{8,11},{9,10},{10,... | collective-permute-start | bytes 1769480 | tf_op jit(solution)/shard_map/ppermute | solution.py:369
  14.2 9.4 %collective-permute-done.6.refs_1_.refs_3_ = bf16[256,1536]{1,0:T(8,128)(2,1)} collective-permute-done((bf16[256,1536]{1,0:T(8,128)(2,1)S(1)}, bf16[256,1536]{1,0:T(8,128)(2,1)}, u32[]{:S(2)}, u32[]{:S(2)}) %collective-permute-start.6) | collective-permute-done | bytes 786464 | tf_op jit(solution)/shard_map/ppermute | solution.py:369
  23.7 1.8 slice.89
  25.4 2.0 collective-permute-start.8
  27.5 1.0 slice.90
  28.5 1.6 collective-permute-start.9
  30.1 6.1 %collective-permute-done.refs_1_ = bf16[3,256,384]{2,1,0:T(8,128)(2,1)S(1)} collective-permute-done((bf16[3,256,384]{2,1,0:T(8,128)(2,1)}, bf16[3,256,384]{2,1,0:T(8,128)(2,1)S(1)}, u32[]{:S(2)}, u32[]{:S(2)}) %collective-permute-start) | collective-permute-done | bytes 589856 | tf_op jit(solution)/shard_map/ppermute | solution.py:369
  36.2 14.7 %collective-permute-done.1.refs_2_ = bf16[3,256,384]{2,1,0:T(8,128)(2,1)S(1)} collective-permute-done((bf16[3,256,384]{2,1,0:T(8,128)(2,1)}, bf16[3,256,384]{2,1,0:T(8,128)(2,1)S(1)}, u32[]{:S(2)}, u32[]{:S(2)}) %collective-permute-start.1) | collective-permute-done | bytes 589856 | tf_op jit(solution)/shard_map/ppermute | solution.py:369
  50.9 0.8 copy-done.4
  51.9 12.6 %forward.1 = (bf16[3,1024,1024]{2,1,0:T(8,128)(2,1)}, bf16[384,1024]{1,0:T(8,128)(2,1)}) custom-call(bf16[3,256,384]{2,1,0:T(8,128)(2,1)} %get-tuple-element.40.refs_0_, bf16[3,256,384]{2,1,0:T(8,128)(2,1)} %copy-done.3, bf16[3,256,384]{2,1,0:T(8,128)(2,1)} %copy-done.4, bf16[3,256,384]{2,1,0:T(8,128)(2,1)} %copy-done.5), custom_call_target="tpu_custom_call" | custom-call | flops 3221225472 | bytes 6291456 | tf_op jit(solution)/shard_map/forward/pallas_call | solution.py:150
  64.5 0.7 copy-done.12
  65.2 5.1 %weight_terms.2 = (bf16[4,48,1536]{2,1,0:T(8,128)(2,1)}, bf16[4,48,1536]{2,1,0:T(8,128)(2,1)}) custom-call(s32[3]{0:T(128)} %pad_add_fusion.place_ref, bf16[384,1024]{1,0:T(8,128)(2,1)} %get-tuple-element.48.attended_ref, bf16[256,1536]{1,0:T(8,128)(2,1)} %copy-done.2, bf16[256,1536]{1,0:T(8,128)(2,1)} %collective-permute-done.6.refs_1_.refs_3_, ...), custom_call_target="tpu_custom_call" | custom-call | flops 1207959552 | bytes 3932160 | tf_op jit(solution)/shard_map/weight_terms/pallas_call | solution.py:299
  70.3 0.8 collective-permute-start.14
  71.2 1.3 collective-permute-start.15
  72.5 1.3 add_convert_fusion.9
  73.8 1.5 collective-permute-start.11
  75.3 0.7 collective-permute-start.12
  75.9 1.4 collective-permute-start.13
  77.4 16.6 %collective-permute-done.11 = bf16[48,1536]{1,0:T(8,128)(2,1)S(1)} collective-permute-done((bf16[48,1536]{1,0:T(8,128)(2,1)S(1)}, bf16[48,1536]{1,0:T(8,128)(2,1)S(1)}, u32[]{:S(2)}, u32[]{:S(2)}) %collective-permute-start.11) | collective-permute-done | bytes 147488 | tf_op jit(solution)/shard_map/ppermute | solution.py:369
  94.0 4.5 %collective-permute-start.3 = (bf16[192,3072]{1,0:T(8,128)(2,1)}, bf16[192,3072]{1,0:T(8,128)(2,1)}, u32[]{:S(2)}, u32[]{:S(2)}) collective-permute-start(bf16[192,3072]{1,0:T(8,128)(2,1)} %param.9), channel_id=1, source_target_pairs={{0,8},{4,12},{9,17},{13,21},{18,26},{22,30},{27,3},{31,7}} | collective-permute-start | bytes 3538952 | tf_op jit(solution)/shard_map/ppermute | solution.py:369
  98.5 3.0 %collective-permute-start.4 = (bf16[192,3072]{1,0:T(8,128)(2,1)}, bf16[192,3072]{1,0:T(8,128)(2,1)}, u32[]{:S(2)}, u32[]{:S(2)}) collective-permute-start(bf16[192,3072]{1,0:T(8,128)(2,1)} %param.9), channel_id=1, source_target_pairs={{0,16},{4,20},{9,25},{13,29},{18,2},{22,6},{27,11},{31,15}} | collective-permute-start | bytes 3538952 | tf_op jit(solution)/shard_map/ppermute | solution.py:369
  101.5 2.8 collective-permute-start.5
  104.4 0.8 dynamic-slice_bitcast_fusion.5
  105.3 72.4 %collective-permute-done.29 = bf16[48,1536]{1,0:T(8,128)(2,1)S(1)} collective-permute-done((bf16[48,1536]{1,0:T(8,128)(2,1)S(1)}, bf16[48,1536]{1,0:T(8,128)(2,1)S(1)}, u32[]{:S(2)}, u32[]{:S(2)}) %collective-permute-start.29) | collective-permute-done | bytes 147488 | tf_op jit(solution)/shard_map/ppermute | solution.py:369
  177.8 2.9 %collective-permute-done.30 = bf16[48,1536]{1,0:T(8,128)(2,1)} collective-permute-done((bf16[48,1536]{1,0:T(8,128)(2,1)}, bf16[48,1536]{1,0:T(8,128)(2,1)}, u32[]{:S(2)}, u32[]{:S(2)}) %collective-permute-start.30) | collective-permute-done | bytes 147488 | tf_op jit(solution)/shard_map/ppermute | solution.py:369
  180.7 3.0 %collective-permute-done.31 = bf16[48,1536]{1,0:T(8,128)(2,1)} collective-permute-done((bf16[48,1536]{1,0:T(8,128)(2,1)}, bf16[48,1536]{1,0:T(8,128)(2,1)}, u32[]{:S(2)}, u32[]{:S(2)}) %collective-permute-start.31) | collective-permute-done | bytes 147488 | tf_op jit(solution)/shard_map/ppermute | solution.py:369
  183.6 1.7 add_convert_fusion.1
  185.3 3.1 %collective-permute-done.16.refs_3_.refs_10_ = bf16[256,768]{1,0:T(8,128)(2,1)S(1)} collective-permute-done((bf16[256,768]{1,0:T(8,128)(2,1)S(1)}, bf16[256,768]{1,0:T(8,128)(2,1)S(1)}, u32[]{:S(2)}, u32[]{:S(2)}) %collective-permute-start.16) | collective-permute-done | bytes 393248 | tf_op jit(solution)/shard_map/ppermute | solution.py:369
  188.4 3.0 %collective-permute-done.17.refs_4_.refs_11_ = bf16[256,768]{1,0:T(8,128)(2,1)S(1)} collective-permute-done((bf16[256,768]{1,0:T(8,128)(2,1)S(1)}, bf16[256,768]{1,0:T(8,128)(2,1)S(1)}, u32[]{:S(2)}, u32[]{:S(2)}) %collective-permute-start.17) | collective-permute-done | bytes 393248 | tf_op jit(solution)/shard_map/ppermute | solution.py:369
  191.5 0.7 copy-done.14
  192.2 5.1 %weight_terms.3 = (bf16[4,48,1536]{2,1,0:T(8,128)(2,1)}, bf16[4,48,1536]{2,1,0:T(8,128)(2,1)}) custom-call(s32[3]{0:T(128)} %pad_add_fusion.place_ref, bf16[384,1024]{1,0:T(8,128)(2,1)} %get-tuple-element.48.attended_ref, bf16[256,1536]{1,0:T(8,128)(2,1)} %copy-done.1, bf16[256,1536]{1,0:T(8,128)(2,1)} %copy-done.6, bf16[256,1536]{1,0:T(8,128)(2,1)} %copy-done.7, ...), custom_call_target="tpu_custom_call" | custom-call | flops 1207959552 | bytes 3932160 | tf_op jit(solution)/shard_map/weight_terms/pallas_call | solution.py:299
  197.4 1.6 select_select_fusion.refs_0_
  199.1 0.5 collective-permute-start.22
  199.6 0.6 collective-permute-start.32
  200.2 3.7 %collective-permute-start.33 = (bf16[48,1536]{1,0:T(8,128)(2,1)S(1)}, bf16[48,1536]{1,0:T(8,128)(2,1)}, u32[]{:S(2)}, u32[]{:S(2)}) collective-permute-start(bf16[48,1536]{1,0:T(8,128)(2,1)S(1)} %copy-done.10), channel_id=1, source_target_pairs={{0,2},{1,3},{2,0},{3,1},{4,6},{5,7},{6,4},{7,5},{8,10},{9,11},{10,... | collective-permute-start | bytes 442376 | tf_op jit(solution)/shard_map/ppermute | solution.py:369
  204.4 2.8 %collective-permute-start.24 = (bf16[48,1536]{1,0:T(8,128)(2,1)S(1)}, bf16[48,1536]{1,0:T(8,128)(2,1)S(1)}, u32[]{:S(2)}, u32[]{:S(2)}) collective-permute-start(bf16[48,1536]{1,0:T(8,128)(2,1)S(1)} %get-tuple-element.81), channel_id=1, source_target_pairs={{0,2},{1,3},{2,0},{3,1},{4,6},{5,7},{6,4},{7,5},{8,10},{9,11},{10,... | collective-permute-start | bytes 442376 | tf_op jit(solution)/shard_map/ppermute | solution.py:369
  207.6 0.8 copy-done.8
  208.3 8.2 %project.1.refs_5_ = bf16[384,1024]{1,0:T(8,128)(2,1)} custom-call(s32[3]{0:T(128)} %pad_add_fusion.place_ref, bf16[192,3072]{1,0:T(8,128)(2,1)} %copy-done, bf16[192,3072]{1,0:T(8,128)(2,1)} %copy-done.8, bf16[256,1536]{1,0:T(8,128)(2,1)} %copy-done.2, bf16[256,1536]{1,0:T(8,128)(2,1)} %collective-permute-done.6.refs_1_.refs_3_, ...), custom_call_target="tpu_custom_call" | custom-call | flops 2415919104 | bytes 8650752 | tf_op jit(solution)/shard_map/project/pallas_call | solution.py:257
  216.6 5.7 %backward.2 = (bf16[3,256,128]{2,1,0:T(8,128)(2,1)}, bf16[3,256,128]{2,1,0:T(8,128)(2,1)}, bf16[3,256,128]{2,1,0:T(8,128)(2,1)}, bf16[3,256,128]{2,1,0:T(8,128)(2,1)}) custom-call(bf16[3,256,384]{2,1,0:T(8,128)(2,1)} %get-tuple-element.40.refs_0_, bf16[3,256,384]{2,1,0:T(8,128)(2,1)} %copy-done.3, bf16[3,256,384]{2,1,0:T(8,128)(2,1)} %copy-done.4, ...), custom_call_target="tpu_custom_call" | custom-call | flops 1073741824 | bytes 2097152 | tf_op jit(solution)/shard_map/backward/pallas_call | solution.py:199
  222.7 2.9 %collective-permute-start.36 = (bf16[48,1536]{1,0:T(8,128)(2,1)S(1)}, bf16[48,1536]{1,0:T(8,128)(2,1)S(1)}, u32[]{:S(2)}, u32[]{:S(2)}) collective-permute-start(bf16[48,1536]{1,0:T(8,128)(2,1)S(1)} %get-tuple-element.89), channel_id=1, source_target_pairs={{0,16},{1,17},{2,18},{3,19},{4,20},{5,21},{6,22},{7,23},{8,24},{9,... | collective-permute-start | bytes 442376 | tf_op jit(solution)/shard_map/ppermute | solution.py:369
  225.6 1.1 collective-permute-start.37
  226.7 8.5 %backward.3 = (bf16[3,256,256]{2,1,0:T(8,128)(2,1)}, bf16[3,256,256]{2,1,0:T(8,128)(2,1)}, bf16[3,256,256]{2,1,0:T(8,128)(2,1)}, bf16[3,256,256]{2,1,0:T(8,128)(2,1)}) custom-call(bf16[3,256,384]{2,1,0:T(8,128)(2,1)} %get-tuple-element.40.refs_0_, bf16[3,256,384]{2,1,0:T(8,128)(2,1)} %copy-done.3, bf16[3,256,384]{2,1,0:T(8,128)(2,1)} %copy-done.4, ...), custom_call_target="tpu_custom_call" | custom-call | flops 2147483648 | bytes 4194304 | tf_op jit(solution)/shard_map/backward/pallas_call | solution.py:199
  235.2 1.9 collective-permute-start.34
  237.4 1.9 collective-permute-start.38
  239.5 1.5 collective-permute-start.27
  241.0 1.9 collective-permute-done.34.refs_3_
  242.9 1.8 collective-permute-start.28
  244.8 1.5 collective-permute-done.19.refs_1_
  246.2 1.5 collective-permute-start.39
  247.7 1.7 collective-permute-done.38.refs_5_
  249.4 1.4 collective-permute-start.40
  250.7 2.3 collective-permute-done.39.refs_6_
  253.0 1.1 collective-permute-start.20
  254.1 14.2 %collective-permute-done.40.refs_7_ = bf16[48,1536]{1,0:T(8,128)(2,1)S(1)} collective-permute-done((bf16[48,1536]{1,0:T(8,128)(2,1)S(1)}, bf16[48,1536]{1,0:T(8,128)(2,1)S(1)}, u32[]{:S(2)}, u32[]{:S(2)}) %collective-permute-start.40) | collective-permute-done | bytes 147488 | tf_op jit(solution)/shard_map/ppermute | solution.py:369
  268.3 1.5 collective-permute-start.21
  269.9 4.7 %assemble.1 = f32[192,3072]{1,0:T(8,128)} custom-call(s32[3]{0:T(128)} %pad_add_fusion.place_ref, bf16[48,1536]{1,0:T(8,128)(2,1)} %add_convert_fusion.1, bf16[48,1536]{1,0:T(8,128)(2,1)} %collective-permute-done.32.refs_1_, bf16[48,1536]{1,0:T(8,128)(2,1)} %collective-permute-done.33.refs_2_, bf16[48,1536]{1,0:T(8,128)(2,1)} %copy-done.21, ...), custom_call_target="tpu_custom_call" | custom-call | bytes 3538944 | tf_op jit(solution)/shard_map/assemble/pallas_call | solution.py:336
  275.9 0.7 copy-done.17
  276.6 3.5 %unpack.1 = (bf16[1,256,1536]{2,1,0:T(8,128)(2,1)}, bf16[1,256,1536]{2,1,0:T(8,128)(2,1)}, bf16[1,256,1536]{2,1,0:T(8,128)(2,1)}) custom-call(s32[3]{0:T(128)} %pad_add_fusion.place_ref, bf16[3,256,128]{2,1,0:T(8,128)(2,1)} %get-tuple-element.55.refs_0_, bf16[3,256,128]{2,1,0:T(8,128)(2,1)} %copy-done.18, bf16[3,256,128]{2,1,0:T(8,128)(2,1)} %copy-done.19, ...), custom_call_target="tpu_custom_call" | custom-call | bytes 4718592 | tf_op jit(solution)/shard_map/unpack/pallas_call | solution.py:111
  (100 shorter events, 3.8 us)
Async XLA Ops:
  2.1 8.5 %copy-start.2 = (bf16[256,1536]{1,0:T(8,128)(2,1)}, bf16[256,1536]{1,0:T(8,128)(2,1)S(1)}, u32[]{:S(2)}) copy-start(bf16[256,1536]{1,0:T(8,128)(2,1)S(1)} %get-tuple-element.79.refs_0_.refs_2_) | copy-start | bytes 2359300
  2.1 69.0 %copy-start.1 = (bf16[256,1536]{1,0:T(8,128)(2,1)}, bf16[256,1536]{1,0:T(8,128)(2,1)S(1)}, u32[]{:S(2)}) copy-start(bf16[256,1536]{1,0:T(8,128)(2,1)S(1)} %get-tuple-element.49.refs_0_.refs_7_) | copy-start | bytes 2359300
  2.1 21.5 %collective-permute-start.6 = (bf16[256,1536]{1,0:T(8,128)(2,1)S(1)}, bf16[256,1536]{1,0:T(8,128)(2,1)}, u32[]{:S(2)}, u32[]{:S(2)}) collective-permute-start(bf16[256,1536]{1,0:T(8,128)(2,1)S(1)} %get-tuple-element.79.refs_0_.refs_2_), channel_id=1, source_target_pairs={{0,1},{1,0},{2,3},{3,2},{4,5},{5,4},{6,7},{7,6},{8,9},{9,8},{10,11... | collective-permute-start | bytes 2359304 | tf_op jit(solution)/shard_map/ppermute | solution.py:369
  5.2 22.3 %collective-permute-start.7 = (bf16[256,1536]{1,0:T(8,128)(2,1)S(1)}, bf16[256,1536]{1,0:T(8,128)(2,1)}, u32[]{:S(2)}, u32[]{:S(2)}) collective-permute-start(bf16[256,1536]{1,0:T(8,128)(2,1)S(1)} %get-tuple-element.79.refs_0_.refs_2_), channel_id=1, source_target_pairs={{0,2},{1,3},{2,0},{3,1},{4,6},{5,7},{6,4},{7,5},{8,10},{9,11},{10,... | collective-permute-start | bytes 2359304 | tf_op jit(solution)/shard_map/ppermute | solution.py:369
  10.7 25.5 %collective-permute-start = (bf16[3,256,384]{2,1,0:T(8,128)(2,1)}, bf16[3,256,384]{2,1,0:T(8,128)(2,1)S(1)}, u32[]{:S(2)}, u32[]{:S(2)}) collective-permute-start(bf16[3,256,384]{2,1,0:T(8,128)(2,1)} %get-tuple-element.41), channel_id=1, source_target_pairs={{0,1},{1,0},{2,3},{3,2},{4,5},{5,4},{6,7},{7,6},{8,9},{9,8},{10,11... | collective-permute-start | bytes 1769480 | tf_op jit(solution)/shard_map/ppermute | solution.py:369
  11.3 39.6 %collective-permute-start.1 = (bf16[3,256,384]{2,1,0:T(8,128)(2,1)}, bf16[3,256,384]{2,1,0:T(8,128)(2,1)S(1)}, u32[]{:S(2)}, u32[]{:S(2)}) collective-permute-start(bf16[3,256,384]{2,1,0:T(8,128)(2,1)} %get-tuple-element.42), channel_id=1, source_target_pairs={{0,2},{1,3},{2,0},{3,1},{4,6},{5,7},{6,4},{7,5},{8,10},{9,11},{10,... | collective-permute-start | bytes 1769480 | tf_op jit(solution)/shard_map/ppermute | solution.py:369
  11.3 39.5 %collective-permute-start.2 = (bf16[3,256,384]{2,1,0:T(8,128)(2,1)}, bf16[3,256,384]{2,1,0:T(8,128)(2,1)S(1)}, u32[]{:S(2)}, u32[]{:S(2)}) collective-permute-start(bf16[3,256,384]{2,1,0:T(8,128)(2,1)} %get-tuple-element.43), channel_id=1, source_target_pairs={{0,3},{1,2},{2,1},{3,0},{4,7},{5,6},{6,5},{7,4},{8,11},{9,10},{10,... | collective-permute-start | bytes 1769480 | tf_op jit(solution)/shard_map/ppermute | solution.py:369
  25.4 39.0 %collective-permute-start.8 = (bf16[256,768]{1,0:T(8,128)(2,1)}, bf16[256,768]{1,0:T(8,128)(2,1)}, u32[]{:S(2)}, u32[]{:S(2)}) collective-permute-start(bf16[256,768]{1,0:T(8,128)(2,1)} %slice.89), channel_id=1, source_target_pairs={{0,2},{1,3},{2,0},{3,1},{4,6},{5,7},{6,4},{7,5},{8,10},{9,11},{10,... | collective-permute-start | bytes 1179656 | tf_op jit(solution)/shard_map/ppermute | solution.py:369
  28.5 36.0 %collective-permute-start.9 = (bf16[256,768]{1,0:T(8,128)(2,1)S(1)}, bf16[256,768]{1,0:T(8,128)(2,1)S(1)}, u32[]{:S(2)}, u32[]{:S(2)}) collective-permute-start(bf16[256,768]{1,0:T(8,128)(2,1)S(1)} %slice.90), channel_id=1, source_target_pairs={{0,1},{1,0},{2,3},{3,2},{4,5},{5,4},{6,7},{7,6},{8,9},{9,8},{10,11... | collective-permute-start | bytes 1179656 | tf_op jit(solution)/shard_map/ppermute | solution.py:369
  36.2 14.7 %copy-start.3 = (bf16[3,256,384]{2,1,0:T(8,128)(2,1)}, bf16[3,256,384]{2,1,0:T(8,128)(2,1)S(1)}, u32[]{:S(2)}) copy-start(bf16[3,256,384]{2,1,0:T(8,128)(2,1)S(1)} %collective-permute-done.refs_1_) | copy-start | bytes 1769476
  50.9 1.0 copy-start.5
  70.3 2.2 collective-permute-start.10
  70.3 34.8 %collective-permute-start.14 = (bf16[256,1536]{1,0:T(8,128)(2,1)S(1)}, bf16[256,1536]{1,0:T(8,128)(2,1)S(1)}, u32[]{:S(2)}, u32[]{:S(2)}) collective-permute-start(bf16[256,1536]{1,0:T(8,128)(2,1)S(1)} %get-tuple-element.49.refs_0_.refs_7_), channel_id=1, source_target_pairs={{0,1},{1,0},{2,3},{3,2},{4,5},{5,4},{6,7},{7,6},{8,9},{9,8},{10,11... | collective-permute-start | bytes 2359304 | tf_op jit(solution)/shard_map/ppermute | solution.py:369
  71.2 34.0 %collective-permute-start.15 = (bf16[256,1536]{1,0:T(8,128)(2,1)S(1)}, bf16[256,1536]{1,0:T(8,128)(2,1)S(1)}, u32[]{:S(2)}, u32[]{:S(2)}) collective-permute-start(bf16[256,1536]{1,0:T(8,128)(2,1)S(1)} %get-tuple-element.49.refs_0_.refs_7_), channel_id=1, source_target_pairs={{0,2},{1,3},{2,0},{3,1},{4,6},{5,7},{6,4},{7,5},{8,10},{9,11},{10,... | collective-permute-start | bytes 2359304 | tf_op jit(solution)/shard_map/ppermute | solution.py:369
  73.8 20.2 %collective-permute-start.11 = (bf16[48,1536]{1,0:T(8,128)(2,1)S(1)}, bf16[48,1536]{1,0:T(8,128)(2,1)S(1)}, u32[]{:S(2)}, u32[]{:S(2)}) collective-permute-start(bf16[48,1536]{1,0:T(8,128)(2,1)S(1)} %get-tuple-element.87), channel_id=1, source_target_pairs={{0,1},{1,0},{2,3},{3,2},{4,5},{5,4},{6,7},{7,6},{8,9},{9,8},{10,11... | collective-permute-start | bytes 442376 | tf_op jit(solution)/shard_map/ppermute | solution.py:369
  75.3 23.2 %collective-permute-start.12 = (bf16[48,1536]{1,0:T(8,128)(2,1)S(1)}, bf16[48,1536]{1,0:T(8,128)(2,1)S(1)}, u32[]{:S(2)}, u32[]{:S(2)}) collective-permute-start(bf16[48,1536]{1,0:T(8,128)(2,1)S(1)} %get-tuple-element.86), channel_id=1, source_target_pairs={{0,2},{1,3},{2,0},{3,1},{4,6},{5,7},{6,4},{7,5},{8,10},{9,11},{10,... | collective-permute-start | bytes 442376 | tf_op jit(solution)/shard_map/ppermute | solution.py:369
  75.9 25.6 %collective-permute-start.13 = (bf16[48,1536]{1,0:T(8,128)(2,1)S(1)}, bf16[48,1536]{1,0:T(8,128)(2,1)S(1)}, u32[]{:S(2)}, u32[]{:S(2)}) collective-permute-start(bf16[48,1536]{1,0:T(8,128)(2,1)S(1)} %get-tuple-element.85), channel_id=1, source_target_pairs={{0,3},{1,2},{2,1},{3,0},{4,7},{5,6},{6,5},{7,4},{8,11},{9,10},{10,... | collective-permute-start | bytes 442376 | tf_op jit(solution)/shard_map/ppermute | solution.py:369
  94.0 103.4 %collective-permute-start.3 = (bf16[192,3072]{1,0:T(8,128)(2,1)}, bf16[192,3072]{1,0:T(8,128)(2,1)}, u32[]{:S(2)}, u32[]{:S(2)}) collective-permute-start(bf16[192,3072]{1,0:T(8,128)(2,1)} %param.9), channel_id=1, source_target_pairs={{0,8},{4,12},{9,17},{13,21},{18,26},{22,30},{27,3},{31,7}} | collective-permute-start | bytes 3538952 | tf_op jit(solution)/shard_map/ppermute | solution.py:369
  98.5 98.9 %collective-permute-start.4 = (bf16[192,3072]{1,0:T(8,128)(2,1)}, bf16[192,3072]{1,0:T(8,128)(2,1)}, u32[]{:S(2)}, u32[]{:S(2)}) collective-permute-start(bf16[192,3072]{1,0:T(8,128)(2,1)} %param.9), channel_id=1, source_target_pairs={{0,16},{4,20},{9,25},{13,29},{18,2},{22,6},{27,11},{31,15}} | collective-permute-start | bytes 3538952 | tf_op jit(solution)/shard_map/ppermute | solution.py:369
  101.5 95.8 %collective-permute-start.5 = (bf16[192,3072]{1,0:T(8,128)(2,1)}, bf16[192,3072]{1,0:T(8,128)(2,1)}, u32[]{:S(2)}, u32[]{:S(2)}) collective-permute-start(bf16[192,3072]{1,0:T(8,128)(2,1)} %param.9), channel_id=1, source_target_pairs={{0,24},{4,28},{9,1},{13,5},{18,10},{22,14},{27,19},{31,23}} | collective-permute-start | bytes 3538952 | tf_op jit(solution)/shard_map/ppermute | solution.py:369
  105.2 80.2 %copy-start.6 = (bf16[256,1536]{1,0:T(8,128)(2,1)}, bf16[256,1536]{1,0:T(8,128)(2,1)S(1)}, u32[]{:S(2)}) copy-start(bf16[256,1536]{1,0:T(8,128)(2,1)S(1)} %collective-permute-done.14.refs_1_.refs_8_) | copy-start | bytes 2359300
  105.2 72.5 %collective-permute-start.29 = (bf16[48,1536]{1,0:T(8,128)(2,1)S(1)}, bf16[48,1536]{1,0:T(8,128)(2,1)S(1)}, u32[]{:S(2)}, u32[]{:S(2)}) collective-permute-start(bf16[48,1536]{1,0:T(8,128)(2,1)S(1)} %get-tuple-element.92), channel_id=1, source_target_pairs={{0,8},{1,9},{2,10},{3,11},{4,12},{5,13},{6,14},{7,15},{8,16},{9,17... | collective-permute-start | bytes 442376 | tf_op jit(solution)/shard_map/ppermute | solution.py:369
  105.2 80.2 %copy-start.7 = (bf16[256,1536]{1,0:T(8,128)(2,1)}, bf16[256,1536]{1,0:T(8,128)(2,1)S(1)}, u32[]{:S(2)}) copy-start(bf16[256,1536]{1,0:T(8,128)(2,1)S(1)} %collective-permute-done.15.refs_2_.refs_9_) | copy-start | bytes 2359300
  105.2 75.5 %collective-permute-start.30 = (bf16[48,1536]{1,0:T(8,128)(2,1)}, bf16[48,1536]{1,0:T(8,128)(2,1)}, u32[]{:S(2)}, u32[]{:S(2)}) collective-permute-start(bf16[48,1536]{1,0:T(8,128)(2,1)} %get-tuple-element.94), channel_id=1, source_target_pairs={{0,16},{1,17},{2,18},{3,19},{4,20},{5,21},{6,22},{7,23},{8,24},{9,... | collective-permute-start | bytes 442376 | tf_op jit(solution)/shard_map/ppermute | solution.py:369
  177.7 5.9 %collective-permute-start.31 = (bf16[48,1536]{1,0:T(8,128)(2,1)}, bf16[48,1536]{1,0:T(8,128)(2,1)}, u32[]{:S(2)}, u32[]{:S(2)}) collective-permute-start(bf16[48,1536]{1,0:T(8,128)(2,1)} %get-tuple-element.93), channel_id=1, source_target_pairs={{0,24},{1,25},{2,26},{3,27},{4,28},{5,29},{6,30},{7,31},{8,0},{9,1... | collective-permute-start | bytes 442376 | tf_op jit(solution)/shard_map/ppermute | solution.py:369
  180.7 7.8 %collective-permute-start.16 = (bf16[256,768]{1,0:T(8,128)(2,1)S(1)}, bf16[256,768]{1,0:T(8,128)(2,1)S(1)}, u32[]{:S(2)}, u32[]{:S(2)}) collective-permute-start(bf16[256,768]{1,0:T(8,128)(2,1)S(1)} %slice.96), channel_id=1, source_target_pairs={{0,2},{1,3},{2,0},{3,1},{4,6},{5,7},{6,4},{7,5},{8,10},{9,11},{10,... | collective-permute-start | bytes 1179656 | tf_op jit(solution)/shard_map/ppermute | solution.py:369
  183.6 7.8 %collective-permute-start.17 = (bf16[256,768]{1,0:T(8,128)(2,1)S(1)}, bf16[256,768]{1,0:T(8,128)(2,1)S(1)}, u32[]{:S(2)}, u32[]{:S(2)}) collective-permute-start(bf16[256,768]{1,0:T(8,128)(2,1)S(1)} %slice.97), channel_id=1, source_target_pairs={{0,1},{1,0},{2,3},{3,2},{4,5},{5,4},{6,7},{7,6},{8,9},{9,8},{10,11... | collective-permute-start | bytes 1179656 | tf_op jit(solution)/shard_map/ppermute | solution.py:369
  188.4 3.0 %copy-start.13 = (bf16[256,768]{1,0:T(8,128)(2,1)}, bf16[256,768]{1,0:T(8,128)(2,1)S(1)}, u32[]{:S(2)}) copy-start(bf16[256,768]{1,0:T(8,128)(2,1)S(1)} %collective-permute-done.16.refs_3_.refs_10_) | copy-start | bytes 1179652
  197.3 1.7 copy-start.25
  197.3 2.2 copy-start.10
  197.4 6.5 %copy-start.9 = (bf16[4,48,1536]{2,1,0:T(8,128)(2,1)S(1)}, bf16[4,48,1536]{2,1,0:T(8,128)(2,1)}, u32[]{:S(2)}) copy-start(bf16[4,48,1536]{2,1,0:T(8,128)(2,1)} %get-tuple-element.50) | copy-start | bytes 1769476
  199.0 8.6 %copy-start = (bf16[192,3072]{1,0:T(8,128)(2,1)}, bf16[192,3072]{1,0:T(8,128)(2,1)S(1)}, u32[]{:S(2)}) copy-start(bf16[192,3072]{1,0:T(8,128)(2,1)S(1)} %select_select_fusion.refs_0_) | copy-start | bytes 3538948
  199.0 8.3 %collective-permute-start.18 = (bf16[192,3072]{1,0:T(8,128)(2,1)S(1)}, bf16[192,3072]{1,0:T(8,128)(2,1)S(1)}, u32[]{:S(2)}, u32[]{:S(2)}) collective-permute-start(bf16[192,3072]{1,0:T(8,128)(2,1)S(1)} %select_select_fusion.refs_0_), channel_id=1, source_target_pairs={{0,4},{1,5},{2,6},{3,7},{4,0},{5,1},{6,2},{7,3},{8,12},{9,13},{10,... | collective-permute-start | bytes 3538952 | tf_op jit(solution)/shard_map/ppermute | solution.py:369
  199.1 4.8 %collective-permute-start.22 = (bf16[4,48,1536]{2,1,0:T(8,128)(2,1)S(1)}, bf16[4,48,1536]{2,1,0:T(8,128)(2,1)S(1)}, u32[]{:S(2)}, u32[]{:S(2)}) collective-permute-start(bf16[4,48,1536]{2,1,0:T(8,128)(2,1)S(1)} %copy-done.25), channel_id=1, source_target_pairs={{0,4},{1,5},{2,6},{3,7},{4,0},{5,1},{6,2},{7,3},{8,12},{9,13},{10,... | collective-permute-start | bytes 1769480 | tf_op jit(solution)/shard_map/ppermute | solution.py:369
  199.6 39.8 %collective-permute-start.32 = (bf16[48,1536]{1,0:T(8,128)(2,1)S(1)}, bf16[48,1536]{1,0:T(8,128)(2,1)}, u32[]{:S(2)}, u32[]{:S(2)}) collective-permute-start(bf16[48,1536]{1,0:T(8,128)(2,1)S(1)} %copy-done.10), channel_id=1, source_target_pairs={{0,1},{1,0},{2,3},{3,2},{4,5},{5,4},{6,7},{7,6},{8,9},{9,8},{10,11... | collective-permute-start | bytes 442376 | tf_op jit(solution)/shard_map/ppermute | solution.py:369
  200.2 39.3 %collective-permute-start.33 = (bf16[48,1536]{1,0:T(8,128)(2,1)S(1)}, bf16[48,1536]{1,0:T(8,128)(2,1)}, u32[]{:S(2)}, u32[]{:S(2)}) collective-permute-start(bf16[48,1536]{1,0:T(8,128)(2,1)S(1)} %copy-done.10), channel_id=1, source_target_pairs={{0,2},{1,3},{2,0},{3,1},{4,6},{5,7},{6,4},{7,5},{8,10},{9,11},{10,... | collective-permute-start | bytes 442376 | tf_op jit(solution)/shard_map/ppermute | solution.py:369
  204.0 18.2 %collective-permute-start.23 = (bf16[48,1536]{1,0:T(8,128)(2,1)S(1)}, bf16[48,1536]{1,0:T(8,128)(2,1)S(1)}, u32[]{:S(2)}, u32[]{:S(2)}) collective-permute-start(bf16[48,1536]{1,0:T(8,128)(2,1)S(1)} %get-tuple-element.82), channel_id=1, source_target_pairs={{0,1},{1,0},{2,3},{3,2},{4,5},{5,4},{6,7},{7,6},{8,9},{9,8},{10,11... | collective-permute-start | bytes 442376 | tf_op jit(solution)/shard_map/ppermute | solution.py:369
  204.4 17.8 %collective-permute-start.24 = (bf16[48,1536]{1,0:T(8,128)(2,1)S(1)}, bf16[48,1536]{1,0:T(8,128)(2,1)S(1)}, u32[]{:S(2)}, u32[]{:S(2)}) collective-permute-start(bf16[48,1536]{1,0:T(8,128)(2,1)S(1)} %get-tuple-element.81), channel_id=1, source_target_pairs={{0,2},{1,3},{2,0},{3,1},{4,6},{5,7},{6,4},{7,5},{8,10},{9,11},{10,... | collective-permute-start | bytes 442376 | tf_op jit(solution)/shard_map/ppermute | solution.py:369
  207.2 1.1 copy-start.8
  207.2 15.0 %collective-permute-start.25 = (bf16[48,1536]{1,0:T(8,128)(2,1)S(1)}, bf16[48,1536]{1,0:T(8,128)(2,1)S(1)}, u32[]{:S(2)}, u32[]{:S(2)}) collective-permute-start(bf16[48,1536]{1,0:T(8,128)(2,1)S(1)} %get-tuple-element.80), channel_id=1, source_target_pairs={{0,3},{1,2},{2,1},{3,0},{4,7},{5,6},{6,5},{7,4},{8,11},{9,10},{10,... | collective-permute-start | bytes 442376 | tf_op jit(solution)/shard_map/ppermute | solution.py:369
  222.4 12.8 %collective-permute-start.35 = (bf16[48,1536]{1,0:T(8,128)(2,1)S(1)}, bf16[48,1536]{1,0:T(8,128)(2,1)S(1)}, u32[]{:S(2)}, u32[]{:S(2)}) collective-permute-start(bf16[48,1536]{1,0:T(8,128)(2,1)S(1)} %get-tuple-element.90), channel_id=1, source_target_pairs={{0,8},{1,9},{2,10},{3,11},{4,12},{5,13},{6,14},{7,15},{8,16},{9,17... | collective-permute-start | bytes 442376 | tf_op jit(solution)/shard_map/ppermute | solution.py:369
  222.7 14.4 %collective-permute-start.36 = (bf16[48,1536]{1,0:T(8,128)(2,1)S(1)}, bf16[48,1536]{1,0:T(8,128)(2,1)S(1)}, u32[]{:S(2)}, u32[]{:S(2)}) collective-permute-start(bf16[48,1536]{1,0:T(8,128)(2,1)S(1)} %get-tuple-element.89), channel_id=1, source_target_pairs={{0,16},{1,17},{2,18},{3,19},{4,20},{5,21},{6,22},{7,23},{8,24},{9,... | collective-permute-start | bytes 442376 | tf_op jit(solution)/shard_map/ppermute | solution.py:369
  225.6 11.5 %copy-start.28 = (bf16[3,256,128]{2,1,0:T(8,128)(2,1)S(1)}, bf16[3,256,128]{2,1,0:T(8,128)(2,1)}, u32[]{:S(2)}) copy-start(bf16[3,256,128]{2,1,0:T(8,128)(2,1)} %get-tuple-element.56) | copy-start | bytes 589828
  225.6 27.4 %copy-start.27 = (bf16[3,256,128]{2,1,0:T(8,128)(2,1)S(1)}, bf16[3,256,128]{2,1,0:T(8,128)(2,1)}, u32[]{:S(2)}) copy-start(bf16[3,256,128]{2,1,0:T(8,128)(2,1)} %get-tuple-element.57) | copy-start | bytes 589828
  225.6 42.7 %copy-start.26 = (bf16[3,256,128]{2,1,0:T(8,128)(2,1)S(1)}, bf16[3,256,128]{2,1,0:T(8,128)(2,1)}, u32[]{:S(2)}) copy-start(bf16[3,256,128]{2,1,0:T(8,128)(2,1)} %get-tuple-element.58) | copy-start | bytes 589828
  225.6 11.7 %collective-permute-start.37 = (bf16[48,1536]{1,0:T(8,128)(2,1)S(1)}, bf16[48,1536]{1,0:T(8,128)(2,1)S(1)}, u32[]{:S(2)}, u32[]{:S(2)}) collective-permute-start(bf16[48,1536]{1,0:T(8,128)(2,1)S(1)} %get-tuple-element.88), channel_id=1, source_target_pairs={{0,24},{1,25},{2,26},{3,27},{4,28},{5,29},{6,30},{7,31},{8,0},{9,1... | collective-permute-start | bytes 442376 | tf_op jit(solution)/shard_map/ppermute | solution.py:369
  235.2 7.7 %collective-permute-start.34 = (bf16[48,1536]{1,0:T(8,128)(2,1)S(1)}, bf16[48,1536]{1,0:T(8,128)(2,1)S(1)}, u32[]{:S(2)}, u32[]{:S(2)}) collective-permute-start(bf16[48,1536]{1,0:T(8,128)(2,1)S(1)} %copy-done.10), channel_id=1, source_target_pairs={{0,3},{1,2},{2,1},{3,0},{4,7},{5,6},{6,5},{7,4},{8,11},{9,10},{10,... | collective-permute-start | bytes 442376 | tf_op jit(solution)/shard_map/ppermute | solution.py:369
  237.1 9.1 %collective-permute-start.19 = (bf16[3,256,128]{2,1,0:T(8,128)(2,1)S(1)}, bf16[3,256,128]{2,1,0:T(8,128)(2,1)S(1)}, u32[]{:S(2)}, u32[]{:S(2)}) collective-permute-start(bf16[3,256,128]{2,1,0:T(8,128)(2,1)S(1)} %copy-done.28), channel_id=1, source_target_pairs={{0,1},{1,0},{2,3},{3,2},{4,5},{5,4},{6,7},{7,6},{8,9},{9,8},{10,11... | collective-permute-start | bytes 589832 | tf_op jit(solution)/shard_map/ppermute | solution.py:369
  237.4 32.4 %copy-start.11 = (bf16[48,1536]{1,0:T(8,128)(2,1)}, bf16[48,1536]{1,0:T(8,128)(2,1)S(1)}, u32[]{:S(2)}) copy-start(bf16[48,1536]{1,0:T(8,128)(2,1)S(1)} %add_convert_fusion.refs_4_) | copy-start | bytes 442372
  237.4 12.0 %collective-permute-start.38 = (bf16[48,1536]{1,0:T(8,128)(2,1)S(1)}, bf16[48,1536]{1,0:T(8,128)(2,1)S(1)}, u32[]{:S(2)}, u32[]{:S(2)}) collective-permute-start(bf16[48,1536]{1,0:T(8,128)(2,1)S(1)} %add_convert_fusion.refs_4_), channel_id=1, source_target_pairs={{0,1},{1,0},{2,3},{3,2},{4,5},{5,4},{6,7},{7,6},{8,9},{9,8},{10,11... | collective-permute-start | bytes 442376 | tf_op jit(solution)/shard_map/ppermute | solution.py:369
  239.3 35.5 %collective-permute-start.26 = (bf16[3,256,256]{2,1,0:T(8,128)(2,1)}, bf16[3,256,256]{2,1,0:T(8,128)(2,1)S(1)}, u32[]{:S(2)}, u32[]{:S(2)}) collective-permute-start(bf16[3,256,256]{2,1,0:T(8,128)(2,1)} %get-tuple-element.66), channel_id=1, source_target_pairs={{0,1},{1,0},{2,3},{3,2},{4,5},{5,4},{6,7},{7,6},{8,9},{9,8},{10,11... | collective-permute-start | bytes 1179656 | tf_op jit(solution)/shard_map/ppermute | solution.py:369
  239.5 35.4 %collective-permute-start.27 = (bf16[3,256,256]{2,1,0:T(8,128)(2,1)}, bf16[3,256,256]{2,1,0:T(8,128)(2,1)S(1)}, u32[]{:S(2)}, u32[]{:S(2)}) collective-permute-start(bf16[3,256,256]{2,1,0:T(8,128)(2,1)} %get-tuple-element.67), channel_id=1, source_target_pairs={{0,2},{1,3},{2,0},{3,1},{4,6},{5,7},{6,4},{7,5},{8,10},{9,11},{10,... | collective-permute-start | bytes 1179656 | tf_op jit(solution)/shard_map/ppermute | solution.py:369
  242.9 26.9 %copy-start.21 = (bf16[48,1536]{1,0:T(8,128)(2,1)}, bf16[48,1536]{1,0:T(8,128)(2,1)S(1)}, u32[]{:S(2)}) copy-start(bf16[48,1536]{1,0:T(8,128)(2,1)S(1)} %collective-permute-done.34.refs_3_) | copy-start | bytes 442372
  242.9 31.9 %collective-permute-start.28 = (bf16[3,256,256]{2,1,0:T(8,128)(2,1)}, bf16[3,256,256]{2,1,0:T(8,128)(2,1)S(1)}, u32[]{:S(2)}, u32[]{:S(2)}) collective-permute-start(bf16[3,256,256]{2,1,0:T(8,128)(2,1)} %get-tuple-element.68), channel_id=1, source_target_pairs={{0,3},{1,2},{2,1},{3,0},{4,7},{5,6},{6,5},{7,4},{8,11},{9,10},{10,... | collective-permute-start | bytes 1179656 | tf_op jit(solution)/shard_map/ppermute | solution.py:369
  246.2 28.4 %copy-start.18 = (bf16[3,256,128]{2,1,0:T(8,128)(2,1)}, bf16[3,256,128]{2,1,0:T(8,128)(2,1)S(1)}, u32[]{:S(2)}) copy-start(bf16[3,256,128]{2,1,0:T(8,128)(2,1)S(1)} %collective-permute-done.19.refs_1_) | copy-start | bytes 589828
  246.2 6.8 %collective-permute-start.39 = (bf16[48,1536]{1,0:T(8,128)(2,1)S(1)}, bf16[48,1536]{1,0:T(8,128)(2,1)S(1)}, u32[]{:S(2)}, u32[]{:S(2)}) collective-permute-start(bf16[48,1536]{1,0:T(8,128)(2,1)S(1)} %add_convert_fusion.refs_4_), channel_id=1, source_target_pairs={{0,2},{1,3},{2,0},{3,1},{4,6},{5,7},{6,4},{7,5},{8,10},{9,11},{10,... | collective-permute-start | bytes 442376 | tf_op jit(solution)/shard_map/ppermute | solution.py:369
  249.4 20.5 %copy-start.22 = (bf16[48,1536]{1,0:T(8,128)(2,1)}, bf16[48,1536]{1,0:T(8,128)(2,1)S(1)}, u32[]{:S(2)}) copy-start(bf16[48,1536]{1,0:T(8,128)(2,1)S(1)} %collective-permute-done.38.refs_5_) | copy-start | bytes 442372
  249.4 18.9 %collective-permute-start.40 = (bf16[48,1536]{1,0:T(8,128)(2,1)S(1)}, bf16[48,1536]{1,0:T(8,128)(2,1)S(1)}, u32[]{:S(2)}, u32[]{:S(2)}) collective-permute-start(bf16[48,1536]{1,0:T(8,128)(2,1)S(1)} %add_convert_fusion.refs_4_), channel_id=1, source_target_pairs={{0,3},{1,2},{2,1},{3,0},{4,7},{5,6},{6,5},{7,4},{8,11},{9,10},{10,... | collective-permute-start | bytes 442376 | tf_op jit(solution)/shard_map/ppermute | solution.py:369
  253.0 16.8 %copy-start.23 = (bf16[48,1536]{1,0:T(8,128)(2,1)}, bf16[48,1536]{1,0:T(8,128)(2,1)S(1)}, u32[]{:S(2)}) copy-start(bf16[48,1536]{1,0:T(8,128)(2,1)S(1)} %collective-permute-done.39.refs_6_) | copy-start | bytes 442372
  253.0 21.6 %collective-permute-start.20 = (bf16[3,256,128]{2,1,0:T(8,128)(2,1)S(1)}, bf16[3,256,128]{2,1,0:T(8,128)(2,1)S(1)}, u32[]{:S(2)}, u32[]{:S(2)}) collective-permute-start(bf16[3,256,128]{2,1,0:T(8,128)(2,1)S(1)} %copy-done.27), channel_id=1, source_target_pairs={{0,2},{1,3},{2,0},{3,1},{4,6},{5,7},{6,4},{7,5},{8,10},{9,11},{10,... | collective-permute-start | bytes 589832 | tf_op jit(solution)/shard_map/ppermute | solution.py:369
  268.3 1.6 copy-start.24
  268.3 6.6 %collective-permute-start.21 = (bf16[3,256,128]{2,1,0:T(8,128)(2,1)S(1)}, bf16[3,256,128]{2,1,0:T(8,128)(2,1)S(1)}, u32[]{:S(2)}, u32[]{:S(2)}) collective-permute-start(bf16[3,256,128]{2,1,0:T(8,128)(2,1)S(1)} %copy-done.26), channel_id=1, source_target_pairs={{0,3},{1,2},{2,1},{3,0},{4,7},{5,6},{6,5},{7,4},{8,11},{9,10},{10,... | collective-permute-start | bytes 589832 | tf_op jit(solution)/shard_map/ppermute | solution.py:369
  274.9 0.8 copy-start.15
  274.9 1.0 copy-start.16
  (6 other events, 4.5 us)

commit v3 on v2

--- a/solution.py
+++ b/solution.py
@@ -54,8 +54,8 @@
         grid_spec=pltpu.PrefetchScalarGridSpec(
             num_scalar_prefetch=1,
             grid=(1,),
-            in_specs=[pl.BlockSpec(memory_space=pl.ANY)] * 3,
-            out_specs=[pl.BlockSpec(memory_space=pl.ANY)] * rows,
+            in_specs=[pl.BlockSpec(memory_space=pltpu.HBM)] * 3,
+            out_specs=[pl.BlockSpec(memory_space=pltpu.HBM)] * rows,
             scratch_shapes=[
                 pltpu.VMEM((rows, *shape), query.dtype),
                 pltpu.SemaphoreType.DMA((2, rows, 3)),
@@ -113,8 +113,8 @@
         grid_spec=pltpu.PrefetchScalarGridSpec(
             num_scalar_prefetch=1,
             grid=(1,),
-            in_specs=[pl.BlockSpec(memory_space=pl.ANY)] * (calls * rows),
-            out_specs=[pl.BlockSpec(memory_space=pl.ANY)] * 3,
+            in_specs=[pl.BlockSpec(memory_space=pltpu.HBM)] * (calls * rows),
+            out_specs=[pl.BlockSpec(memory_space=pltpu.HBM)] * 3,
             scratch_shapes=[
                 pltpu.VMEM((rows, 3, tokens, width), parts[0][0].dtype),
                 pltpu.SemaphoreType.DMA((2, calls, rows, 3)),
@@ -212,16 +212,14 @@
     )(*parts, probs, grad_attn)
 
 
-def columns_of(blocks, odd):
-    return jnp.concatenate(
-        [ref[...] for ref in blocks[:-2]] + [jnp.where(odd, blocks[-1][...], blocks[-2][...])], axis=0
-    )
+def stacked(refs):
+    return jnp.concatenate([ref[...] for ref in refs], axis=0)
 
 
 def project(place, weights, grads):
     chunks, count = len(grads), len(grads[0])
     half, depth = weights[0].shape
-    tokens, step = grads[0][-1].shape
+    step = grads[0][0].shape[1] // 2
 
     def body(place_ref, *refs):
         first, second = refs[:2]
@@ -232,8 +230,7 @@
 
             @pl.when(at // 2 == chunk)
             def _():
-                columns = columns_of(ins[chunk * count : (chunk + 1) * count], at % 2 == 1)
-                term = dot(lines, columns, NT)
+                term = dot(lines, stacked(ins[chunk * count : (chunk + 1) * count]), NT)
                 if chunk:
                     total[...] += term
                 else:
@@ -248,23 +245,19 @@
                     out[core * half : (core + 1) * half] = total[:half].astype(out.dtype)
                     out[(1 - core) * half : (2 - core) * half] = total[half:].astype(out.dtype)
 
-    def block_of(chunk):
+    def block_of(chunk, block):
         return pl.BlockSpec(
-            (tokens, step), lambda i, place_ref: (0, jnp.clip(i - chunk * 2, 0, 1))
+            (block.shape[0], step), lambda i, place_ref: (0, jnp.clip(i - chunk * 2, 0, 1))
         )
 
-    shape = (2 * half, (count - 1) * tokens)
+    shape = (2 * half, sum(block.shape[0] for block in grads[0]))
     return pl.pallas_call(
         body,
         grid_spec=pltpu.PrefetchScalarGridSpec(
             num_scalar_prefetch=1,
             grid=(chunks * 2,),
             in_specs=[pl.BlockSpec((half, step), lambda i, place_ref: (0, i))] * 2
-            + [
-                spec
-                for chunk in range(chunks)
-                for spec in [block_of(chunk)] * (count - 2) + [whole((tokens, step))] * 2
-            ],
+            + [block_of(chunk, block) for chunk in range(chunks) for block in grads[chunk]],
             out_specs=whole(shape),
             scratch_shapes=[pltpu.VMEM(shape, jnp.float32)],
         ),
@@ -274,16 +267,14 @@
     )(place, *weights, *(block for chunk in grads for block in chunk))
 
 
-def weight_terms(place, attended, grads):
-    rows = len(grads) - 1
+def weight_terms(place, attended, grads, rows):
     width, length = attended.shape
-    tokens, step = grads[-1].shape
+    step = grads[0].shape[1] // 2
     piece = width // 2 // rows
 
     def body(place_ref, attended_ref, *refs):
         ins, (keep, give) = refs[:-2], refs[-2:]
-        columns = columns_of(ins, pl.program_id(0) == 1)
-        term = dot(attended_ref[...], columns).astype(jnp.bfloat16)
+        term = dot(attended_ref[...], stacked(ins)).astype(jnp.bfloat16)
         row, core = place_ref[0], place_ref[2]
         for side in range(2):
             for out, mine in ((keep, core == side), (give, core != side)):
@@ -302,8 +293,7 @@
             num_scalar_prefetch=1,
             grid=(2,),
             in_specs=[whole((width, length))]
-            + [pl.BlockSpec((tokens, step), lambda i, place_ref: (0, i))] * (rows - 1)
-            + [whole((tokens, step))] * 2,
+            + [pl.BlockSpec((block.shape[0], step), lambda i, place_ref: (0, i)) for block in grads],
             out_specs=[spec] * 2,
         ),
         out_shape=[shape] * 2,
@@ -315,31 +305,24 @@
 def assemble(place, pieces):
     chunks, rows = len(pieces), len(pieces[0])
     piece, wide = pieces[0][0].shape
-    step = wide // 2
 
     def body(place_ref, *refs):
         ins, out = refs[:-1], refs[-1]
         for chunk in range(chunks):
-
-            @pl.when(pl.program_id(0) // 2 == chunk)
-            def _():
-                for slot in range(rows):
-                    start = (place_ref[0] ^ slot) * piece
-                    out[pl.ds(pl.multiple_of(start, 16), piece), :] = ins[chunk * rows + slot][
-                        ...
-                    ].astype(out.dtype)
-
-    def block_of(chunk):
-        return pl.BlockSpec((piece, step), lambda i, place_ref: (0, jnp.clip(i - 2 * chunk, 0, 1)))
+            for slot in range(rows):
+                start = pl.multiple_of((place_ref[0] ^ slot) * piece, 16)
+                out[pl.ds(start, piece), chunk * wide : (chunk + 1) * wide] = ins[
+                    chunk * rows + slot
+                ][...].astype(out.dtype)
 
     shape = (rows * piece, chunks * wide)
     return pl.pallas_call(
         body,
         grid_spec=pltpu.PrefetchScalarGridSpec(
             num_scalar_prefetch=1,
-            grid=(2 * chunks,),
-            in_specs=[block_of(chunk) for chunk in range(chunks) for _ in range(rows)],
-            out_specs=pl.BlockSpec((rows * piece, step), lambda i, place_ref: (0, i)),
+            grid=(1,),
+            in_specs=[whole((piece, wide))] * (chunks * rows),
+            out_specs=whole(shape),
         ),
         out_shape=jax.ShapeDtypeStruct(shape, jnp.float32),
         cost_estimate=cost(0, 6 * shape[0] * shape[1]),
@@ -382,9 +365,10 @@
 
     def gather(chunk):
         by_x, by_y = to_row(chunk, 1), to_row(chunk, 2)
-        even = to_row(by_x[:, : wide // 2], 2)
-        odd = to_row(by_y[:, wide // 2 :], 1)
-        return [chunk, by_x, by_y, even, odd]
+        cut = chunk.shape[0] // 2
+        upper = to_row(by_x[:cut], 2)
+        lower = to_row(by_y[cut:], 1)
+        return [chunk, by_x, by_y, upper, lower]
 
     grads = [gather(grad_flat[:, :wide])]
 
@@ -399,7 +383,7 @@
     grads.append(gather(after(grad_flat[:, wide:], parts)))
 
     def reduce_cores(attended, chunk):
-        keep, give = weight_terms(place, attended, chunk)
+        keep, give = weight_terms(place, attended, chunk, rows)
         return keep, to_core(give)
 
     def spread(keep, got):
@@ -432,16 +416,16 @@
     other = to_core(here)
     grad_attn = project(place, [here, other], grads)
     heads = probs.shape[0]
+    blocks = spread(*after(late, grad_attn))
     sent = [backward(parts, probs, grad_attn, 0, 1)]
-    blocks = after(spread(*late), sent[0][0])
-    late = reduce_planes(blocks)
+    late = reduce_planes(after(blocks, sent[0][0]))
     sent.append(backward(parts, after(probs, late[0]), grad_attn, 1, heads - 1))
     back = [
         [message[0]]
         + [to_row(message[slot], slot) for slot in range(1, rows)]
         for message in sent
     ]
-    pieces = [collect(*early), collect(*after(late, sent[1][0]))]
+    pieces = [collect(*after(early, grad_attn)), collect(*after(late, sent[1][0]))]
     grad_query, grad_key, grad_value = unpack(place, back)
     grad_w_out = assemble(place, pieces)
     return grad_query, grad_key, grad_value, grad_w_out

time: 281 us -> 243 us (0.86)
  waiting for transfers between devices: 153 us -> 110 us
  starting transfers between devices: 53.4 us -> 60.9 us
    ppermute x41, waiting for transfers between devices: 153 us -> 110 us  [send(): return lax.ppermute(array, ('fsdp', 'rows'), pairs)]
    ppermute x41, starting transfers between devices: 53.4 us -> 60.9 us  [send(): return lax.ppermute(array, ('fsdp', 'rows'), pairs)]
  transfers between devices with their start and end apart: 41 -> 41, of which waited for: 16 -> 19; matrix products, arithmetic and copies ran while one was open for 3% -> 4% of each run, Pallas kernels for 17% -> 19%
where the time goes in v3:
time: 243 us; the launch traced here: 242 us
  waiting for transfers between devices  110 us (45%)
  starting transfers between devices  60.9 us (25%)
  Pallas kernels  55.4 us (23%)
  local copies, waits for them, and re-layouts  9.72 us (4%)
  other arithmetic  5.16 us (2%)
    ppermute x41, waiting for transfers between devices, send(): return lax.ppermute(array, ('fsdp', 'rows'), pairs)  110 us
    ppermute x41, starting transfers between devices, send(): return lax.ppermute(array, ('fsdp', 'rows'), pairs)  60.9 us
    pallas_call x2, Pallas kernels, backward(): pl.pallas_call(body, grid=(count,), in_specs=[part] * rows + [pl.BlockSpe...  14.2 us
    pallas_call x1, Pallas kernels, forward(): pl.pallas_call(body, grid=(heads,), in_specs=[part] * rows, out_specs=[pl...  12.6 us
    pallas_call x2, Pallas kernels, weight_terms(): pl.pallas_call(body, grid_spec=pltpu.PrefetchScalarGridSpec(num_scalar_pr...  10.5 us
    pallas_call x1, Pallas kernels, project(): pl.pallas_call(body, grid_spec=pltpu.PrefetchScalarGridSpec(num_scalar_pr...  7.86 us
  transfers between devices with their start and end apart: 41, of which 19 were waited for; matrix products, arithmetic and copies ran while one was open for 4% of the time, Pallas kernels for 19%

profile of v3, /device:TPU:0, one launch (start us, length us, event | category | flops | bytes accessed | tf_op | source)
XLA Modules:
  0.0 242.1 jit_solution(4932542482684002842)
XLA Ops:
  0.6 1.5 fusion.7
  2.1 3.1 %collective-permute-start.7 = (bf16[256,1536]{1,0:T(8,128)(2,1)S(1)}, bf16[256,1536]{1,0:T(8,128)(2,1)}, u32[]{:S(2)}, u32[]{:S(2)}) collective-permute-start(bf16[256,1536]{1,0:T(8,128)(2,1)S(1)} %get-tuple-element.89.refs_0_.refs_2_), channel_id=1, source_target_pairs={{0,2},{1,3},{2,0},{3,1},{4,6},{5,7},{6,4},{7,5},{8,10},{9,11},{10,... | collective-permute-start | bytes 2359304 | tf_op jit(solution)/shard_map/ppermute | solution.py:352
  5.2 1.5 collective-permute-start.6
  7.3 3.3 %pack.1 = (bf16[3,256,384]{2,1,0:T(8,128)(2,1)}, bf16[3,256,384]{2,1,0:T(8,128)(2,1)}, bf16[3,256,384]{2,1,0:T(8,128)(2,1)}, bf16[3,256,384]{2,1,0:T(8,128)(2,1)}) custom-call(s32[3]{0:T(128)} %pad_add_fusion.place_ref, bf16[1,256,1536]{2,1,0:T(8,128)(2,1)} %refs_0_.1, bf16[1,256,1536]{2,1,0:T(8,128)(2,1)} %refs_1_.1, bf16[1,256,1536]{2,1,0:T(8,128)(2,1)} %refs_2_.1), custom_call_target="tpu_custom_call" | custom-call | bytes 4718592 | tf_op jit(solution)/shard_map/pack/pallas_call | solution.py:52
  11.3 2.9 %collective-permute-start.2 = (bf16[3,256,384]{2,1,0:T(8,128)(2,1)}, bf16[3,256,384]{2,1,0:T(8,128)(2,1)S(1)}, u32[]{:S(2)}, u32[]{:S(2)}) collective-permute-start(bf16[3,256,384]{2,1,0:T(8,128)(2,1)} %get-tuple-element.49), channel_id=1, source_target_pairs={{0,3},{1,2},{2,1},{3,0},{4,7},{5,6},{6,5},{7,4},{8,11},{9,10},{10,... | collective-permute-start | bytes 1769480 | tf_op jit(solution)/shard_map/ppermute | solution.py:352
  14.1 9.6 %collective-permute-done.7.refs_2_.refs_4_ = bf16[256,1536]{1,0:T(8,128)(2,1)} collective-permute-done((bf16[256,1536]{1,0:T(8,128)(2,1)S(1)}, bf16[256,1536]{1,0:T(8,128)(2,1)}, u32[]{:S(2)}, u32[]{:S(2)}) %collective-permute-start.7) | collective-permute-done | bytes 786464 | tf_op jit(solution)/shard_map/ppermute | solution.py:352
  23.7 1.8 slice.90
  25.5 2.0 collective-permute-start.9
  27.5 1.0 slice.89
  28.5 1.6 collective-permute-start.8
  30.1 8.2 %collective-permute-done.refs_1_ = bf16[3,256,384]{2,1,0:T(8,128)(2,1)S(1)} collective-permute-done((bf16[3,256,384]{2,1,0:T(8,128)(2,1)}, bf16[3,256,384]{2,1,0:T(8,128)(2,1)S(1)}, u32[]{:S(2)}, u32[]{:S(2)}) %collective-permute-start) | collective-permute-done | bytes 589856 | tf_op jit(solution)/shard_map/ppermute | solution.py:352
  38.3 12.2 %collective-permute-done.2.refs_3_ = bf16[3,256,384]{2,1,0:T(8,128)(2,1)S(1)} collective-permute-done((bf16[3,256,384]{2,1,0:T(8,128)(2,1)}, bf16[3,256,384]{2,1,0:T(8,128)(2,1)S(1)}, u32[]{:S(2)}, u32[]{:S(2)}) %collective-permute-start.2) | collective-permute-done | bytes 589856 | tf_op jit(solution)/shard_map/ppermute | solution.py:352
  50.5 0.8 copy-done.5
  51.3 12.6 %forward.1 = (bf16[3,1024,1024]{2,1,0:T(8,128)(2,1)}, bf16[384,1024]{1,0:T(8,128)(2,1)}) custom-call(bf16[3,256,384]{2,1,0:T(8,128)(2,1)} %get-tuple-element.46.refs_0_, bf16[3,256,384]{2,1,0:T(8,128)(2,1)} %copy-done.3, bf16[3,256,384]{2,1,0:T(8,128)(2,1)} %copy-done.4, bf16[3,256,384]{2,1,0:T(8,128)(2,1)} %copy-done.5), custom_call_target="tpu_custom_call" | custom-call | flops 3221225472 | bytes 6291456 | tf_op jit(solution)/shard_map/forward/pallas_call | solution.py:150
  64.6 5.3 %weight_terms.2 = (bf16[4,48,1536]{2,1,0:T(8,128)(2,1)}, bf16[4,48,1536]{2,1,0:T(8,128)(2,1)}) custom-call(s32[3]{0:T(128)} %pad_add_fusion.place_ref, bf16[384,1024]{1,0:T(8,128)(2,1)} %get-tuple-element.54.attended_ref, bf16[256,1536]{1,0:T(8,128)(2,1)} %copy-done.2, bf16[256,1536]{1,0:T(8,128)(2,1)} %collective-permute-done.6.refs_1_.refs_3_, ...), custom_call_target="tpu_custom_call" | custom-call | flops 1207959552 | bytes 3932160 | tf_op jit(solution)/shard_map/weight_terms/pallas_call | solution.py:290
  69.9 2.0 collective-permute-start.15
  71.9 1.5 collective-permute-start.14
  73.4 5.6 %collective-permute-start.4 = (bf16[192,3072]{1,0:T(8,128)(2,1)S(1)}, bf16[192,3072]{1,0:T(8,128)(2,1)}, u32[]{:S(2)}, u32[]{:S(2)}) collective-permute-start(bf16[192,3072]{1,0:T(8,128)(2,1)S(1)} %copy-done.9), channel_id=1, source_target_pairs={{0,16},{4,20},{9,25},{13,29},{18,2},{22,6},{27,11},{31,15}} | collective-permute-start | bytes 3538952 | tf_op jit(solution)/shard_map/ppermute | solution.py:352
  79.0 2.4 collective-permute-start.3
  81.4 2.3 collective-permute-start.5
  83.8 2.0 add_convert_fusion.9
  85.7 4.4 %collective-permute-done.15.refs_2_.refs_9_ = bf16[256,1536]{1,0:T(8,128)(2,1)S(1)} collective-permute-done((bf16[256,1536]{1,0:T(8,128)(2,1)S(1)}, bf16[256,1536]{1,0:T(8,128)(2,1)S(1)}, u32[]{:S(2)}, u32[]{:S(2)}) %collective-permute-start.15) | collective-permute-done | bytes 786464 | tf_op jit(solution)/shard_map/ppermute | solution.py:352
  90.1 2.7 %collective-permute-start.13 = (bf16[48,1536]{1,0:T(8,128)(2,1)S(1)}, bf16[48,1536]{1,0:T(8,128)(2,1)}, u32[]{:S(2)}, u32[]{:S(2)}) collective-permute-start(bf16[48,1536]{1,0:T(8,128)(2,1)S(1)} %get-tuple-element.95), channel_id=1, source_target_pairs={{0,3},{1,2},{2,1},{3,0},{4,7},{5,6},{6,5},{7,4},{8,11},{9,10},{10,... | collective-permute-start | bytes 442376 | tf_op jit(solution)/shard_map/ppermute | solution.py:352
  93.3 3.5 %collective-permute-done.13 = bf16[48,1536]{1,0:T(8,128)(2,1)} collective-permute-done((bf16[48,1536]{1,0:T(8,128)(2,1)S(1)}, bf16[48,1536]{1,0:T(8,128)(2,1)}, u32[]{:S(2)}, u32[]{:S(2)}) %collective-permute-start.13) | collective-permute-done | bytes 147488 | tf_op jit(solution)/shard_map/ppermute | solution.py:352
  96.7 1.6 collective-permute-start.11
  98.4 1.3 collective-permute-done.12
  99.7 1.6 collective-permute-start.17
  101.3 0.8 collective-permute-done.11
  102.1 1.6 collective-permute-start.16
  103.7 1.0 pad_maximum_fusion
  104.7 0.8 dynamic-slice_bitcast_fusion.3
  105.6 5.2 %collective-permute-done.17.refs_4_.refs_11_ = bf16[128,1536]{1,0:T(8,128)(2,1)} collective-permute-done((bf16[128,1536]{1,0:T(8,128)(2,1)S(1)}, bf16[128,1536]{1,0:T(8,128)(2,1)}, u32[]{:S(2)}, u32[]{:S(2)}) %collective-permute-start.17) | collective-permute-done | bytes 393248 | tf_op jit(solution)/shard_map/ppermute | solution.py:352
  110.8 1.4 collective-permute-done.16.refs_3_.refs_10_
  112.3 5.2 %weight_terms.3 = (bf16[4,48,1536]{2,1,0:T(8,128)(2,1)}, bf16[4,48,1536]{2,1,0:T(8,128)(2,1)}) custom-call(s32[3]{0:T(128)} %pad_add_fusion.place_ref, bf16[384,1024]{1,0:T(8,128)(2,1)} %get-tuple-element.54.attended_ref, bf16[256,1536]{1,0:T(8,128)(2,1)} %copy-done.1, bf16[256,1536]{1,0:T(8,128)(2,1)} %copy-done.7, bf16[256,1536]{1,0:T(8,128)(2,1)} %copy-done.6, ...), custom_call_target="tpu_custom_call" | custom-call | flops 1207959552 | bytes 3932160 | tf_op jit(solution)/shard_map/weight_terms/pallas_call | solution.py:290
  117.5 12.1 %collective-permute-done.3 = bf16[192,3072]{1,0:T(8,128)(2,1)} collective-permute-done((bf16[192,3072]{1,0:T(8,128)(2,1)S(1)}, bf16[192,3072]{1,0:T(8,128)(2,1)}, u32[]{:S(2)}, u32[]{:S(2)}) %collective-permute-start.3) | collective-permute-done | bytes 1179680 | tf_op jit(solution)/shard_map/ppermute | solution.py:352
  129.5 24.2 %collective-permute-done.5 = bf16[192,3072]{1,0:T(8,128)(2,1)} collective-permute-done((bf16[192,3072]{1,0:T(8,128)(2,1)S(1)}, bf16[192,3072]{1,0:T(8,128)(2,1)}, u32[]{:S(2)}, u32[]{:S(2)}) %collective-permute-start.5) | collective-permute-done | bytes 1179680 | tf_op jit(solution)/shard_map/ppermute | solution.py:352
  154.5 5.7 %collective-permute-start.31 = (bf16[48,1536]{1,0:T(8,128)(2,1)}, bf16[48,1536]{1,0:T(8,128)(2,1)}, u32[]{:S(2)}, u32[]{:S(2)}) collective-permute-start(bf16[48,1536]{1,0:T(8,128)(2,1)} %get-tuple-element.102), channel_id=1, source_target_pairs={{0,24},{1,25},{2,26},{3,27},{4,28},{5,29},{6,30},{7,31},{8,0},{9,1... | collective-permute-start | bytes 442376 | tf_op jit(solution)/shard_map/ppermute | solution.py:352
  160.8 1.1 copy-done.8
  161.9 7.9 %project.1.refs_5_ = bf16[384,1024]{1,0:T(8,128)(2,1)} custom-call(s32[3]{0:T(128)} %pad_add_fusion.place_ref, bf16[192,3072]{1,0:T(8,128)(2,1)} %copy-done, bf16[192,3072]{1,0:T(8,128)(2,1)} %copy-done.8, bf16[256,1536]{1,0:T(8,128)(2,1)} %copy-done.2, bf16[256,1536]{1,0:T(8,128)(2,1)} %collective-permute-done.6.refs_1_.refs_3_, ...), custom_call_target="tpu_custom_call" | custom-call | flops 2415919104 | bytes 8650752 | tf_op jit(solution)/shard_map/project/pallas_call | solution.py:254
  169.8 3.5 %collective-permute-done.30 = bf16[48,1536]{1,0:T(8,128)(2,1)} collective-permute-done((bf16[48,1536]{1,0:T(8,128)(2,1)}, bf16[48,1536]{1,0:T(8,128)(2,1)}, u32[]{:S(2)}, u32[]{:S(2)}) %collective-permute-start.30) | collective-permute-done | bytes 147488 | tf_op jit(solution)/shard_map/ppermute | solution.py:352
  173.6 3.4 %collective-permute-start.23 = (bf16[48,1536]{1,0:T(8,128)(2,1)S(1)}, bf16[48,1536]{1,0:T(8,128)(2,1)S(1)}, u32[]{:S(2)}, u32[]{:S(2)}) collective-permute-start(bf16[48,1536]{1,0:T(8,128)(2,1)S(1)} %get-tuple-element.92), channel_id=1, source_target_pairs={{0,1},{1,0},{2,3},{3,2},{4,5},{5,4},{6,7},{7,6},{8,9},{9,8},{10,11... | collective-permute-start | bytes 442376 | tf_op jit(solution)/shard_map/ppermute | solution.py:352
  177.0 1.1 add_convert_fusion.1.refs_0_
  178.3 1.4 collective-permute-start.33
  179.7 5.6 %backward.2 = (bf16[3,256,128]{2,1,0:T(8,128)(2,1)}, bf16[3,256,128]{2,1,0:T(8,128)(2,1)}, bf16[3,256,128]{2,1,0:T(8,128)(2,1)}, bf16[3,256,128]{2,1,0:T(8,128)(2,1)}) custom-call(bf16[3,256,384]{2,1,0:T(8,128)(2,1)} %get-tuple-element.46.refs_0_, bf16[3,256,384]{2,1,0:T(8,128)(2,1)} %copy-done.3, bf16[3,256,384]{2,1,0:T(8,128)(2,1)} %copy-done.4, ...), custom_call_target="tpu_custom_call" | custom-call | flops 1073741824 | bytes 2097152 | tf_op jit(solution)/shard_map/backward/pallas_call | solution.py:199
  186.1 0.8 collective-permute-start.37
  186.9 1.9 collective-permute-start.36
  188.8 1.9 collective-permute-start.35
  190.8 8.6 %backward.3 = (bf16[3,256,256]{2,1,0:T(8,128)(2,1)}, bf16[3,256,256]{2,1,0:T(8,128)(2,1)}, bf16[3,256,256]{2,1,0:T(8,128)(2,1)}, bf16[3,256,256]{2,1,0:T(8,128)(2,1)}) custom-call(bf16[3,256,384]{2,1,0:T(8,128)(2,1)} %get-tuple-element.46.refs_0_, bf16[3,256,384]{2,1,0:T(8,128)(2,1)} %copy-done.3, bf16[3,256,384]{2,1,0:T(8,128)(2,1)} %copy-done.4, ...), custom_call_target="tpu_custom_call" | custom-call | flops 2147483648 | bytes 4194304 | tf_op jit(solution)/shard_map/backward/pallas_call | solution.py:199
  199.3 1.6 collective-permute-start.32
  201.7 0.9 collective-permute-start.40
  202.6 0.9 collective-permute-start.26
  203.5 1.7 collective-permute-start.27
  205.3 0.9 collective-permute-done.32.refs_1_
  206.1 1.0 collective-permute-start.28
  207.1 3.2 %collective-permute-done.19.refs_1_ = bf16[3,256,128]{2,1,0:T(8,128)(2,1)S(1)} collective-permute-done((bf16[3,256,128]{2,1,0:T(8,128)(2,1)S(1)}, bf16[3,256,128]{2,1,0:T(8,128)(2,1)S(1)}, u32[]{:S(2)}, u32[]{:S(2)}) %collective-permute-start.19) | collective-permute-done | bytes 196640 | tf_op jit(solution)/shard_map/ppermute | solution.py:352
  210.5 2.6 %collective-permute-done.40.refs_7_ = bf16[48,1536]{1,0:T(8,128)(2,1)S(1)} collective-permute-done((bf16[48,1536]{1,0:T(8,128)(2,1)S(1)}, bf16[48,1536]{1,0:T(8,128)(2,1)S(1)}, u32[]{:S(2)}, u32[]{:S(2)}) %collective-permute-start.40) | collective-permute-done | bytes 147488 | tf_op jit(solution)/shard_map/ppermute | solution.py:352
  213.1 1.4 collective-permute-start.38
  214.5 9.8 %collective-permute-done.39.refs_6_ = bf16[48,1536]{1,0:T(8,128)(2,1)S(1)} collective-permute-done((bf16[48,1536]{1,0:T(8,128)(2,1)S(1)}, bf16[48,1536]{1,0:T(8,128)(2,1)S(1)}, u32[]{:S(2)}, u32[]{:S(2)}) %collective-permute-start.39) | collective-permute-done | bytes 147488 | tf_op jit(solution)/shard_map/ppermute | solution.py:352
  224.4 1.7 collective-permute-start.20
  226.0 4.2 %collective-permute-done.38.refs_5_ = bf16[48,1536]{1,0:T(8,128)(2,1)S(1)} collective-permute-done((bf16[48,1536]{1,0:T(8,128)(2,1)S(1)}, bf16[48,1536]{1,0:T(8,128)(2,1)S(1)}, u32[]{:S(2)}, u32[]{:S(2)}) %collective-permute-start.38) | collective-permute-done | bytes 147488 | tf_op jit(solution)/shard_map/ppermute | solution.py:352
  230.2 0.8 collective-permute-start.21
  231.0 3.6 %assemble.1 = f32[192,3072]{1,0:T(8,128)} custom-call(s32[3]{0:T(128)} %pad_add_fusion.place_ref, bf16[48,1536]{1,0:T(8,128)(2,1)} %copy-done.14, bf16[48,1536]{1,0:T(8,128)(2,1)} %copy-done.25, bf16[48,1536]{1,0:T(8,128)(2,1)} %copy-done.24, bf16[48,1536]{1,0:T(8,128)(2,1)} %copy-done.23, bf16[48,1536]{1,0:T(8,128)(2,1)} %copy-done.15, ...), custom_call_target="tpu_custom_call" | custom-call | bytes 3538944 | tf_op jit(solution)/shard_map/assemble/pallas_call | solution.py:319
  234.6 2.1 collective-permute-done.21.refs_3_
  238.5 3.5 %unpack.1 = (bf16[1,256,1536]{2,1,0:T(8,128)(2,1)}, bf16[1,256,1536]{2,1,0:T(8,128)(2,1)}, bf16[1,256,1536]{2,1,0:T(8,128)(2,1)}) custom-call(s32[3]{0:T(128)} %pad_add_fusion.place_ref, bf16[3,256,128]{2,1,0:T(8,128)(2,1)} %get-tuple-element.61.refs_0_, bf16[3,256,128]{2,1,0:T(8,128)(2,1)} %copy-done.20, bf16[3,256,128]{2,1,0:T(8,128)(2,1)} %copy-done.21, ...), custom_call_target="tpu_custom_call" | custom-call | bytes 4718592 | tf_op jit(solution)/shard_map/unpack/pallas_call | solution.py:111
  (106 shorter events, 7.9 us)
Async XLA Ops:
  2.1 8.5 %copy-start.2 = (bf16[256,1536]{1,0:T(8,128)(2,1)}, bf16[256,1536]{1,0:T(8,128)(2,1)S(1)}, u32[]{:S(2)}) copy-start(bf16[256,1536]{1,0:T(8,128)(2,1)S(1)} %get-tuple-element.89.refs_0_.refs_2_) | copy-start | bytes 2359300
  2.1 69.8 %copy-start.1 = (bf16[256,1536]{1,0:T(8,128)(2,1)}, bf16[256,1536]{1,0:T(8,128)(2,1)S(1)}, u32[]{:S(2)}) copy-start(bf16[256,1536]{1,0:T(8,128)(2,1)S(1)} %get-tuple-element.55.refs_0_.refs_7_) | copy-start | bytes 2359300
  2.1 21.6 %collective-permute-start.7 = (bf16[256,1536]{1,0:T(8,128)(2,1)S(1)}, bf16[256,1536]{1,0:T(8,128)(2,1)}, u32[]{:S(2)}, u32[]{:S(2)}) collective-permute-start(bf16[256,1536]{1,0:T(8,128)(2,1)S(1)} %get-tuple-element.89.refs_0_.refs_2_), channel_id=1, source_target_pairs={{0,2},{1,3},{2,0},{3,1},{4,6},{5,7},{6,4},{7,5},{8,10},{9,11},{10,... | collective-permute-start | bytes 2359304 | tf_op jit(solution)/shard_map/ppermute | solution.py:352
  5.2 22.3 %collective-permute-start.6 = (bf16[256,1536]{1,0:T(8,128)(2,1)S(1)}, bf16[256,1536]{1,0:T(8,128)(2,1)}, u32[]{:S(2)}, u32[]{:S(2)}) collective-permute-start(bf16[256,1536]{1,0:T(8,128)(2,1)S(1)} %get-tuple-element.89.refs_0_.refs_2_), channel_id=1, source_target_pairs={{0,1},{1,0},{2,3},{3,2},{4,5},{5,4},{6,7},{7,6},{8,9},{9,8},{10,11... | collective-permute-start | bytes 2359304 | tf_op jit(solution)/shard_map/ppermute | solution.py:352
  10.6 27.7 %collective-permute-start = (bf16[3,256,384]{2,1,0:T(8,128)(2,1)}, bf16[3,256,384]{2,1,0:T(8,128)(2,1)S(1)}, u32[]{:S(2)}, u32[]{:S(2)}) collective-permute-start(bf16[3,256,384]{2,1,0:T(8,128)(2,1)} %get-tuple-element.47), channel_id=1, source_target_pairs={{0,1},{1,0},{2,3},{3,2},{4,5},{5,4},{6,7},{7,6},{8,9},{9,8},{10,11... | collective-permute-start | bytes 1769480 | tf_op jit(solution)/shard_map/ppermute | solution.py:352
  11.2 27.1 %collective-permute-start.1 = (bf16[3,256,384]{2,1,0:T(8,128)(2,1)}, bf16[3,256,384]{2,1,0:T(8,128)(2,1)S(1)}, u32[]{:S(2)}, u32[]{:S(2)}) collective-permute-start(bf16[3,256,384]{2,1,0:T(8,128)(2,1)} %get-tuple-element.48), channel_id=1, source_target_pairs={{0,2},{1,3},{2,0},{3,1},{4,6},{5,7},{6,4},{7,5},{8,10},{9,11},{10,... | collective-permute-start | bytes 1769480 | tf_op jit(solution)/shard_map/ppermute | solution.py:352
  11.3 39.2 %collective-permute-start.2 = (bf16[3,256,384]{2,1,0:T(8,128)(2,1)}, bf16[3,256,384]{2,1,0:T(8,128)(2,1)S(1)}, u32[]{:S(2)}, u32[]{:S(2)}) collective-permute-start(bf16[3,256,384]{2,1,0:T(8,128)(2,1)} %get-tuple-element.49), channel_id=1, source_target_pairs={{0,3},{1,2},{2,1},{3,0},{4,7},{5,6},{6,5},{7,4},{8,11},{9,10},{10,... | collective-permute-start | bytes 1769480 | tf_op jit(solution)/shard_map/ppermute | solution.py:352
  25.5 38.4 %collective-permute-start.9 = (bf16[128,1536]{1,0:T(8,128)(2,1)}, bf16[128,1536]{1,0:T(8,128)(2,1)}, u32[]{:S(2)}, u32[]{:S(2)}) collective-permute-start(bf16[128,1536]{1,0:T(8,128)(2,1)} %slice.90), channel_id=1, source_target_pairs={{0,1},{1,0},{2,3},{3,2},{4,5},{5,4},{6,7},{7,6},{8,9},{9,8},{10,11... | collective-permute-start | bytes 1179656 | tf_op jit(solution)/shard_map/ppermute | solution.py:352
  28.5 35.4 %collective-permute-start.8 = (bf16[128,1536]{1,0:T(8,128)(2,1)S(1)}, bf16[128,1536]{1,0:T(8,128)(2,1)S(1)}, u32[]{:S(2)}, u32[]{:S(2)}) collective-permute-start(bf16[128,1536]{1,0:T(8,128)(2,1)S(1)} %slice.89), channel_id=1, source_target_pairs={{0,2},{1,3},{2,0},{3,1},{4,6},{5,7},{6,4},{7,5},{8,10},{9,11},{10,... | collective-permute-start | bytes 1179656 | tf_op jit(solution)/shard_map/ppermute | solution.py:352
  38.2 12.2 %copy-start.3 = (bf16[3,256,384]{2,1,0:T(8,128)(2,1)}, bf16[3,256,384]{2,1,0:T(8,128)(2,1)S(1)}, u32[]{:S(2)}) copy-start(bf16[3,256,384]{2,1,0:T(8,128)(2,1)S(1)} %collective-permute-done.refs_1_) | copy-start | bytes 1769476
  38.2 12.2 %copy-start.4 = (bf16[3,256,384]{2,1,0:T(8,128)(2,1)}, bf16[3,256,384]{2,1,0:T(8,128)(2,1)S(1)}, u32[]{:S(2)}) copy-start(bf16[3,256,384]{2,1,0:T(8,128)(2,1)S(1)} %collective-permute-done.1.refs_2_) | copy-start | bytes 1769476
  64.6 8.8 %copy-start.9 = (bf16[192,3072]{1,0:T(8,128)(2,1)S(1)}, bf16[192,3072]{1,0:T(8,128)(2,1)}, u32[]{:S(2)}) copy-start(bf16[192,3072]{1,0:T(8,128)(2,1)} %param.9) | copy-start | bytes 3538948
  69.9 11.5 %collective-permute-start.10 = (bf16[4,48,1536]{2,1,0:T(8,128)(2,1)}, bf16[4,48,1536]{2,1,0:T(8,128)(2,1)S(1)}, u32[]{:S(2)}, u32[]{:S(2)}) collective-permute-start(bf16[4,48,1536]{2,1,0:T(8,128)(2,1)} %get-tuple-element.53), channel_id=1, source_target_pairs={{0,4},{1,5},{2,6},{3,7},{4,0},{5,1},{6,2},{7,3},{8,12},{9,13},{10,... | collective-permute-start | bytes 1769480 | tf_op jit(solution)/shard_map/ppermute | solution.py:352
  69.9 20.2 %collective-permute-start.15 = (bf16[256,1536]{1,0:T(8,128)(2,1)S(1)}, bf16[256,1536]{1,0:T(8,128)(2,1)S(1)}, u32[]{:S(2)}, u32[]{:S(2)}) collective-permute-start(bf16[256,1536]{1,0:T(8,128)(2,1)S(1)} %get-tuple-element.55.refs_0_.refs_7_), channel_id=1, source_target_pairs={{0,2},{1,3},{2,0},{3,1},{4,6},{5,7},{6,4},{7,5},{8,10},{9,11},{10,... | collective-permute-start | bytes 2359304 | tf_op jit(solution)/shard_map/ppermute | solution.py:352
  71.9 20.8 %collective-permute-start.14 = (bf16[256,1536]{1,0:T(8,128)(2,1)S(1)}, bf16[256,1536]{1,0:T(8,128)(2,1)S(1)}, u32[]{:S(2)}, u32[]{:S(2)}) collective-permute-start(bf16[256,1536]{1,0:T(8,128)(2,1)S(1)} %get-tuple-element.55.refs_0_.refs_7_), channel_id=1, source_target_pairs={{0,1},{1,0},{2,3},{3,2},{4,5},{5,4},{6,7},{7,6},{8,9},{9,8},{10,11... | collective-permute-start | bytes 2359304 | tf_op jit(solution)/shard_map/ppermute | solution.py:352
  73.4 44.0 %collective-permute-start.4 = (bf16[192,3072]{1,0:T(8,128)(2,1)S(1)}, bf16[192,3072]{1,0:T(8,128)(2,1)}, u32[]{:S(2)}, u32[]{:S(2)}) collective-permute-start(bf16[192,3072]{1,0:T(8,128)(2,1)S(1)} %copy-done.9), channel_id=1, source_target_pairs={{0,16},{4,20},{9,25},{13,29},{18,2},{22,6},{27,11},{31,15}} | collective-permute-start | bytes 3538952 | tf_op jit(solution)/shard_map/ppermute | solution.py:352
  79.0 50.5 %collective-permute-start.3 = (bf16[192,3072]{1,0:T(8,128)(2,1)S(1)}, bf16[192,3072]{1,0:T(8,128)(2,1)}, u32[]{:S(2)}, u32[]{:S(2)}) collective-permute-start(bf16[192,3072]{1,0:T(8,128)(2,1)S(1)} %copy-done.9), channel_id=1, source_target_pairs={{0,8},{4,12},{9,17},{13,21},{18,26},{22,30},{27,3},{31,7}} | collective-permute-start | bytes 3538952 | tf_op jit(solution)/shard_map/ppermute | solution.py:352
  81.4 72.3 %collective-permute-start.5 = (bf16[192,3072]{1,0:T(8,128)(2,1)S(1)}, bf16[192,3072]{1,0:T(8,128)(2,1)}, u32[]{:S(2)}, u32[]{:S(2)}) collective-permute-start(bf16[192,3072]{1,0:T(8,128)(2,1)S(1)} %copy-done.9), channel_id=1, source_target_pairs={{0,24},{4,28},{9,1},{13,5},{18,10},{22,14},{27,19},{31,23}} | collective-permute-start | bytes 3538952 | tf_op jit(solution)/shard_map/ppermute | solution.py:352
  90.1 14.6 %copy-start.6 = (bf16[256,1536]{1,0:T(8,128)(2,1)}, bf16[256,1536]{1,0:T(8,128)(2,1)S(1)}, u32[]{:S(2)}) copy-start(bf16[256,1536]{1,0:T(8,128)(2,1)S(1)} %collective-permute-done.15.refs_2_.refs_9_) | copy-start | bytes 2359300
  90.1 6.6 %collective-permute-start.13 = (bf16[48,1536]{1,0:T(8,128)(2,1)S(1)}, bf16[48,1536]{1,0:T(8,128)(2,1)}, u32[]{:S(2)}, u32[]{:S(2)}) collective-permute-start(bf16[48,1536]{1,0:T(8,128)(2,1)S(1)} %get-tuple-element.95), channel_id=1, source_target_pairs={{0,3},{1,2},{2,1},{3,0},{4,7},{5,6},{6,5},{7,4},{8,11},{9,10},{10,... | collective-permute-start | bytes 442376 | tf_op jit(solution)/shard_map/ppermute | solution.py:352
  92.8 12.0 %copy-start.7 = (bf16[256,1536]{1,0:T(8,128)(2,1)}, bf16[256,1536]{1,0:T(8,128)(2,1)S(1)}, u32[]{:S(2)}) copy-start(bf16[256,1536]{1,0:T(8,128)(2,1)S(1)} %collective-permute-done.14.refs_1_.refs_8_) | copy-start | bytes 2359300
  92.8 11.0 %copy-start.11 = (bf16[1,48,1536]{2,1,0:T(8,128)(2,1)S(1)}, bf16[1,48,1536]{2,1,0:T(8,128)(2,1)}, u32[]{:S(2)}) copy-start(bf16[1,48,1536]{2,1,0:T(8,128)(2,1)} %get-tuple-element.94) | copy-start | bytes 442372
  92.8 6.9 %collective-permute-start.12 = (bf16[48,1536]{1,0:T(8,128)(2,1)}, bf16[48,1536]{1,0:T(8,128)(2,1)S(1)}, u32[]{:S(2)}, u32[]{:S(2)}) collective-permute-start(bf16[48,1536]{1,0:T(8,128)(2,1)} %get-tuple-element.96), channel_id=1, source_target_pairs={{0,2},{1,3},{2,0},{3,1},{4,6},{5,7},{6,4},{7,5},{8,10},{9,11},{10,... | collective-permute-start | bytes 442376 | tf_op jit(solution)/shard_map/ppermute | solution.py:352
  96.7 5.4 %collective-permute-start.11 = (bf16[48,1536]{1,0:T(8,128)(2,1)}, bf16[48,1536]{1,0:T(8,128)(2,1)S(1)}, u32[]{:S(2)}, u32[]{:S(2)}) collective-permute-start(bf16[48,1536]{1,0:T(8,128)(2,1)} %get-tuple-element.97), channel_id=1, source_target_pairs={{0,1},{1,0},{2,3},{3,2},{4,5},{5,4},{6,7},{7,6},{8,9},{9,8},{10,11... | collective-permute-start | bytes 442376 | tf_op jit(solution)/shard_map/ppermute | solution.py:352
  99.7 11.1 %collective-permute-start.17 = (bf16[128,1536]{1,0:T(8,128)(2,1)S(1)}, bf16[128,1536]{1,0:T(8,128)(2,1)}, u32[]{:S(2)}, u32[]{:S(2)}) collective-permute-start(bf16[128,1536]{1,0:T(8,128)(2,1)S(1)} %slice.97), channel_id=1, source_target_pairs={{0,1},{1,0},{2,3},{3,2},{4,5},{5,4},{6,7},{7,6},{8,9},{9,8},{10,11... | collective-permute-start | bytes 1179656 | tf_op jit(solution)/shard_map/ppermute | solution.py:352
  102.1 10.2 %collective-permute-start.16 = (bf16[128,1536]{1,0:T(8,128)(2,1)S(1)}, bf16[128,1536]{1,0:T(8,128)(2,1)}, u32[]{:S(2)}, u32[]{:S(2)}) collective-permute-start(bf16[128,1536]{1,0:T(8,128)(2,1)S(1)} %slice.96), channel_id=1, source_target_pairs={{0,2},{1,3},{2,0},{3,1},{4,6},{5,7},{6,4},{7,5},{8,10},{9,11},{10,... | collective-permute-start | bytes 1179656 | tf_op jit(solution)/shard_map/ppermute | solution.py:352
  105.6 48.2 %copy-start.10 = (bf16[192,3072]{1,0:T(8,128)(2,1)S(1)}, bf16[192,3072]{1,0:T(8,128)(2,1)}, u32[]{:S(2)}) copy-start(bf16[192,3072]{1,0:T(8,128)(2,1)} %param.9) | copy-start | bytes 3538948
  153.9 6.8 %copy-start = (bf16[192,3072]{1,0:T(8,128)(2,1)}, bf16[192,3072]{1,0:T(8,128)(2,1)S(1)}, u32[]{:S(2)}) copy-start(bf16[192,3072]{1,0:T(8,128)(2,1)S(1)} %select_select_fusion.refs_0_) | copy-start | bytes 3538948
  154.0 6.8 %collective-permute-start.18 = (bf16[192,3072]{1,0:T(8,128)(2,1)S(1)}, bf16[192,3072]{1,0:T(8,128)(2,1)S(1)}, u32[]{:S(2)}, u32[]{:S(2)}) collective-permute-start(bf16[192,3072]{1,0:T(8,128)(2,1)S(1)} %select_select_fusion.refs_0_), channel_id=1, source_target_pairs={{0,4},{1,5},{2,6},{3,7},{4,0},{5,1},{6,2},{7,3},{8,12},{9,13},{10,... | collective-permute-start | bytes 3538952 | tf_op jit(solution)/shard_map/ppermute | solution.py:352
  154.0 19.2 %collective-permute-start.22 = (bf16[4,48,1536]{2,1,0:T(8,128)(2,1)}, bf16[4,48,1536]{2,1,0:T(8,128)(2,1)S(1)}, u32[]{:S(2)}, u32[]{:S(2)}) collective-permute-start(bf16[4,48,1536]{2,1,0:T(8,128)(2,1)} %get-tuple-element.65), channel_id=1, source_target_pairs={{0,4},{1,5},{2,6},{3,7},{4,0},{5,1},{6,2},{7,3},{8,12},{9,13},{10,... | collective-permute-start | bytes 1769480 | tf_op jit(solution)/shard_map/ppermute | solution.py:352
  154.5 15.2 %collective-permute-start.31 = (bf16[48,1536]{1,0:T(8,128)(2,1)}, bf16[48,1536]{1,0:T(8,128)(2,1)}, u32[]{:S(2)}, u32[]{:S(2)}) collective-permute-start(bf16[48,1536]{1,0:T(8,128)(2,1)} %get-tuple-element.102), channel_id=1, source_target_pairs={{0,24},{1,25},{2,26},{3,27},{4,28},{5,29},{6,30},{7,31},{8,0},{9,1... | collective-permute-start | bytes 442376 | tf_op jit(solution)/shard_map/ppermute | solution.py:352
  160.2 13.1 %collective-permute-start.30 = (bf16[48,1536]{1,0:T(8,128)(2,1)}, bf16[48,1536]{1,0:T(8,128)(2,1)}, u32[]{:S(2)}, u32[]{:S(2)}) collective-permute-start(bf16[48,1536]{1,0:T(8,128)(2,1)} %get-tuple-element.103), channel_id=1, source_target_pairs={{0,16},{1,17},{2,18},{3,19},{4,20},{5,21},{6,22},{7,23},{8,24},{9,... | collective-permute-start | bytes 442376 | tf_op jit(solution)/shard_map/ppermute | solution.py:352
  160.2 13.1 %copy-start.12 = (bf16[4,48,1536]{2,1,0:T(8,128)(2,1)S(1)}, bf16[4,48,1536]{2,1,0:T(8,128)(2,1)}, u32[]{:S(2)}) copy-start(bf16[4,48,1536]{2,1,0:T(8,128)(2,1)} %get-tuple-element.66) | copy-start | bytes 1769476
  160.2 13.1 %collective-permute-start.29 = (bf16[48,1536]{1,0:T(8,128)(2,1)}, bf16[48,1536]{1,0:T(8,128)(2,1)}, u32[]{:S(2)}, u32[]{:S(2)}) collective-permute-start(bf16[48,1536]{1,0:T(8,128)(2,1)} %get-tuple-element.104), channel_id=1, source_target_pairs={{0,8},{1,9},{2,10},{3,11},{4,12},{5,13},{6,14},{7,15},{8,16},{9,17... | collective-permute-start | bytes 442376 | tf_op jit(solution)/shard_map/ppermute | solution.py:352
  169.8 7.2 %copy-start.13 = (bf16[48,1536]{1,0:T(8,128)(2,1)S(1)}, bf16[48,1536]{1,0:T(8,128)(2,1)}, u32[]{:S(2)}) copy-start(bf16[48,1536]{1,0:T(8,128)(2,1)} %get-tuple-element.80) | copy-start | bytes 442372
  173.4 11.9 %collective-permute-start.25 = (bf16[48,1536]{1,0:T(8,128)(2,1)S(1)}, bf16[48,1536]{1,0:T(8,128)(2,1)S(1)}, u32[]{:S(2)}, u32[]{:S(2)}) collective-permute-start(bf16[48,1536]{1,0:T(8,128)(2,1)S(1)} %get-tuple-element.90), channel_id=1, source_target_pairs={{0,3},{1,2},{2,1},{3,0},{4,7},{5,6},{6,5},{7,4},{8,11},{9,10},{10,... | collective-permute-start | bytes 442376 | tf_op jit(solution)/shard_map/ppermute | solution.py:352
  173.5 12.5 %collective-permute-start.24 = (bf16[48,1536]{1,0:T(8,128)(2,1)S(1)}, bf16[48,1536]{1,0:T(8,128)(2,1)S(1)}, u32[]{:S(2)}, u32[]{:S(2)}) collective-permute-start(bf16[48,1536]{1,0:T(8,128)(2,1)S(1)} %get-tuple-element.91), channel_id=1, source_target_pairs={{0,2},{1,3},{2,0},{3,1},{4,6},{5,7},{6,4},{7,5},{8,10},{9,11},{10,... | collective-permute-start | bytes 442376 | tf_op jit(solution)/shard_map/ppermute | solution.py:352
  173.6 12.4 %collective-permute-start.23 = (bf16[48,1536]{1,0:T(8,128)(2,1)S(1)}, bf16[48,1536]{1,0:T(8,128)(2,1)S(1)}, u32[]{:S(2)}, u32[]{:S(2)}) collective-permute-start(bf16[48,1536]{1,0:T(8,128)(2,1)S(1)} %get-tuple-element.92), channel_id=1, source_target_pairs={{0,1},{1,0},{2,3},{3,2},{4,5},{5,4},{6,7},{7,6},{8,9},{9,8},{10,11... | collective-permute-start | bytes 442376 | tf_op jit(solution)/shard_map/ppermute | solution.py:352
  178.1 21.2 %copy-start.14 = (bf16[48,1536]{1,0:T(8,128)(2,1)}, bf16[48,1536]{1,0:T(8,128)(2,1)S(1)}, u32[]{:S(2)}) copy-start(bf16[48,1536]{1,0:T(8,128)(2,1)S(1)} %add_convert_fusion.1.refs_0_) | copy-start | bytes 442372
  178.1 24.5 %collective-permute-start.34 = (bf16[48,1536]{1,0:T(8,128)(2,1)S(1)}, bf16[48,1536]{1,0:T(8,128)(2,1)S(1)}, u32[]{:S(2)}, u32[]{:S(2)}) collective-permute-start(bf16[48,1536]{1,0:T(8,128)(2,1)S(1)} %add_convert_fusion.1.refs_0_), channel_id=1, source_target_pairs={{0,3},{1,2},{2,1},{3,0},{4,7},{5,6},{6,5},{7,4},{8,11},{9,10},{10,... | collective-permute-start | bytes 442376 | tf_op jit(solution)/shard_map/ppermute | solution.py:352
  178.3 25.2 %collective-permute-start.33 = (bf16[48,1536]{1,0:T(8,128)(2,1)S(1)}, bf16[48,1536]{1,0:T(8,128)(2,1)S(1)}, u32[]{:S(2)}, u32[]{:S(2)}) collective-permute-start(bf16[48,1536]{1,0:T(8,128)(2,1)S(1)} %add_convert_fusion.1.refs_0_), channel_id=1, source_target_pairs={{0,2},{1,3},{2,0},{3,1},{4,6},{5,7},{6,4},{7,5},{8,10},{9,11},{10,... | collective-permute-start | bytes 442376 | tf_op jit(solution)/shard_map/ppermute | solution.py:352
  186.1 13.2 %collective-permute-start.37 = (bf16[48,1536]{1,0:T(8,128)(2,1)S(1)}, bf16[48,1536]{1,0:T(8,128)(2,1)S(1)}, u32[]{:S(2)}, u32[]{:S(2)}) collective-permute-start(bf16[48,1536]{1,0:T(8,128)(2,1)S(1)} %get-tuple-element.98), channel_id=1, source_target_pairs={{0,24},{1,25},{2,26},{3,27},{4,28},{5,29},{6,30},{7,31},{8,0},{9,1... | collective-permute-start | bytes 442376 | tf_op jit(solution)/shard_map/ppermute | solution.py:352
  186.9 14.0 %collective-permute-start.36 = (bf16[48,1536]{1,0:T(8,128)(2,1)S(1)}, bf16[48,1536]{1,0:T(8,128)(2,1)S(1)}, u32[]{:S(2)}, u32[]{:S(2)}) collective-permute-start(bf16[48,1536]{1,0:T(8,128)(2,1)S(1)} %get-tuple-element.99), channel_id=1, source_target_pairs={{0,16},{1,17},{2,18},{3,19},{4,20},{5,21},{6,22},{7,23},{8,24},{9,... | collective-permute-start | bytes 442376 | tf_op jit(solution)/shard_map/ppermute | solution.py:352
  188.8 12.1 %copy-start.31 = (bf16[3,256,128]{2,1,0:T(8,128)(2,1)S(1)}, bf16[3,256,128]{2,1,0:T(8,128)(2,1)}, u32[]{:S(2)}) copy-start(bf16[3,256,128]{2,1,0:T(8,128)(2,1)} %get-tuple-element.62) | copy-start | bytes 589828
  188.8 35.5 %copy-start.30 = (bf16[3,256,128]{2,1,0:T(8,128)(2,1)S(1)}, bf16[3,256,128]{2,1,0:T(8,128)(2,1)}, u32[]{:S(2)}) copy-start(bf16[3,256,128]{2,1,0:T(8,128)(2,1)} %get-tuple-element.63) | copy-start | bytes 589828
  188.8 41.4 %copy-start.29 = (bf16[3,256,128]{2,1,0:T(8,128)(2,1)S(1)}, bf16[3,256,128]{2,1,0:T(8,128)(2,1)}, u32[]{:S(2)}) copy-start(bf16[3,256,128]{2,1,0:T(8,128)(2,1)} %get-tuple-element.64) | copy-start | bytes 589828
  188.8 12.8 %collective-permute-start.35 = (bf16[48,1536]{1,0:T(8,128)(2,1)S(1)}, bf16[48,1536]{1,0:T(8,128)(2,1)S(1)}, u32[]{:S(2)}, u32[]{:S(2)}) collective-permute-start(bf16[48,1536]{1,0:T(8,128)(2,1)S(1)} %get-tuple-element.100), channel_id=1, source_target_pairs={{0,8},{1,9},{2,10},{3,11},{4,12},{5,13},{6,14},{7,15},{8,16},{9,17... | collective-permute-start | bytes 442376 | tf_op jit(solution)/shard_map/ppermute | solution.py:352
  199.3 6.8 %collective-permute-start.32 = (bf16[48,1536]{1,0:T(8,128)(2,1)S(1)}, bf16[48,1536]{1,0:T(8,128)(2,1)S(1)}, u32[]{:S(2)}, u32[]{:S(2)}) collective-permute-start(bf16[48,1536]{1,0:T(8,128)(2,1)S(1)} %add_convert_fusion.1.refs_0_), channel_id=1, source_target_pairs={{0,1},{1,0},{2,3},{3,2},{4,5},{5,4},{6,7},{7,6},{8,9},{9,8},{10,11... | collective-permute-start | bytes 442376 | tf_op jit(solution)/shard_map/ppermute | solution.py:352
  201.0 9.4 %collective-permute-start.19 = (bf16[3,256,128]{2,1,0:T(8,128)(2,1)S(1)}, bf16[3,256,128]{2,1,0:T(8,128)(2,1)S(1)}, u32[]{:S(2)}, u32[]{:S(2)}) collective-permute-start(bf16[3,256,128]{2,1,0:T(8,128)(2,1)S(1)} %copy-done.31), channel_id=1, source_target_pairs={{0,1},{1,0},{2,3},{3,2},{4,5},{5,4},{6,7},{7,6},{8,9},{9,8},{10,11... | collective-permute-start | bytes 589832 | tf_op jit(solution)/shard_map/ppermute | solution.py:352
  201.7 29.3 %copy-start.15 = (bf16[48,1536]{1,0:T(8,128)(2,1)}, bf16[48,1536]{1,0:T(8,128)(2,1)S(1)}, u32[]{:S(2)}) copy-start(bf16[48,1536]{1,0:T(8,128)(2,1)S(1)} %add_convert_fusion.refs_4_) | copy-start | bytes 442372
  201.7 11.4 %collective-permute-start.40 = (bf16[48,1536]{1,0:T(8,128)(2,1)S(1)}, bf16[48,1536]{1,0:T(8,128)(2,1)S(1)}, u32[]{:S(2)}, u32[]{:S(2)}) collective-permute-start(bf16[48,1536]{1,0:T(8,128)(2,1)S(1)} %add_convert_fusion.refs_4_), channel_id=1, source_target_pairs={{0,3},{1,2},{2,1},{3,0},{4,7},{5,6},{6,5},{7,4},{8,11},{9,10},{10,... | collective-permute-start | bytes 442376 | tf_op jit(solution)/shard_map/ppermute | solution.py:352
  202.6 28.4 %copy-start.23 = (bf16[48,1536]{1,0:T(8,128)(2,1)}, bf16[48,1536]{1,0:T(8,128)(2,1)S(1)}, u32[]{:S(2)}) copy-start(bf16[48,1536]{1,0:T(8,128)(2,1)S(1)} %collective-permute-done.34.refs_3_) | copy-start | bytes 442372
  202.6 34.2 %collective-permute-start.26 = (bf16[3,256,256]{2,1,0:T(8,128)(2,1)}, bf16[3,256,256]{2,1,0:T(8,128)(2,1)S(1)}, u32[]{:S(2)}, u32[]{:S(2)}) collective-permute-start(bf16[3,256,256]{2,1,0:T(8,128)(2,1)} %get-tuple-element.74), channel_id=1, source_target_pairs={{0,1},{1,0},{2,3},{3,2},{4,5},{5,4},{6,7},{7,6},{8,9},{9,8},{10,11... | collective-permute-start | bytes 1179656 | tf_op jit(solution)/shard_map/ppermute | solution.py:352
  203.5 27.5 %copy-start.24 = (bf16[48,1536]{1,0:T(8,128)(2,1)}, bf16[48,1536]{1,0:T(8,128)(2,1)S(1)}, u32[]{:S(2)}) copy-start(bf16[48,1536]{1,0:T(8,128)(2,1)S(1)} %collective-permute-done.33.refs_2_) | copy-start | bytes 442372
  203.5 33.3 %collective-permute-start.27 = (bf16[3,256,256]{2,1,0:T(8,128)(2,1)}, bf16[3,256,256]{2,1,0:T(8,128)(2,1)S(1)}, u32[]{:S(2)}, u32[]{:S(2)}) collective-permute-start(bf16[3,256,256]{2,1,0:T(8,128)(2,1)} %get-tuple-element.75), channel_id=1, source_target_pairs={{0,2},{1,3},{2,0},{3,1},{4,6},{5,7},{6,4},{7,5},{8,10},{9,11},{10,... | collective-permute-start | bytes 1179656 | tf_op jit(solution)/shard_map/ppermute | solution.py:352
  206.1 24.9 %copy-start.25 = (bf16[48,1536]{1,0:T(8,128)(2,1)}, bf16[48,1536]{1,0:T(8,128)(2,1)S(1)}, u32[]{:S(2)}) copy-start(bf16[48,1536]{1,0:T(8,128)(2,1)S(1)} %collective-permute-done.32.refs_1_) | copy-start | bytes 442372
  206.1 30.7 %collective-permute-start.28 = (bf16[3,256,256]{2,1,0:T(8,128)(2,1)}, bf16[3,256,256]{2,1,0:T(8,128)(2,1)S(1)}, u32[]{:S(2)}, u32[]{:S(2)}) collective-permute-start(bf16[3,256,256]{2,1,0:T(8,128)(2,1)} %get-tuple-element.76), channel_id=1, source_target_pairs={{0,3},{1,2},{2,1},{3,0},{4,7},{5,6},{6,5},{7,4},{8,11},{9,10},{10,... | collective-permute-start | bytes 1179656 | tf_op jit(solution)/shard_map/ppermute | solution.py:352
  210.3 24.3 %copy-start.20 = (bf16[3,256,128]{2,1,0:T(8,128)(2,1)}, bf16[3,256,128]{2,1,0:T(8,128)(2,1)S(1)}, u32[]{:S(2)}) copy-start(bf16[3,256,128]{2,1,0:T(8,128)(2,1)S(1)} %collective-permute-done.19.refs_1_) | copy-start | bytes 589828
  210.3 14.0 %collective-permute-start.39 = (bf16[48,1536]{1,0:T(8,128)(2,1)S(1)}, bf16[48,1536]{1,0:T(8,128)(2,1)S(1)}, u32[]{:S(2)}, u32[]{:S(2)}) collective-permute-start(bf16[48,1536]{1,0:T(8,128)(2,1)S(1)} %add_convert_fusion.refs_4_), channel_id=1, source_target_pairs={{0,2},{1,3},{2,0},{3,1},{4,6},{5,7},{6,4},{7,5},{8,10},{9,11},{10,... | collective-permute-start | bytes 442376 | tf_op jit(solution)/shard_map/ppermute | solution.py:352
  213.1 17.9 %copy-start.26 = (bf16[48,1536]{1,0:T(8,128)(2,1)}, bf16[48,1536]{1,0:T(8,128)(2,1)S(1)}, u32[]{:S(2)}) copy-start(bf16[48,1536]{1,0:T(8,128)(2,1)S(1)} %collective-permute-done.40.refs_7_) | copy-start | bytes 442372
  213.1 17.1 %collective-permute-start.38 = (bf16[48,1536]{1,0:T(8,128)(2,1)S(1)}, bf16[48,1536]{1,0:T(8,128)(2,1)S(1)}, u32[]{:S(2)}, u32[]{:S(2)}) collective-permute-start(bf16[48,1536]{1,0:T(8,128)(2,1)S(1)} %add_convert_fusion.refs_4_), channel_id=1, source_target_pairs={{0,1},{1,0},{2,3},{3,2},{4,5},{5,4},{6,7},{7,6},{8,9},{9,8},{10,11... | collective-permute-start | bytes 442376 | tf_op jit(solution)/shard_map/ppermute | solution.py:352
  224.3 6.7 %copy-start.27 = (bf16[48,1536]{1,0:T(8,128)(2,1)}, bf16[48,1536]{1,0:T(8,128)(2,1)S(1)}, u32[]{:S(2)}) copy-start(bf16[48,1536]{1,0:T(8,128)(2,1)S(1)} %collective-permute-done.39.refs_6_) | copy-start | bytes 442372
  224.4 10.3 %collective-permute-start.20 = (bf16[3,256,128]{2,1,0:T(8,128)(2,1)S(1)}, bf16[3,256,128]{2,1,0:T(8,128)(2,1)S(1)}, u32[]{:S(2)}, u32[]{:S(2)}) collective-permute-start(bf16[3,256,128]{2,1,0:T(8,128)(2,1)S(1)} %copy-done.30), channel_id=1, source_target_pairs={{0,2},{1,3},{2,0},{3,1},{4,6},{5,7},{6,4},{7,5},{8,10},{9,11},{10,... | collective-permute-start | bytes 589832 | tf_op jit(solution)/shard_map/ppermute | solution.py:352
  230.2 6.6 %collective-permute-start.21 = (bf16[3,256,128]{2,1,0:T(8,128)(2,1)S(1)}, bf16[3,256,128]{2,1,0:T(8,128)(2,1)S(1)}, u32[]{:S(2)}, u32[]{:S(2)}) collective-permute-start(bf16[3,256,128]{2,1,0:T(8,128)(2,1)S(1)} %copy-done.29), channel_id=1, source_target_pairs={{0,3},{1,2},{2,1},{3,0},{4,7},{5,6},{6,5},{7,4},{8,11},{9,10},{10,... | collective-permute-start | bytes 589832 | tf_op jit(solution)/shard_map/ppermute | solution.py:352
  (9 other events, 9.0 us)

commit v4 on v3

--- a/solution.py
+++ b/solution.py
@@ -18,6 +18,10 @@
 
 def dot(a, b, dims=NN):
     return lax.dot_general(a, b, dims, preferred_element_type=jnp.float32)
+
+
+def far(*arrays):
+    return [pltpu.with_memory_space_constraint(array, pltpu.HBM) for array in arrays]
 
 
 def whole(shape):
@@ -123,7 +127,7 @@
         out_shape=[full] * 3,
         cost_estimate=cost(0, 12 * tokens * width * rows),
         name="unpack",
-    )(place, *(block for part in parts for block in part))
+    )(place, *far(*(block for part in parts for block in part)))
 
 
 def forward(parts):
@@ -163,7 +167,7 @@
             8 * heads * length * length * HDIM, 2 * heads * length * length, heads * length * length
         ),
         name="forward",
-    )(*parts)
+    )(*far(*parts))
 
 
 def backward(parts, probs, grad_attn, first, count):
@@ -209,7 +213,7 @@
         scratch_shapes=[pltpu.VMEM((length, length), jnp.bfloat16)],
         cost_estimate=cost(8 * count * length * length * HDIM, 2 * count * length * length),
         name="backward",
-    )(*parts, probs, grad_attn)
+    )(*far(*parts, probs, grad_attn))
 
 
 def stacked(refs):
@@ -264,7 +268,7 @@
         out_shape=jax.ShapeDtypeStruct(shape, jnp.bfloat16),
         cost_estimate=cost(2 * shape[0] * shape[1] * depth, 2 * depth * (shape[0] + shape[1])),
         name="project",
-    )(place, *weights, *(block for chunk in grads for block in chunk))
+    )(place, *far(*weights, *(block for chunk in grads for block in chunk)))
 
 
 def weight_terms(place, attended, grads, rows):
@@ -299,7 +303,7 @@
         out_shape=[shape] * 2,
         cost_estimate=cost(4 * width * length * step, 2 * (width * length + 2 * length * step)),
         name="weight_terms",
-    )(place, attended, *grads)
+    )(place, *far(attended, *grads))
 
 
 def assemble(place, pieces):
@@ -327,7 +331,7 @@
         out_shape=jax.ShapeDtypeStruct(shape, jnp.float32),
         cost_estimate=cost(0, 6 * shape[0] * shape[1]),
         name="assemble",
-    )(place, *(block for chunk in pieces for block in chunk))
+    )(place, *far(*(block for chunk in pieces for block in chunk)))
 
 
 def after(value, *done):
@@ -363,8 +367,9 @@
     grad_flat = grad_out[0]
     wide = grad_flat.shape[1] // 2
 
-    def gather(chunk):
+    def gather(chunk, *done):
         by_x, by_y = to_row(chunk, 1), to_row(chunk, 2)
+        by_x, by_y = after((by_x, by_y), *done)
         cut = chunk.shape[0] // 2
         upper = to_row(by_x[:cut], 2)
         lower = to_row(by_y[cut:], 1)
@@ -380,7 +385,7 @@
     packed = pack(place, query_rows, key_rows, value_rows, rows)
     parts = [packed[0]] + [to_row(packed[slot], slot) for slot in range(1, rows)]
     probs, attended = forward(parts)
-    grads.append(gather(after(grad_flat[:, wide:], parts)))
+    grads.append(gather(after(grad_flat[:, wide:], parts), attended))
 
     def reduce_cores(attended, chunk):
         keep, give = weight_terms(place, attended, chunk, rows)
@@ -407,8 +412,9 @@
         total = total.astype(jnp.bfloat16)
         return [total] + [to_row(total, slot) for slot in range(1, rows)]
 
-    early = reduce_planes(spread(*reduce_cores(attended, grads[0])))
-    late = reduce_cores(after(attended, early[0]), grads[1])
+    blocks = spread(*reduce_cores(attended, grads[0]))
+    late = reduce_cores(attended, grads[1])
+    early = reduce_planes(after(blocks, late[0]))
     lines = after(lines, late[0])
     here = lines[0]
     for ahead in range(1, planes):
@@ -416,7 +422,7 @@
     other = to_core(here)
     grad_attn = project(place, [here, other], grads)
     heads = probs.shape[0]
-    blocks = spread(*after(late, grad_attn))
+    blocks = spread(*after(late, early[0]))
     sent = [backward(parts, probs, grad_attn, 0, 1)]
     late = reduce_planes(after(blocks, sent[0][0]))
     sent.append(backward(parts, after(probs, late[0]), grad_attn, 1, heads - 1))
@@ -425,7 +431,7 @@
         + [to_row(message[slot], slot) for slot in range(1, rows)]
         for message in sent
     ]
-    pieces = [collect(*after(early, grad_attn)), collect(*after(late, sent[1][0]))]
+    pieces = [collect(*after(early, sent[0][0])), collect(*after(late, sent[1][0]))]
     grad_query, grad_key, grad_value = unpack(place, back)
     grad_w_out = assemble(place, pieces)
     return grad_query, grad_key, grad_value, grad_w_out

time: 243 us -> 216 us (0.89)
  waiting for transfers between devices: 110 us -> 81.4 us
    ppermute x41, waiting for transfers between devices: 110 us -> 81.4 us  [send(): return lax.ppermute(array, ('fsdp', 'rows'), pairs)]
  transfers between devices with their start and end apart: 41 -> 41, of which waited for: 19 -> 16; matrix products, arithmetic and copies ran while one was open for 4% -> 5% of each run, Pallas kernels for 19% -> 23%
where the time goes in v4:
time: 216 us
  waiting for transfers between devices  81.4 us (38%)
  starting transfers between devices  61.4 us (28%)
  Pallas kernels  55.4 us (26%)
  local copies, waits for them, and re-layouts  10.1 us (5%)
  other arithmetic  6.32 us (3%)
    ppermute x41, waiting for transfers between devices, send(): return lax.ppermute(array, ('fsdp', 'rows'), pairs)  81.4 us
    ppermute x41, starting transfers between devices, send(): return lax.ppermute(array, ('fsdp', 'rows'), pairs)  61.4 us
    pallas_call x2, Pallas kernels, backward(): pl.pallas_call(body, grid=(count,), in_specs=[part] * rows + [pl.BlockSpe...  14.2 us
    pallas_call x1, Pallas kernels, forward(): pl.pallas_call(body, grid=(heads,), in_specs=[part] * rows, out_specs=[pl...  12.6 us
    pallas_call x2, Pallas kernels, weight_terms(): pl.pallas_call(body, grid_spec=pltpu.PrefetchScalarGridSpec(num_scalar_pr...  10.4 us
    pallas_call x1, Pallas kernels, project(): pl.pallas_call(body, grid_spec=pltpu.PrefetchScalarGridSpec(num_scalar_pr...  7.88 us
  transfers between devices with their start and end apart: 41, of which 16 were waited for; matrix products, arithmetic and copies ran while one was open for 5% of the time, Pallas kernels for 23%

profile of v4, /device:TPU:0, one launch (start us, length us, event | category | flops | bytes accessed | tf_op | source)
XLA Modules:
  0.0 215.8 jit_solution(17203566503065872959)
XLA Ops:
  1.2 3.3 %pack.1 = (bf16[3,256,384]{2,1,0:T(8,128)(2,1)}, bf16[3,256,384]{2,1,0:T(8,128)(2,1)}, bf16[3,256,384]{2,1,0:T(8,128)(2,1)}, bf16[3,256,384]{2,1,0:T(8,128)(2,1)}) custom-call(s32[3]{0:T(128)} %pad_add_fusion.place_ref, bf16[1,256,1536]{2,1,0:T(8,128)(2,1)} %refs_0_.1, bf16[1,256,1536]{2,1,0:T(8,128)(2,1)} %refs_1_.1, bf16[1,256,1536]{2,1,0:T(8,128)(2,1)} %refs_2_.1), custom_call_target="tpu_custom_call" | custom-call | bytes 4718592 | tf_op jit(solution)/shard_map/pack/pallas_call | solution.py:56
  4.5 3.0 %collective-permute-start = (bf16[3,256,384]{2,1,0:T(8,128)(2,1)}, bf16[3,256,384]{2,1,0:T(8,128)(2,1)S(1)}, u32[]{:S(2)}, u32[]{:S(2)}) collective-permute-start(bf16[3,256,384]{2,1,0:T(8,128)(2,1)} %get-tuple-element.54), channel_id=1, source_target_pairs={{0,1},{1,0},{2,3},{3,2},{4,5},{5,4},{6,7},{7,6},{8,9},{9,8},{10,11... | collective-permute-start | bytes 1769480 | tf_op jit(solution)/shard_map/ppermute | solution.py:356
  7.6 1.5 collective-permute-start.1
  9.1 1.5 fusion.8
  10.6 2.0 collective-permute-start.11
  12.6 1.5 collective-permute-start.12
  14.1 7.8 %collective-permute-done.refs_1_ = bf16[3,256,384]{2,1,0:T(8,128)(2,1)S(1)} collective-permute-done((bf16[3,256,384]{2,1,0:T(8,128)(2,1)}, bf16[3,256,384]{2,1,0:T(8,128)(2,1)S(1)}, u32[]{:S(2)}, u32[]{:S(2)}) %collective-permute-start) | collective-permute-done | bytes 589856 | tf_op jit(solution)/shard_map/ppermute | solution.py:356
  22.0 14.7 %collective-permute-done.1.refs_2_ = bf16[3,256,384]{2,1,0:T(8,128)(2,1)S(1)} collective-permute-done((bf16[3,256,384]{2,1,0:T(8,128)(2,1)}, bf16[3,256,384]{2,1,0:T(8,128)(2,1)S(1)}, u32[]{:S(2)}, u32[]{:S(2)}) %collective-permute-start.1) | collective-permute-done | bytes 589856 | tf_op jit(solution)/shard_map/ppermute | solution.py:356
  36.6 1.0 collective-permute-start.6
  37.6 1.1 collective-permute-start.7
  38.7 4.6 %collective-permute-start.3 = (bf16[192,3072]{1,0:T(8,128)(2,1)}, bf16[192,3072]{1,0:T(8,128)(2,1)}, u32[]{:S(2)}, u32[]{:S(2)}) collective-permute-start(bf16[192,3072]{1,0:T(8,128)(2,1)} %param.9), channel_id=1, source_target_pairs={{0,8},{4,12},{9,17},{13,21},{18,26},{22,30},{27,3},{31,7}} | collective-permute-start | bytes 3538952 | tf_op jit(solution)/shard_map/ppermute | solution.py:356
  43.3 8.2 %collective-permute-done.11.refs_3_.refs_1_ = bf16[256,1536]{1,0:T(8,128)(2,1)S(1)} collective-permute-done((bf16[256,1536]{1,0:T(8,128)(2,1)S(1)}, bf16[256,1536]{1,0:T(8,128)(2,1)S(1)}, u32[]{:S(2)}, u32[]{:S(2)}) %collective-permute-start.11) | collective-permute-done | bytes 786464 | tf_op jit(solution)/shard_map/ppermute | solution.py:356
  51.5 6.1 %collective-permute-start.4 = (bf16[192,3072]{1,0:T(8,128)(2,1)}, bf16[192,3072]{1,0:T(8,128)(2,1)}, u32[]{:S(2)}, u32[]{:S(2)}) collective-permute-start(bf16[192,3072]{1,0:T(8,128)(2,1)} %param.9), channel_id=1, source_target_pairs={{0,16},{4,20},{9,25},{13,29},{18,2},{22,6},{27,11},{31,15}} | collective-permute-start | bytes 3538952 | tf_op jit(solution)/shard_map/ppermute | solution.py:356
  57.6 2.7 %collective-permute-start.5 = (bf16[192,3072]{1,0:T(8,128)(2,1)}, bf16[192,3072]{1,0:T(8,128)(2,1)}, u32[]{:S(2)}, u32[]{:S(2)}) collective-permute-start(bf16[192,3072]{1,0:T(8,128)(2,1)} %param.9), channel_id=1, source_target_pairs={{0,24},{4,28},{9,1},{13,5},{18,10},{22,14},{27,19},{31,23}} | collective-permute-start | bytes 3538952 | tf_op jit(solution)/shard_map/ppermute | solution.py:356
  61.1 6.4 %collective-permute-done.6.refs_1_.refs_8_ = bf16[256,1536]{1,0:T(8,128)(2,1)S(1)} collective-permute-done((bf16[256,1536]{1,0:T(8,128)(2,1)S(1)}, bf16[256,1536]{1,0:T(8,128)(2,1)S(1)}, u32[]{:S(2)}, u32[]{:S(2)}) %collective-permute-start.6) | collective-permute-done | bytes 786464 | tf_op jit(solution)/shard_map/ppermute | solution.py:356
  67.5 1.8 collective-permute-start.13
  70.1 0.9 copy-done.9
  70.9 1.5 collective-permute-start.14
  72.5 12.6 %forward.1 = (bf16[3,1024,1024]{2,1,0:T(8,128)(2,1)}, bf16[384,1024]{1,0:T(8,128)(2,1)}) custom-call(bf16[3,256,384]{2,1,0:T(8,128)(2,1)} %get-tuple-element.53.refs_0_, bf16[3,256,384]{2,1,0:T(8,128)(2,1)} %copy-done.3, bf16[3,256,384]{2,1,0:T(8,128)(2,1)} %copy-done.4, bf16[3,256,384]{2,1,0:T(8,128)(2,1)} %copy-done.5), custom_call_target="tpu_custom_call" | custom-call | flops 3221225472 | bytes 6291456 | tf_op jit(solution)/shard_map/forward/pallas_call | solution.py:154
  85.0 1.0 slice.67
  86.6 1.0 slice.68
  88.1 5.2 %weight_terms.3 = (bf16[4,48,1536]{2,1,0:T(8,128)(2,1)}, bf16[4,48,1536]{2,1,0:T(8,128)(2,1)}) custom-call(s32[3]{0:T(128)} %pad_add_fusion.place_ref, bf16[384,1024]{1,0:T(8,128)(2,1)} %get-tuple-element.58.attended_ref, bf16[256,1536]{1,0:T(8,128)(2,1)} %copy-done.1, bf16[256,1536]{1,0:T(8,128)(2,1)} %copy-done.6, bf16[256,1536]{1,0:T(8,128)(2,1)} %copy-done.7, ...), custom_call_target="tpu_custom_call" | custom-call | flops 1207959552 | bytes 3932160 | tf_op jit(solution)/shard_map/weight_terms/pallas_call | solution.py:294
  93.4 2.3 %collective-permute-done.8.refs_3_.refs_10_ = bf16[128,1536]{1,0:T(8,128)(2,1)S(1)} collective-permute-done((bf16[128,1536]{1,0:T(8,128)(2,1)S(1)}, bf16[128,1536]{1,0:T(8,128)(2,1)S(1)}, u32[]{:S(2)}, u32[]{:S(2)}) %collective-permute-start.8) | collective-permute-done | bytes 393248 | tf_op jit(solution)/shard_map/ppermute | solution.py:356
  95.7 1.4 collective-permute-done.9.refs_4_.refs_11_
  97.9 5.2 %weight_terms.2 = (bf16[4,48,1536]{2,1,0:T(8,128)(2,1)}, bf16[4,48,1536]{2,1,0:T(8,128)(2,1)}) custom-call(s32[3]{0:T(128)} %pad_add_fusion.place_ref, bf16[384,1024]{1,0:T(8,128)(2,1)} %get-tuple-element.58.attended_ref, bf16[256,1536]{1,0:T(8,128)(2,1)} %copy-done.2, bf16[256,1536]{1,0:T(8,128)(2,1)} %copy-done.8, bf16[256,1536]{1,0:T(8,128)(2,1)} %copy-done.9, ...), custom_call_target="tpu_custom_call" | custom-call | flops 1207959552 | bytes 3932160 | tf_op jit(solution)/shard_map/weight_terms/pallas_call | solution.py:294
  103.1 12.0 %collective-permute-done.5 = bf16[192,3072]{1,0:T(8,128)(2,1)} collective-permute-done((bf16[192,3072]{1,0:T(8,128)(2,1)}, bf16[192,3072]{1,0:T(8,128)(2,1)}, u32[]{:S(2)}, u32[]{:S(2)}) %collective-permute-start.5) | collective-permute-done | bytes 1179680 | tf_op jit(solution)/shard_map/ppermute | solution.py:356
  115.1 1.5 select_select_fusion.refs_0_
  116.8 0.9 fusion.3
  117.8 3.5 %collective-permute-start.22 = (bf16[48,1536]{1,0:T(8,128)(2,1)S(1)}, bf16[48,1536]{1,0:T(8,128)(2,1)}, u32[]{:S(2)}, u32[]{:S(2)}) collective-permute-start(bf16[48,1536]{1,0:T(8,128)(2,1)S(1)} %get-tuple-element.108), channel_id=1, source_target_pairs={{0,3},{1,2},{2,1},{3,0},{4,7},{5,6},{6,5},{7,4},{8,11},{9,10},{10,... | collective-permute-start | bytes 442376 | tf_op jit(solution)/shard_map/ppermute | solution.py:356
  121.2 3.4 %collective-permute-done.20 = bf16[48,1536]{1,0:T(8,128)(2,1)S(1)} collective-permute-done((bf16[48,1536]{1,0:T(8,128)(2,1)}, bf16[48,1536]{1,0:T(8,128)(2,1)S(1)}, u32[]{:S(2)}, u32[]{:S(2)}) %collective-permute-start.20) | collective-permute-done | bytes 147488 | tf_op jit(solution)/shard_map/ppermute | solution.py:356
  124.7 2.4 %collective-permute-done.21 = bf16[48,1536]{1,0:T(8,128)(2,1)} collective-permute-done((bf16[48,1536]{1,0:T(8,128)(2,1)S(1)}, bf16[48,1536]{1,0:T(8,128)(2,1)}, u32[]{:S(2)}, u32[]{:S(2)}) %collective-permute-start.21) | collective-permute-done | bytes 147488 | tf_op jit(solution)/shard_map/ppermute | solution.py:356
  127.1 1.1 pad_maximum_fusion
  129.0 5.2 %collective-permute-start.30 = (bf16[48,1536]{1,0:T(8,128)(2,1)}, bf16[48,1536]{1,0:T(8,128)(2,1)}, u32[]{:S(2)}, u32[]{:S(2)}) collective-permute-start(bf16[48,1536]{1,0:T(8,128)(2,1)} %get-tuple-element.117), channel_id=1, source_target_pairs={{0,16},{1,17},{2,18},{3,19},{4,20},{5,21},{6,22},{7,23},{8,24},{9,... | collective-permute-start | bytes 442376 | tf_op jit(solution)/shard_map/ppermute | solution.py:356
  134.2 1.4 collective-permute-start.31
  135.6 0.9 fusion.7
  136.4 1.7 collective-permute-start.23
  139.2 7.9 %project.1.refs_5_ = bf16[384,1024]{1,0:T(8,128)(2,1)} custom-call(s32[3]{0:T(128)} %pad_add_fusion.place_ref, bf16[192,3072]{1,0:T(8,128)(2,1)} %copy-done, bf16[192,3072]{1,0:T(8,128)(2,1)} %copy-done.10, bf16[256,1536]{1,0:T(8,128)(2,1)} %copy-done.1, bf16[256,1536]{1,0:T(8,128)(2,1)} %copy-done.6, bf16[256,1536]{1,0:T(8,128)(2,1)} %copy-done.7, ...), custom_call_target="tpu_custom_call" | custom-call | flops 2415919104 | bytes 8650752 | tf_op jit(solution)/shard_map/project/pallas_call | solution.py:258
  147.1 5.6 %backward.2 = (bf16[3,256,128]{2,1,0:T(8,128)(2,1)}, bf16[3,256,128]{2,1,0:T(8,128)(2,1)}, bf16[3,256,128]{2,1,0:T(8,128)(2,1)}, bf16[3,256,128]{2,1,0:T(8,128)(2,1)}) custom-call(bf16[3,256,384]{2,1,0:T(8,128)(2,1)} %get-tuple-element.53.refs_0_, bf16[3,256,384]{2,1,0:T(8,128)(2,1)} %copy-done.3, bf16[3,256,384]{2,1,0:T(8,128)(2,1)} %copy-done.4, ...), custom_call_target="tpu_custom_call" | custom-call | flops 1073741824 | bytes 2097152 | tf_op jit(solution)/shard_map/backward/pallas_call | solution.py:203
  152.8 1.5 collective-permute-start.25
  154.3 1.1 add_convert_fusion.1.refs_0_
  155.4 0.9 collective-permute-start.32
  156.3 1.1 collective-permute-start.33
  157.5 2.0 collective-permute-done.25
  159.6 0.9 collective-permute-start.35
  160.7 2.9 %collective-permute-start.37 = (bf16[48,1536]{1,0:T(8,128)(2,1)S(1)}, bf16[48,1536]{1,0:T(8,128)(2,1)S(1)}, u32[]{:S(2)}, u32[]{:S(2)}) collective-permute-start(bf16[48,1536]{1,0:T(8,128)(2,1)S(1)} %get-tuple-element.112), channel_id=1, source_target_pairs={{0,24},{1,25},{2,26},{3,27},{4,28},{5,29},{6,30},{7,31},{8,0},{9,1... | collective-permute-start | bytes 442376 | tf_op jit(solution)/shard_map/ppermute | solution.py:356
  163.7 8.5 %backward.3 = (bf16[3,256,256]{2,1,0:T(8,128)(2,1)}, bf16[3,256,256]{2,1,0:T(8,128)(2,1)}, bf16[3,256,256]{2,1,0:T(8,128)(2,1)}, bf16[3,256,256]{2,1,0:T(8,128)(2,1)}) custom-call(bf16[3,256,384]{2,1,0:T(8,128)(2,1)} %get-tuple-element.53.refs_0_, bf16[3,256,384]{2,1,0:T(8,128)(2,1)} %copy-done.3, bf16[3,256,384]{2,1,0:T(8,128)(2,1)} %copy-done.4, ...), custom_call_target="tpu_custom_call" | custom-call | flops 2147483648 | bytes 4194304 | tf_op jit(solution)/shard_map/backward/pallas_call | solution.py:203
  172.2 1.5 collective-permute-start.34
  173.8 1.2 collective-permute-start.15
  175.0 0.9 collective-permute-start.38
  175.9 1.2 collective-permute-start.26
  177.1 0.8 collective-permute-start.27
  178.0 1.9 collective-permute-done.34.refs_3_
  179.9 1.5 collective-permute-start.28
  181.4 2.5 %collective-permute-done.15.refs_1_ = bf16[3,256,128]{2,1,0:T(8,128)(2,1)S(1)} collective-permute-done((bf16[3,256,128]{2,1,0:T(8,128)(2,1)}, bf16[3,256,128]{2,1,0:T(8,128)(2,1)S(1)}, u32[]{:S(2)}, u32[]{:S(2)}) %collective-permute-start.15) | collective-permute-done | bytes 196640 | tf_op jit(solution)/shard_map/ppermute | solution.py:356
  183.8 0.8 collective-permute-start.39
  184.7 2.3 %collective-permute-done.38.refs_5_ = bf16[48,1536]{1,0:T(8,128)(2,1)S(1)} collective-permute-done((bf16[48,1536]{1,0:T(8,128)(2,1)S(1)}, bf16[48,1536]{1,0:T(8,128)(2,1)S(1)}, u32[]{:S(2)}, u32[]{:S(2)}) %collective-permute-start.38) | collective-permute-done | bytes 147488 | tf_op jit(solution)/shard_map/ppermute | solution.py:356
  187.0 1.7 collective-permute-start.40
  188.7 4.7 %collective-permute-done.39.refs_6_ = bf16[48,1536]{1,0:T(8,128)(2,1)S(1)} collective-permute-done((bf16[48,1536]{1,0:T(8,128)(2,1)S(1)}, bf16[48,1536]{1,0:T(8,128)(2,1)S(1)}, u32[]{:S(2)}, u32[]{:S(2)}) %collective-permute-start.39) | collective-permute-done | bytes 147488 | tf_op jit(solution)/shard_map/ppermute | solution.py:356
  193.4 2.6 %collective-permute-start.16 = (bf16[3,256,128]{2,1,0:T(8,128)(2,1)S(1)}, bf16[3,256,128]{2,1,0:T(8,128)(2,1)S(1)}, u32[]{:S(2)}, u32[]{:S(2)}) collective-permute-start(bf16[3,256,128]{2,1,0:T(8,128)(2,1)S(1)} %copy-done.30), channel_id=1, source_target_pairs={{0,2},{1,3},{2,0},{3,1},{4,6},{5,7},{6,4},{7,5},{8,10},{9,11},{10,... | collective-permute-start | bytes 589832 | tf_op jit(solution)/shard_map/ppermute | solution.py:356
  196.0 7.8 %collective-permute-done.40.refs_7_ = bf16[48,1536]{1,0:T(8,128)(2,1)S(1)} collective-permute-done((bf16[48,1536]{1,0:T(8,128)(2,1)S(1)}, bf16[48,1536]{1,0:T(8,128)(2,1)S(1)}, u32[]{:S(2)}, u32[]{:S(2)}) %collective-permute-start.40) | collective-permute-done | bytes 147488 | tf_op jit(solution)/shard_map/ppermute | solution.py:356
  203.8 1.5 collective-permute-start.17
  205.3 3.6 %assemble.1 = f32[192,3072]{1,0:T(8,128)} custom-call(s32[3]{0:T(128)} %pad_add_fusion.place_ref, bf16[48,1536]{1,0:T(8,128)(2,1)} %copy-done.13, bf16[48,1536]{1,0:T(8,128)(2,1)} %copy-done.23, bf16[48,1536]{1,0:T(8,128)(2,1)} %copy-done.24, bf16[48,1536]{1,0:T(8,128)(2,1)} %copy-done.25, bf16[48,1536]{1,0:T(8,128)(2,1)} %copy-done.14, ...), custom_call_target="tpu_custom_call" | custom-call | bytes 3538944 | tf_op jit(solution)/shard_map/assemble/pallas_call | solution.py:323
  208.9 1.5 collective-permute-done.17.refs_3_
  212.1 3.5 %unpack.1 = (bf16[1,256,1536]{2,1,0:T(8,128)(2,1)}, bf16[1,256,1536]{2,1,0:T(8,128)(2,1)}, bf16[1,256,1536]{2,1,0:T(8,128)(2,1)}) custom-call(s32[3]{0:T(128)} %pad_add_fusion.place_ref, bf16[3,256,128]{2,1,0:T(8,128)(2,1)} %get-tuple-element.69.refs_0_, bf16[3,256,128]{2,1,0:T(8,128)(2,1)} %copy-done.20, bf16[3,256,128]{2,1,0:T(8,128)(2,1)} %copy-done.21, ...), custom_call_target="tpu_custom_call" | custom-call | bytes 4718592 | tf_op jit(solution)/shard_map/unpack/pallas_call | solution.py:115
  (104 shorter events, 8.3 us)
Async XLA Ops:
  4.5 17.4 %collective-permute-start = (bf16[3,256,384]{2,1,0:T(8,128)(2,1)}, bf16[3,256,384]{2,1,0:T(8,128)(2,1)S(1)}, u32[]{:S(2)}, u32[]{:S(2)}) collective-permute-start(bf16[3,256,384]{2,1,0:T(8,128)(2,1)} %get-tuple-element.54), channel_id=1, source_target_pairs={{0,1},{1,0},{2,3},{3,2},{4,5},{5,4},{6,7},{7,6},{8,9},{9,8},{10,11... | collective-permute-start | bytes 1769480 | tf_op jit(solution)/shard_map/ppermute | solution.py:356
  7.6 29.0 %collective-permute-start.1 = (bf16[3,256,384]{2,1,0:T(8,128)(2,1)}, bf16[3,256,384]{2,1,0:T(8,128)(2,1)S(1)}, u32[]{:S(2)}, u32[]{:S(2)}) collective-permute-start(bf16[3,256,384]{2,1,0:T(8,128)(2,1)} %get-tuple-element.55), channel_id=1, source_target_pairs={{0,2},{1,3},{2,0},{3,1},{4,6},{5,7},{6,4},{7,5},{8,10},{9,11},{10,... | collective-permute-start | bytes 1769480 | tf_op jit(solution)/shard_map/ppermute | solution.py:356
  9.1 27.5 %collective-permute-start.2 = (bf16[3,256,384]{2,1,0:T(8,128)(2,1)}, bf16[3,256,384]{2,1,0:T(8,128)(2,1)S(1)}, u32[]{:S(2)}, u32[]{:S(2)}) collective-permute-start(bf16[3,256,384]{2,1,0:T(8,128)(2,1)} %get-tuple-element.56), channel_id=1, source_target_pairs={{0,3},{1,2},{2,1},{3,0},{4,7},{5,6},{6,5},{7,4},{8,11},{9,10},{10,... | collective-permute-start | bytes 1769480 | tf_op jit(solution)/shard_map/ppermute | solution.py:356
  10.6 74.4 %copy-start.1 = (bf16[256,1536]{1,0:T(8,128)(2,1)}, bf16[256,1536]{1,0:T(8,128)(2,1)S(1)}, u32[]{:S(2)}) copy-start(bf16[256,1536]{1,0:T(8,128)(2,1)S(1)} %get-tuple-element.102.refs_2_.refs_0_) | copy-start | bytes 2359300
  10.6 74.4 %copy-start.2 = (bf16[256,1536]{1,0:T(8,128)(2,1)}, bf16[256,1536]{1,0:T(8,128)(2,1)S(1)}, u32[]{:S(2)}) copy-start(bf16[256,1536]{1,0:T(8,128)(2,1)S(1)} %get-tuple-element.59.refs_0_.refs_7_) | copy-start | bytes 2359300
  10.6 40.9 %collective-permute-start.11 = (bf16[256,1536]{1,0:T(8,128)(2,1)S(1)}, bf16[256,1536]{1,0:T(8,128)(2,1)S(1)}, u32[]{:S(2)}, u32[]{:S(2)}) collective-permute-start(bf16[256,1536]{1,0:T(8,128)(2,1)S(1)} %get-tuple-element.102.refs_2_.refs_0_), channel_id=1, source_target_pairs={{0,1},{1,0},{2,3},{3,2},{4,5},{5,4},{6,7},{7,6},{8,9},{9,8},{10,11... | collective-permute-start | bytes 2359304 | tf_op jit(solution)/shard_map/ppermute | solution.py:356
  12.6 45.0 %collective-permute-start.12 = (bf16[256,1536]{1,0:T(8,128)(2,1)S(1)}, bf16[256,1536]{1,0:T(8,128)(2,1)S(1)}, u32[]{:S(2)}, u32[]{:S(2)}) collective-permute-start(bf16[256,1536]{1,0:T(8,128)(2,1)S(1)} %get-tuple-element.102.refs_2_.refs_0_), channel_id=1, source_target_pairs={{0,2},{1,3},{2,0},{3,1},{4,6},{5,7},{6,4},{7,5},{8,10},{9,11},{10,... | collective-permute-start | bytes 2359304 | tf_op jit(solution)/shard_map/ppermute | solution.py:356
  22.0 50.5 %copy-start.3 = (bf16[3,256,384]{2,1,0:T(8,128)(2,1)}, bf16[3,256,384]{2,1,0:T(8,128)(2,1)S(1)}, u32[]{:S(2)}) copy-start(bf16[3,256,384]{2,1,0:T(8,128)(2,1)S(1)} %collective-permute-done.refs_1_) | copy-start | bytes 1769476
  36.6 35.8 %copy-start.4 = (bf16[3,256,384]{2,1,0:T(8,128)(2,1)}, bf16[3,256,384]{2,1,0:T(8,128)(2,1)S(1)}, u32[]{:S(2)}) copy-start(bf16[3,256,384]{2,1,0:T(8,128)(2,1)S(1)} %collective-permute-done.1.refs_2_) | copy-start | bytes 1769476
  36.6 35.8 %copy-start.5 = (bf16[3,256,384]{2,1,0:T(8,128)(2,1)}, bf16[3,256,384]{2,1,0:T(8,128)(2,1)S(1)}, u32[]{:S(2)}) copy-start(bf16[3,256,384]{2,1,0:T(8,128)(2,1)S(1)} %collective-permute-done.2.refs_3_) | copy-start | bytes 1769476
  36.6 30.9 %collective-permute-start.6 = (bf16[256,1536]{1,0:T(8,128)(2,1)S(1)}, bf16[256,1536]{1,0:T(8,128)(2,1)S(1)}, u32[]{:S(2)}, u32[]{:S(2)}) collective-permute-start(bf16[256,1536]{1,0:T(8,128)(2,1)S(1)} %get-tuple-element.59.refs_0_.refs_7_), channel_id=1, source_target_pairs={{0,1},{1,0},{2,3},{3,2},{4,5},{5,4},{6,7},{7,6},{8,9},{9,8},{10,11... | collective-permute-start | bytes 2359304 | tf_op jit(solution)/shard_map/ppermute | solution.py:356
  37.6 32.4 %collective-permute-start.7 = (bf16[256,1536]{1,0:T(8,128)(2,1)S(1)}, bf16[256,1536]{1,0:T(8,128)(2,1)S(1)}, u32[]{:S(2)}, u32[]{:S(2)}) collective-permute-start(bf16[256,1536]{1,0:T(8,128)(2,1)S(1)} %get-tuple-element.59.refs_0_.refs_7_), channel_id=1, source_target_pairs={{0,2},{1,3},{2,0},{3,1},{4,6},{5,7},{6,4},{7,5},{8,10},{9,11},{10,... | collective-permute-start | bytes 2359304 | tf_op jit(solution)/shard_map/ppermute | solution.py:356
  38.7 64.4 %collective-permute-start.3 = (bf16[192,3072]{1,0:T(8,128)(2,1)}, bf16[192,3072]{1,0:T(8,128)(2,1)}, u32[]{:S(2)}, u32[]{:S(2)}) collective-permute-start(bf16[192,3072]{1,0:T(8,128)(2,1)} %param.9), channel_id=1, source_target_pairs={{0,8},{4,12},{9,17},{13,21},{18,26},{22,30},{27,3},{31,7}} | collective-permute-start | bytes 3538952 | tf_op jit(solution)/shard_map/ppermute | solution.py:356
  51.5 18.6 %copy-start.6 = (bf16[256,1536]{1,0:T(8,128)(2,1)}, bf16[256,1536]{1,0:T(8,128)(2,1)S(1)}, u32[]{:S(2)}) copy-start(bf16[256,1536]{1,0:T(8,128)(2,1)S(1)} %collective-permute-done.11.refs_3_.refs_1_) | copy-start | bytes 2359300
  51.5 51.6 %collective-permute-start.4 = (bf16[192,3072]{1,0:T(8,128)(2,1)}, bf16[192,3072]{1,0:T(8,128)(2,1)}, u32[]{:S(2)}, u32[]{:S(2)}) collective-permute-start(bf16[192,3072]{1,0:T(8,128)(2,1)} %param.9), channel_id=1, source_target_pairs={{0,16},{4,20},{9,25},{13,29},{18,2},{22,6},{27,11},{31,15}} | collective-permute-start | bytes 3538952 | tf_op jit(solution)/shard_map/ppermute | solution.py:356
  57.6 12.4 %copy-start.7 = (bf16[256,1536]{1,0:T(8,128)(2,1)}, bf16[256,1536]{1,0:T(8,128)(2,1)S(1)}, u32[]{:S(2)}) copy-start(bf16[256,1536]{1,0:T(8,128)(2,1)S(1)} %collective-permute-done.12.refs_4_.refs_2_) | copy-start | bytes 2359300
  57.6 57.5 %collective-permute-start.5 = (bf16[192,3072]{1,0:T(8,128)(2,1)}, bf16[192,3072]{1,0:T(8,128)(2,1)}, u32[]{:S(2)}, u32[]{:S(2)}) collective-permute-start(bf16[192,3072]{1,0:T(8,128)(2,1)} %param.9), channel_id=1, source_target_pairs={{0,24},{4,28},{9,1},{13,5},{18,10},{22,14},{27,19},{31,23}} | collective-permute-start | bytes 3538952 | tf_op jit(solution)/shard_map/ppermute | solution.py:356
  67.5 2.6 %copy-start.8 = (bf16[256,1536]{1,0:T(8,128)(2,1)}, bf16[256,1536]{1,0:T(8,128)(2,1)S(1)}, u32[]{:S(2)}) copy-start(bf16[256,1536]{1,0:T(8,128)(2,1)S(1)} %collective-permute-done.6.refs_1_.refs_8_) | copy-start | bytes 2359300
  67.5 18.6 %collective-permute-start.13 = (bf16[128,1536]{1,0:T(8,128)(2,1)}, bf16[128,1536]{1,0:T(8,128)(2,1)}, u32[]{:S(2)}, u32[]{:S(2)}) collective-permute-start(bf16[128,1536]{1,0:T(8,128)(2,1)} %slice.70), channel_id=1, source_target_pairs={{0,2},{1,3},{2,0},{3,1},{4,6},{5,7},{6,4},{7,5},{8,10},{9,11},{10,... | collective-permute-start | bytes 1179656 | tf_op jit(solution)/shard_map/ppermute | solution.py:356
  70.9 16.7 %collective-permute-start.14 = (bf16[128,1536]{1,0:T(8,128)(2,1)}, bf16[128,1536]{1,0:T(8,128)(2,1)}, u32[]{:S(2)}, u32[]{:S(2)}) collective-permute-start(bf16[128,1536]{1,0:T(8,128)(2,1)} %slice.71), channel_id=1, source_target_pairs={{0,1},{1,0},{2,3},{3,2},{4,5},{5,4},{6,7},{7,6},{8,9},{9,8},{10,11... | collective-permute-start | bytes 1179656 | tf_op jit(solution)/shard_map/ppermute | solution.py:356
  86.1 9.6 %collective-permute-start.8 = (bf16[128,1536]{1,0:T(8,128)(2,1)S(1)}, bf16[128,1536]{1,0:T(8,128)(2,1)S(1)}, u32[]{:S(2)}, u32[]{:S(2)}) collective-permute-start(bf16[128,1536]{1,0:T(8,128)(2,1)S(1)} %slice.67), channel_id=1, source_target_pairs={{0,2},{1,3},{2,0},{3,1},{4,6},{5,7},{6,4},{7,5},{8,10},{9,11},{10,... | collective-permute-start | bytes 1179656 | tf_op jit(solution)/shard_map/ppermute | solution.py:356
  87.7 9.4 %collective-permute-start.9 = (bf16[128,1536]{1,0:T(8,128)(2,1)S(1)}, bf16[128,1536]{1,0:T(8,128)(2,1)S(1)}, u32[]{:S(2)}, u32[]{:S(2)}) collective-permute-start(bf16[128,1536]{1,0:T(8,128)(2,1)S(1)} %slice.68), channel_id=1, source_target_pairs={{0,1},{1,0},{2,3},{3,2},{4,5},{5,4},{6,7},{7,6},{8,9},{9,8},{10,11... | collective-permute-start | bytes 1179656 | tf_op jit(solution)/shard_map/ppermute | solution.py:356
  95.7 21.1 %collective-permute-start.19 = (bf16[4,48,1536]{2,1,0:T(8,128)(2,1)}, bf16[4,48,1536]{2,1,0:T(8,128)(2,1)S(1)}, u32[]{:S(2)}, u32[]{:S(2)}) collective-permute-start(bf16[4,48,1536]{2,1,0:T(8,128)(2,1)} %get-tuple-element.75), channel_id=1, source_target_pairs={{0,4},{1,5},{2,6},{3,7},{4,0},{5,1},{6,2},{7,3},{8,12},{9,13},{10,... | collective-permute-start | bytes 1769480 | tf_op jit(solution)/shard_map/ppermute | solution.py:356
  115.1 1.7 copy-start.12
  116.7 11.6 %copy-start = (bf16[192,3072]{1,0:T(8,128)(2,1)}, bf16[192,3072]{1,0:T(8,128)(2,1)S(1)}, u32[]{:S(2)}) copy-start(bf16[192,3072]{1,0:T(8,128)(2,1)S(1)} %select_select_fusion.refs_0_) | copy-start | bytes 3538948
  116.7 21.4 %collective-permute-start.10 = (bf16[192,3072]{1,0:T(8,128)(2,1)S(1)}, bf16[192,3072]{1,0:T(8,128)(2,1)S(1)}, u32[]{:S(2)}, u32[]{:S(2)}) collective-permute-start(bf16[192,3072]{1,0:T(8,128)(2,1)S(1)} %select_select_fusion.refs_0_), channel_id=1, source_target_pairs={{0,4},{1,5},{2,6},{3,7},{4,0},{5,1},{6,2},{7,3},{8,12},{9,13},{10,... | collective-permute-start | bytes 3538952 | tf_op jit(solution)/shard_map/ppermute | solution.py:356
  117.7 6.9 %collective-permute-start.20 = (bf16[48,1536]{1,0:T(8,128)(2,1)}, bf16[48,1536]{1,0:T(8,128)(2,1)S(1)}, u32[]{:S(2)}, u32[]{:S(2)}) collective-permute-start(bf16[48,1536]{1,0:T(8,128)(2,1)} %get-tuple-element.110), channel_id=1, source_target_pairs={{0,1},{1,0},{2,3},{3,2},{4,5},{5,4},{6,7},{7,6},{8,9},{9,8},{10,11... | collective-permute-start | bytes 442376 | tf_op jit(solution)/shard_map/ppermute | solution.py:356
  117.7 9.4 %collective-permute-start.21 = (bf16[48,1536]{1,0:T(8,128)(2,1)S(1)}, bf16[48,1536]{1,0:T(8,128)(2,1)}, u32[]{:S(2)}, u32[]{:S(2)}) collective-permute-start(bf16[48,1536]{1,0:T(8,128)(2,1)S(1)} %get-tuple-element.109), channel_id=1, source_target_pairs={{0,2},{1,3},{2,0},{3,1},{4,6},{5,7},{6,4},{7,5},{8,10},{9,11},{10,... | collective-permute-start | bytes 442376 | tf_op jit(solution)/shard_map/ppermute | solution.py:356
  117.8 9.4 %collective-permute-start.22 = (bf16[48,1536]{1,0:T(8,128)(2,1)S(1)}, bf16[48,1536]{1,0:T(8,128)(2,1)}, u32[]{:S(2)}, u32[]{:S(2)}) collective-permute-start(bf16[48,1536]{1,0:T(8,128)(2,1)S(1)} %get-tuple-element.108), channel_id=1, source_target_pairs={{0,3},{1,2},{2,1},{3,0},{4,7},{5,6},{6,5},{7,4},{8,11},{9,10},{10,... | collective-permute-start | bytes 442376 | tf_op jit(solution)/shard_map/ppermute | solution.py:356
  121.2 14.3 %collective-permute-start.18 = (bf16[4,48,1536]{2,1,0:T(8,128)(2,1)}, bf16[4,48,1536]{2,1,0:T(8,128)(2,1)S(1)}, u32[]{:S(2)}, u32[]{:S(2)}) collective-permute-start(bf16[4,48,1536]{2,1,0:T(8,128)(2,1)} %get-tuple-element.73), channel_id=1, source_target_pairs={{0,4},{1,5},{2,6},{3,7},{4,0},{5,1},{6,2},{7,3},{8,12},{9,13},{10,... | collective-permute-start | bytes 1769480 | tf_op jit(solution)/shard_map/ppermute | solution.py:356
  127.1 8.5 %copy-start.11 = (bf16[4,48,1536]{2,1,0:T(8,128)(2,1)S(1)}, bf16[4,48,1536]{2,1,0:T(8,128)(2,1)}, u32[]{:S(2)}) copy-start(bf16[4,48,1536]{2,1,0:T(8,128)(2,1)} %get-tuple-element.80) | copy-start | bytes 1769476
  129.0 23.7 %collective-permute-start.29 = (bf16[48,1536]{1,0:T(8,128)(2,1)}, bf16[48,1536]{1,0:T(8,128)(2,1)}, u32[]{:S(2)}, u32[]{:S(2)}) collective-permute-start(bf16[48,1536]{1,0:T(8,128)(2,1)} %get-tuple-element.118), channel_id=1, source_target_pairs={{0,8},{1,9},{2,10},{3,11},{4,12},{5,13},{6,14},{7,15},{8,16},{9,17... | collective-permute-start | bytes 442376 | tf_op jit(solution)/shard_map/ppermute | solution.py:356
  129.0 25.3 %collective-permute-start.30 = (bf16[48,1536]{1,0:T(8,128)(2,1)}, bf16[48,1536]{1,0:T(8,128)(2,1)}, u32[]{:S(2)}, u32[]{:S(2)}) collective-permute-start(bf16[48,1536]{1,0:T(8,128)(2,1)} %get-tuple-element.117), channel_id=1, source_target_pairs={{0,16},{1,17},{2,18},{3,19},{4,20},{5,21},{6,22},{7,23},{8,24},{9,... | collective-permute-start | bytes 442376 | tf_op jit(solution)/shard_map/ppermute | solution.py:356
  134.2 20.1 %collective-permute-start.31 = (bf16[48,1536]{1,0:T(8,128)(2,1)S(1)}, bf16[48,1536]{1,0:T(8,128)(2,1)}, u32[]{:S(2)}, u32[]{:S(2)}) collective-permute-start(bf16[48,1536]{1,0:T(8,128)(2,1)S(1)} %get-tuple-element.116), channel_id=1, source_target_pairs={{0,24},{1,25},{2,26},{3,27},{4,28},{5,29},{6,30},{7,31},{8,0},{9,1... | collective-permute-start | bytes 442376 | tf_op jit(solution)/shard_map/ppermute | solution.py:356
  136.4 21.0 %collective-permute-start.23 = (bf16[48,1536]{1,0:T(8,128)(2,1)}, bf16[48,1536]{1,0:T(8,128)(2,1)S(1)}, u32[]{:S(2)}, u32[]{:S(2)}) collective-permute-start(bf16[48,1536]{1,0:T(8,128)(2,1)} %get-tuple-element.106), channel_id=1, source_target_pairs={{0,1},{1,0},{2,3},{3,2},{4,5},{5,4},{6,7},{7,6},{8,9},{9,8},{10,11... | collective-permute-start | bytes 442376 | tf_op jit(solution)/shard_map/ppermute | solution.py:356
  138.1 19.3 %collective-permute-start.24 = (bf16[48,1536]{1,0:T(8,128)(2,1)}, bf16[48,1536]{1,0:T(8,128)(2,1)S(1)}, u32[]{:S(2)}, u32[]{:S(2)}) collective-permute-start(bf16[48,1536]{1,0:T(8,128)(2,1)} %get-tuple-element.105), channel_id=1, source_target_pairs={{0,2},{1,3},{2,0},{3,1},{4,6},{5,7},{6,4},{7,5},{8,10},{9,11},{10,... | collective-permute-start | bytes 442376 | tf_op jit(solution)/shard_map/ppermute | solution.py:356
  152.8 6.7 %collective-permute-start.25 = (bf16[48,1536]{1,0:T(8,128)(2,1)S(1)}, bf16[48,1536]{1,0:T(8,128)(2,1)S(1)}, u32[]{:S(2)}, u32[]{:S(2)}) collective-permute-start(bf16[48,1536]{1,0:T(8,128)(2,1)S(1)} %get-tuple-element.104), channel_id=1, source_target_pairs={{0,3},{1,2},{2,1},{3,0},{4,7},{5,6},{6,5},{7,4},{8,11},{9,10},{10,... | collective-permute-start | bytes 442376 | tf_op jit(solution)/shard_map/ppermute | solution.py:356
  155.4 16.8 %copy-start.13 = (bf16[48,1536]{1,0:T(8,128)(2,1)}, bf16[48,1536]{1,0:T(8,128)(2,1)S(1)}, u32[]{:S(2)}) copy-start(bf16[48,1536]{1,0:T(8,128)(2,1)S(1)} %add_convert_fusion.1.refs_0_) | copy-start | bytes 442372
  155.4 20.5 %collective-permute-start.32 = (bf16[48,1536]{1,0:T(8,128)(2,1)S(1)}, bf16[48,1536]{1,0:T(8,128)(2,1)S(1)}, u32[]{:S(2)}, u32[]{:S(2)}) collective-permute-start(bf16[48,1536]{1,0:T(8,128)(2,1)S(1)} %add_convert_fusion.1.refs_0_), channel_id=1, source_target_pairs={{0,1},{1,0},{2,3},{3,2},{4,5},{5,4},{6,7},{7,6},{8,9},{9,8},{10,11... | collective-permute-start | bytes 442376 | tf_op jit(solution)/shard_map/ppermute | solution.py:356
  156.3 20.8 %collective-permute-start.33 = (bf16[48,1536]{1,0:T(8,128)(2,1)S(1)}, bf16[48,1536]{1,0:T(8,128)(2,1)S(1)}, u32[]{:S(2)}, u32[]{:S(2)}) collective-permute-start(bf16[48,1536]{1,0:T(8,128)(2,1)S(1)} %add_convert_fusion.1.refs_0_), channel_id=1, source_target_pairs={{0,2},{1,3},{2,0},{3,1},{4,6},{5,7},{6,4},{7,5},{8,10},{9,11},{10,... | collective-permute-start | bytes 442376 | tf_op jit(solution)/shard_map/ppermute | solution.py:356
  159.6 12.6 %collective-permute-start.35 = (bf16[48,1536]{1,0:T(8,128)(2,1)S(1)}, bf16[48,1536]{1,0:T(8,128)(2,1)S(1)}, u32[]{:S(2)}, u32[]{:S(2)}) collective-permute-start(bf16[48,1536]{1,0:T(8,128)(2,1)S(1)} %get-tuple-element.114), channel_id=1, source_target_pairs={{0,8},{1,9},{2,10},{3,11},{4,12},{5,13},{6,14},{7,15},{8,16},{9,17... | collective-permute-start | bytes 442376 | tf_op jit(solution)/shard_map/ppermute | solution.py:356
  160.5 13.3 %collective-permute-start.36 = (bf16[48,1536]{1,0:T(8,128)(2,1)S(1)}, bf16[48,1536]{1,0:T(8,128)(2,1)S(1)}, u32[]{:S(2)}, u32[]{:S(2)}) collective-permute-start(bf16[48,1536]{1,0:T(8,128)(2,1)S(1)} %get-tuple-element.113), channel_id=1, source_target_pairs={{0,16},{1,17},{2,18},{3,19},{4,20},{5,21},{6,22},{7,23},{8,24},{9,... | collective-permute-start | bytes 442376 | tf_op jit(solution)/shard_map/ppermute | solution.py:356
  160.7 32.6 %copy-start.30 = (bf16[3,256,128]{2,1,0:T(8,128)(2,1)S(1)}, bf16[3,256,128]{2,1,0:T(8,128)(2,1)}, u32[]{:S(2)}) copy-start(bf16[3,256,128]{2,1,0:T(8,128)(2,1)} %get-tuple-element.71) | copy-start | bytes 589828
  160.7 43.1 %copy-start.29 = (bf16[3,256,128]{2,1,0:T(8,128)(2,1)S(1)}, bf16[3,256,128]{2,1,0:T(8,128)(2,1)}, u32[]{:S(2)}) copy-start(bf16[3,256,128]{2,1,0:T(8,128)(2,1)} %get-tuple-element.72) | copy-start | bytes 589828
  160.7 14.2 %collective-permute-start.37 = (bf16[48,1536]{1,0:T(8,128)(2,1)S(1)}, bf16[48,1536]{1,0:T(8,128)(2,1)S(1)}, u32[]{:S(2)}, u32[]{:S(2)}) collective-permute-start(bf16[48,1536]{1,0:T(8,128)(2,1)S(1)} %get-tuple-element.112), channel_id=1, source_target_pairs={{0,24},{1,25},{2,26},{3,27},{4,28},{5,29},{6,30},{7,31},{8,0},{9,1... | collective-permute-start | bytes 442376 | tf_op jit(solution)/shard_map/ppermute | solution.py:356
  172.2 7.7 %collective-permute-start.34 = (bf16[48,1536]{1,0:T(8,128)(2,1)S(1)}, bf16[48,1536]{1,0:T(8,128)(2,1)S(1)}, u32[]{:S(2)}, u32[]{:S(2)}) collective-permute-start(bf16[48,1536]{1,0:T(8,128)(2,1)S(1)} %add_convert_fusion.1.refs_0_), channel_id=1, source_target_pairs={{0,3},{1,2},{2,1},{3,0},{4,7},{5,6},{6,5},{7,4},{8,11},{9,10},{10,... | collective-permute-start | bytes 442376 | tf_op jit(solution)/shard_map/ppermute | solution.py:356
  173.8 10.1 %collective-permute-start.15 = (bf16[3,256,128]{2,1,0:T(8,128)(2,1)}, bf16[3,256,128]{2,1,0:T(8,128)(2,1)S(1)}, u32[]{:S(2)}, u32[]{:S(2)}) collective-permute-start(bf16[3,256,128]{2,1,0:T(8,128)(2,1)} %get-tuple-element.70), channel_id=1, source_target_pairs={{0,1},{1,0},{2,3},{3,2},{4,5},{5,4},{6,7},{7,6},{8,9},{9,8},{10,11... | collective-permute-start | bytes 589832 | tf_op jit(solution)/shard_map/ppermute | solution.py:356
  175.0 30.3 %copy-start.14 = (bf16[48,1536]{1,0:T(8,128)(2,1)}, bf16[48,1536]{1,0:T(8,128)(2,1)S(1)}, u32[]{:S(2)}) copy-start(bf16[48,1536]{1,0:T(8,128)(2,1)S(1)} %add_convert_fusion.refs_4_) | copy-start | bytes 442372
  175.0 12.0 %collective-permute-start.38 = (bf16[48,1536]{1,0:T(8,128)(2,1)S(1)}, bf16[48,1536]{1,0:T(8,128)(2,1)S(1)}, u32[]{:S(2)}, u32[]{:S(2)}) collective-permute-start(bf16[48,1536]{1,0:T(8,128)(2,1)S(1)} %add_convert_fusion.refs_4_), channel_id=1, source_target_pairs={{0,1},{1,0},{2,3},{3,2},{4,5},{5,4},{6,7},{7,6},{8,9},{9,8},{10,11... | collective-permute-start | bytes 442376 | tf_op jit(solution)/shard_map/ppermute | solution.py:356
  175.9 29.4 %copy-start.23 = (bf16[48,1536]{1,0:T(8,128)(2,1)}, bf16[48,1536]{1,0:T(8,128)(2,1)S(1)}, u32[]{:S(2)}) copy-start(bf16[48,1536]{1,0:T(8,128)(2,1)S(1)} %collective-permute-done.32.refs_1_) | copy-start | bytes 442372
  175.9 34.4 %collective-permute-start.26 = (bf16[3,256,256]{2,1,0:T(8,128)(2,1)}, bf16[3,256,256]{2,1,0:T(8,128)(2,1)S(1)}, u32[]{:S(2)}, u32[]{:S(2)}) collective-permute-start(bf16[3,256,256]{2,1,0:T(8,128)(2,1)} %get-tuple-element.88), channel_id=1, source_target_pairs={{0,1},{1,0},{2,3},{3,2},{4,5},{5,4},{6,7},{7,6},{8,9},{9,8},{10,11... | collective-permute-start | bytes 1179656 | tf_op jit(solution)/shard_map/ppermute | solution.py:356
  177.1 28.2 %copy-start.24 = (bf16[48,1536]{1,0:T(8,128)(2,1)}, bf16[48,1536]{1,0:T(8,128)(2,1)S(1)}, u32[]{:S(2)}) copy-start(bf16[48,1536]{1,0:T(8,128)(2,1)S(1)} %collective-permute-done.33.refs_2_) | copy-start | bytes 442372
  177.1 33.3 %collective-permute-start.27 = (bf16[3,256,256]{2,1,0:T(8,128)(2,1)}, bf16[3,256,256]{2,1,0:T(8,128)(2,1)S(1)}, u32[]{:S(2)}, u32[]{:S(2)}) collective-permute-start(bf16[3,256,256]{2,1,0:T(8,128)(2,1)} %get-tuple-element.89), channel_id=1, source_target_pairs={{0,2},{1,3},{2,0},{3,1},{4,6},{5,7},{6,4},{7,5},{8,10},{9,11},{10,... | collective-permute-start | bytes 1179656 | tf_op jit(solution)/shard_map/ppermute | solution.py:356
  179.9 25.4 %copy-start.25 = (bf16[48,1536]{1,0:T(8,128)(2,1)}, bf16[48,1536]{1,0:T(8,128)(2,1)S(1)}, u32[]{:S(2)}) copy-start(bf16[48,1536]{1,0:T(8,128)(2,1)S(1)} %collective-permute-done.34.refs_3_) | copy-start | bytes 442372
  179.9 30.5 %collective-permute-start.28 = (bf16[3,256,256]{2,1,0:T(8,128)(2,1)}, bf16[3,256,256]{2,1,0:T(8,128)(2,1)S(1)}, u32[]{:S(2)}, u32[]{:S(2)}) collective-permute-start(bf16[3,256,256]{2,1,0:T(8,128)(2,1)} %get-tuple-element.90), channel_id=1, source_target_pairs={{0,3},{1,2},{2,1},{3,0},{4,7},{5,6},{6,5},{7,4},{8,11},{9,10},{10,... | collective-permute-start | bytes 1179656 | tf_op jit(solution)/shard_map/ppermute | solution.py:356
  183.8 25.1 %copy-start.20 = (bf16[3,256,128]{2,1,0:T(8,128)(2,1)}, bf16[3,256,128]{2,1,0:T(8,128)(2,1)S(1)}, u32[]{:S(2)}) copy-start(bf16[3,256,128]{2,1,0:T(8,128)(2,1)S(1)} %collective-permute-done.15.refs_1_) | copy-start | bytes 589828
  183.8 9.5 %collective-permute-start.39 = (bf16[48,1536]{1,0:T(8,128)(2,1)S(1)}, bf16[48,1536]{1,0:T(8,128)(2,1)S(1)}, u32[]{:S(2)}, u32[]{:S(2)}) collective-permute-start(bf16[48,1536]{1,0:T(8,128)(2,1)S(1)} %add_convert_fusion.refs_4_), channel_id=1, source_target_pairs={{0,2},{1,3},{2,0},{3,1},{4,6},{5,7},{6,4},{7,5},{8,10},{9,11},{10,... | collective-permute-start | bytes 442376 | tf_op jit(solution)/shard_map/ppermute | solution.py:356
  187.0 18.3 %copy-start.26 = (bf16[48,1536]{1,0:T(8,128)(2,1)}, bf16[48,1536]{1,0:T(8,128)(2,1)S(1)}, u32[]{:S(2)}) copy-start(bf16[48,1536]{1,0:T(8,128)(2,1)S(1)} %collective-permute-done.38.refs_5_) | copy-start | bytes 442372
  187.0 16.8 %collective-permute-start.40 = (bf16[48,1536]{1,0:T(8,128)(2,1)S(1)}, bf16[48,1536]{1,0:T(8,128)(2,1)S(1)}, u32[]{:S(2)}, u32[]{:S(2)}) collective-permute-start(bf16[48,1536]{1,0:T(8,128)(2,1)S(1)} %add_convert_fusion.refs_4_), channel_id=1, source_target_pairs={{0,3},{1,2},{2,1},{3,0},{4,7},{5,6},{6,5},{7,4},{8,11},{9,10},{10,... | collective-permute-start | bytes 442376 | tf_op jit(solution)/shard_map/ppermute | solution.py:356
  193.4 12.0 %copy-start.27 = (bf16[48,1536]{1,0:T(8,128)(2,1)}, bf16[48,1536]{1,0:T(8,128)(2,1)S(1)}, u32[]{:S(2)}) copy-start(bf16[48,1536]{1,0:T(8,128)(2,1)S(1)} %collective-permute-done.39.refs_6_) | copy-start | bytes 442372
  193.4 15.5 %collective-permute-start.16 = (bf16[3,256,128]{2,1,0:T(8,128)(2,1)S(1)}, bf16[3,256,128]{2,1,0:T(8,128)(2,1)S(1)}, u32[]{:S(2)}, u32[]{:S(2)}) collective-permute-start(bf16[3,256,128]{2,1,0:T(8,128)(2,1)S(1)} %copy-done.30), channel_id=1, source_target_pairs={{0,2},{1,3},{2,0},{3,1},{4,6},{5,7},{6,4},{7,5},{8,10},{9,11},{10,... | collective-permute-start | bytes 589832 | tf_op jit(solution)/shard_map/ppermute | solution.py:356
  203.8 1.5 copy-start.28
  203.8 6.6 %collective-permute-start.17 = (bf16[3,256,128]{2,1,0:T(8,128)(2,1)S(1)}, bf16[3,256,128]{2,1,0:T(8,128)(2,1)S(1)}, u32[]{:S(2)}, u32[]{:S(2)}) collective-permute-start(bf16[3,256,128]{2,1,0:T(8,128)(2,1)S(1)} %copy-done.29), channel_id=1, source_target_pairs={{0,3},{1,2},{2,1},{3,0},{4,7},{5,6},{6,5},{7,4},{8,11},{9,10},{10,... | collective-permute-start | bytes 589832 | tf_op jit(solution)/shard_map/ppermute | solution.py:356
  208.9 1.5 copy-start.21
  (8 other events, 7.5 us)

commit v5 on v4

--- a/solution.py
+++ b/solution.py
@@ -18,10 +18,6 @@
 
 def dot(a, b, dims=NN):
     return lax.dot_general(a, b, dims, preferred_element_type=jnp.float32)
-
-
-def far(*arrays):
-    return [pltpu.with_memory_space_constraint(array, pltpu.HBM) for array in arrays]
 
 
 def whole(shape):
@@ -81,35 +77,61 @@
         store.wait()
 
 
-def unpack(place, parts):
-    calls, rows = len(parts), len(parts[0])
+def finish(place, parts, pieces):
+    calls, rows, chunks = len(parts), len(parts[0]), len(pieces)
     tokens = parts[0][0].shape[1]
     widths = [part[0].shape[2] for part in parts]
     starts = [sum(widths[:at]) for at in range(calls + 1)]
     width = starts[-1]
+    piece, wide = pieces[0][0].shape
 
     def body(place_ref, *refs):
-        ins, outs, held, sems = refs[: calls * rows], refs[calls * rows : -2], refs[-2], refs[-1]
-        moves = []
+        ins, terms = refs[: calls * rows], refs[calls * rows : (calls + chunks) * rows]
+        outs, total = refs[(calls + chunks) * rows :][:3], refs[(calls + chunks) * rows + 3]
+        held, low, high, sems, term_sems = refs[-5:]
+        moves, sums = [], []
         for call in range(calls):
             for slot in range(rows):
                 start = (place_ref[0] ^ slot) * width + starts[call]
                 start = pl.multiple_of(start, HDIM)
                 for at in range(3):
                     box = held.at[slot, at, :, starts[call] : starts[call + 1]]
-                    moves.append(
-                        (
-                            pltpu.make_async_copy(
-                                ins[call * rows + slot].at[at], box, sems.at[0, call, slot, at]
-                            ),
-                            pltpu.make_async_copy(
-                                box,
-                                outs[at].at[0, :, pl.ds(start, widths[call])],
-                                sems.at[1, call, slot, at],
-                            ),
-                        )
+                    fetch = pltpu.make_async_copy(
+                        ins[call * rows + slot].at[at], box, sems.at[0, call, slot, at]
                     )
-        run(moves)
+                    store = pltpu.make_async_copy(
+                        box,
+                        outs[at].at[0, :, pl.ds(start, widths[call])],
+                        sems.at[1, call, slot, at],
+                    )
+                    moves.append((fetch, store))
+        for chunk in range(chunks):
+            for slot in range(rows):
+                start = pl.multiple_of((place_ref[0] ^ slot) * piece, 16)
+                fetch = pltpu.make_async_copy(
+                    terms[chunk * rows + slot], low.at[chunk, slot], term_sems.at[0, chunk, slot]
+                )
+                store = pltpu.make_async_copy(
+                    high.at[chunk, slot],
+                    total.at[pl.ds(start, piece), chunk * wide : (chunk + 1) * wide],
+                    term_sems.at[1, chunk, slot],
+                )
+                sums.append((chunk, slot, fetch, store))
+        for _, _, fetch, _ in sums:
+            fetch.start()
+        for fetch, _ in moves:
+            fetch.start()
+        for chunk, slot, fetch, store in sums:
+            fetch.wait()
+            high[chunk, slot] = low[chunk, slot].astype(jnp.float32)
+            store.start()
+        for fetch, store in moves:
+            fetch.wait()
+            store.start()
+        for _, _, _, store in sums:
+            store.wait()
+        for _, store in moves:
+            store.wait()
 
     full = jax.ShapeDtypeStruct((1, tokens, width * rows), parts[0][0].dtype)
     return pl.pallas_call(
@@ -117,17 +139,20 @@
         grid_spec=pltpu.PrefetchScalarGridSpec(
             num_scalar_prefetch=1,
             grid=(1,),
-            in_specs=[pl.BlockSpec(memory_space=pltpu.HBM)] * (calls * rows),
-            out_specs=[pl.BlockSpec(memory_space=pltpu.HBM)] * 3,
+            in_specs=[pl.BlockSpec(memory_space=pltpu.HBM)] * ((calls + chunks) * rows),
+            out_specs=[pl.BlockSpec(memory_space=pltpu.HBM)] * 4,
             scratch_shapes=[
                 pltpu.VMEM((rows, 3, tokens, width), parts[0][0].dtype),
+                pltpu.VMEM((chunks, rows, piece, wide), pieces[0][0].dtype),
+                pltpu.VMEM((chunks, rows, piece, wide), jnp.float32),
                 pltpu.SemaphoreType.DMA((2, calls, rows, 3)),
+                pltpu.SemaphoreType.DMA((2, chunks, rows)),
             ],
         ),
-        out_shape=[full] * 3,
-        cost_estimate=cost(0, 12 * tokens * width * rows),
-        name="unpack",
-    )(place, *far(*(block for part in parts for block in part)))
+        out_shape=[full] * 3 + [jax.ShapeDtypeStruct((rows * piece, chunks * wide), jnp.float32)],
+        cost_estimate=cost(0, 12 * tokens * width * rows + 6 * rows * piece * chunks * wide),
+        name="finish",
+    )(place, *(block for part in (*parts, *pieces) for block in part))
 
 
 def forward(parts):
@@ -167,7 +192,7 @@
             8 * heads * length * length * HDIM, 2 * heads * length * length, heads * length * length
         ),
         name="forward",
-    )(*far(*parts))
+    )(*parts)
 
 
 def backward(parts, probs, grad_attn, first, count):
@@ -213,7 +238,7 @@
         scratch_shapes=[pltpu.VMEM((length, length), jnp.bfloat16)],
         cost_estimate=cost(8 * count * length * length * HDIM, 2 * count * length * length),
         name="backward",
-    )(*far(*parts, probs, grad_attn))
+    )(*parts, probs, grad_attn)
 
 
 def stacked(refs):
@@ -223,13 +248,13 @@
 def project(place, weights, grads):
     chunks, count = len(grads), len(grads[0])
     half, depth = weights[0].shape
+    half = half * len(weights) // 2
     step = grads[0][0].shape[1] // 2
 
     def body(place_ref, *refs):
-        first, second = refs[:2]
-        ins, out, total = refs[2:-2], refs[-2], refs[-1]
+        ins, out, total = refs[len(weights) : -2], refs[-2], refs[-1]
         at = pl.program_id(0)
-        lines = jnp.concatenate([first[...], second[...]], axis=0)
+        lines = stacked(refs[: len(weights)])
         for chunk in range(chunks):
 
             @pl.when(at // 2 == chunk)
@@ -260,7 +285,9 @@
         grid_spec=pltpu.PrefetchScalarGridSpec(
             num_scalar_prefetch=1,
             grid=(chunks * 2,),
-            in_specs=[pl.BlockSpec((half, step), lambda i, place_ref: (0, i))] * 2
+            in_specs=[
+                pl.BlockSpec((part.shape[0], step), lambda i, place_ref: (0, i)) for part in weights
+            ]
             + [block_of(chunk, block) for chunk in range(chunks) for block in grads[chunk]],
             out_specs=whole(shape),
             scratch_shapes=[pltpu.VMEM(shape, jnp.float32)],
@@ -268,7 +295,7 @@
         out_shape=jax.ShapeDtypeStruct(shape, jnp.bfloat16),
         cost_estimate=cost(2 * shape[0] * shape[1] * depth, 2 * depth * (shape[0] + shape[1])),
         name="project",
-    )(place, *far(*weights, *(block for chunk in grads for block in chunk)))
+    )(place, *weights, *(block for chunk in grads for block in chunk))
 
 
 def weight_terms(place, attended, grads, rows):
@@ -303,39 +330,16 @@
         out_shape=[shape] * 2,
         cost_estimate=cost(4 * width * length * step, 2 * (width * length + 2 * length * step)),
         name="weight_terms",
-    )(place, *far(attended, *grads))
-
-
-def assemble(place, pieces):
-    chunks, rows = len(pieces), len(pieces[0])
-    piece, wide = pieces[0][0].shape
-
-    def body(place_ref, *refs):
-        ins, out = refs[:-1], refs[-1]
-        for chunk in range(chunks):
-            for slot in range(rows):
-                start = pl.multiple_of((place_ref[0] ^ slot) * piece, 16)
-                out[pl.ds(start, piece), chunk * wide : (chunk + 1) * wide] = ins[
-                    chunk * rows + slot
-                ][...].astype(out.dtype)
-
-    shape = (rows * piece, chunks * wide)
-    return pl.pallas_call(
-        body,
-        grid_spec=pltpu.PrefetchScalarGridSpec(
-            num_scalar_prefetch=1,
-            grid=(1,),
-            in_specs=[whole((piece, wide))] * (chunks * rows),
-            out_specs=whole(shape),
-        ),
-        out_shape=jax.ShapeDtypeStruct(shape, jnp.float32),
-        cost_estimate=cost(0, 6 * shape[0] * shape[1]),
-        name="assemble",
-    )(place, *far(*(block for chunk in pieces for block in chunk)))
+    )(place, attended, *grads)
 
 
 def after(value, *done):
     return lax.optimization_barrier((value, done))[0]
+
+
+def onward(planes, hop, z, c, r):
+    to = z + 1 if z > r else z - 1
+    return (to, c, r) if abs(z - r) == hop and 0 <= to < planes else None
 
 
 def by_heads(fsdp, rows, query_rows, key_rows, value_rows, grad_out, w_out):
@@ -371,20 +375,45 @@
         by_x, by_y = to_row(chunk, 1), to_row(chunk, 2)
         by_x, by_y = after((by_x, by_y), *done)
         cut = chunk.shape[0] // 2
-        upper = to_row(by_x[:cut], 2)
-        lower = to_row(by_y[cut:], 1)
+        upper, lower = by_x[:cut], by_y[cut:]
+        upper = to_row(upper, 2)
+        lower = to_row(lower, 1)
         return [chunk, by_x, by_y, upper, lower]
 
     grads = [gather(grad_flat[:, :wide])]
 
-    lines = [w_out] + [
-        send(w_out, lambda z, c, r: ((z + ahead) % planes, c, r) if z == r else None)
-        for ahead in range(1, planes)
-    ]
+    away = jnp.abs(plane - row)
+    cut = w_out.shape[0] // 2
+
+    def leave(lines):
+        above = send(lines, lambda z, c, r: (z + 1, c, r) if z == r and z + 1 < planes else None)
+        below = send(lines, lambda z, c, r: (z - 1, c, r) if z == r and z > 0 else None)
+        return jnp.where(plane > row, above, below)
+
+    def go_on(hop, lines):
+        return send(lines, functools.partial(onward, planes, hop))
+
+    first = [w_out[:cut]]
+    first.append(leave(first[0]))
+    first.append(go_on(1, first[1]))
+    second = [w_out[cut:]]
+    second.append(leave(after(second[0], first[1])))
+    first.append(go_on(2, first[2]))
+    second.append(go_on(1, second[1]))
 
     packed = pack(place, query_rows, key_rows, value_rows, rows)
     parts = [packed[0]] + [to_row(packed[slot], slot) for slot in range(1, rows)]
     probs, attended = forward(parts)
+    second.append(go_on(2, after(second[2], attended)))
+
+    def mine(stages):
+        here = stages[0]
+        for hop in range(1, planes):
+            here = jnp.where(away == hop, stages[hop], here)
+        return here
+
+    weights = [mine(first), mine(second)]
+    weights += [to_core(part) for part in weights]
     grads.append(gather(after(grad_flat[:, wide:], parts), attended))
 
     def reduce_cores(attended, chunk):
@@ -415,12 +444,7 @@
     blocks = spread(*reduce_cores(attended, grads[0]))
     late = reduce_cores(attended, grads[1])
     early = reduce_planes(after(blocks, late[0]))
-    lines = after(lines, late[0])
-    here = lines[0]
-    for ahead in range(1, planes):
-        here = jnp.where((plane - row) % planes == ahead, lines[ahead], here)
-    other = to_core(here)
-    grad_attn = project(place, [here, other], grads)
+    grad_attn = project(place, weights, grads)
     heads = probs.shape[0]
     blocks = spread(*after(late, early[0]))
     sent = [backward(parts, probs, grad_attn, 0, 1)]
@@ -432,9 +456,7 @@
         for message in sent
     ]
     pieces = [collect(*after(early, sent[0][0])), collect(*after(late, sent[1][0]))]
-    grad_query, grad_key, grad_value = unpack(place, back)
-    grad_w_out = assemble(place, pieces)
-    return grad_query, grad_key, grad_value, grad_w_out
+    return tuple(finish(place, back, pieces))
 
 
 def by_tokens(query_rows, key_rows, value_rows, grad_out, w_out):

time: 216 us -> 227 us (1.051)
  waiting for transfers between devices: 81.4 us -> 89.4 us
  starting transfers between devices: 61.4 us -> 66.1 us
    ppermute x41 -> x47, waiting for transfers between devices: 81.4 us -> 89.4 us  [send(): return lax.ppermute(array, ('fsdp', 'rows'), pairs)]
    ppermute x41 -> x47, starting transfers between devices: 61.4 us -> 66.1 us  [send(): return lax.ppermute(array, ('fsdp', 'rows'), pairs)]
    pallas_call x2 -> x1, Pallas kernels: 7.03 us -> 4.81 us  [finish(): pl.pallas_call(body, grid_spec=pltpu.PrefetchScalarGridSpec(num_scalar_pr...]
    slice x5 -> x6, local copies, waits for them, and re-layouts: 5.06 us -> 4.45 us  [the longest x1 2.25 us: by_heads(): second = [w_out[cut:]]]
  transfers between devices with their start and end apart: 41 -> 47, of which waited for: 16 -> 13; matrix products, arithmetic and copies ran while one was open for 5% -> 5% of each run, Pallas kernels for 23% -> 21%
where the time goes in v5:
time: 227 us; the launch traced here: 226 us
  waiting for transfers between devices  89.4 us (39%)
  starting transfers between devices  66.1 us (29%)
  Pallas kernels  53.3 us (23%)
  local copies, waits for them, and re-layouts  7.98 us (4%)
  other arithmetic  7.96 us (4%)
    ppermute x47, waiting for transfers between devices, send(): return lax.ppermute(array, ('fsdp', 'rows'), pairs)  89.4 us
    ppermute x47, starting transfers between devices, send(): return lax.ppermute(array, ('fsdp', 'rows'), pairs)  66.1 us
    pallas_call x2, Pallas kernels, backward(): pl.pallas_call(body, grid=(count,), in_specs=[part] * rows + [pl.BlockSpe...  14.1 us
    pallas_call x1, Pallas kernels, forward(): pl.pallas_call(body, grid=(heads,), in_specs=[part] * rows, out_specs=[pl...  12.6 us
    pallas_call x2, Pallas kernels, weight_terms(): pl.pallas_call(body, grid_spec=pltpu.PrefetchScalarGridSpec(num_scalar_pr...  10.4 us
    pallas_call x1, Pallas kernels, project(): pl.pallas_call(body, grid_spec=pltpu.PrefetchScalarGridSpec(num_scalar_pr...  8.01 us
    pallas_call x1, Pallas kernels, finish(): pl.pallas_call(body, grid_spec=pltpu.PrefetchScalarGridSpec(num_scalar_pr...  4.81 us
  transfers between devices with their start and end apart: 47, of which 13 were waited for; matrix products, arithmetic and copies ran while one was open for 5% of the time, Pallas kernels for 21%

profile of v5, /device:TPU:0, one launch (start us, length us, event | category | flops | bytes accessed | tf_op | source)
XLA Modules:
  0.0 225.9 jit_solution(17542399088590237669)
XLA Ops:
  0.6 2.2 fusion.9
  2.9 5.0 %collective-permute-start.3 = (bf16[96,3072]{1,0:T(8,128)(2,1)S(1)}, bf16[96,3072]{1,0:T(8,128)(2,1)S(1)}, u32[]{:S(2)}, u32[]{:S(2)}) collective-permute-start(bf16[96,3072]{1,0:T(8,128)(2,1)S(1)} %get-tuple-element.105), channel_id=1, source_target_pairs={{0,8},{4,12},{9,17},{13,21},{18,26},{22,30}} | collective-permute-start | bytes 1769480 | tf_op jit(solution)/shard_map/ppermute | solution.py:360
  7.9 1.5 collective-permute-start.4
  9.8 0.7 pad_add_fusion.place_ref
  10.5 3.3 %pack.1 = (bf16[3,256,384]{2,1,0:T(8,128)(2,1)}, bf16[3,256,384]{2,1,0:T(8,128)(2,1)}, bf16[3,256,384]{2,1,0:T(8,128)(2,1)}, bf16[3,256,384]{2,1,0:T(8,128)(2,1)}) custom-call(s32[3]{0:T(128)} %pad_add_fusion.place_ref, bf16[1,256,1536]{2,1,0:T(8,128)(2,1)} %refs_0_.1, bf16[1,256,1536]{2,1,0:T(8,128)(2,1)} %refs_1_.1, bf16[1,256,1536]{2,1,0:T(8,128)(2,1)} %refs_2_.1), custom_call_target="tpu_custom_call" | custom-call | bytes 4718592 | tf_op jit(solution)/shard_map/pack/pallas_call | solution.py:52
  13.8 1.7 collective-permute-start
  15.5 4.9 %collective-permute-done.3 = bf16[96,3072]{1,0:T(8,128)(2,1)S(1)} collective-permute-done((bf16[96,3072]{1,0:T(8,128)(2,1)S(1)}, bf16[96,3072]{1,0:T(8,128)(2,1)S(1)}, u32[]{:S(2)}, u32[]{:S(2)}) %collective-permute-start.3) | collective-permute-done | bytes 589856 | tf_op jit(solution)/shard_map/ppermute | solution.py:360
  20.4 0.8 copy-done.15
  21.2 2.0 broadcast_select_fusion.1
  23.2 19.4 %collective-permute-done.refs_1_ = bf16[3,256,384]{2,1,0:T(8,128)(2,1)S(1)} collective-permute-done((bf16[3,256,384]{2,1,0:T(8,128)(2,1)}, bf16[3,256,384]{2,1,0:T(8,128)(2,1)S(1)}, u32[]{:S(2)}, u32[]{:S(2)}) %collective-permute-start) | collective-permute-done | bytes 589856 | tf_op jit(solution)/shard_map/ppermute | solution.py:360
  42.6 4.4 %collective-permute-start.7 = (bf16[96,3072]{1,0:T(8,128)(2,1)}, bf16[96,3072]{1,0:T(8,128)(2,1)}, u32[]{:S(2)}, u32[]{:S(2)}) collective-permute-start(bf16[96,3072]{1,0:T(8,128)(2,1)} %get-tuple-element.53), channel_id=1, source_target_pairs={{0,8},{4,12},{9,17},{13,21},{18,26},{22,30}} | collective-permute-start | bytes 1769480 | tf_op jit(solution)/shard_map/ppermute | solution.py:360
  47.0 6.9 %collective-permute-done.1.refs_2_ = bf16[3,256,384]{2,1,0:T(8,128)(2,1)S(1)} collective-permute-done((bf16[3,256,384]{2,1,0:T(8,128)(2,1)}, bf16[3,256,384]{2,1,0:T(8,128)(2,1)S(1)}, u32[]{:S(2)}, u32[]{:S(2)}) %collective-permute-start.1) | collective-permute-done | bytes 589856 | tf_op jit(solution)/shard_map/ppermute | solution.py:360
  53.9 1.5 collective-permute-start.8
  55.4 1.5 collective-permute-start.5
  56.9 12.6 %forward.1 = (bf16[3,1024,1024]{2,1,0:T(8,128)(2,1)}, bf16[384,1024]{1,0:T(8,128)(2,1)}) custom-call(bf16[3,256,384]{2,1,0:T(8,128)(2,1)} %get-tuple-element.48.refs_0_, bf16[3,256,384]{2,1,0:T(8,128)(2,1)} %copy-done.3, bf16[3,256,384]{2,1,0:T(8,128)(2,1)} %copy-done.4, bf16[3,256,384]{2,1,0:T(8,128)(2,1)} %copy-done.5), custom_call_target="tpu_custom_call" | custom-call | flops 3221225472 | bytes 6291456 | tf_op jit(solution)/shard_map/forward/pallas_call | solution.py:179
  69.5 1.6 collective-permute-start.17
  71.5 1.0 slice.75
  72.5 1.0 slice.76
  73.6 1.7 collective-permute-start.15
  75.2 0.5 collective-permute-start.16
  75.7 1.1 broadcast_select_fusion
  76.9 20.2 %collective-permute-done.15.refs_7_.refs_3_ = bf16[128,1536]{1,0:T(8,128)(2,1)S(1)} collective-permute-done((bf16[128,1536]{1,0:T(8,128)(2,1)S(1)}, bf16[128,1536]{1,0:T(8,128)(2,1)S(1)}, u32[]{:S(2)}, u32[]{:S(2)}) %collective-permute-start.15) | collective-permute-done | bytes 393248 | tf_op jit(solution)/shard_map/ppermute | solution.py:360
  97.1 1.5 collective-permute-start.9
  98.6 5.2 %weight_terms.3 = (bf16[4,48,1536]{2,1,0:T(8,128)(2,1)}, bf16[4,48,1536]{2,1,0:T(8,128)(2,1)}) custom-call(s32[3]{0:T(128)} %pad_add_fusion.place_ref, bf16[384,1024]{1,0:T(8,128)(2,1)} %get-tuple-element.54.attended_ref, bf16[256,1536]{1,0:T(8,128)(2,1)} %copy-done.2, bf16[256,1536]{1,0:T(8,128)(2,1)} %collective-permute-done.13.refs_5_.refs_1_, ...), custom_call_target="tpu_custom_call" | custom-call | flops 1207959552 | bytes 3932160 | tf_op jit(solution)/shard_map/weight_terms/pallas_call | solution.py:321
  103.8 1.6 collective-permute-start.6
  105.7 0.9 collective-permute-start.20
  106.6 1.5 collective-permute-start.10
  108.1 0.8 fusion.3
  108.9 1.2 collective-permute-start.26
  110.1 6.9 %collective-permute-done.19.refs_12_.refs_3_ = bf16[128,1536]{1,0:T(8,128)(2,1)S(1)} collective-permute-done((bf16[128,1536]{1,0:T(8,128)(2,1)S(1)}, bf16[128,1536]{1,0:T(8,128)(2,1)S(1)}, u32[]{:S(2)}, u32[]{:S(2)}) %collective-permute-start.19) | collective-permute-done | bytes 393248 | tf_op jit(solution)/shard_map/ppermute | solution.py:360
  117.2 0.5 collective-permute-done.20.refs_13_.refs_4_
  117.8 2.1 collective-permute-start.28
  119.9 5.2 %weight_terms.2 = (bf16[4,48,1536]{2,1,0:T(8,128)(2,1)}, bf16[4,48,1536]{2,1,0:T(8,128)(2,1)}) custom-call(s32[3]{0:T(128)} %pad_add_fusion.place_ref, bf16[384,1024]{1,0:T(8,128)(2,1)} %get-tuple-element.54.attended_ref, bf16[256,1536]{1,0:T(8,128)(2,1)} %copy-done.1, bf16[256,1536]{1,0:T(8,128)(2,1)} %copy-done.8, bf16[256,1536]{1,0:T(8,128)(2,1)} %copy-done.9, ...), custom_call_target="tpu_custom_call" | custom-call | flops 1207959552 | bytes 3932160 | tf_op jit(solution)/shard_map/weight_terms/pallas_call | solution.py:321
  125.5 1.0 copy-done
  126.8 0.5 collective-permute-start.12
  127.3 6.0 %collective-permute-start.35 = (bf16[48,1536]{1,0:T(8,128)(2,1)S(1)}, bf16[48,1536]{1,0:T(8,128)(2,1)}, u32[]{:S(2)}, u32[]{:S(2)}) collective-permute-start(bf16[48,1536]{1,0:T(8,128)(2,1)S(1)} %get-tuple-element.112), channel_id=1, source_target_pairs={{0,8},{1,9},{2,10},{3,11},{4,12},{5,13},{6,14},{7,15},{8,16},{9,17... | collective-permute-start | bytes 442376 | tf_op jit(solution)/shard_map/ppermute | solution.py:360
  133.3 9.6 %collective-permute-start.36 = (bf16[48,1536]{1,0:T(8,128)(2,1)S(1)}, bf16[48,1536]{1,0:T(8,128)(2,1)}, u32[]{:S(2)}, u32[]{:S(2)}) collective-permute-start(bf16[48,1536]{1,0:T(8,128)(2,1)S(1)} %get-tuple-element.111), channel_id=1, source_target_pairs={{0,16},{1,17},{2,18},{3,19},{4,20},{5,21},{6,22},{7,23},{8,24},{9,... | collective-permute-start | bytes 442376 | tf_op jit(solution)/shard_map/ppermute | solution.py:360
  142.9 0.8 fusion.7
  143.9 3.4 %collective-permute-start.31 = (bf16[48,1536]{1,0:T(8,128)(2,1)S(1)}, bf16[48,1536]{1,0:T(8,128)(2,1)}, u32[]{:S(2)}, u32[]{:S(2)}) collective-permute-start(bf16[48,1536]{1,0:T(8,128)(2,1)S(1)} %get-tuple-element.94), channel_id=1, source_target_pairs={{0,3},{1,2},{2,1},{3,0},{4,7},{5,6},{6,5},{7,4},{8,11},{9,10},{10,... | collective-permute-start | bytes 442376 | tf_op jit(solution)/shard_map/ppermute | solution.py:360
  147.3 8.0 %project.1.refs_5_ = bf16[384,1024]{1,0:T(8,128)(2,1)} custom-call(s32[3]{0:T(128)} %pad_add_fusion.place_ref, bf16[96,3072]{1,0:T(8,128)(2,1)} %copy-done.7, bf16[96,3072]{1,0:T(8,128)(2,1)} %copy-done.6, bf16[96,3072]{1,0:T(8,128)(2,1)} %copy-done.11, bf16[96,3072]{1,0:T(8,128)(2,1)} %copy-done.12, bf16[256,1536]{1,0:T(8,128)(2,1)} %copy-done.2, ...), custom_call_target="tpu_custom_call" | custom-call | flops 2415919104 | bytes 8650752 | tf_op jit(solution)/shard_map/project/pallas_call | solution.py:283
  155.3 5.6 %backward.2 = (bf16[3,256,128]{2,1,0:T(8,128)(2,1)}, bf16[3,256,128]{2,1,0:T(8,128)(2,1)}, bf16[3,256,128]{2,1,0:T(8,128)(2,1)}, bf16[3,256,128]{2,1,0:T(8,128)(2,1)}) custom-call(bf16[3,256,384]{2,1,0:T(8,128)(2,1)} %get-tuple-element.48.refs_0_, bf16[3,256,384]{2,1,0:T(8,128)(2,1)} %copy-done.3, bf16[3,256,384]{2,1,0:T(8,128)(2,1)} %copy-done.4, ...), custom_call_target="tpu_custom_call" | custom-call | flops 1073741824 | bytes 2097152 | tf_op jit(solution)/shard_map/backward/pallas_call | solution.py:228
  160.9 0.5 collective-permute-start.37
  161.4 1.1 pad_maximum_fusion.1
  162.6 3.6 %collective-permute-done.37 = bf16[48,1536]{1,0:T(8,128)(2,1)S(1)} collective-permute-done((bf16[48,1536]{1,0:T(8,128)(2,1)S(1)}, bf16[48,1536]{1,0:T(8,128)(2,1)S(1)}, u32[]{:S(2)}, u32[]{:S(2)}) %collective-permute-start.37) | collective-permute-done | bytes 147488 | tf_op jit(solution)/shard_map/ppermute | solution.py:360
  166.2 2.8 %collective-permute-start.42 = (bf16[48,1536]{1,0:T(8,128)(2,1)S(1)}, bf16[48,1536]{1,0:T(8,128)(2,1)S(1)}, u32[]{:S(2)}, u32[]{:S(2)}) collective-permute-start(bf16[48,1536]{1,0:T(8,128)(2,1)S(1)} %get-tuple-element.107), channel_id=1, source_target_pairs={{0,16},{1,17},{2,18},{3,19},{4,20},{5,21},{6,22},{7,23},{8,24},{9,... | collective-permute-start | bytes 442376 | tf_op jit(solution)/shard_map/ppermute | solution.py:360
  169.0 1.1 add_convert_fusion.1.refs_8_
  170.2 1.3 collective-permute-start.39
  171.5 2.2 collective-permute-start.40
  173.7 3.4 %collective-permute-done.42 = bf16[48,1536]{1,0:T(8,128)(2,1)S(1)} collective-permute-done((bf16[48,1536]{1,0:T(8,128)(2,1)S(1)}, bf16[48,1536]{1,0:T(8,128)(2,1)S(1)}, u32[]{:S(2)}, u32[]{:S(2)}) %collective-permute-start.42) | collective-permute-done | bytes 147488 | tf_op jit(solution)/shard_map/ppermute | solution.py:360
  177.1 1.4 collective-permute-start.43
  178.5 8.5 %backward.3 = (bf16[3,256,256]{2,1,0:T(8,128)(2,1)}, bf16[3,256,256]{2,1,0:T(8,128)(2,1)}, bf16[3,256,256]{2,1,0:T(8,128)(2,1)}, bf16[3,256,256]{2,1,0:T(8,128)(2,1)}) custom-call(bf16[3,256,384]{2,1,0:T(8,128)(2,1)} %get-tuple-element.48.refs_0_, bf16[3,256,384]{2,1,0:T(8,128)(2,1)} %copy-done.3, bf16[3,256,384]{2,1,0:T(8,128)(2,1)} %copy-done.4, ...), custom_call_target="tpu_custom_call" | custom-call | flops 2147483648 | bytes 4194304 | tf_op jit(solution)/shard_map/backward/pallas_call | solution.py:228
  187.2 1.5 collective-permute-start.23
  188.7 1.9 collective-permute-start.32
  190.7 1.4 collective-permute-start.34
  192.3 5.3 %collective-permute-done.22.refs_2_ = bf16[3,256,128]{2,1,0:T(8,128)(2,1)S(1)} collective-permute-done((bf16[3,256,128]{2,1,0:T(8,128)(2,1)S(1)}, bf16[3,256,128]{2,1,0:T(8,128)(2,1)S(1)}, u32[]{:S(2)}, u32[]{:S(2)}) %collective-permute-start.22) | collective-permute-done | bytes 196640 | tf_op jit(solution)/shard_map/ppermute | solution.py:360
  197.6 1.3 collective-permute-start.44
  198.8 0.8 collective-permute-start.45
  199.6 13.6 %collective-permute-done.44.refs_13_ = bf16[48,1536]{1,0:T(8,128)(2,1)S(1)} collective-permute-done((bf16[48,1536]{1,0:T(8,128)(2,1)S(1)}, bf16[48,1536]{1,0:T(8,128)(2,1)S(1)}, u32[]{:S(2)}, u32[]{:S(2)}) %collective-permute-start.44) | collective-permute-done | bytes 147488 | tf_op jit(solution)/shard_map/ppermute | solution.py:360
  213.2 1.5 collective-permute-start.46
  214.6 3.0 %collective-permute-done.45.refs_14_ = bf16[48,1536]{1,0:T(8,128)(2,1)S(1)} collective-permute-done((bf16[48,1536]{1,0:T(8,128)(2,1)S(1)}, bf16[48,1536]{1,0:T(8,128)(2,1)S(1)}, u32[]{:S(2)}, u32[]{:S(2)}) %collective-permute-start.45) | collective-permute-done | bytes 147488 | tf_op jit(solution)/shard_map/ppermute | solution.py:360
  217.6 1.6 collective-permute-done.46.refs_15_
  219.3 0.5 copy-done.32
  220.2 0.7 copy-done.23
  220.9 4.8 %finish.1 = (bf16[1,256,1536]{2,1,0:T(8,128)(2,1)}, bf16[1,256,1536]{2,1,0:T(8,128)(2,1)}, bf16[1,256,1536]{2,1,0:T(8,128)(2,1)}, f32[192,3072]{1,0:T(8,128)}) custom-call(s32[3]{0:T(128)} %pad_add_fusion.place_ref, bf16[3,256,128]{2,1,0:T(8,128)(2,1)} %get-tuple-element.61.refs_0_, bf16[3,256,128]{2,1,0:T(8,128)(2,1)} %copy-done.24, ...), custom_call_target="tpu_custom_call" | custom-call | bytes 8257536 | tf_op jit(solution)/shard_map/finish/pallas_call | solution.py:137
  (128 shorter events, 3.2 us)
Async XLA Ops:
  2.9 17.5 %collective-permute-start.3 = (bf16[96,3072]{1,0:T(8,128)(2,1)S(1)}, bf16[96,3072]{1,0:T(8,128)(2,1)S(1)}, u32[]{:S(2)}, u32[]{:S(2)}) collective-permute-start(bf16[96,3072]{1,0:T(8,128)(2,1)S(1)} %get-tuple-element.105), channel_id=1, source_target_pairs={{0,8},{4,12},{9,17},{13,21},{18,26},{22,30}} | collective-permute-start | bytes 1769480 | tf_op jit(solution)/shard_map/ppermute | solution.py:360
  7.9 13.4 %collective-permute-start.4 = (bf16[96,3072]{1,0:T(8,128)(2,1)S(1)}, bf16[96,3072]{1,0:T(8,128)(2,1)}, u32[]{:S(2)}, u32[]{:S(2)}) collective-permute-start(bf16[96,3072]{1,0:T(8,128)(2,1)S(1)} %get-tuple-element.105), channel_id=1, source_target_pairs={{9,1},{13,5},{18,10},{22,14},{27,19},{31,23}} | collective-permute-start | bytes 1769480 | tf_op jit(solution)/shard_map/ppermute | solution.py:360
  9.5 13.8 %copy-start.2 = (bf16[256,1536]{1,0:T(8,128)(2,1)}, bf16[256,1536]{1,0:T(8,128)(2,1)S(1)}, u32[]{:S(2)}) copy-start(bf16[256,1536]{1,0:T(8,128)(2,1)S(1)} %get-tuple-element.93.refs_4_.refs_0_) | copy-start | bytes 2359300
  9.5 61.6 %copy-start.1 = (bf16[256,1536]{1,0:T(8,128)(2,1)}, bf16[256,1536]{1,0:T(8,128)(2,1)S(1)}, u32[]{:S(2)}) copy-start(bf16[256,1536]{1,0:T(8,128)(2,1)S(1)} %get-tuple-element.58.refs_9_.refs_0_) | copy-start | bytes 2359300
  9.5 60.0 %collective-permute-start.13 = (bf16[256,1536]{1,0:T(8,128)(2,1)S(1)}, bf16[256,1536]{1,0:T(8,128)(2,1)}, u32[]{:S(2)}, u32[]{:S(2)}) collective-permute-start(bf16[256,1536]{1,0:T(8,128)(2,1)S(1)} %get-tuple-element.93.refs_4_.refs_0_), channel_id=1, source_target_pairs={{0,1},{1,0},{2,3},{3,2},{4,5},{5,4},{6,7},{7,6},{8,9},{9,8},{10,11... | collective-permute-start | bytes 2359304 | tf_op jit(solution)/shard_map/ppermute | solution.py:360
  9.6 61.5 %collective-permute-start.14 = (bf16[256,1536]{1,0:T(8,128)(2,1)S(1)}, bf16[256,1536]{1,0:T(8,128)(2,1)}, u32[]{:S(2)}, u32[]{:S(2)}) collective-permute-start(bf16[256,1536]{1,0:T(8,128)(2,1)S(1)} %get-tuple-element.93.refs_4_.refs_0_), channel_id=1, source_target_pairs={{0,2},{1,3},{2,0},{3,1},{4,6},{5,7},{6,4},{7,5},{8,10},{9,11},{10,... | collective-permute-start | bytes 2359304 | tf_op jit(solution)/shard_map/ppermute | solution.py:360
  13.8 28.8 %collective-permute-start = (bf16[3,256,384]{2,1,0:T(8,128)(2,1)}, bf16[3,256,384]{2,1,0:T(8,128)(2,1)S(1)}, u32[]{:S(2)}, u32[]{:S(2)}) collective-permute-start(bf16[3,256,384]{2,1,0:T(8,128)(2,1)} %get-tuple-element.49), channel_id=1, source_target_pairs={{0,1},{1,0},{2,3},{3,2},{4,5},{5,4},{6,7},{7,6},{8,9},{9,8},{10,11... | collective-permute-start | bytes 1769480 | tf_op jit(solution)/shard_map/ppermute | solution.py:360
  21.2 32.7 %collective-permute-start.1 = (bf16[3,256,384]{2,1,0:T(8,128)(2,1)}, bf16[3,256,384]{2,1,0:T(8,128)(2,1)S(1)}, u32[]{:S(2)}, u32[]{:S(2)}) collective-permute-start(bf16[3,256,384]{2,1,0:T(8,128)(2,1)} %get-tuple-element.50), channel_id=1, source_target_pairs={{0,2},{1,3},{2,0},{3,1},{4,6},{5,7},{6,4},{7,5},{8,10},{9,11},{10,... | collective-permute-start | bytes 1769480 | tf_op jit(solution)/shard_map/ppermute | solution.py:360
  21.2 34.2 %collective-permute-start.2 = (bf16[3,256,384]{2,1,0:T(8,128)(2,1)}, bf16[3,256,384]{2,1,0:T(8,128)(2,1)S(1)}, u32[]{:S(2)}, u32[]{:S(2)}) collective-permute-start(bf16[3,256,384]{2,1,0:T(8,128)(2,1)} %get-tuple-element.51), channel_id=1, source_target_pairs={{0,3},{1,2},{2,1},{3,0},{4,7},{5,6},{6,5},{7,4},{8,11},{9,10},{10,... | collective-permute-start | bytes 1769480 | tf_op jit(solution)/shard_map/ppermute | solution.py:360
  42.6 14.3 %copy-start.3 = (bf16[3,256,384]{2,1,0:T(8,128)(2,1)}, bf16[3,256,384]{2,1,0:T(8,128)(2,1)S(1)}, u32[]{:S(2)}) copy-start(bf16[3,256,384]{2,1,0:T(8,128)(2,1)S(1)} %collective-permute-done.refs_1_) | copy-start | bytes 1769476
  42.6 30.9 %collective-permute-start.7 = (bf16[96,3072]{1,0:T(8,128)(2,1)}, bf16[96,3072]{1,0:T(8,128)(2,1)}, u32[]{:S(2)}, u32[]{:S(2)}) collective-permute-start(bf16[96,3072]{1,0:T(8,128)(2,1)} %get-tuple-element.53), channel_id=1, source_target_pairs={{0,8},{4,12},{9,17},{13,21},{18,26},{22,30}} | collective-permute-start | bytes 1769480 | tf_op jit(solution)/shard_map/ppermute | solution.py:360
  53.9 21.3 %collective-permute-start.8 = (bf16[96,3072]{1,0:T(8,128)(2,1)}, bf16[96,3072]{1,0:T(8,128)(2,1)}, u32[]{:S(2)}, u32[]{:S(2)}) collective-permute-start(bf16[96,3072]{1,0:T(8,128)(2,1)} %get-tuple-element.53), channel_id=1, source_target_pairs={{9,1},{13,5},{18,10},{22,14},{27,19},{31,23}} | collective-permute-start | bytes 1769480 | tf_op jit(solution)/shard_map/ppermute | solution.py:360
  55.4 48.4 %collective-permute-start.5 = (bf16[96,3072]{1,0:T(8,128)(2,1)}, bf16[96,3072]{1,0:T(8,128)(2,1)}, u32[]{:S(2)}, u32[]{:S(2)}) collective-permute-start(bf16[96,3072]{1,0:T(8,128)(2,1)} %broadcast_select_fusion.1), channel_id=1, source_target_pairs={{8,16},{10,2},{12,20},{14,6},{17,25},{19,11},{21,29},{23,15}} | collective-permute-start | bytes 1769480 | tf_op jit(solution)/shard_map/ppermute | solution.py:360
  69.5 36.0 %collective-permute-start.17 = (bf16[256,1536]{1,0:T(8,128)(2,1)S(1)}, bf16[256,1536]{1,0:T(8,128)(2,1)S(1)}, u32[]{:S(2)}, u32[]{:S(2)}) collective-permute-start(bf16[256,1536]{1,0:T(8,128)(2,1)S(1)} %get-tuple-element.58.refs_9_.refs_0_), channel_id=1, source_target_pairs={{0,1},{1,0},{2,3},{3,2},{4,5},{5,4},{6,7},{7,6},{8,9},{9,8},{10,11... | collective-permute-start | bytes 2359304 | tf_op jit(solution)/shard_map/ppermute | solution.py:360
  71.1 34.4 %collective-permute-start.18 = (bf16[256,1536]{1,0:T(8,128)(2,1)S(1)}, bf16[256,1536]{1,0:T(8,128)(2,1)S(1)}, u32[]{:S(2)}, u32[]{:S(2)}) collective-permute-start(bf16[256,1536]{1,0:T(8,128)(2,1)S(1)} %get-tuple-element.58.refs_9_.refs_0_), channel_id=1, source_target_pairs={{0,2},{1,3},{2,0},{3,1},{4,6},{5,7},{6,4},{7,5},{8,10},{9,11},{10,... | collective-permute-start | bytes 2359304 | tf_op jit(solution)/shard_map/ppermute | solution.py:360
  73.6 23.5 %collective-permute-start.15 = (bf16[128,1536]{1,0:T(8,128)(2,1)S(1)}, bf16[128,1536]{1,0:T(8,128)(2,1)S(1)}, u32[]{:S(2)}, u32[]{:S(2)}) collective-permute-start(bf16[128,1536]{1,0:T(8,128)(2,1)S(1)} %slice.75), channel_id=1, source_target_pairs={{0,2},{1,3},{2,0},{3,1},{4,6},{5,7},{6,4},{7,5},{8,10},{9,11},{10,... | collective-permute-start | bytes 1179656 | tf_op jit(solution)/shard_map/ppermute | solution.py:360
  75.2 23.3 %collective-permute-start.16 = (bf16[128,1536]{1,0:T(8,128)(2,1)S(1)}, bf16[128,1536]{1,0:T(8,128)(2,1)}, u32[]{:S(2)}, u32[]{:S(2)}) collective-permute-start(bf16[128,1536]{1,0:T(8,128)(2,1)S(1)} %slice.76), channel_id=1, source_target_pairs={{0,1},{1,0},{2,3},{3,2},{4,5},{5,4},{6,7},{7,6},{8,9},{9,8},{10,11... | collective-permute-start | bytes 1179656 | tf_op jit(solution)/shard_map/ppermute | solution.py:360
  97.1 9.5 %collective-permute-start.9 = (bf16[96,3072]{1,0:T(8,128)(2,1)S(1)}, bf16[96,3072]{1,0:T(8,128)(2,1)}, u32[]{:S(2)}, u32[]{:S(2)}) collective-permute-start(bf16[96,3072]{1,0:T(8,128)(2,1)S(1)} %broadcast_select_fusion), channel_id=1, source_target_pairs={{8,16},{10,2},{12,20},{14,6},{17,25},{19,11},{21,29},{23,15}} | collective-permute-start | bytes 1769480 | tf_op jit(solution)/shard_map/ppermute | solution.py:360
  103.8 4.3 %collective-permute-start.25 = (bf16[4,48,1536]{2,1,0:T(8,128)(2,1)}, bf16[4,48,1536]{2,1,0:T(8,128)(2,1)S(1)}, u32[]{:S(2)}, u32[]{:S(2)}) collective-permute-start(bf16[4,48,1536]{2,1,0:T(8,128)(2,1)} %get-tuple-element.68), channel_id=1, source_target_pairs={{0,4},{1,5},{2,6},{3,7},{4,0},{5,1},{6,2},{7,3},{8,12},{9,13},{10,... | collective-permute-start | bytes 1769480 | tf_op jit(solution)/shard_map/ppermute | solution.py:360
  103.8 21.6 %collective-permute-start.6 = (bf16[96,3072]{1,0:T(8,128)(2,1)}, bf16[96,3072]{1,0:T(8,128)(2,1)}, u32[]{:S(2)}, u32[]{:S(2)}) collective-permute-start(bf16[96,3072]{1,0:T(8,128)(2,1)} %collective-permute-done.5), channel_id=1, source_target_pairs={{11,3},{15,7},{16,24},{20,28}} | collective-permute-start | bytes 1769480 | tf_op jit(solution)/shard_map/ppermute | solution.py:360
  105.5 11.4 %collective-permute-start.19 = (bf16[128,1536]{1,0:T(8,128)(2,1)S(1)}, bf16[128,1536]{1,0:T(8,128)(2,1)S(1)}, u32[]{:S(2)}, u32[]{:S(2)}) collective-permute-start(bf16[128,1536]{1,0:T(8,128)(2,1)S(1)} %slice.78), channel_id=1, source_target_pairs={{0,2},{1,3},{2,0},{3,1},{4,6},{5,7},{6,4},{7,5},{8,10},{9,11},{10,... | collective-permute-start | bytes 1179656 | tf_op jit(solution)/shard_map/ppermute | solution.py:360
  105.7 12.1 %collective-permute-start.20 = (bf16[128,1536]{1,0:T(8,128)(2,1)S(1)}, bf16[128,1536]{1,0:T(8,128)(2,1)S(1)}, u32[]{:S(2)}, u32[]{:S(2)}) collective-permute-start(bf16[128,1536]{1,0:T(8,128)(2,1)S(1)} %slice.79), channel_id=1, source_target_pairs={{0,1},{1,0},{2,3},{3,2},{4,5},{5,4},{6,7},{7,6},{8,9},{9,8},{10,11... | collective-permute-start | bytes 1179656 | tf_op jit(solution)/shard_map/ppermute | solution.py:360
  106.6 18.8 %collective-permute-start.10 = (bf16[96,3072]{1,0:T(8,128)(2,1)}, bf16[96,3072]{1,0:T(8,128)(2,1)}, u32[]{:S(2)}, u32[]{:S(2)}) collective-permute-start(bf16[96,3072]{1,0:T(8,128)(2,1)} %collective-permute-done.9), channel_id=1, source_target_pairs={{11,3},{15,7},{16,24},{20,28}} | collective-permute-start | bytes 1769480 | tf_op jit(solution)/shard_map/ppermute | solution.py:360
  108.9 16.3 %collective-permute-start.26 = (bf16[48,1536]{1,0:T(8,128)(2,1)}, bf16[48,1536]{1,0:T(8,128)(2,1)S(1)}, u32[]{:S(2)}, u32[]{:S(2)}) collective-permute-start(bf16[48,1536]{1,0:T(8,128)(2,1)} %get-tuple-element.100), channel_id=1, source_target_pairs={{0,1},{1,0},{2,3},{3,2},{4,5},{5,4},{6,7},{7,6},{8,9},{9,8},{10,11... | collective-permute-start | bytes 442376 | tf_op jit(solution)/shard_map/ppermute | solution.py:360
  116.9 8.4 %collective-permute-start.27 = (bf16[48,1536]{1,0:T(8,128)(2,1)S(1)}, bf16[48,1536]{1,0:T(8,128)(2,1)S(1)}, u32[]{:S(2)}, u32[]{:S(2)}) collective-permute-start(bf16[48,1536]{1,0:T(8,128)(2,1)S(1)} %get-tuple-element.99), channel_id=1, source_target_pairs={{0,2},{1,3},{2,0},{3,1},{4,6},{5,7},{6,4},{7,5},{8,10},{9,11},{10,... | collective-permute-start | bytes 442376 | tf_op jit(solution)/shard_map/ppermute | solution.py:360
  117.8 7.6 %collective-permute-start.28 = (bf16[48,1536]{1,0:T(8,128)(2,1)S(1)}, bf16[48,1536]{1,0:T(8,128)(2,1)S(1)}, u32[]{:S(2)}, u32[]{:S(2)}) collective-permute-start(bf16[48,1536]{1,0:T(8,128)(2,1)S(1)} %get-tuple-element.98), channel_id=1, source_target_pairs={{0,3},{1,2},{2,1},{3,0},{4,7},{5,6},{6,5},{7,4},{8,11},{9,10},{10,... | collective-permute-start | bytes 442376 | tf_op jit(solution)/shard_map/ppermute | solution.py:360
  125.1 17.8 %collective-permute-start.24 = (bf16[4,48,1536]{2,1,0:T(8,128)(2,1)}, bf16[4,48,1536]{2,1,0:T(8,128)(2,1)S(1)}, u32[]{:S(2)}, u32[]{:S(2)}) collective-permute-start(bf16[4,48,1536]{2,1,0:T(8,128)(2,1)} %get-tuple-element.66), channel_id=1, source_target_pairs={{0,4},{1,5},{2,6},{3,7},{4,0},{5,1},{6,2},{7,3},{8,12},{9,13},{10,... | collective-permute-start | bytes 1769480 | tf_op jit(solution)/shard_map/ppermute | solution.py:360
  126.7 20.6 %copy-start.6 = (bf16[96,3072]{1,0:T(8,128)(2,1)}, bf16[96,3072]{1,0:T(8,128)(2,1)S(1)}, u32[]{:S(2)}) copy-start(bf16[96,3072]{1,0:T(8,128)(2,1)S(1)} %get-tuple-element.102.refs_1_) | copy-start | bytes 1769476
  126.7 20.6 %copy-start.7 = (bf16[96,3072]{1,0:T(8,128)(2,1)}, bf16[96,3072]{1,0:T(8,128)(2,1)S(1)}, u32[]{:S(2)}) copy-start(bf16[96,3072]{1,0:T(8,128)(2,1)S(1)} %get-tuple-element.103.refs_0_) | copy-start | bytes 1769476
  126.7 16.3 %copy-start.13 = (bf16[4,48,1536]{2,1,0:T(8,128)(2,1)S(1)}, bf16[4,48,1536]{2,1,0:T(8,128)(2,1)}, u32[]{:S(2)}) copy-start(bf16[4,48,1536]{2,1,0:T(8,128)(2,1)} %get-tuple-element.73) | copy-start | bytes 1769476
  126.7 17.1 %collective-permute-start.11 = (bf16[96,3072]{1,0:T(8,128)(2,1)S(1)}, bf16[96,3072]{1,0:T(8,128)(2,1)S(1)}, u32[]{:S(2)}, u32[]{:S(2)}) collective-permute-start(bf16[96,3072]{1,0:T(8,128)(2,1)S(1)} %get-tuple-element.103.refs_0_), channel_id=1, source_target_pairs={{0,4},{1,5},{2,6},{3,7},{4,0},{5,1},{6,2},{7,3},{8,12},{9,13},{10,... | collective-permute-start | bytes 1769480 | tf_op jit(solution)/shard_map/ppermute | solution.py:360
  126.8 17.1 %collective-permute-start.12 = (bf16[96,3072]{1,0:T(8,128)(2,1)S(1)}, bf16[96,3072]{1,0:T(8,128)(2,1)S(1)}, u32[]{:S(2)}, u32[]{:S(2)}) collective-permute-start(bf16[96,3072]{1,0:T(8,128)(2,1)S(1)} %get-tuple-element.102.refs_1_), channel_id=1, source_target_pairs={{0,4},{1,5},{2,6},{3,7},{4,0},{5,1},{6,2},{7,3},{8,12},{9,13},{10,... | collective-permute-start | bytes 1769480 | tf_op jit(solution)/shard_map/ppermute | solution.py:360
  127.3 35.2 %collective-permute-start.35 = (bf16[48,1536]{1,0:T(8,128)(2,1)S(1)}, bf16[48,1536]{1,0:T(8,128)(2,1)}, u32[]{:S(2)}, u32[]{:S(2)}) collective-permute-start(bf16[48,1536]{1,0:T(8,128)(2,1)S(1)} %get-tuple-element.112), channel_id=1, source_target_pairs={{0,8},{1,9},{2,10},{3,11},{4,12},{5,13},{6,14},{7,15},{8,16},{9,17... | collective-permute-start | bytes 442376 | tf_op jit(solution)/shard_map/ppermute | solution.py:360
  133.3 29.2 %collective-permute-start.36 = (bf16[48,1536]{1,0:T(8,128)(2,1)S(1)}, bf16[48,1536]{1,0:T(8,128)(2,1)}, u32[]{:S(2)}, u32[]{:S(2)}) collective-permute-start(bf16[48,1536]{1,0:T(8,128)(2,1)S(1)} %get-tuple-element.111), channel_id=1, source_target_pairs={{0,16},{1,17},{2,18},{3,19},{4,20},{5,21},{6,22},{7,23},{8,24},{9,... | collective-permute-start | bytes 442376 | tf_op jit(solution)/shard_map/ppermute | solution.py:360
  143.8 17.2 %collective-permute-start.29 = (bf16[48,1536]{1,0:T(8,128)(2,1)}, bf16[48,1536]{1,0:T(8,128)(2,1)S(1)}, u32[]{:S(2)}, u32[]{:S(2)}) collective-permute-start(bf16[48,1536]{1,0:T(8,128)(2,1)} %get-tuple-element.96), channel_id=1, source_target_pairs={{0,1},{1,0},{2,3},{3,2},{4,5},{5,4},{6,7},{7,6},{8,9},{9,8},{10,11... | collective-permute-start | bytes 442376 | tf_op jit(solution)/shard_map/ppermute | solution.py:360
  143.8 17.6 %collective-permute-start.30 = (bf16[48,1536]{1,0:T(8,128)(2,1)S(1)}, bf16[48,1536]{1,0:T(8,128)(2,1)}, u32[]{:S(2)}, u32[]{:S(2)}) collective-permute-start(bf16[48,1536]{1,0:T(8,128)(2,1)S(1)} %get-tuple-element.95), channel_id=1, source_target_pairs={{0,2},{1,3},{2,0},{3,1},{4,6},{5,7},{6,4},{7,5},{8,10},{9,11},{10,... | collective-permute-start | bytes 442376 | tf_op jit(solution)/shard_map/ppermute | solution.py:360
  143.9 17.5 %collective-permute-start.31 = (bf16[48,1536]{1,0:T(8,128)(2,1)S(1)}, bf16[48,1536]{1,0:T(8,128)(2,1)}, u32[]{:S(2)}, u32[]{:S(2)}) collective-permute-start(bf16[48,1536]{1,0:T(8,128)(2,1)S(1)} %get-tuple-element.94), channel_id=1, source_target_pairs={{0,3},{1,2},{2,1},{3,0},{4,7},{5,6},{6,5},{7,4},{8,11},{9,10},{10,... | collective-permute-start | bytes 442376 | tf_op jit(solution)/shard_map/ppermute | solution.py:360
  160.9 12.7 %copy-start.35 = (bf16[3,256,128]{2,1,0:T(8,128)(2,1)S(1)}, bf16[3,256,128]{2,1,0:T(8,128)(2,1)}, u32[]{:S(2)}) copy-start(bf16[3,256,128]{2,1,0:T(8,128)(2,1)} %get-tuple-element.62) | copy-start | bytes 589828
  160.9 5.2 %collective-permute-start.37 = (bf16[48,1536]{1,0:T(8,128)(2,1)S(1)}, bf16[48,1536]{1,0:T(8,128)(2,1)S(1)}, u32[]{:S(2)}, u32[]{:S(2)}) collective-permute-start(bf16[48,1536]{1,0:T(8,128)(2,1)S(1)} %get-tuple-element.110), channel_id=1, source_target_pairs={{0,24},{1,25},{2,26},{3,27},{4,28},{5,29},{6,30},{7,31},{8,0},{9,1... | collective-permute-start | bytes 442376 | tf_op jit(solution)/shard_map/ppermute | solution.py:360
  166.1 7.5 %collective-permute-start.41 = (bf16[48,1536]{1,0:T(8,128)(2,1)S(1)}, bf16[48,1536]{1,0:T(8,128)(2,1)S(1)}, u32[]{:S(2)}, u32[]{:S(2)}) collective-permute-start(bf16[48,1536]{1,0:T(8,128)(2,1)S(1)} %get-tuple-element.108), channel_id=1, source_target_pairs={{0,8},{1,9},{2,10},{3,11},{4,12},{5,13},{6,14},{7,15},{8,16},{9,17... | collective-permute-start | bytes 442376 | tf_op jit(solution)/shard_map/ppermute | solution.py:360
  166.2 10.9 %collective-permute-start.42 = (bf16[48,1536]{1,0:T(8,128)(2,1)S(1)}, bf16[48,1536]{1,0:T(8,128)(2,1)S(1)}, u32[]{:S(2)}, u32[]{:S(2)}) collective-permute-start(bf16[48,1536]{1,0:T(8,128)(2,1)S(1)} %get-tuple-element.107), channel_id=1, source_target_pairs={{0,16},{1,17},{2,18},{3,19},{4,20},{5,21},{6,22},{7,23},{8,24},{9,... | collective-permute-start | bytes 442376 | tf_op jit(solution)/shard_map/ppermute | solution.py:360
  170.1 16.9 %copy-start.16 = (bf16[48,1536]{1,0:T(8,128)(2,1)}, bf16[48,1536]{1,0:T(8,128)(2,1)S(1)}, u32[]{:S(2)}) copy-start(bf16[48,1536]{1,0:T(8,128)(2,1)S(1)} %add_convert_fusion.1.refs_8_) | copy-start | bytes 442372
  170.1 17.1 %collective-permute-start.38 = (bf16[48,1536]{1,0:T(8,128)(2,1)S(1)}, bf16[48,1536]{1,0:T(8,128)(2,1)S(1)}, u32[]{:S(2)}, u32[]{:S(2)}) collective-permute-start(bf16[48,1536]{1,0:T(8,128)(2,1)S(1)} %add_convert_fusion.1.refs_8_), channel_id=1, source_target_pairs={{0,1},{1,0},{2,3},{3,2},{4,5},{5,4},{6,7},{7,6},{8,9},{9,8},{10,11... | collective-permute-start | bytes 442376 | tf_op jit(solution)/shard_map/ppermute | solution.py:360
  170.2 18.5 %collective-permute-start.39 = (bf16[48,1536]{1,0:T(8,128)(2,1)S(1)}, bf16[48,1536]{1,0:T(8,128)(2,1)S(1)}, u32[]{:S(2)}, u32[]{:S(2)}) collective-permute-start(bf16[48,1536]{1,0:T(8,128)(2,1)S(1)} %add_convert_fusion.1.refs_8_), channel_id=1, source_target_pairs={{0,2},{1,3},{2,0},{3,1},{4,6},{5,7},{6,4},{7,5},{8,10},{9,11},{10,... | collective-permute-start | bytes 442376 | tf_op jit(solution)/shard_map/ppermute | solution.py:360
  171.5 19.2 %collective-permute-start.40 = (bf16[48,1536]{1,0:T(8,128)(2,1)S(1)}, bf16[48,1536]{1,0:T(8,128)(2,1)S(1)}, u32[]{:S(2)}, u32[]{:S(2)}) collective-permute-start(bf16[48,1536]{1,0:T(8,128)(2,1)S(1)} %add_convert_fusion.1.refs_8_), channel_id=1, source_target_pairs={{0,3},{1,2},{2,1},{3,0},{4,7},{5,6},{6,5},{7,4},{8,11},{9,10},{10,... | collective-permute-start | bytes 442376 | tf_op jit(solution)/shard_map/ppermute | solution.py:360
  173.6 17.1 %collective-permute-start.21 = (bf16[3,256,128]{2,1,0:T(8,128)(2,1)S(1)}, bf16[3,256,128]{2,1,0:T(8,128)(2,1)S(1)}, u32[]{:S(2)}, u32[]{:S(2)}) collective-permute-start(bf16[3,256,128]{2,1,0:T(8,128)(2,1)S(1)} %copy-done.35), channel_id=1, source_target_pairs={{0,1},{1,0},{2,3},{3,2},{4,5},{5,4},{6,7},{7,6},{8,9},{9,8},{10,11... | collective-permute-start | bytes 589832 | tf_op jit(solution)/shard_map/ppermute | solution.py:360
  177.1 9.9 %copy-start.34 = (bf16[3,256,128]{2,1,0:T(8,128)(2,1)S(1)}, bf16[3,256,128]{2,1,0:T(8,128)(2,1)}, u32[]{:S(2)}) copy-start(bf16[3,256,128]{2,1,0:T(8,128)(2,1)} %get-tuple-element.63) | copy-start | bytes 589828
  177.1 10.1 %copy-start.33 = (bf16[3,256,128]{2,1,0:T(8,128)(2,1)S(1)}, bf16[3,256,128]{2,1,0:T(8,128)(2,1)}, u32[]{:S(2)}) copy-start(bf16[3,256,128]{2,1,0:T(8,128)(2,1)} %get-tuple-element.64) | copy-start | bytes 589828
  177.1 9.9 %collective-permute-start.43 = (bf16[48,1536]{1,0:T(8,128)(2,1)S(1)}, bf16[48,1536]{1,0:T(8,128)(2,1)S(1)}, u32[]{:S(2)}, u32[]{:S(2)}) collective-permute-start(bf16[48,1536]{1,0:T(8,128)(2,1)S(1)} %get-tuple-element.106), channel_id=1, source_target_pairs={{0,24},{1,25},{2,26},{3,27},{4,28},{5,29},{6,30},{7,31},{8,0},{9,1... | collective-permute-start | bytes 442376 | tf_op jit(solution)/shard_map/ppermute | solution.py:360
  187.0 10.6 %collective-permute-start.22 = (bf16[3,256,128]{2,1,0:T(8,128)(2,1)S(1)}, bf16[3,256,128]{2,1,0:T(8,128)(2,1)S(1)}, u32[]{:S(2)}, u32[]{:S(2)}) collective-permute-start(bf16[3,256,128]{2,1,0:T(8,128)(2,1)S(1)} %copy-done.34), channel_id=1, source_target_pairs={{0,2},{1,3},{2,0},{3,1},{4,6},{5,7},{6,4},{7,5},{8,10},{9,11},{10,... | collective-permute-start | bytes 589832 | tf_op jit(solution)/shard_map/ppermute | solution.py:360
  187.2 32.1 %copy-start.27 = (bf16[48,1536]{1,0:T(8,128)(2,1)}, bf16[48,1536]{1,0:T(8,128)(2,1)S(1)}, u32[]{:S(2)}) copy-start(bf16[48,1536]{1,0:T(8,128)(2,1)S(1)} %collective-permute-done.38.refs_9_) | copy-start | bytes 442372
  187.2 11.7 %collective-permute-start.23 = (bf16[3,256,128]{2,1,0:T(8,128)(2,1)S(1)}, bf16[3,256,128]{2,1,0:T(8,128)(2,1)S(1)}, u32[]{:S(2)}, u32[]{:S(2)}) collective-permute-start(bf16[3,256,128]{2,1,0:T(8,128)(2,1)S(1)} %copy-done.33), channel_id=1, source_target_pairs={{0,3},{1,2},{2,1},{3,0},{4,7},{5,6},{6,5},{7,4},{8,11},{9,10},{10,... | collective-permute-start | bytes 589832 | tf_op jit(solution)/shard_map/ppermute | solution.py:360
  188.7 30.6 %copy-start.28 = (bf16[48,1536]{1,0:T(8,128)(2,1)}, bf16[48,1536]{1,0:T(8,128)(2,1)S(1)}, u32[]{:S(2)}) copy-start(bf16[48,1536]{1,0:T(8,128)(2,1)S(1)} %collective-permute-done.39.refs_10_) | copy-start | bytes 442372
  188.7 30.5 %collective-permute-start.32 = (bf16[3,256,256]{2,1,0:T(8,128)(2,1)}, bf16[3,256,256]{2,1,0:T(8,128)(2,1)S(1)}, u32[]{:S(2)}, u32[]{:S(2)}) collective-permute-start(bf16[3,256,256]{2,1,0:T(8,128)(2,1)} %get-tuple-element.81), channel_id=1, source_target_pairs={{0,1},{1,0},{2,3},{3,2},{4,5},{5,4},{6,7},{7,6},{8,9},{9,8},{10,11... | collective-permute-start | bytes 1179656 | tf_op jit(solution)/shard_map/ppermute | solution.py:360
  190.6 28.6 %copy-start.29 = (bf16[48,1536]{1,0:T(8,128)(2,1)}, bf16[48,1536]{1,0:T(8,128)(2,1)S(1)}, u32[]{:S(2)}) copy-start(bf16[48,1536]{1,0:T(8,128)(2,1)S(1)} %collective-permute-done.40.refs_11_) | copy-start | bytes 442372
  190.6 28.6 %collective-permute-start.33 = (bf16[3,256,256]{2,1,0:T(8,128)(2,1)}, bf16[3,256,256]{2,1,0:T(8,128)(2,1)S(1)}, u32[]{:S(2)}, u32[]{:S(2)}) collective-permute-start(bf16[3,256,256]{2,1,0:T(8,128)(2,1)} %get-tuple-element.82), channel_id=1, source_target_pairs={{0,2},{1,3},{2,0},{3,1},{4,6},{5,7},{6,4},{7,5},{8,10},{9,11},{10,... | collective-permute-start | bytes 1179656 | tf_op jit(solution)/shard_map/ppermute | solution.py:360
  190.7 28.5 %copy-start.24 = (bf16[3,256,128]{2,1,0:T(8,128)(2,1)}, bf16[3,256,128]{2,1,0:T(8,128)(2,1)S(1)}, u32[]{:S(2)}) copy-start(bf16[3,256,128]{2,1,0:T(8,128)(2,1)S(1)} %collective-permute-done.21.refs_1_) | copy-start | bytes 589828
  190.7 28.5 %collective-permute-start.34 = (bf16[3,256,256]{2,1,0:T(8,128)(2,1)}, bf16[3,256,256]{2,1,0:T(8,128)(2,1)S(1)}, u32[]{:S(2)}, u32[]{:S(2)}) collective-permute-start(bf16[3,256,256]{2,1,0:T(8,128)(2,1)} %get-tuple-element.83), channel_id=1, source_target_pairs={{0,3},{1,2},{2,1},{3,0},{4,7},{5,6},{6,5},{7,4},{8,11},{9,10},{10,... | collective-permute-start | bytes 1179656 | tf_op jit(solution)/shard_map/ppermute | solution.py:360
  192.3 27.0 %copy-start.17 = (bf16[48,1536]{1,0:T(8,128)(2,1)}, bf16[48,1536]{1,0:T(8,128)(2,1)S(1)}, u32[]{:S(2)}) copy-start(bf16[48,1536]{1,0:T(8,128)(2,1)S(1)} %add_convert_fusion.refs_12_) | copy-start | bytes 442372
  197.6 21.7 %copy-start.25 = (bf16[3,256,128]{2,1,0:T(8,128)(2,1)}, bf16[3,256,128]{2,1,0:T(8,128)(2,1)S(1)}, u32[]{:S(2)}) copy-start(bf16[3,256,128]{2,1,0:T(8,128)(2,1)S(1)} %collective-permute-done.22.refs_2_) | copy-start | bytes 589828
  197.6 15.6 %collective-permute-start.44 = (bf16[48,1536]{1,0:T(8,128)(2,1)S(1)}, bf16[48,1536]{1,0:T(8,128)(2,1)S(1)}, u32[]{:S(2)}, u32[]{:S(2)}) collective-permute-start(bf16[48,1536]{1,0:T(8,128)(2,1)S(1)} %add_convert_fusion.refs_12_), channel_id=1, source_target_pairs={{0,1},{1,0},{2,3},{3,2},{4,5},{5,4},{6,7},{7,6},{8,9},{9,8},{10,11... | collective-permute-start | bytes 442376 | tf_op jit(solution)/shard_map/ppermute | solution.py:360
  198.8 20.5 %copy-start.26 = (bf16[3,256,128]{2,1,0:T(8,128)(2,1)}, bf16[3,256,128]{2,1,0:T(8,128)(2,1)S(1)}, u32[]{:S(2)}) copy-start(bf16[3,256,128]{2,1,0:T(8,128)(2,1)S(1)} %collective-permute-done.23.refs_3_) | copy-start | bytes 589828
  198.8 18.8 %collective-permute-start.45 = (bf16[48,1536]{1,0:T(8,128)(2,1)S(1)}, bf16[48,1536]{1,0:T(8,128)(2,1)S(1)}, u32[]{:S(2)}, u32[]{:S(2)}) collective-permute-start(bf16[48,1536]{1,0:T(8,128)(2,1)S(1)} %add_convert_fusion.refs_12_), channel_id=1, source_target_pairs={{0,2},{1,3},{2,0},{3,1},{4,6},{5,7},{6,4},{7,5},{8,10},{9,11},{10,... | collective-permute-start | bytes 442376 | tf_op jit(solution)/shard_map/ppermute | solution.py:360
  213.2 6.0 %collective-permute-start.46 = (bf16[48,1536]{1,0:T(8,128)(2,1)S(1)}, bf16[48,1536]{1,0:T(8,128)(2,1)S(1)}, u32[]{:S(2)}, u32[]{:S(2)}) collective-permute-start(bf16[48,1536]{1,0:T(8,128)(2,1)S(1)} %add_convert_fusion.refs_12_), channel_id=1, source_target_pairs={{0,3},{1,2},{2,1},{3,0},{4,7},{5,6},{6,5},{7,4},{8,11},{9,10},{10,... | collective-permute-start | bytes 442376 | tf_op jit(solution)/shard_map/ppermute | solution.py:360
  (19 other events, 50.9 us)

commit v6 on v5

--- a/solution.py
+++ b/solution.py
@@ -245,57 +245,53 @@
     return jnp.concatenate([ref[...] for ref in refs], axis=0)
 
 
-def project(place, weights, grads):
-    chunks, count = len(grads), len(grads[0])
-    half, depth = weights[0].shape
-    half = half * len(weights) // 2
-    step = grads[0][0].shape[1] // 2
+def project(place, weights, grads, chunk, before=None):
+    half = sum(part.shape[0] for part in weights) // 2
+    step = grads[0].shape[1] // 2
+    parts, count = len(weights), len(grads)
+    shape = (2 * half, sum(block.shape[0] for block in grads))
 
     def body(place_ref, *refs):
-        ins, out, total = refs[len(weights) : -2], refs[-2], refs[-1]
+        ins = refs[parts : parts + count]
+        out, total = refs[-2:]
         at = pl.program_id(0)
-        lines = stacked(refs[: len(weights)])
-        for chunk in range(chunks):
-
-            @pl.when(at // 2 == chunk)
-            def _():
-                term = dot(lines, stacked(ins[chunk * count : (chunk + 1) * count]), NT)
-                if chunk:
-                    total[...] += term
-                else:
-                    total[...] = jnp.where(at == 0, 0.0, total[...]) + term
-
-        @pl.when(at == chunks * 2 - 1)
+        start = pl.multiple_of((2 * chunk + at) * step, HDIM)
+        lines = jnp.concatenate([ref[:, pl.ds(start, step)] for ref in refs[:parts]], axis=0)
+        term = dot(lines, stacked(ins), NT)
+
+        @pl.when(at == 0)
         def _():
+            total[...] = term
+
+        @pl.when(at == 1)
+        def _():
+            if before is None:
+                out[...] = total[...] + term
+                return
+            whole_sum = (refs[parts + count][...] + total[...] + term).astype(out.dtype)
             for core in range(2):
 
                 @pl.when(place_ref[2] == core)
                 def _():
-                    out[core * half : (core + 1) * half] = total[:half].astype(out.dtype)
-                    out[(1 - core) * half : (2 - core) * half] = total[half:].astype(out.dtype)
-
-    def block_of(chunk, block):
-        return pl.BlockSpec(
-            (block.shape[0], step), lambda i, place_ref: (0, jnp.clip(i - chunk * 2, 0, 1))
-        )
-
-    shape = (2 * half, sum(block.shape[0] for block in grads[0]))
+                    out[core * half : (core + 1) * half] = whole_sum[:half]
+                    out[(1 - core) * half : (2 - core) * half] = whole_sum[half:]
+
+    more = [] if before is None else [before]
     return pl.pallas_call(
         body,
         grid_spec=pltpu.PrefetchScalarGridSpec(
             num_scalar_prefetch=1,
-            grid=(chunks * 2,),
-            in_specs=[
-                pl.BlockSpec((part.shape[0], step), lambda i, place_ref: (0, i)) for part in weights
-            ]
-            + [block_of(chunk, block) for chunk in range(chunks) for block in grads[chunk]],
+            grid=(2,),
+            in_specs=[pl.BlockSpec(memory_space=pltpu.VMEM)] * parts
+            + [pl.BlockSpec((block.shape[0], step), lambda i, place_ref: (0, i)) for block in grads]
+            + [whole(shape) for _ in more],
             out_specs=whole(shape),
             scratch_shapes=[pltpu.VMEM(shape, jnp.float32)],
         ),
-        out_shape=jax.ShapeDtypeStruct(shape, jnp.bfloat16),
-        cost_estimate=cost(2 * shape[0] * shape[1] * depth, 2 * depth * (shape[0] + shape[1])),
+        out_shape=jax.ShapeDtypeStruct(shape, jnp.bfloat16 if more else jnp.float32),
+        cost_estimate=cost(4 * shape[0] * shape[1] * step, 4 * step * (shape[0] + shape[1])),
         name="project",
-    )(place, *weights, *(block for chunk in grads for block in chunk))
+    )(place, *weights, *grads, *more)
 
 
 def weight_terms(place, attended, grads, rows):
@@ -365,8 +361,8 @@
     def to_core(array):
         return send(array, lambda z, c, r: (z, 1 - c, r))
 
-    def to_plane(array, ahead):
-        return send(array, lambda z, c, r: ((z + ahead) % planes, c, r))
+    def to_plane(array, turn):
+        return send(array, lambda z, c, r: (z ^ turn, c, r))
 
     grad_flat = grad_out[0]
     wide = grad_flat.shape[1] // 2
@@ -376,11 +372,10 @@
         by_x, by_y = after((by_x, by_y), *done)
         cut = chunk.shape[0] // 2
         upper, lower = by_x[:cut], by_y[cut:]
-        upper = to_row(upper, 2)
-        lower = to_row(lower, 1)
-        return [chunk, by_x, by_y, upper, lower]
-
-    grads = [gather(grad_flat[:, :wide])]
+        by_both = [to_row(upper, 2), to_row(lower, 1)]
+        return [chunk, by_x, by_y, *by_both], (upper, lower)
+
+    grads = [gather(grad_flat[:, :wide])[0]]
 
     away = jnp.abs(plane - row)
     cut = w_out.shape[0] // 2
@@ -412,9 +407,11 @@
             here = jnp.where(away == hop, stages[hop], here)
         return here
 
+    block, handed = gather(after(grad_flat[:, wide:], parts), attended)
+    grads.append(block)
+    first[-1], second[-1] = after((first[-1], second[-1]), handed)
     weights = [mine(first), mine(second)]
     weights += [to_core(part) for part in weights]
-    grads.append(gather(after(grad_flat[:, wide:], parts), attended))
 
     def reduce_cores(attended, chunk):
         keep, give = weight_terms(place, attended, chunk, rows)
@@ -428,12 +425,10 @@
         return [both[0]] + [to_row(both[slot], slot) for slot in range(1, rows)]
 
     def reduce_planes(blocks):
-        stack = jnp.stack(blocks)
-
-        def block_of(ahead):
-            return lax.dynamic_index_in_dim(stack, ((plane + ahead) % planes) ^ row, 0, False)
-
-        return block_of(0), [to_plane(block_of(ahead), ahead) for ahead in range(1, planes)]
+        picked = [
+            lax.select_n((plane ^ turn) ^ row, *blocks) for turn in range(planes)
+        ]
+        return picked[0], [to_plane(picked[turn], turn) for turn in range(1, planes)]
 
     def collect(total, got):
         for part in got:
@@ -444,19 +439,13 @@
     blocks = spread(*reduce_cores(attended, grads[0]))
     late = reduce_cores(attended, grads[1])
     early = reduce_planes(after(blocks, late[0]))
-    grad_attn = project(place, weights, grads)
-    heads = probs.shape[0]
-    blocks = spread(*after(late, early[0]))
-    sent = [backward(parts, probs, grad_attn, 0, 1)]
-    late = reduce_planes(after(blocks, sent[0][0]))
-    sent.append(backward(parts, after(probs, late[0]), grad_attn, 1, heads - 1))
-    back = [
-        [message[0]]
-        + [to_row(message[slot], slot) for slot in range(1, rows)]
-        for message in sent
-    ]
-    pieces = [collect(*after(early, sent[0][0])), collect(*after(late, sent[1][0]))]
-    return tuple(finish(place, back, pieces))
+    grad_attn = project(place, weights, grads[0], 0)
+    grad_attn = project(place, weights, grads[1], 1, grad_attn)
+    sent = backward(parts, probs, grad_attn, 0, probs.shape[0])
+    back = [sent[0]] + [to_row(sent[slot], slot) for slot in range(1, rows)]
+    late = reduce_planes(after(spread(*after(late, early[0])), sent[0]))
+    pieces = [collect(*after(early, sent[0])), collect(*late)]
+    return tuple(finish(place, [back], pieces))
 
 
 def by_tokens(query_rows, key_rows, value_rows, grad_out, w_out):

time: 227 us -> 233 us (1.026)
  waiting for transfers between devices: 89.4 us -> 98.1 us
  starting transfers between devices: 66.1 us -> 60.8 us
    ppermute x47 -> x44, waiting for transfers between devices: 89.4 us -> 98.1 us  [send(): return lax.ppermute(array, ('fsdp', 'rows'), pairs)]
    ppermute x47 -> x44, starting transfers between devices: 66.1 us -> 60.8 us  [send(): return lax.ppermute(array, ('fsdp', 'rows'), pairs)]
    pallas_call x1 -> x2, Pallas kernels: 8.01 us -> 12.5 us  [project(): pl.pallas_call(body, grid_spec=pltpu.PrefetchScalarGridSpec(num_scalar_pr...]
    pallas_call x2 -> x1, Pallas kernels: 14.1 us -> 11.4 us  [backward(): pl.pallas_call(body, grid=(count,), in_specs=[part] * rows + [pl.BlockSpe...]
  transfers between devices with their start and end apart: 47 -> 44, of which waited for: 13 -> 12; matrix products, arithmetic and copies ran while one was open for 5% -> 4% of each run, Pallas kernels for 21% -> 22%
where the time goes in v6:
time: 233 us; the launch traced here: 232 us
  waiting for transfers between devices  98.1 us (42%)
  starting transfers between devices  60.8 us (26%)
  Pallas kernels  54.7 us (23%)
  local copies, waits for them, and re-layouts  9.25 us (4%)
  other arithmetic  7.98 us (3%)
    ppermute x44, waiting for transfers between devices, send(): return lax.ppermute(array, ('fsdp', 'rows'), pairs)  98.1 us
    ppermute x44, starting transfers between devices, send(): return lax.ppermute(array, ('fsdp', 'rows'), pairs)  60.8 us
    pallas_call x1, Pallas kernels, forward(): pl.pallas_call(body, grid=(heads,), in_specs=[part] * rows, out_specs=[pl...  12.6 us
    pallas_call x2, Pallas kernels, project(): pl.pallas_call(body, grid_spec=pltpu.PrefetchScalarGridSpec(num_scalar_pr...  12.5 us
    pallas_call x1, Pallas kernels, backward(): pl.pallas_call(body, grid=(count,), in_specs=[part] * rows + [pl.BlockSpe...  11.4 us
    pallas_call x2, Pallas kernels, weight_terms(): pl.pallas_call(body, grid_spec=pltpu.PrefetchScalarGridSpec(num_scalar_pr...  10.5 us
  transfers between devices with their start and end apart: 44, of which 12 were waited for; matrix products, arithmetic and copies ran while one was open for 4% of the time, Pallas kernels for 22%

profile of v6, /device:TPU:0, one launch (start us, length us, event | category | flops | bytes accessed | tf_op | source)
XLA Modules:
  0.0 232.1 jit_solution(1985931824451635853)
XLA Ops:
  0.6 2.5 %fusion.9 = (bf16[96,3072]{1,0:T(8,128)(2,1)}, bf16[96,3072]{1,0:T(8,128)(2,1)}) fusion(bf16[192,3072]{1,0:T(8,128)(2,1)} %param.9), kind=kLoop, calls=%fused_computation.31 | loop fusion | bytes 2359296 | tf_op jit(solution)/shard_map/slice | solution.py:394
  3.1 5.8 %collective-permute-start.3 = (bf16[96,3072]{1,0:T(8,128)(2,1)}, bf16[96,3072]{1,0:T(8,128)(2,1)}, u32[]{:S(2)}, u32[]{:S(2)}) collective-permute-start(bf16[96,3072]{1,0:T(8,128)(2,1)} %get-tuple-element.91), channel_id=1, source_target_pairs={{0,8},{4,12},{9,17},{13,21},{18,26},{22,30}} | collective-permute-start | bytes 1769480 | tf_op jit(solution)/shard_map/ppermute | solution.py:356
  8.9 1.5 collective-permute-start.4
  10.7 0.8 pad_add_fusion.place_ref
  11.5 3.3 %pack.1 = (bf16[3,256,384]{2,1,0:T(8,128)(2,1)}, bf16[3,256,384]{2,1,0:T(8,128)(2,1)}, bf16[3,256,384]{2,1,0:T(8,128)(2,1)}, bf16[3,256,384]{2,1,0:T(8,128)(2,1)}) custom-call(s32[3]{0:T(128)} %pad_add_fusion.place_ref, bf16[1,256,1536]{2,1,0:T(8,128)(2,1)} %refs_0_.1, bf16[1,256,1536]{2,1,0:T(8,128)(2,1)} %refs_1_.1, bf16[1,256,1536]{2,1,0:T(8,128)(2,1)} %refs_2_.1), custom_call_target="tpu_custom_call" | custom-call | bytes 4718592 | tf_op jit(solution)/shard_map/pack/pallas_call | solution.py:52
  14.8 1.7 collective-permute-start
  16.5 4.4 %collective-permute-done.3 = bf16[96,3072]{1,0:T(8,128)(2,1)} collective-permute-done((bf16[96,3072]{1,0:T(8,128)(2,1)}, bf16[96,3072]{1,0:T(8,128)(2,1)}, u32[]{:S(2)}, u32[]{:S(2)}) %collective-permute-start.3) | collective-permute-done | bytes 589856 | tf_op jit(solution)/shard_map/ppermute | solution.py:356
  21.0 1.1 broadcast_select_fusion.1
  22.1 21.6 %collective-permute-done.refs_1_ = bf16[3,256,384]{2,1,0:T(8,128)(2,1)} collective-permute-done((bf16[3,256,384]{2,1,0:T(8,128)(2,1)}, bf16[3,256,384]{2,1,0:T(8,128)(2,1)}, u32[]{:S(2)}, u32[]{:S(2)}) %collective-permute-start) | collective-permute-done | bytes 589856 | tf_op jit(solution)/shard_map/ppermute | solution.py:356
  43.7 4.4 %collective-permute-start.7 = (bf16[96,3072]{1,0:T(8,128)(2,1)}, bf16[96,3072]{1,0:T(8,128)(2,1)}, u32[]{:S(2)}, u32[]{:S(2)}) collective-permute-start(bf16[96,3072]{1,0:T(8,128)(2,1)} %get-tuple-element.46), channel_id=1, source_target_pairs={{0,8},{4,12},{9,17},{13,21},{18,26},{22,30}} | collective-permute-start | bytes 1769480 | tf_op jit(solution)/shard_map/ppermute | solution.py:356
  48.1 6.8 %collective-permute-done.1.refs_2_ = bf16[3,256,384]{2,1,0:T(8,128)(2,1)S(1)} collective-permute-done((bf16[3,256,384]{2,1,0:T(8,128)(2,1)}, bf16[3,256,384]{2,1,0:T(8,128)(2,1)S(1)}, u32[]{:S(2)}, u32[]{:S(2)}) %collective-permute-start.1) | collective-permute-done | bytes 589856 | tf_op jit(solution)/shard_map/ppermute | solution.py:356
  54.9 1.5 collective-permute-start.8
  56.4 0.8 copy-done.32
  57.2 1.5 collective-permute-start.5
  58.7 12.6 %forward.1 = (bf16[3,1024,1024]{2,1,0:T(8,128)(2,1)}, bf16[384,1024]{1,0:T(8,128)(2,1)}) custom-call(bf16[3,256,384]{2,1,0:T(8,128)(2,1)} %get-tuple-element.41.refs_0_, bf16[3,256,384]{2,1,0:T(8,128)(2,1)} %collective-permute-done.refs_1_, bf16[3,256,384]{2,1,0:T(8,128)(2,1)} %copy-done.31, bf16[3,256,384]{2,1,0:T(8,128)(2,1)} %copy-done.32), custom_call_target="tpu_custom_call" | custom-call | flops 3221225472 | bytes 6291456 | tf_op jit(solution)/shard_map/forward/pallas_call | solution.py:179
  71.3 1.6 collective-permute-start.11
  72.9 0.5 collective-permute-start.12
  73.4 1.0 slice.79
  74.4 1.6 collective-permute-start.19
  76.0 0.5 collective-permute-start.20
  76.6 1.1 broadcast_select_fusion
  77.7 21.2 %collective-permute-done.19.refs_7_.refs_3_ = bf16[128,1536]{1,0:T(8,128)(2,1)S(1)} collective-permute-done((bf16[128,1536]{1,0:T(8,128)(2,1)S(1)}, bf16[128,1536]{1,0:T(8,128)(2,1)S(1)}, u32[]{:S(2)}, u32[]{:S(2)}) %collective-permute-start.19) | collective-permute-done | bytes 393248 | tf_op jit(solution)/shard_map/ppermute | solution.py:356
  98.9 0.7 copy-done.20
  99.6 1.5 collective-permute-start.9
  101.1 5.2 %weight_terms.2 = (bf16[4,48,1536]{2,1,0:T(8,128)(2,1)}, bf16[4,48,1536]{2,1,0:T(8,128)(2,1)}) custom-call(s32[3]{0:T(128)} %pad_add_fusion.place_ref, bf16[384,1024]{1,0:T(8,128)(2,1)} %get-tuple-element.47.attended_ref, bf16[256,1536]{1,0:T(8,128)(2,1)} %copy-done.3, bf16[256,1536]{1,0:T(8,128)(2,1)} %copy-done.9, ...), custom_call_target="tpu_custom_call" | custom-call | flops 1207959552 | bytes 3932160 | tf_op jit(solution)/shard_map/weight_terms/pallas_call | solution.py:317
  106.4 1.6 collective-permute-start.6
  108.0 1.3 slice.75
  109.5 0.9 collective-permute-start.16
  110.4 1.5 collective-permute-start.10
  111.8 0.9 fusion.3
  112.7 1.1 collective-permute-start.25
  113.9 6.9 %collective-permute-done.15.refs_7_.refs_3_ = bf16[128,1536]{1,0:T(8,128)(2,1)S(1)} collective-permute-done((bf16[128,1536]{1,0:T(8,128)(2,1)S(1)}, bf16[128,1536]{1,0:T(8,128)(2,1)S(1)}, u32[]{:S(2)}, u32[]{:S(2)}) %collective-permute-start.15) | collective-permute-done | bytes 393248 | tf_op jit(solution)/shard_map/ppermute | solution.py:356
  121.0 0.4 collective-permute-done.16.refs_8_.refs_4_
  121.5 2.2 collective-permute-start.27
  123.7 5.3 %weight_terms.3 = (bf16[4,48,1536]{2,1,0:T(8,128)(2,1)}, bf16[4,48,1536]{2,1,0:T(8,128)(2,1)}) custom-call(s32[3]{0:T(128)} %pad_add_fusion.place_ref, bf16[384,1024]{1,0:T(8,128)(2,1)} %get-tuple-element.47.attended_ref, bf16[256,1536]{1,0:T(8,128)(2,1)} %copy-done.4, bf16[256,1536]{1,0:T(8,128)(2,1)} %collective-permute-done.11.refs_5_.refs_1_, ...), custom_call_target="tpu_custom_call" | custom-call | flops 1207959552 | bytes 3932160 | tf_op jit(solution)/shard_map/weight_terms/pallas_call | solution.py:317
  129.1 0.4 collective-permute-done.26
  129.5 0.7 copy-done.23
  130.6 0.4 collective-permute-start.14
  131.1 1.7 select_select_fusion.5
  132.8 5.5 %collective-permute-start.28 = (bf16[48,1536]{1,0:T(8,128)(2,1)}, bf16[48,1536]{1,0:T(8,128)(2,1)}, u32[]{:S(2)}, u32[]{:S(2)}) collective-permute-start(bf16[48,1536]{1,0:T(8,128)(2,1)} %get-tuple-element.97), channel_id=1, source_target_pairs={{0,8},{1,9},{2,10},{3,11},{4,12},{5,13},{6,14},{7,15},{8,0},{9,1},... | collective-permute-start | bytes 442376 | tf_op jit(solution)/shard_map/ppermute | solution.py:356
  138.3 8.7 %collective-permute-start.29 = (bf16[48,1536]{1,0:T(8,128)(2,1)S(1)}, bf16[48,1536]{1,0:T(8,128)(2,1)}, u32[]{:S(2)}, u32[]{:S(2)}) collective-permute-start(bf16[48,1536]{1,0:T(8,128)(2,1)S(1)} %get-tuple-element.96), channel_id=1, source_target_pairs={{0,16},{1,17},{2,18},{3,19},{4,20},{5,21},{6,22},{7,23},{8,24},{9,... | collective-permute-start | bytes 442376 | tf_op jit(solution)/shard_map/ppermute | solution.py:356
  147.0 0.8 fusion.7
  147.8 0.9 collective-permute-start.36
  148.8 6.0 %project.2.refs_9_ = f32[384,1024]{1,0:T(8,128)} custom-call(s32[3]{0:T(128)} %pad_add_fusion.place_ref, bf16[96,3072]{1,0:T(8,128)(2,1)} %copy-done.1, bf16[96,3072]{1,0:T(8,128)(2,1)} %copy-done, bf16[96,3072]{1,0:T(8,128)(2,1)} %copy-done.7, bf16[96,3072]{1,0:T(8,128)(2,1)} %copy-done.8, bf16[256,1536]{1,0:T(8,128)(2,1)} %copy-done.3, ...), custom_call_target="tpu_custom_call" | custom-call | flops 1207959552 | bytes 4325376 | tf_op jit(solution)/shard_map/project/pallas_call | solution.py:280
  154.8 6.5 %project.3.refs_5_ = bf16[384,1024]{1,0:T(8,128)(2,1)} custom-call(s32[3]{0:T(128)} %pad_add_fusion.place_ref, bf16[96,3072]{1,0:T(8,128)(2,1)} %copy-done.1, bf16[96,3072]{1,0:T(8,128)(2,1)} %copy-done, bf16[96,3072]{1,0:T(8,128)(2,1)} %copy-done.7, bf16[96,3072]{1,0:T(8,128)(2,1)} %copy-done.8, bf16[256,1536]{1,0:T(8,128)(2,1)} %copy-done.4, ...), custom_call_target="tpu_custom_call" | custom-call | flops 1207959552 | bytes 4325376 | tf_op jit(solution)/shard_map/project/pallas_call | solution.py:280
  161.3 2.6 %collective-permute-start.37 = (bf16[48,1536]{1,0:T(8,128)(2,1)S(1)}, bf16[48,1536]{1,0:T(8,128)(2,1)S(1)}, u32[]{:S(2)}, u32[]{:S(2)}) collective-permute-start(bf16[48,1536]{1,0:T(8,128)(2,1)S(1)} %get-tuple-element.80), channel_id=1, source_target_pairs={{0,3},{1,2},{2,1},{3,0},{4,7},{5,6},{6,5},{7,4},{8,11},{9,10},{10,... | collective-permute-start | bytes 442376 | tf_op jit(solution)/shard_map/ppermute | solution.py:356
  163.8 11.4 %backward.1 = (bf16[3,256,384]{2,1,0:T(8,128)(2,1)}, bf16[3,256,384]{2,1,0:T(8,128)(2,1)}, bf16[3,256,384]{2,1,0:T(8,128)(2,1)}, bf16[3,256,384]{2,1,0:T(8,128)(2,1)}) custom-call(bf16[3,256,384]{2,1,0:T(8,128)(2,1)} %get-tuple-element.41.refs_0_, bf16[3,256,384]{2,1,0:T(8,128)(2,1)} %collective-permute-done.refs_1_, bf16[3,256,384]{2,1,0:T(8,128)(2,1)} %copy-done.31, ...), custom_call_target="tpu_custom_call" | custom-call | flops 3221225472 | bytes 6291456 | tf_op jit(solution)/shard_map/backward/pallas_call | solution.py:228
  175.3 3.9 %collective-permute-start.40 = (bf16[48,1536]{1,0:T(8,128)(2,1)S(1)}, bf16[48,1536]{1,0:T(8,128)(2,1)S(1)}, u32[]{:S(2)}, u32[]{:S(2)}) collective-permute-start(bf16[48,1536]{1,0:T(8,128)(2,1)S(1)} %get-tuple-element.93), channel_id=1, source_target_pairs={{0,24},{1,25},{2,26},{3,27},{4,28},{5,29},{6,30},{7,31},{8,16},{9,... | collective-permute-start | bytes 442376 | tf_op jit(solution)/shard_map/ppermute | solution.py:356
  179.2 0.6 collective-permute-start.38
  179.9 1.1 add_convert_fusion.5.refs_4_
  181.2 0.9 collective-permute-start.32
  182.1 1.9 collective-permute-done.40
  184.0 5.5 %collective-permute-done.39 = bf16[48,1536]{1,0:T(8,128)(2,1)S(1)} collective-permute-done((bf16[48,1536]{1,0:T(8,128)(2,1)S(1)}, bf16[48,1536]{1,0:T(8,128)(2,1)S(1)}, u32[]{:S(2)}, u32[]{:S(2)}) %collective-permute-start.39) | collective-permute-done | bytes 147488 | tf_op jit(solution)/shard_map/ppermute | solution.py:356
  189.5 1.1 collective-permute-start.22
  190.6 0.8 collective-permute-start.23
  191.5 2.2 collective-permute-start.33
  193.8 0.4 collective-permute-start.41
  194.2 21.0 %collective-permute-done.33.refs_7_ = bf16[48,1536]{1,0:T(8,128)(2,1)S(1)} collective-permute-done((bf16[48,1536]{1,0:T(8,128)(2,1)S(1)}, bf16[48,1536]{1,0:T(8,128)(2,1)S(1)}, u32[]{:S(2)}, u32[]{:S(2)}) %collective-permute-start.33) | collective-permute-done | bytes 147488 | tf_op jit(solution)/shard_map/ppermute | solution.py:356
  215.2 1.0 collective-permute-start.42
  216.3 1.4 collective-permute-start.43
  217.7 7.9 %collective-permute-done.42.refs_10_ = bf16[48,1536]{1,0:T(8,128)(2,1)S(1)} collective-permute-done((bf16[48,1536]{1,0:T(8,128)(2,1)S(1)}, bf16[48,1536]{1,0:T(8,128)(2,1)S(1)}, u32[]{:S(2)}, u32[]{:S(2)}) %collective-permute-start.42) | collective-permute-done | bytes 147488 | tf_op jit(solution)/shard_map/ppermute | solution.py:356
  225.6 0.5 copy-done.29
  226.6 0.8 copy-done.18
  227.4 4.5 %finish.1 = (bf16[1,256,1536]{2,1,0:T(8,128)(2,1)}, bf16[1,256,1536]{2,1,0:T(8,128)(2,1)}, bf16[1,256,1536]{2,1,0:T(8,128)(2,1)}, f32[192,3072]{1,0:T(8,128)}) custom-call(s32[3]{0:T(128)} %pad_add_fusion.place_ref, bf16[3,256,384]{2,1,0:T(8,128)(2,1)} %get-tuple-element.56.refs_0_, bf16[3,256,384]{2,1,0:T(8,128)(2,1)} %copy-done.16, ...), custom_call_target="tpu_custom_call" | custom-call | bytes 8257536 | tf_op jit(solution)/shard_map/finish/pallas_call | solution.py:137
  (120 shorter events, 2.7 us)
Async XLA Ops:
  0.6 9.7 %copy-start.11 = (bf16[1,256,3072]{2,1,0:T(8,128)(2,1)S(1)}, bf16[1,256,3072]{2,1,0:T(8,128)(2,1)}, u32[]{:S(2)}) copy-start(bf16[1,256,3072]{2,1,0:T(8,128)(2,1)} %param.8) | copy-start | bytes 4718596
  3.1 17.8 %collective-permute-start.3 = (bf16[96,3072]{1,0:T(8,128)(2,1)}, bf16[96,3072]{1,0:T(8,128)(2,1)}, u32[]{:S(2)}, u32[]{:S(2)}) collective-permute-start(bf16[96,3072]{1,0:T(8,128)(2,1)} %get-tuple-element.91), channel_id=1, source_target_pairs={{0,8},{4,12},{9,17},{13,21},{18,26},{22,30}} | collective-permute-start | bytes 1769480 | tf_op jit(solution)/shard_map/ppermute | solution.py:356
  8.9 12.1 %collective-permute-start.4 = (bf16[96,3072]{1,0:T(8,128)(2,1)}, bf16[96,3072]{1,0:T(8,128)(2,1)}, u32[]{:S(2)}, u32[]{:S(2)}) collective-permute-start(bf16[96,3072]{1,0:T(8,128)(2,1)} %get-tuple-element.91), channel_id=1, source_target_pairs={{9,1},{13,5},{18,10},{22,14},{27,19},{31,23}} | collective-permute-start | bytes 1769480 | tf_op jit(solution)/shard_map/ppermute | solution.py:356
  10.5 11.6 %copy-start.3 = (bf16[256,1536]{1,0:T(8,128)(2,1)}, bf16[256,1536]{1,0:T(8,128)(2,1)S(1)}, u32[]{:S(2)}) copy-start(bf16[256,1536]{1,0:T(8,128)(2,1)S(1)} %get-tuple-element.78.refs_4_.refs_0_) | copy-start | bytes 2359300
  10.5 62.4 %copy-start.4 = (bf16[256,1536]{1,0:T(8,128)(2,1)}, bf16[256,1536]{1,0:T(8,128)(2,1)S(1)}, u32[]{:S(2)}) copy-start(bf16[256,1536]{1,0:T(8,128)(2,1)S(1)} %get-tuple-element.49.refs_4_.refs_0_) | copy-start | bytes 2359300
  10.5 60.8 %collective-permute-start.17 = (bf16[256,1536]{1,0:T(8,128)(2,1)S(1)}, bf16[256,1536]{1,0:T(8,128)(2,1)S(1)}, u32[]{:S(2)}, u32[]{:S(2)}) collective-permute-start(bf16[256,1536]{1,0:T(8,128)(2,1)S(1)} %get-tuple-element.78.refs_4_.refs_0_), channel_id=1, source_target_pairs={{0,1},{1,0},{2,3},{3,2},{4,5},{5,4},{6,7},{7,6},{8,9},{9,8},{10,11... | collective-permute-start | bytes 2359304 | tf_op jit(solution)/shard_map/ppermute | solution.py:356
  10.6 62.3 %collective-permute-start.18 = (bf16[256,1536]{1,0:T(8,128)(2,1)S(1)}, bf16[256,1536]{1,0:T(8,128)(2,1)}, u32[]{:S(2)}, u32[]{:S(2)}) collective-permute-start(bf16[256,1536]{1,0:T(8,128)(2,1)S(1)} %get-tuple-element.78.refs_4_.refs_0_), channel_id=1, source_target_pairs={{0,2},{1,3},{2,0},{3,1},{4,6},{5,7},{6,4},{7,5},{8,10},{9,11},{10,... | collective-permute-start | bytes 2359304 | tf_op jit(solution)/shard_map/ppermute | solution.py:356
  14.8 28.9 %collective-permute-start = (bf16[3,256,384]{2,1,0:T(8,128)(2,1)}, bf16[3,256,384]{2,1,0:T(8,128)(2,1)}, u32[]{:S(2)}, u32[]{:S(2)}) collective-permute-start(bf16[3,256,384]{2,1,0:T(8,128)(2,1)} %get-tuple-element.42), channel_id=1, source_target_pairs={{0,1},{1,0},{2,3},{3,2},{4,5},{5,4},{6,7},{7,6},{8,9},{9,8},{10,11... | collective-permute-start | bytes 1769480 | tf_op jit(solution)/shard_map/ppermute | solution.py:356
  20.9 34.0 %collective-permute-start.1 = (bf16[3,256,384]{2,1,0:T(8,128)(2,1)}, bf16[3,256,384]{2,1,0:T(8,128)(2,1)S(1)}, u32[]{:S(2)}, u32[]{:S(2)}) collective-permute-start(bf16[3,256,384]{2,1,0:T(8,128)(2,1)} %get-tuple-element.43), channel_id=1, source_target_pairs={{0,2},{1,3},{2,0},{3,1},{4,6},{5,7},{6,4},{7,5},{8,10},{9,11},{10,... | collective-permute-start | bytes 1769480 | tf_op jit(solution)/shard_map/ppermute | solution.py:356
  20.9 35.4 %collective-permute-start.2 = (bf16[3,256,384]{2,1,0:T(8,128)(2,1)}, bf16[3,256,384]{2,1,0:T(8,128)(2,1)S(1)}, u32[]{:S(2)}, u32[]{:S(2)}) collective-permute-start(bf16[3,256,384]{2,1,0:T(8,128)(2,1)} %get-tuple-element.44), channel_id=1, source_target_pairs={{0,3},{1,2},{2,1},{3,0},{4,7},{5,6},{6,5},{7,4},{8,11},{9,10},{10,... | collective-permute-start | bytes 1769480 | tf_op jit(solution)/shard_map/ppermute | solution.py:356
  22.1 49.2 %copy-start.5 = (bf16[96,3072]{1,0:T(8,128)(2,1)}, bf16[96,3072]{1,0:T(8,128)(2,1)S(1)}, u32[]{:S(2)}) copy-start(bf16[96,3072]{1,0:T(8,128)(2,1)S(1)} %broadcast_select_fusion.1) | copy-start | bytes 1769476
  43.7 30.7 %collective-permute-start.7 = (bf16[96,3072]{1,0:T(8,128)(2,1)}, bf16[96,3072]{1,0:T(8,128)(2,1)}, u32[]{:S(2)}, u32[]{:S(2)}) collective-permute-start(bf16[96,3072]{1,0:T(8,128)(2,1)} %get-tuple-element.46), channel_id=1, source_target_pairs={{0,8},{4,12},{9,17},{13,21},{18,26},{22,30}} | collective-permute-start | bytes 1769480 | tf_op jit(solution)/shard_map/ppermute | solution.py:356
  54.9 21.1 %collective-permute-start.8 = (bf16[96,3072]{1,0:T(8,128)(2,1)}, bf16[96,3072]{1,0:T(8,128)(2,1)}, u32[]{:S(2)}, u32[]{:S(2)}) collective-permute-start(bf16[96,3072]{1,0:T(8,128)(2,1)} %get-tuple-element.46), channel_id=1, source_target_pairs={{9,1},{13,5},{18,10},{22,14},{27,19},{31,23}} | collective-permute-start | bytes 1769480 | tf_op jit(solution)/shard_map/ppermute | solution.py:356
  57.2 49.1 %collective-permute-start.5 = (bf16[96,3072]{1,0:T(8,128)(2,1)S(1)}, bf16[96,3072]{1,0:T(8,128)(2,1)}, u32[]{:S(2)}, u32[]{:S(2)}) collective-permute-start(bf16[96,3072]{1,0:T(8,128)(2,1)S(1)} %broadcast_select_fusion.1), channel_id=1, source_target_pairs={{8,16},{10,2},{12,20},{14,6},{17,25},{19,11},{21,29},{23,15}} | collective-permute-start | bytes 1769480 | tf_op jit(solution)/shard_map/ppermute | solution.py:356
  71.3 6.4 %copy-start.9 = (bf16[256,1536]{1,0:T(8,128)(2,1)}, bf16[256,1536]{1,0:T(8,128)(2,1)S(1)}, u32[]{:S(2)}) copy-start(bf16[256,1536]{1,0:T(8,128)(2,1)S(1)} %collective-permute-done.17.refs_5_.refs_1_) | copy-start | bytes 2359300
  71.3 36.7 %collective-permute-start.11 = (bf16[256,1536]{1,0:T(8,128)(2,1)S(1)}, bf16[256,1536]{1,0:T(8,128)(2,1)}, u32[]{:S(2)}, u32[]{:S(2)}) collective-permute-start(bf16[256,1536]{1,0:T(8,128)(2,1)S(1)} %get-tuple-element.49.refs_4_.refs_0_), channel_id=1, source_target_pairs={{0,1},{1,0},{2,3},{3,2},{4,5},{5,4},{6,7},{7,6},{8,9},{9,8},{10,11... | collective-permute-start | bytes 2359304 | tf_op jit(solution)/shard_map/ppermute | solution.py:356
  72.9 35.1 %collective-permute-start.12 = (bf16[256,1536]{1,0:T(8,128)(2,1)S(1)}, bf16[256,1536]{1,0:T(8,128)(2,1)S(1)}, u32[]{:S(2)}, u32[]{:S(2)}) collective-permute-start(bf16[256,1536]{1,0:T(8,128)(2,1)S(1)} %get-tuple-element.49.refs_4_.refs_0_), channel_id=1, source_target_pairs={{0,2},{1,3},{2,0},{3,1},{4,6},{5,7},{6,4},{7,5},{8,10},{9,11},{10,... | collective-permute-start | bytes 2359304 | tf_op jit(solution)/shard_map/ppermute | solution.py:356
  74.4 24.5 %collective-permute-start.19 = (bf16[128,1536]{1,0:T(8,128)(2,1)S(1)}, bf16[128,1536]{1,0:T(8,128)(2,1)S(1)}, u32[]{:S(2)}, u32[]{:S(2)}) collective-permute-start(bf16[128,1536]{1,0:T(8,128)(2,1)S(1)} %slice.78), channel_id=1, source_target_pairs={{0,2},{1,3},{2,0},{3,1},{4,6},{5,7},{6,4},{7,5},{8,10},{9,11},{10,... | collective-permute-start | bytes 1179656 | tf_op jit(solution)/shard_map/ppermute | solution.py:356
  76.0 25.1 %collective-permute-start.20 = (bf16[128,1536]{1,0:T(8,128)(2,1)S(1)}, bf16[128,1536]{1,0:T(8,128)(2,1)}, u32[]{:S(2)}, u32[]{:S(2)}) collective-permute-start(bf16[128,1536]{1,0:T(8,128)(2,1)S(1)} %slice.79), channel_id=1, source_target_pairs={{0,1},{1,0},{2,3},{3,2},{4,5},{5,4},{6,7},{7,6},{8,9},{9,8},{10,11... | collective-permute-start | bytes 1179656 | tf_op jit(solution)/shard_map/ppermute | solution.py:356
  99.6 10.7 %collective-permute-start.9 = (bf16[96,3072]{1,0:T(8,128)(2,1)S(1)}, bf16[96,3072]{1,0:T(8,128)(2,1)}, u32[]{:S(2)}, u32[]{:S(2)}) collective-permute-start(bf16[96,3072]{1,0:T(8,128)(2,1)S(1)} %broadcast_select_fusion), channel_id=1, source_target_pairs={{8,16},{10,2},{12,20},{14,6},{17,25},{19,11},{21,29},{23,15}} | collective-permute-start | bytes 1769480 | tf_op jit(solution)/shard_map/ppermute | solution.py:356
  106.3 5.5 %copy-start.14 = (bf16[4,48,1536]{2,1,0:T(8,128)(2,1)S(1)}, bf16[4,48,1536]{2,1,0:T(8,128)(2,1)}, u32[]{:S(2)}) copy-start(bf16[4,48,1536]{2,1,0:T(8,128)(2,1)} %get-tuple-element.60) | copy-start | bytes 1769476
  106.3 5.5 %collective-permute-start.24 = (bf16[4,48,1536]{2,1,0:T(8,128)(2,1)}, bf16[4,48,1536]{2,1,0:T(8,128)(2,1)S(1)}, u32[]{:S(2)}, u32[]{:S(2)}) collective-permute-start(bf16[4,48,1536]{2,1,0:T(8,128)(2,1)} %get-tuple-element.61), channel_id=1, source_target_pairs={{0,4},{1,5},{2,6},{3,7},{4,0},{5,1},{6,2},{7,3},{8,12},{9,13},{10,... | collective-permute-start | bytes 1769480 | tf_op jit(solution)/shard_map/ppermute | solution.py:356
  106.4 23.1 %collective-permute-start.6 = (bf16[96,3072]{1,0:T(8,128)(2,1)}, bf16[96,3072]{1,0:T(8,128)(2,1)}, u32[]{:S(2)}, u32[]{:S(2)}) collective-permute-start(bf16[96,3072]{1,0:T(8,128)(2,1)} %collective-permute-done.5), channel_id=1, source_target_pairs={{11,3},{15,7},{16,24},{20,28}} | collective-permute-start | bytes 1769480 | tf_op jit(solution)/shard_map/ppermute | solution.py:356
  109.3 11.4 %collective-permute-start.15 = (bf16[128,1536]{1,0:T(8,128)(2,1)S(1)}, bf16[128,1536]{1,0:T(8,128)(2,1)S(1)}, u32[]{:S(2)}, u32[]{:S(2)}) collective-permute-start(bf16[128,1536]{1,0:T(8,128)(2,1)S(1)} %slice.75), channel_id=1, source_target_pairs={{0,2},{1,3},{2,0},{3,1},{4,6},{5,7},{6,4},{7,5},{8,10},{9,11},{10,... | collective-permute-start | bytes 1179656 | tf_op jit(solution)/shard_map/ppermute | solution.py:356
  109.5 12.0 %collective-permute-start.16 = (bf16[128,1536]{1,0:T(8,128)(2,1)S(1)}, bf16[128,1536]{1,0:T(8,128)(2,1)S(1)}, u32[]{:S(2)}, u32[]{:S(2)}) collective-permute-start(bf16[128,1536]{1,0:T(8,128)(2,1)S(1)} %slice.76), channel_id=1, source_target_pairs={{0,1},{1,0},{2,3},{3,2},{4,5},{5,4},{6,7},{7,6},{8,9},{9,8},{10,11... | collective-permute-start | bytes 1179656 | tf_op jit(solution)/shard_map/ppermute | solution.py:356
  110.4 19.8 %collective-permute-start.10 = (bf16[96,3072]{1,0:T(8,128)(2,1)}, bf16[96,3072]{1,0:T(8,128)(2,1)}, u32[]{:S(2)}, u32[]{:S(2)}) collective-permute-start(bf16[96,3072]{1,0:T(8,128)(2,1)} %collective-permute-done.9), channel_id=1, source_target_pairs={{11,3},{15,7},{16,24},{20,28}} | collective-permute-start | bytes 1769480 | tf_op jit(solution)/shard_map/ppermute | solution.py:356
  112.7 16.3 %collective-permute-start.25 = (bf16[48,1536]{1,0:T(8,128)(2,1)}, bf16[48,1536]{1,0:T(8,128)(2,1)}, u32[]{:S(2)}, u32[]{:S(2)}) collective-permute-start(bf16[48,1536]{1,0:T(8,128)(2,1)} %get-tuple-element.86), channel_id=1, source_target_pairs={{0,1},{1,0},{2,3},{3,2},{4,5},{5,4},{6,7},{7,6},{8,9},{9,8},{10,11... | collective-permute-start | bytes 442376 | tf_op jit(solution)/shard_map/ppermute | solution.py:356
  120.8 8.7 %collective-permute-start.26 = (bf16[48,1536]{1,0:T(8,128)(2,1)}, bf16[48,1536]{1,0:T(8,128)(2,1)}, u32[]{:S(2)}, u32[]{:S(2)}) collective-permute-start(bf16[48,1536]{1,0:T(8,128)(2,1)} %get-tuple-element.85), channel_id=1, source_target_pairs={{0,2},{1,3},{2,0},{3,1},{4,6},{5,7},{6,4},{7,5},{8,10},{9,11},{10,... | collective-permute-start | bytes 442376 | tf_op jit(solution)/shard_map/ppermute | solution.py:356
  121.5 8.0 %collective-permute-start.27 = (bf16[48,1536]{1,0:T(8,128)(2,1)}, bf16[48,1536]{1,0:T(8,128)(2,1)S(1)}, u32[]{:S(2)}, u32[]{:S(2)}) collective-permute-start(bf16[48,1536]{1,0:T(8,128)(2,1)} %get-tuple-element.84), channel_id=1, source_target_pairs={{0,3},{1,2},{2,1},{3,0},{4,7},{5,6},{6,5},{7,4},{8,11},{9,10},{10,... | collective-permute-start | bytes 442376 | tf_op jit(solution)/shard_map/ppermute | solution.py:356
  123.7 6.5 %copy-start.2 = (bf16[192,3072]{1,0:T(8,128)(2,1)S(1)}, bf16[192,3072]{1,0:T(8,128)(2,1)}, u32[]{:S(2)}) copy-start(bf16[192,3072]{1,0:T(8,128)(2,1)} %param.9) | copy-start | bytes 3538948
  123.7 6.5 %copy-start.6 = (bf16[96,3072]{1,0:T(8,128)(2,1)S(1)}, bf16[96,3072]{1,0:T(8,128)(2,1)}, u32[]{:S(2)}) copy-start(bf16[96,3072]{1,0:T(8,128)(2,1)} %copy-done.5) | copy-start | bytes 1769476
  129.0 17.9 %collective-permute-start.34 = (bf16[4,48,1536]{2,1,0:T(8,128)(2,1)}, bf16[4,48,1536]{2,1,0:T(8,128)(2,1)S(1)}, u32[]{:S(2)}, u32[]{:S(2)}) collective-permute-start(bf16[4,48,1536]{2,1,0:T(8,128)(2,1)} %get-tuple-element.71), channel_id=1, source_target_pairs={{0,4},{1,5},{2,6},{3,7},{4,0},{5,1},{6,2},{7,3},{8,12},{9,13},{10,... | collective-permute-start | bytes 1769480 | tf_op jit(solution)/shard_map/ppermute | solution.py:356
  130.4 18.3 %copy-start = (bf16[96,3072]{1,0:T(8,128)(2,1)}, bf16[96,3072]{1,0:T(8,128)(2,1)S(1)}, u32[]{:S(2)}) copy-start(bf16[96,3072]{1,0:T(8,128)(2,1)S(1)} %get-tuple-element.88.refs_1_) | copy-start | bytes 1769476
  130.4 18.3 %copy-start.1 = (bf16[96,3072]{1,0:T(8,128)(2,1)}, bf16[96,3072]{1,0:T(8,128)(2,1)S(1)}, u32[]{:S(2)}) copy-start(bf16[96,3072]{1,0:T(8,128)(2,1)S(1)} %get-tuple-element.89.refs_0_) | copy-start | bytes 1769476
  130.4 16.5 %copy-start.13 = (bf16[4,48,1536]{2,1,0:T(8,128)(2,1)S(1)}, bf16[4,48,1536]{2,1,0:T(8,128)(2,1)}, u32[]{:S(2)}) copy-start(bf16[4,48,1536]{2,1,0:T(8,128)(2,1)} %get-tuple-element.72) | copy-start | bytes 1769476
  130.4 17.3 %collective-permute-start.13 = (bf16[96,3072]{1,0:T(8,128)(2,1)S(1)}, bf16[96,3072]{1,0:T(8,128)(2,1)S(1)}, u32[]{:S(2)}, u32[]{:S(2)}) collective-permute-start(bf16[96,3072]{1,0:T(8,128)(2,1)S(1)} %get-tuple-element.89.refs_0_), channel_id=1, source_target_pairs={{0,4},{1,5},{2,6},{3,7},{4,0},{5,1},{6,2},{7,3},{8,12},{9,13},{10,... | collective-permute-start | bytes 1769480 | tf_op jit(solution)/shard_map/ppermute | solution.py:356
  130.6 17.2 %collective-permute-start.14 = (bf16[96,3072]{1,0:T(8,128)(2,1)S(1)}, bf16[96,3072]{1,0:T(8,128)(2,1)S(1)}, u32[]{:S(2)}, u32[]{:S(2)}) collective-permute-start(bf16[96,3072]{1,0:T(8,128)(2,1)S(1)} %get-tuple-element.88.refs_1_), channel_id=1, source_target_pairs={{0,4},{1,5},{2,6},{3,7},{4,0},{5,1},{6,2},{7,3},{8,12},{9,13},{10,... | collective-permute-start | bytes 1769480 | tf_op jit(solution)/shard_map/ppermute | solution.py:356
  132.8 28.5 %collective-permute-start.28 = (bf16[48,1536]{1,0:T(8,128)(2,1)}, bf16[48,1536]{1,0:T(8,128)(2,1)}, u32[]{:S(2)}, u32[]{:S(2)}) collective-permute-start(bf16[48,1536]{1,0:T(8,128)(2,1)} %get-tuple-element.97), channel_id=1, source_target_pairs={{0,8},{1,9},{2,10},{3,11},{4,12},{5,13},{6,14},{7,15},{8,0},{9,1},... | collective-permute-start | bytes 442376 | tf_op jit(solution)/shard_map/ppermute | solution.py:356
  138.3 37.0 %collective-permute-start.29 = (bf16[48,1536]{1,0:T(8,128)(2,1)S(1)}, bf16[48,1536]{1,0:T(8,128)(2,1)}, u32[]{:S(2)}, u32[]{:S(2)}) collective-permute-start(bf16[48,1536]{1,0:T(8,128)(2,1)S(1)} %get-tuple-element.96), channel_id=1, source_target_pairs={{0,16},{1,17},{2,18},{3,19},{4,20},{5,21},{6,22},{7,23},{8,24},{9,... | collective-permute-start | bytes 442376 | tf_op jit(solution)/shard_map/ppermute | solution.py:356
  147.0 28.3 %collective-permute-start.30 = (bf16[48,1536]{1,0:T(8,128)(2,1)S(1)}, bf16[48,1536]{1,0:T(8,128)(2,1)}, u32[]{:S(2)}, u32[]{:S(2)}) collective-permute-start(bf16[48,1536]{1,0:T(8,128)(2,1)S(1)} %get-tuple-element.95), channel_id=1, source_target_pairs={{0,24},{1,25},{2,26},{3,27},{4,28},{5,29},{6,30},{7,31},{8,16},{9,... | collective-permute-start | bytes 442376 | tf_op jit(solution)/shard_map/ppermute | solution.py:356
  147.8 27.5 %collective-permute-start.35 = (bf16[48,1536]{1,0:T(8,128)(2,1)}, bf16[48,1536]{1,0:T(8,128)(2,1)S(1)}, u32[]{:S(2)}, u32[]{:S(2)}) collective-permute-start(bf16[48,1536]{1,0:T(8,128)(2,1)} %get-tuple-element.82), channel_id=1, source_target_pairs={{0,1},{1,0},{2,3},{3,2},{4,5},{5,4},{6,7},{7,6},{8,9},{9,8},{10,11... | collective-permute-start | bytes 442376 | tf_op jit(solution)/shard_map/ppermute | solution.py:356
  147.8 27.5 %collective-permute-start.36 = (bf16[48,1536]{1,0:T(8,128)(2,1)S(1)}, bf16[48,1536]{1,0:T(8,128)(2,1)S(1)}, u32[]{:S(2)}, u32[]{:S(2)}) collective-permute-start(bf16[48,1536]{1,0:T(8,128)(2,1)S(1)} %get-tuple-element.81), channel_id=1, source_target_pairs={{0,2},{1,3},{2,0},{3,1},{4,6},{5,7},{6,4},{7,5},{8,10},{9,11},{10,... | collective-permute-start | bytes 442376 | tf_op jit(solution)/shard_map/ppermute | solution.py:356
  161.3 14.0 %collective-permute-start.37 = (bf16[48,1536]{1,0:T(8,128)(2,1)S(1)}, bf16[48,1536]{1,0:T(8,128)(2,1)S(1)}, u32[]{:S(2)}, u32[]{:S(2)}) collective-permute-start(bf16[48,1536]{1,0:T(8,128)(2,1)S(1)} %get-tuple-element.80), channel_id=1, source_target_pairs={{0,3},{1,2},{2,1},{3,0},{4,7},{5,6},{6,5},{7,4},{8,11},{9,10},{10,... | collective-permute-start | bytes 442376 | tf_op jit(solution)/shard_map/ppermute | solution.py:356
  175.2 8.8 %copy-start.35 = (bf16[3,256,384]{2,1,0:T(8,128)(2,1)S(1)}, bf16[3,256,384]{2,1,0:T(8,128)(2,1)}, u32[]{:S(2)}) copy-start(bf16[3,256,384]{2,1,0:T(8,128)(2,1)} %get-tuple-element.57) | copy-start | bytes 1769476
  175.2 14.3 %copy-start.34 = (bf16[3,256,384]{2,1,0:T(8,128)(2,1)S(1)}, bf16[3,256,384]{2,1,0:T(8,128)(2,1)}, u32[]{:S(2)}) copy-start(bf16[3,256,384]{2,1,0:T(8,128)(2,1)} %get-tuple-element.58) | copy-start | bytes 1769476
  175.2 15.4 %copy-start.33 = (bf16[3,256,384]{2,1,0:T(8,128)(2,1)S(1)}, bf16[3,256,384]{2,1,0:T(8,128)(2,1)}, u32[]{:S(2)}) copy-start(bf16[3,256,384]{2,1,0:T(8,128)(2,1)} %get-tuple-element.59) | copy-start | bytes 1769476
  175.3 8.6 %collective-permute-start.40 = (bf16[48,1536]{1,0:T(8,128)(2,1)S(1)}, bf16[48,1536]{1,0:T(8,128)(2,1)S(1)}, u32[]{:S(2)}, u32[]{:S(2)}) collective-permute-start(bf16[48,1536]{1,0:T(8,128)(2,1)S(1)} %get-tuple-element.93), channel_id=1, source_target_pairs={{0,24},{1,25},{2,26},{3,27},{4,28},{5,29},{6,30},{7,31},{8,16},{9,... | collective-permute-start | bytes 442376 | tf_op jit(solution)/shard_map/ppermute | solution.py:356
  179.2 10.3 %collective-permute-start.39 = (bf16[48,1536]{1,0:T(8,128)(2,1)S(1)}, bf16[48,1536]{1,0:T(8,128)(2,1)S(1)}, u32[]{:S(2)}, u32[]{:S(2)}) collective-permute-start(bf16[48,1536]{1,0:T(8,128)(2,1)S(1)} %get-tuple-element.94), channel_id=1, source_target_pairs={{0,16},{1,17},{2,18},{3,19},{4,20},{5,21},{6,22},{7,23},{8,24},{9,... | collective-permute-start | bytes 442376 | tf_op jit(solution)/shard_map/ppermute | solution.py:356
  179.2 11.4 %collective-permute-start.38 = (bf16[48,1536]{1,0:T(8,128)(2,1)S(1)}, bf16[48,1536]{1,0:T(8,128)(2,1)S(1)}, u32[]{:S(2)}, u32[]{:S(2)}) collective-permute-start(bf16[48,1536]{1,0:T(8,128)(2,1)S(1)} %get-tuple-element.92), channel_id=1, source_target_pairs={{0,8},{1,9},{2,10},{3,11},{4,12},{5,13},{6,14},{7,15},{8,0},{9,1},... | collective-permute-start | bytes 442376 | tf_op jit(solution)/shard_map/ppermute | solution.py:356
  181.0 44.6 %copy-start.19 = (bf16[48,1536]{1,0:T(8,128)(2,1)}, bf16[48,1536]{1,0:T(8,128)(2,1)S(1)}, u32[]{:S(2)}) copy-start(bf16[48,1536]{1,0:T(8,128)(2,1)S(1)} %add_convert_fusion.5.refs_4_) | copy-start | bytes 442372
  181.0 10.5 %collective-permute-start.31 = (bf16[48,1536]{1,0:T(8,128)(2,1)S(1)}, bf16[48,1536]{1,0:T(8,128)(2,1)S(1)}, u32[]{:S(2)}, u32[]{:S(2)}) collective-permute-start(bf16[48,1536]{1,0:T(8,128)(2,1)S(1)} %add_convert_fusion.5.refs_4_), channel_id=1, source_target_pairs={{0,1},{1,0},{2,3},{3,2},{4,5},{5,4},{6,7},{7,6},{8,9},{9,8},{10,11... | collective-permute-start | bytes 442376 | tf_op jit(solution)/shard_map/ppermute | solution.py:356
  181.2 12.6 %collective-permute-start.32 = (bf16[48,1536]{1,0:T(8,128)(2,1)S(1)}, bf16[48,1536]{1,0:T(8,128)(2,1)S(1)}, u32[]{:S(2)}, u32[]{:S(2)}) collective-permute-start(bf16[48,1536]{1,0:T(8,128)(2,1)S(1)} %add_convert_fusion.5.refs_4_), channel_id=1, source_target_pairs={{0,2},{1,3},{2,0},{3,1},{4,6},{5,7},{6,4},{7,5},{8,10},{9,11},{10,... | collective-permute-start | bytes 442376 | tf_op jit(solution)/shard_map/ppermute | solution.py:356
  184.0 41.6 %collective-permute-start.21 = (bf16[3,256,384]{2,1,0:T(8,128)(2,1)S(1)}, bf16[3,256,384]{2,1,0:T(8,128)(2,1)S(1)}, u32[]{:S(2)}, u32[]{:S(2)}) collective-permute-start(bf16[3,256,384]{2,1,0:T(8,128)(2,1)S(1)} %copy-done.35), channel_id=1, source_target_pairs={{0,1},{1,0},{2,3},{3,2},{4,5},{5,4},{6,7},{7,6},{8,9},{9,8},{10,11... | collective-permute-start | bytes 1769480 | tf_op jit(solution)/shard_map/ppermute | solution.py:356
  189.5 36.0 %collective-permute-start.22 = (bf16[3,256,384]{2,1,0:T(8,128)(2,1)S(1)}, bf16[3,256,384]{2,1,0:T(8,128)(2,1)S(1)}, u32[]{:S(2)}, u32[]{:S(2)}) collective-permute-start(bf16[3,256,384]{2,1,0:T(8,128)(2,1)S(1)} %copy-done.34), channel_id=1, source_target_pairs={{0,2},{1,3},{2,0},{3,1},{4,6},{5,7},{6,4},{7,5},{8,10},{9,11},{10,... | collective-permute-start | bytes 1769480 | tf_op jit(solution)/shard_map/ppermute | solution.py:356
  190.6 35.0 %collective-permute-start.23 = (bf16[3,256,384]{2,1,0:T(8,128)(2,1)S(1)}, bf16[3,256,384]{2,1,0:T(8,128)(2,1)S(1)}, u32[]{:S(2)}, u32[]{:S(2)}) collective-permute-start(bf16[3,256,384]{2,1,0:T(8,128)(2,1)S(1)} %copy-done.33), channel_id=1, source_target_pairs={{0,3},{1,2},{2,1},{3,0},{4,7},{5,6},{6,5},{7,4},{8,11},{9,10},{10,... | collective-permute-start | bytes 1769480 | tf_op jit(solution)/shard_map/ppermute | solution.py:356
  191.5 34.1 %copy-start.15 = (bf16[48,1536]{1,0:T(8,128)(2,1)}, bf16[48,1536]{1,0:T(8,128)(2,1)S(1)}, u32[]{:S(2)}) copy-start(bf16[48,1536]{1,0:T(8,128)(2,1)S(1)} %add_convert_fusion.refs_8_) | copy-start | bytes 442372
  191.5 34.1 %copy-start.25 = (bf16[48,1536]{1,0:T(8,128)(2,1)}, bf16[48,1536]{1,0:T(8,128)(2,1)S(1)}, u32[]{:S(2)}) copy-start(bf16[48,1536]{1,0:T(8,128)(2,1)S(1)} %collective-permute-done.31.refs_5_) | copy-start | bytes 442372
  191.5 23.7 %collective-permute-start.33 = (bf16[48,1536]{1,0:T(8,128)(2,1)S(1)}, bf16[48,1536]{1,0:T(8,128)(2,1)S(1)}, u32[]{:S(2)}, u32[]{:S(2)}) collective-permute-start(bf16[48,1536]{1,0:T(8,128)(2,1)S(1)} %add_convert_fusion.5.refs_4_), channel_id=1, source_target_pairs={{0,3},{1,2},{2,1},{3,0},{4,7},{5,6},{6,5},{7,4},{8,11},{9,10},{10,... | collective-permute-start | bytes 442376 | tf_op jit(solution)/shard_map/ppermute | solution.py:356
  193.8 31.8 %copy-start.26 = (bf16[48,1536]{1,0:T(8,128)(2,1)}, bf16[48,1536]{1,0:T(8,128)(2,1)S(1)}, u32[]{:S(2)}) copy-start(bf16[48,1536]{1,0:T(8,128)(2,1)S(1)} %collective-permute-done.32.refs_6_) | copy-start | bytes 442372
  193.8 22.5 %collective-permute-start.41 = (bf16[48,1536]{1,0:T(8,128)(2,1)S(1)}, bf16[48,1536]{1,0:T(8,128)(2,1)S(1)}, u32[]{:S(2)}, u32[]{:S(2)}) collective-permute-start(bf16[48,1536]{1,0:T(8,128)(2,1)S(1)} %add_convert_fusion.refs_8_), channel_id=1, source_target_pairs={{0,1},{1,0},{2,3},{3,2},{4,5},{5,4},{6,7},{7,6},{8,9},{9,8},{10,11... | collective-permute-start | bytes 442376 | tf_op jit(solution)/shard_map/ppermute | solution.py:356
  215.2 10.4 %copy-start.27 = (bf16[48,1536]{1,0:T(8,128)(2,1)}, bf16[48,1536]{1,0:T(8,128)(2,1)S(1)}, u32[]{:S(2)}) copy-start(bf16[48,1536]{1,0:T(8,128)(2,1)S(1)} %collective-permute-done.33.refs_7_) | copy-start | bytes 442372
  215.2 10.3 %collective-permute-start.42 = (bf16[48,1536]{1,0:T(8,128)(2,1)S(1)}, bf16[48,1536]{1,0:T(8,128)(2,1)S(1)}, u32[]{:S(2)}, u32[]{:S(2)}) collective-permute-start(bf16[48,1536]{1,0:T(8,128)(2,1)S(1)} %add_convert_fusion.refs_8_), channel_id=1, source_target_pairs={{0,2},{1,3},{2,0},{3,1},{4,6},{5,7},{6,4},{7,5},{8,10},{9,11},{10,... | collective-permute-start | bytes 442376 | tf_op jit(solution)/shard_map/ppermute | solution.py:356
  216.3 9.3 %copy-start.28 = (bf16[48,1536]{1,0:T(8,128)(2,1)}, bf16[48,1536]{1,0:T(8,128)(2,1)S(1)}, u32[]{:S(2)}) copy-start(bf16[48,1536]{1,0:T(8,128)(2,1)S(1)} %collective-permute-done.41.refs_9_) | copy-start | bytes 442372
  216.3 9.2 %collective-permute-start.43 = (bf16[48,1536]{1,0:T(8,128)(2,1)S(1)}, bf16[48,1536]{1,0:T(8,128)(2,1)S(1)}, u32[]{:S(2)}, u32[]{:S(2)}) collective-permute-start(bf16[48,1536]{1,0:T(8,128)(2,1)S(1)} %add_convert_fusion.refs_8_), channel_id=1, source_target_pairs={{0,3},{1,2},{2,1},{3,0},{4,7},{5,6},{6,5},{7,4},{8,11},{9,10},{10,... | collective-permute-start | bytes 442376 | tf_op jit(solution)/shard_map/ppermute | solution.py:356
  (16 other events, 22.1 us)

commit v7 on v5

--- a/solution.py
+++ b/solution.py
@@ -107,7 +107,8 @@
                     moves.append((fetch, store))
         for chunk in range(chunks):
             for slot in range(rows):
-                start = pl.multiple_of((place_ref[0] ^ slot) * piece, 16)
+                owner = place_ref[0] ^ slot if chunk else (place_ref[1] - slot) & (rows - 1)
+                start = pl.multiple_of(owner * piece, 16)
                 fetch = pltpu.make_async_copy(
                     terms[chunk * rows + slot], low.at[chunk, slot], term_sems.at[0, chunk, slot]
                 )
@@ -298,26 +299,27 @@
     )(place, *weights, *(block for chunk in grads for block in chunk))
 
 
-def weight_terms(place, attended, grads, rows):
+def weight_terms(place, attended, grads, parts, by_plane):
     width, length = attended.shape
     step = grads[0].shape[1] // 2
-    piece = width // 2 // rows
+    piece = width // 2 // parts
 
     def body(place_ref, attended_ref, *refs):
         ins, (keep, give) = refs[:-2], refs[-2:]
         term = dot(attended_ref[...], stacked(ins)).astype(jnp.bfloat16)
-        row, core = place_ref[0], place_ref[2]
+        row, plane, core = place_ref[0], place_ref[1], place_ref[2]
         for side in range(2):
             for out, mine in ((keep, core == side), (give, core != side)):
 
                 @pl.when(mine)
                 def _():
-                    for at in range(rows):
-                        start = (side * rows + at) * piece
-                        out[at ^ row] = term[start : start + piece]
-
-    shape = jax.ShapeDtypeStruct((rows, piece, 2 * step), jnp.bfloat16)
-    spec = pl.BlockSpec((rows, piece, step), lambda i, place_ref: (0, 0, i))
+                    for at in range(parts):
+                        start = (side * parts + at) * piece
+                        slot = (at - plane) & (parts - 1) if by_plane else at ^ row
+                        out[slot] = term[start : start + piece]
+
+    shape = jax.ShapeDtypeStruct((parts, piece, 2 * step), jnp.bfloat16)
+    spec = pl.BlockSpec((parts, piece, step), lambda i, place_ref: (0, 0, i))
     return pl.pallas_call(
         body,
         grid_spec=pltpu.PrefetchScalarGridSpec(
@@ -376,11 +378,10 @@
         by_x, by_y = after((by_x, by_y), *done)
         cut = chunk.shape[0] // 2
         upper, lower = by_x[:cut], by_y[cut:]
-        upper = to_row(upper, 2)
-        lower = to_row(lower, 1)
-        return [chunk, by_x, by_y, upper, lower]
-
-    grads = [gather(grad_flat[:, :wide])]
+        by_both = [to_row(upper, 2), to_row(lower, 1)]
+        return [chunk, by_x, by_y, *by_both], (upper, lower)
+
+    grads = [gather(grad_flat[:, :wide])[0]]
 
     away = jnp.abs(plane - row)
     cut = w_out.shape[0] // 2
@@ -414,49 +415,47 @@
 
     weights = [mine(first), mine(second)]
     weights += [to_core(part) for part in weights]
-    grads.append(gather(after(grad_flat[:, wide:], parts), attended))
-
-    def reduce_cores(attended, chunk):
-        keep, give = weight_terms(place, attended, chunk, rows)
+    block, handed = gather(after(grad_flat[:, wide:], parts), attended)
+    grads.append(block)
+    first[-1], second[-1] = after((first[-1], second[-1]), handed)
+
+    def reduce_cores(at, attended, chunk):
+        keep, give = weight_terms(place, attended, chunk, rows, not at)
         return keep, to_core(give)
 
-    def spread(keep, got):
-        both = [
+    def add_cores(keep, got):
+        return [
             (keep[slot].astype(jnp.float32) + got[slot].astype(jnp.float32)).astype(jnp.bfloat16)
             for slot in range(rows)
         ]
-        return [both[0]] + [to_row(both[slot], slot) for slot in range(1, rows)]
-
-    def reduce_planes(blocks):
-        stack = jnp.stack(blocks)
-
-        def block_of(ahead):
-            return lax.dynamic_index_in_dim(stack, ((plane + ahead) % planes) ^ row, 0, False)
-
-        return block_of(0), [to_plane(block_of(ahead), ahead) for ahead in range(1, planes)]
-
-    def collect(total, got):
-        for part in got:
-            total = total.astype(jnp.float32) + part.astype(jnp.float32)
-        total = total.astype(jnp.bfloat16)
-        return [total] + [to_row(total, slot) for slot in range(1, rows)]
-
-    blocks = spread(*reduce_cores(attended, grads[0]))
-    late = reduce_cores(attended, grads[1])
-    early = reduce_planes(after(blocks, late[0]))
+
+    def to_rows(blocks):
+        return [blocks[0]] + [to_row(blocks[slot], slot) for slot in range(1, rows)]
+
+    def to_planes(blocks):
+        return [blocks[0]] + [to_plane(blocks[ahead], ahead) for ahead in range(1, planes)]
+
+    def by_plane(blocks):
+        return [
+            lax.select_n(((plane + ahead) % planes) ^ row, *blocks) for ahead in range(planes)
+        ]
+
+    def added(blocks):
+        total = blocks[0].astype(jnp.float32)
+        for block in blocks[1:]:
+            total = total + block.astype(jnp.float32)
+        return total.astype(jnp.bfloat16)
+
+    early = to_planes(add_cores(*reduce_cores(0, attended, grads[0])))
+    late = to_rows(add_cores(*reduce_cores(1, attended, grads[1])))
     grad_attn = project(place, weights, grads)
-    heads = probs.shape[0]
-    blocks = spread(*after(late, early[0]))
-    sent = [backward(parts, probs, grad_attn, 0, 1)]
-    late = reduce_planes(after(blocks, sent[0][0]))
-    sent.append(backward(parts, after(probs, late[0]), grad_attn, 1, heads - 1))
-    back = [
-        [message[0]]
-        + [to_row(message[slot], slot) for slot in range(1, rows)]
-        for message in sent
-    ]
-    pieces = [collect(*after(early, sent[0][0])), collect(*after(late, sent[1][0]))]
-    return tuple(finish(place, back, pieces))
+    early = to_rows([added(after(early, grad_attn))] * rows)
+    sent = backward(parts, probs, grad_attn, 0, probs.shape[0])
+    back = to_rows(sent)
+    late = to_planes(by_plane(after(late, sent[0])))
+    early = to_planes(by_plane(after(early, sent[0])))
+    late = to_rows([added(late)] * rows)
+    return tuple(finish(place, [back], [early, late]))
 
 
 def by_tokens(query_rows, key_rows, value_rows, grad_out, w_out):

time: 227 us -> 184 us (0.81)
  waiting for transfers between devices: 89.4 us -> 59.3 us
  starting transfers between devices: 66.1 us -> 60.6 us
  other arithmetic: 7.96 us -> 4.5 us
  Pallas kernels: 53.3 us -> 50.3 us
    ppermute x47 -> x44, waiting for transfers between devices: 89.4 us -> 59.3 us  [send(): return lax.ppermute(array, ('fsdp', 'rows'), pairs)]
    ppermute x47 -> x44, starting transfers between devices: 66.1 us -> 60.6 us  [send(): return lax.ppermute(array, ('fsdp', 'rows'), pairs)]
    slice x4, local copies, waits for them, and re-layouts: 2.1 us -> 5.15 us  [gather(): upper, lower = (by_x[:cut], by_y[cut:])]
    pallas_call x2 -> x1, Pallas kernels: 14.1 us -> 11.4 us  [backward(): pl.pallas_call(body, grid=(count,), in_specs=[part] * rows + [pl.BlockSpe...]
  transfers between devices with their start and end apart: 47 -> 44, of which waited for: 13 -> 15; matrix products, arithmetic and copies ran while one was open for 5% -> 5% of each run, Pallas kernels for 21% -> 25%
where the time goes in v7:
time: 184 us
  starting transfers between devices  60.6 us (33%)
  waiting for transfers between devices  59.3 us (32%)
  Pallas kernels  50.3 us (27%)
  local copies, waits for them, and re-layouts  7.92 us (4%)
  other arithmetic  4.5 us (2%)
    ppermute x44, starting transfers between devices, send(): return lax.ppermute(array, ('fsdp', 'rows'), pairs)  60.6 us
    ppermute x44, waiting for transfers between devices, send(): return lax.ppermute(array, ('fsdp', 'rows'), pairs)  59.3 us
    pallas_call x1, Pallas kernels, forward(): pl.pallas_call(body, grid=(heads,), in_specs=[part] * rows, out_specs=[pl...  12.6 us
    pallas_call x1, Pallas kernels, backward(): pl.pallas_call(body, grid=(count,), in_specs=[part] * rows + [pl.BlockSpe...  11.4 us
    pallas_call x2, Pallas kernels, weight_terms(): pl.pallas_call(body, grid_spec=pltpu.PrefetchScalarGridSpec(num_scalar_pr...  10.4 us
    pallas_call x1, Pallas kernels, project(): pl.pallas_call(body, grid_spec=pltpu.PrefetchScalarGridSpec(num_scalar_pr...  8 us
    slice x4, local copies, waits for them, and re-layouts, gather(): upper, lower = (by_x[:cut], by_y[cut:])  5.15 us
    pallas_call x1, Pallas kernels, finish(): pl.pallas_call(body, grid_spec=pltpu.PrefetchScalarGridSpec(num_scalar_pr...  4.48 us
  transfers between devices with their start and end apart: 44, of which 15 were waited for; matrix products, arithmetic and copies ran while one was open for 5% of the time, Pallas kernels for 25%

profile of v7, /device:TPU:0, one launch (start us, length us, event | category | flops | bytes accessed | tf_op | source)
XLA Modules:
  0.0 183.9 jit_solution(11142371604910260656)
XLA Ops:
  0.6 1.3 fusion.9
  2.0 5.0 %collective-permute-start.3 = (bf16[96,3072]{1,0:T(8,128)(2,1)S(1)}, bf16[96,3072]{1,0:T(8,128)(2,1)S(1)}, u32[]{:S(2)}, u32[]{:S(2)}) collective-permute-start(bf16[96,3072]{1,0:T(8,128)(2,1)S(1)} %get-tuple-element.83), channel_id=1, source_target_pairs={{0,8},{4,12},{9,17},{13,21},{18,26},{22,30}} | collective-permute-start | bytes 1769480 | tf_op jit(solution)/shard_map/ppermute | solution.py:362
  7.0 1.5 collective-permute-start.4
  8.5 0.7 pad_add_fusion.place_ref
  9.1 3.4 %pack.1 = (bf16[3,256,384]{2,1,0:T(8,128)(2,1)}, bf16[3,256,384]{2,1,0:T(8,128)(2,1)}, bf16[3,256,384]{2,1,0:T(8,128)(2,1)}, bf16[3,256,384]{2,1,0:T(8,128)(2,1)}) custom-call(s32[3]{0:T(128)} %pad_add_fusion.place_ref, bf16[1,256,1536]{2,1,0:T(8,128)(2,1)} %refs_0_.1, bf16[1,256,1536]{2,1,0:T(8,128)(2,1)} %refs_1_.1, bf16[1,256,1536]{2,1,0:T(8,128)(2,1)} %refs_2_.1), custom_call_target="tpu_custom_call" | custom-call | bytes 4718592 | tf_op jit(solution)/shard_map/pack/pallas_call | solution.py:52
  12.8 3.3 %collective-permute-start.2 = (bf16[3,256,384]{2,1,0:T(8,128)(2,1)}, bf16[3,256,384]{2,1,0:T(8,128)(2,1)}, u32[]{:S(2)}, u32[]{:S(2)}) collective-permute-start(bf16[3,256,384]{2,1,0:T(8,128)(2,1)} %get-tuple-element.40), channel_id=1, source_target_pairs={{0,3},{1,2},{2,1},{3,0},{4,7},{5,6},{6,5},{7,4},{8,11},{9,10},{10,... | collective-permute-start | bytes 1769480 | tf_op jit(solution)/shard_map/ppermute | solution.py:362
  16.1 3.4 %collective-permute-done.3 = bf16[96,3072]{1,0:T(8,128)(2,1)S(1)} collective-permute-done((bf16[96,3072]{1,0:T(8,128)(2,1)S(1)}, bf16[96,3072]{1,0:T(8,128)(2,1)S(1)}, u32[]{:S(2)}, u32[]{:S(2)}) %collective-permute-start.3) | collective-permute-done | bytes 589856 | tf_op jit(solution)/shard_map/ppermute | solution.py:362
  19.5 1.1 broadcast_select_fusion.1
  20.6 3.4 %collective-permute-start.7 = (bf16[96,3072]{1,0:T(8,128)(2,1)S(1)}, bf16[96,3072]{1,0:T(8,128)(2,1)S(1)}, u32[]{:S(2)}, u32[]{:S(2)}) collective-permute-start(bf16[96,3072]{1,0:T(8,128)(2,1)S(1)} %get-tuple-element.42), channel_id=1, source_target_pairs={{0,8},{4,12},{9,17},{13,21},{18,26},{22,30}} | collective-permute-start | bytes 1769480 | tf_op jit(solution)/shard_map/ppermute | solution.py:362
  24.0 0.7 collective-permute-start.8
  24.8 4.3 %collective-permute-done.refs_1_ = bf16[3,256,384]{2,1,0:T(8,128)(2,1)} collective-permute-done((bf16[3,256,384]{2,1,0:T(8,128)(2,1)}, bf16[3,256,384]{2,1,0:T(8,128)(2,1)}, u32[]{:S(2)}, u32[]{:S(2)}) %collective-permute-start) | collective-permute-done | bytes 589856 | tf_op jit(solution)/shard_map/ppermute | solution.py:362
  29.1 11.3 %collective-permute-done.1.refs_2_ = bf16[3,256,384]{2,1,0:T(8,128)(2,1)} collective-permute-done((bf16[3,256,384]{2,1,0:T(8,128)(2,1)}, bf16[3,256,384]{2,1,0:T(8,128)(2,1)}, u32[]{:S(2)}, u32[]{:S(2)}) %collective-permute-start.1) | collective-permute-done | bytes 589856 | tf_op jit(solution)/shard_map/ppermute | solution.py:362
  40.5 0.7 collective-permute-start.5
  41.2 1.7 collective-permute-start.17
  42.9 2.0 %collective-permute-start.18 = (bf16[256,1536]{1,0:T(8,128)(2,1)S(1)}, bf16[256,1536]{1,0:T(8,128)(2,1)}, u32[]{:S(2)}, u32[]{:S(2)}) collective-permute-start(bf16[256,1536]{1,0:T(8,128)(2,1)S(1)} %get-tuple-element.47.refs_9_.refs_0_), channel_id=1, source_target_pairs={{0,2},{1,3},{2,0},{3,1},{4,6},{5,7},{6,4},{7,5},{8,10},{9,11},{10,... | collective-permute-start | bytes 2359304 | tf_op jit(solution)/shard_map/ppermute | solution.py:362
  45.0 13.5 %collective-permute-done.13.refs_5_.refs_1_ = bf16[256,1536]{1,0:T(8,128)(2,1)S(1)} collective-permute-done((bf16[256,1536]{1,0:T(8,128)(2,1)S(1)}, bf16[256,1536]{1,0:T(8,128)(2,1)S(1)}, u32[]{:S(2)}, u32[]{:S(2)}) %collective-permute-start.13) | collective-permute-done | bytes 786464 | tf_op jit(solution)/shard_map/ppermute | solution.py:362
  58.5 1.5 collective-permute-start.9
  60.0 0.9 collective-permute-done.14.refs_6_.refs_2_
  60.9 0.8 slice.75
  61.7 0.8 slice.76
  62.5 1.7 collective-permute-start.16
  64.2 12.6 %forward.1 = (bf16[3,1024,1024]{2,1,0:T(8,128)(2,1)}, bf16[384,1024]{1,0:T(8,128)(2,1)}) custom-call(bf16[3,256,384]{2,1,0:T(8,128)(2,1)} %get-tuple-element.37.refs_0_, bf16[3,256,384]{2,1,0:T(8,128)(2,1)} %collective-permute-done.refs_1_, bf16[3,256,384]{2,1,0:T(8,128)(2,1)} %collective-permute-done.1.refs_2_, ...), custom_call_target="tpu_custom_call" | custom-call | flops 3221225472 | bytes 6291456 | tf_op jit(solution)/shard_map/forward/pallas_call | solution.py:180
  76.8 1.5 collective-permute-start.6
  78.3 1.5 collective-permute-start.10
  79.9 1.8 slice.78
  81.6 2.0 %collective-permute-start.19 = (bf16[128,1536]{1,0:T(8,128)(2,1)}, bf16[128,1536]{1,0:T(8,128)(2,1)S(1)}, u32[]{:S(2)}, u32[]{:S(2)}) collective-permute-start(bf16[128,1536]{1,0:T(8,128)(2,1)} %slice.78), channel_id=1, source_target_pairs={{0,2},{1,3},{2,0},{3,1},{4,6},{5,7},{6,4},{7,5},{8,10},{9,11},{10,... | collective-permute-start | bytes 1179656 | tf_op jit(solution)/shard_map/ppermute | solution.py:362
  83.6 1.8 slice.79
  85.4 0.8 collective-permute-done.15.refs_7_.refs_3_
  86.2 1.3 collective-permute-start.20
  87.6 5.2 %weight_terms.2 = (bf16[4,48,1536]{2,1,0:T(8,128)(2,1)}, bf16[4,48,1536]{2,1,0:T(8,128)(2,1)}) custom-call(s32[3]{0:T(128)} %pad_add_fusion.place_ref, bf16[384,1024]{1,0:T(8,128)(2,1)} %get-tuple-element.43.attended_ref, bf16[256,1536]{1,0:T(8,128)(2,1)} %copy-done.2, bf16[256,1536]{1,0:T(8,128)(2,1)} %copy-done.5, bf16[256,1536]{1,0:T(8,128)(2,1)} %copy-done.6, ...), custom_call_target="tpu_custom_call" | custom-call | flops 1207959552 | bytes 3932160 | tf_op jit(solution)/shard_map/weight_terms/pallas_call | solution.py:323
  92.9 1.5 collective-permute-done.20.refs_13_.refs_4_
  94.3 5.2 %weight_terms.3 = (bf16[4,48,1536]{2,1,0:T(8,128)(2,1)}, bf16[4,48,1536]{2,1,0:T(8,128)(2,1)}) custom-call(s32[3]{0:T(128)} %pad_add_fusion.place_ref, bf16[384,1024]{1,0:T(8,128)(2,1)} %get-tuple-element.43.attended_ref, bf16[256,1536]{1,0:T(8,128)(2,1)} %copy-done.1, bf16[256,1536]{1,0:T(8,128)(2,1)} %collective-permute-done.17.refs_10_.refs_1_, ...), custom_call_target="tpu_custom_call" | custom-call | flops 1207959552 | bytes 3932160 | tf_op jit(solution)/shard_map/weight_terms/pallas_call | solution.py:323
  99.9 0.5 collective-permute-start.11
  100.6 1.3 fusion.3
  101.9 3.4 %collective-permute-start.25 = (bf16[48,1536]{1,0:T(8,128)(2,1)S(1)}, bf16[48,1536]{1,0:T(8,128)(2,1)S(1)}, u32[]{:S(2)}, u32[]{:S(2)}) collective-permute-start(bf16[48,1536]{1,0:T(8,128)(2,1)S(1)} %get-tuple-element.78), channel_id=1, source_target_pairs={{0,8},{1,9},{2,10},{3,11},{4,12},{5,13},{6,14},{7,15},{8,16},{9,17... | collective-permute-start | bytes 442376 | tf_op jit(solution)/shard_map/ppermute | solution.py:362
  105.3 5.1 %collective-permute-start.26 = (bf16[48,1536]{1,0:T(8,128)(2,1)S(1)}, bf16[48,1536]{1,0:T(8,128)(2,1)S(1)}, u32[]{:S(2)}, u32[]{:S(2)}) collective-permute-start(bf16[48,1536]{1,0:T(8,128)(2,1)S(1)} %get-tuple-element.77), channel_id=1, source_target_pairs={{0,16},{1,17},{2,18},{3,19},{4,20},{5,21},{6,22},{7,23},{8,24},{9,... | collective-permute-start | bytes 442376 | tf_op jit(solution)/shard_map/ppermute | solution.py:362
  110.9 2.1 %collective-permute-start.36 = (bf16[48,1536]{1,0:T(8,128)(2,1)S(1)}, bf16[48,1536]{1,0:T(8,128)(2,1)S(1)}, u32[]{:S(2)}, u32[]{:S(2)}) collective-permute-start(bf16[48,1536]{1,0:T(8,128)(2,1)S(1)} %get-tuple-element.73), channel_id=1, source_target_pairs={{0,2},{1,3},{2,0},{3,1},{4,6},{5,7},{6,4},{7,5},{8,10},{9,11},{10,... | collective-permute-start | bytes 442376 | tf_op jit(solution)/shard_map/ppermute | solution.py:362
  113.0 8.0 %project.1.refs_5_ = bf16[384,1024]{1,0:T(8,128)(2,1)} custom-call(s32[3]{0:T(128)} %pad_add_fusion.place_ref, bf16[96,3072]{1,0:T(8,128)(2,1)} %copy-done.4, bf16[96,3072]{1,0:T(8,128)(2,1)} %copy-done.3, bf16[96,3072]{1,0:T(8,128)(2,1)} %copy-done.8, bf16[96,3072]{1,0:T(8,128)(2,1)} %copy-done.9, bf16[256,1536]{1,0:T(8,128)(2,1)} %copy-done.2, ...), custom_call_target="tpu_custom_call" | custom-call | flops 2415919104 | bytes 8650752 | tf_op jit(solution)/shard_map/project/pallas_call | solution.py:284
  121.0 1.4 collective-permute-start.37
  122.6 1.0 collective-permute-start.28
  123.5 1.2 collective-permute-start.29
  124.7 11.4 %backward.1 = (bf16[3,256,384]{2,1,0:T(8,128)(2,1)}, bf16[3,256,384]{2,1,0:T(8,128)(2,1)}, bf16[3,256,384]{2,1,0:T(8,128)(2,1)}, bf16[3,256,384]{2,1,0:T(8,128)(2,1)}) custom-call(bf16[3,256,384]{2,1,0:T(8,128)(2,1)} %get-tuple-element.37.refs_0_, bf16[3,256,384]{2,1,0:T(8,128)(2,1)} %collective-permute-done.refs_1_, ...), custom_call_target="tpu_custom_call" | custom-call | flops 3221225472 | bytes 6291456 | tf_op jit(solution)/shard_map/backward/pallas_call | solution.py:229
  136.1 1.4 collective-permute-start.30
  137.6 0.9 collective-permute-start.21
  138.5 1.2 collective-permute-start.22
  139.8 0.9 collective-permute-start.40
  140.7 1.8 collective-permute-start.39
  142.4 1.4 collective-permute-done.30
  143.8 1.2 collective-permute-start.38
  145.0 0.7 select_select_fusion.5
  145.7 1.6 collective-permute-done.40
  147.4 0.3 collective-permute-start.23
  147.7 5.8 %collective-permute-done.39 = bf16[48,1536]{1,0:T(8,128)(2,1)S(1)} collective-permute-done((bf16[48,1536]{1,0:T(8,128)(2,1)S(1)}, bf16[48,1536]{1,0:T(8,128)(2,1)S(1)}, u32[]{:S(2)}, u32[]{:S(2)}) %collective-permute-start.39) | collective-permute-done | bytes 147488 | tf_op jit(solution)/shard_map/ppermute | solution.py:362
  153.5 1.1 collective-permute-start.31
  154.6 0.9 collective-permute-start.32
  155.6 6.4 %collective-permute-done.31.refs_5_ = bf16[48,1536]{1,0:T(8,128)(2,1)S(1)} collective-permute-done((bf16[48,1536]{1,0:T(8,128)(2,1)S(1)}, bf16[48,1536]{1,0:T(8,128)(2,1)S(1)}, u32[]{:S(2)}, u32[]{:S(2)}) %collective-permute-start.31) | collective-permute-done | bytes 147488 | tf_op jit(solution)/shard_map/ppermute | solution.py:362
  162.0 3.6 %collective-permute-done.32.refs_6_ = bf16[48,1536]{1,0:T(8,128)(2,1)S(1)} collective-permute-done((bf16[48,1536]{1,0:T(8,128)(2,1)S(1)}, bf16[48,1536]{1,0:T(8,128)(2,1)S(1)}, u32[]{:S(2)}, u32[]{:S(2)}) %collective-permute-start.32) | collective-permute-done | bytes 147488 | tf_op jit(solution)/shard_map/ppermute | solution.py:362
  165.6 1.3 collective-permute-start.41
  167.2 2.1 %collective-permute-start.42 = (bf16[48,1536]{1,0:T(8,128)(2,1)S(1)}, bf16[48,1536]{1,0:T(8,128)(2,1)S(1)}, u32[]{:S(2)}, u32[]{:S(2)}) collective-permute-start(bf16[48,1536]{1,0:T(8,128)(2,1)S(1)} %add_convert_fusion.refs_8_), channel_id=1, source_target_pairs={{0,2},{1,3},{2,0},{3,1},{4,6},{5,7},{6,4},{7,5},{8,10},{9,11},{10,... | collective-permute-start | bytes 442376 | tf_op jit(solution)/shard_map/ppermute | solution.py:362
  169.3 1.5 collective-permute-done.41.refs_9_
  170.8 4.1 %collective-permute-start.43 = (bf16[48,1536]{1,0:T(8,128)(2,1)S(1)}, bf16[48,1536]{1,0:T(8,128)(2,1)S(1)}, u32[]{:S(2)}, u32[]{:S(2)}) collective-permute-start(bf16[48,1536]{1,0:T(8,128)(2,1)S(1)} %add_convert_fusion.refs_8_), channel_id=1, source_target_pairs={{0,3},{1,2},{2,1},{3,0},{4,7},{5,6},{6,5},{7,4},{8,11},{9,10},{10,... | collective-permute-start | bytes 442376 | tf_op jit(solution)/shard_map/ppermute | solution.py:362
  174.8 3.1 %collective-permute-done.43.refs_11_ = bf16[48,1536]{1,0:T(8,128)(2,1)S(1)} collective-permute-done((bf16[48,1536]{1,0:T(8,128)(2,1)S(1)}, bf16[48,1536]{1,0:T(8,128)(2,1)S(1)}, u32[]{:S(2)}, u32[]{:S(2)}) %collective-permute-start.43) | collective-permute-done | bytes 147488 | tf_op jit(solution)/shard_map/ppermute | solution.py:362
  178.0 0.6 copy-done.22
  179.2 4.5 %finish.1 = (bf16[1,256,1536]{2,1,0:T(8,128)(2,1)}, bf16[1,256,1536]{2,1,0:T(8,128)(2,1)}, bf16[1,256,1536]{2,1,0:T(8,128)(2,1)}, f32[192,3072]{1,0:T(8,128)}) custom-call(s32[3]{0:T(128)} %pad_add_fusion.place_ref, bf16[3,256,384]{2,1,0:T(8,128)(2,1)} %get-tuple-element.50.refs_0_, bf16[3,256,384]{2,1,0:T(8,128)(2,1)} %copy-done.13, ...), custom_call_target="tpu_custom_call" | custom-call | bytes 8257536 | tf_op jit(solution)/shard_map/finish/pallas_call | solution.py:138
  (95 shorter events, 2.7 us)
Async XLA Ops:
  2.0 17.5 %collective-permute-start.3 = (bf16[96,3072]{1,0:T(8,128)(2,1)S(1)}, bf16[96,3072]{1,0:T(8,128)(2,1)S(1)}, u32[]{:S(2)}, u32[]{:S(2)}) collective-permute-start(bf16[96,3072]{1,0:T(8,128)(2,1)S(1)} %get-tuple-element.83), channel_id=1, source_target_pairs={{0,8},{4,12},{9,17},{13,21},{18,26},{22,30}} | collective-permute-start | bytes 1769480 | tf_op jit(solution)/shard_map/ppermute | solution.py:362
  7.0 12.5 %collective-permute-start.4 = (bf16[96,3072]{1,0:T(8,128)(2,1)S(1)}, bf16[96,3072]{1,0:T(8,128)(2,1)}, u32[]{:S(2)}, u32[]{:S(2)}) collective-permute-start(bf16[96,3072]{1,0:T(8,128)(2,1)S(1)} %get-tuple-element.83), channel_id=1, source_target_pairs={{9,1},{13,5},{18,10},{22,14},{27,19},{31,23}} | collective-permute-start | bytes 1769480 | tf_op jit(solution)/shard_map/ppermute | solution.py:362
  9.1 15.6 %copy-start.7 = (bf16[1,256,3072]{2,1,0:T(8,128)(2,1)S(1)}, bf16[1,256,3072]{2,1,0:T(8,128)(2,1)}, u32[]{:S(2)}) copy-start(bf16[1,256,3072]{2,1,0:T(8,128)(2,1)} %param.8) | copy-start | bytes 4718596
  12.6 16.6 %collective-permute-start = (bf16[3,256,384]{2,1,0:T(8,128)(2,1)}, bf16[3,256,384]{2,1,0:T(8,128)(2,1)}, u32[]{:S(2)}, u32[]{:S(2)}) collective-permute-start(bf16[3,256,384]{2,1,0:T(8,128)(2,1)} %get-tuple-element.38), channel_id=1, source_target_pairs={{0,1},{1,0},{2,3},{3,2},{4,5},{5,4},{6,7},{7,6},{8,9},{9,8},{10,11... | collective-permute-start | bytes 1769480 | tf_op jit(solution)/shard_map/ppermute | solution.py:362
  12.6 27.8 %collective-permute-start.1 = (bf16[3,256,384]{2,1,0:T(8,128)(2,1)}, bf16[3,256,384]{2,1,0:T(8,128)(2,1)}, u32[]{:S(2)}, u32[]{:S(2)}) collective-permute-start(bf16[3,256,384]{2,1,0:T(8,128)(2,1)} %get-tuple-element.39), channel_id=1, source_target_pairs={{0,2},{1,3},{2,0},{3,1},{4,6},{5,7},{6,4},{7,5},{8,10},{9,11},{10,... | collective-permute-start | bytes 1769480 | tf_op jit(solution)/shard_map/ppermute | solution.py:362
  12.8 27.6 %collective-permute-start.2 = (bf16[3,256,384]{2,1,0:T(8,128)(2,1)}, bf16[3,256,384]{2,1,0:T(8,128)(2,1)}, u32[]{:S(2)}, u32[]{:S(2)}) collective-permute-start(bf16[3,256,384]{2,1,0:T(8,128)(2,1)} %get-tuple-element.40), channel_id=1, source_target_pairs={{0,3},{1,2},{2,1},{3,0},{4,7},{5,6},{6,5},{7,4},{8,11},{9,10},{10,... | collective-permute-start | bytes 1769480 | tf_op jit(solution)/shard_map/ppermute | solution.py:362
  20.6 20.5 %collective-permute-start.7 = (bf16[96,3072]{1,0:T(8,128)(2,1)S(1)}, bf16[96,3072]{1,0:T(8,128)(2,1)S(1)}, u32[]{:S(2)}, u32[]{:S(2)}) collective-permute-start(bf16[96,3072]{1,0:T(8,128)(2,1)S(1)} %get-tuple-element.42), channel_id=1, source_target_pairs={{0,8},{4,12},{9,17},{13,21},{18,26},{22,30}} | collective-permute-start | bytes 1769480 | tf_op jit(solution)/shard_map/ppermute | solution.py:362
  24.0 18.9 %collective-permute-start.8 = (bf16[96,3072]{1,0:T(8,128)(2,1)S(1)}, bf16[96,3072]{1,0:T(8,128)(2,1)S(1)}, u32[]{:S(2)}, u32[]{:S(2)}) collective-permute-start(bf16[96,3072]{1,0:T(8,128)(2,1)S(1)} %get-tuple-element.42), channel_id=1, source_target_pairs={{9,1},{13,5},{18,10},{22,14},{27,19},{31,23}} | collective-permute-start | bytes 1769480 | tf_op jit(solution)/shard_map/ppermute | solution.py:362
  24.8 37.7 %copy-start.1 = (bf16[256,1536]{1,0:T(8,128)(2,1)}, bf16[256,1536]{1,0:T(8,128)(2,1)S(1)}, u32[]{:S(2)}) copy-start(bf16[256,1536]{1,0:T(8,128)(2,1)S(1)} %get-tuple-element.47.refs_9_.refs_0_) | copy-start | bytes 2359300
  24.8 37.7 %copy-start.2 = (bf16[256,1536]{1,0:T(8,128)(2,1)}, bf16[256,1536]{1,0:T(8,128)(2,1)S(1)}, u32[]{:S(2)}) copy-start(bf16[256,1536]{1,0:T(8,128)(2,1)S(1)} %get-tuple-element.71.refs_4_.refs_0_) | copy-start | bytes 2359300
  29.1 29.4 %collective-permute-start.13 = (bf16[256,1536]{1,0:T(8,128)(2,1)S(1)}, bf16[256,1536]{1,0:T(8,128)(2,1)S(1)}, u32[]{:S(2)}, u32[]{:S(2)}) collective-permute-start(bf16[256,1536]{1,0:T(8,128)(2,1)S(1)} %get-tuple-element.71.refs_4_.refs_0_), channel_id=1, source_target_pairs={{0,1},{1,0},{2,3},{3,2},{4,5},{5,4},{6,7},{7,6},{8,9},{9,8},{10,11... | collective-permute-start | bytes 2359304 | tf_op jit(solution)/shard_map/ppermute | solution.py:362
  40.4 20.4 %collective-permute-start.14 = (bf16[256,1536]{1,0:T(8,128)(2,1)S(1)}, bf16[256,1536]{1,0:T(8,128)(2,1)S(1)}, u32[]{:S(2)}, u32[]{:S(2)}) collective-permute-start(bf16[256,1536]{1,0:T(8,128)(2,1)S(1)} %get-tuple-element.71.refs_4_.refs_0_), channel_id=1, source_target_pairs={{0,2},{1,3},{2,0},{3,1},{4,6},{5,7},{6,4},{7,5},{8,10},{9,11},{10,... | collective-permute-start | bytes 2359304 | tf_op jit(solution)/shard_map/ppermute | solution.py:362
  40.5 22.0 %collective-permute-start.5 = (bf16[96,3072]{1,0:T(8,128)(2,1)S(1)}, bf16[96,3072]{1,0:T(8,128)(2,1)S(1)}, u32[]{:S(2)}, u32[]{:S(2)}) collective-permute-start(bf16[96,3072]{1,0:T(8,128)(2,1)S(1)} %broadcast_select_fusion.1), channel_id=1, source_target_pairs={{8,16},{10,2},{12,20},{14,6},{17,25},{19,11},{21,29},{23,15}} | collective-permute-start | bytes 1769480 | tf_op jit(solution)/shard_map/ppermute | solution.py:362
  41.2 37.1 %collective-permute-start.17 = (bf16[256,1536]{1,0:T(8,128)(2,1)S(1)}, bf16[256,1536]{1,0:T(8,128)(2,1)}, u32[]{:S(2)}, u32[]{:S(2)}) collective-permute-start(bf16[256,1536]{1,0:T(8,128)(2,1)S(1)} %get-tuple-element.47.refs_9_.refs_0_), channel_id=1, source_target_pairs={{0,1},{1,0},{2,3},{3,2},{4,5},{5,4},{6,7},{7,6},{8,9},{9,8},{10,11... | collective-permute-start | bytes 2359304 | tf_op jit(solution)/shard_map/ppermute | solution.py:362
  42.9 37.0 %collective-permute-start.18 = (bf16[256,1536]{1,0:T(8,128)(2,1)S(1)}, bf16[256,1536]{1,0:T(8,128)(2,1)}, u32[]{:S(2)}, u32[]{:S(2)}) collective-permute-start(bf16[256,1536]{1,0:T(8,128)(2,1)S(1)} %get-tuple-element.47.refs_9_.refs_0_), channel_id=1, source_target_pairs={{0,2},{1,3},{2,0},{3,1},{4,6},{5,7},{6,4},{7,5},{8,10},{9,11},{10,... | collective-permute-start | bytes 2359304 | tf_op jit(solution)/shard_map/ppermute | solution.py:362
  58.5 18.3 %copy-start.5 = (bf16[256,1536]{1,0:T(8,128)(2,1)}, bf16[256,1536]{1,0:T(8,128)(2,1)S(1)}, u32[]{:S(2)}) copy-start(bf16[256,1536]{1,0:T(8,128)(2,1)S(1)} %collective-permute-done.13.refs_5_.refs_1_) | copy-start | bytes 2359300
  58.5 18.3 %collective-permute-start.9 = (bf16[96,3072]{1,0:T(8,128)(2,1)S(1)}, bf16[96,3072]{1,0:T(8,128)(2,1)}, u32[]{:S(2)}, u32[]{:S(2)}) collective-permute-start(bf16[96,3072]{1,0:T(8,128)(2,1)S(1)} %broadcast_select_fusion), channel_id=1, source_target_pairs={{8,16},{10,2},{12,20},{14,6},{17,25},{19,11},{21,29},{23,15}} | collective-permute-start | bytes 1769480 | tf_op jit(solution)/shard_map/ppermute | solution.py:362
  60.9 1.6 copy-start.6
  61.7 24.6 %collective-permute-start.15 = (bf16[128,1536]{1,0:T(8,128)(2,1)}, bf16[128,1536]{1,0:T(8,128)(2,1)}, u32[]{:S(2)}, u32[]{:S(2)}) collective-permute-start(bf16[128,1536]{1,0:T(8,128)(2,1)} %slice.75), channel_id=1, source_target_pairs={{0,2},{1,3},{2,0},{3,1},{4,6},{5,7},{6,4},{7,5},{8,10},{9,11},{10,... | collective-permute-start | bytes 1179656 | tf_op jit(solution)/shard_map/ppermute | solution.py:362
  62.5 25.1 %collective-permute-start.16 = (bf16[128,1536]{1,0:T(8,128)(2,1)}, bf16[128,1536]{1,0:T(8,128)(2,1)}, u32[]{:S(2)}, u32[]{:S(2)}) collective-permute-start(bf16[128,1536]{1,0:T(8,128)(2,1)} %slice.76), channel_id=1, source_target_pairs={{0,1},{1,0},{2,3},{3,2},{4,5},{5,4},{6,7},{7,6},{8,9},{9,8},{10,11... | collective-permute-start | bytes 1179656 | tf_op jit(solution)/shard_map/ppermute | solution.py:362
  76.8 22.8 %collective-permute-start.6 = (bf16[96,3072]{1,0:T(8,128)(2,1)S(1)}, bf16[96,3072]{1,0:T(8,128)(2,1)}, u32[]{:S(2)}, u32[]{:S(2)}) collective-permute-start(bf16[96,3072]{1,0:T(8,128)(2,1)S(1)} %collective-permute-done.5), channel_id=1, source_target_pairs={{11,3},{15,7},{16,24},{20,28}} | collective-permute-start | bytes 1769480 | tf_op jit(solution)/shard_map/ppermute | solution.py:362
  78.3 21.3 %collective-permute-start.10 = (bf16[96,3072]{1,0:T(8,128)(2,1)}, bf16[96,3072]{1,0:T(8,128)(2,1)}, u32[]{:S(2)}, u32[]{:S(2)}) collective-permute-start(bf16[96,3072]{1,0:T(8,128)(2,1)} %collective-permute-done.9), channel_id=1, source_target_pairs={{11,3},{15,7},{16,24},{20,28}} | collective-permute-start | bytes 1769480 | tf_op jit(solution)/shard_map/ppermute | solution.py:362
  81.6 11.2 %collective-permute-start.19 = (bf16[128,1536]{1,0:T(8,128)(2,1)}, bf16[128,1536]{1,0:T(8,128)(2,1)S(1)}, u32[]{:S(2)}, u32[]{:S(2)}) collective-permute-start(bf16[128,1536]{1,0:T(8,128)(2,1)} %slice.78), channel_id=1, source_target_pairs={{0,2},{1,3},{2,0},{3,1},{4,6},{5,7},{6,4},{7,5},{8,10},{9,11},{10,... | collective-permute-start | bytes 1179656 | tf_op jit(solution)/shard_map/ppermute | solution.py:362
  86.2 8.1 %collective-permute-start.20 = (bf16[128,1536]{1,0:T(8,128)(2,1)}, bf16[128,1536]{1,0:T(8,128)(2,1)}, u32[]{:S(2)}, u32[]{:S(2)}) collective-permute-start(bf16[128,1536]{1,0:T(8,128)(2,1)} %slice.79), channel_id=1, source_target_pairs={{0,1},{1,0},{2,3},{3,2},{4,5},{5,4},{6,7},{7,6},{8,9},{9,8},{10,11... | collective-permute-start | bytes 1179656 | tf_op jit(solution)/shard_map/ppermute | solution.py:362
  92.8 6.8 %copy-start = (bf16[192,3072]{1,0:T(8,128)(2,1)S(1)}, bf16[192,3072]{1,0:T(8,128)(2,1)}, u32[]{:S(2)}) copy-start(bf16[192,3072]{1,0:T(8,128)(2,1)} %param.9) | copy-start | bytes 3538948
  92.8 7.7 %collective-permute-start.24 = (bf16[4,48,1536]{2,1,0:T(8,128)(2,1)}, bf16[4,48,1536]{2,1,0:T(8,128)(2,1)}, u32[]{:S(2)}, u32[]{:S(2)}) collective-permute-start(bf16[4,48,1536]{2,1,0:T(8,128)(2,1)} %get-tuple-element.55), channel_id=1, source_target_pairs={{0,4},{1,5},{2,6},{3,7},{4,0},{5,1},{6,2},{7,3},{8,12},{9,13},{10,... | collective-permute-start | bytes 1769480 | tf_op jit(solution)/shard_map/ppermute | solution.py:362
  92.9 1.5 copy-start.16
  99.5 10.8 %collective-permute-start.34 = (bf16[4,48,1536]{2,1,0:T(8,128)(2,1)}, bf16[4,48,1536]{2,1,0:T(8,128)(2,1)S(1)}, u32[]{:S(2)}, u32[]{:S(2)}) collective-permute-start(bf16[4,48,1536]{2,1,0:T(8,128)(2,1)} %get-tuple-element.65), channel_id=1, source_target_pairs={{0,4},{1,5},{2,6},{3,7},{4,0},{5,1},{6,2},{7,3},{8,12},{9,13},{10,... | collective-permute-start | bytes 1769480 | tf_op jit(solution)/shard_map/ppermute | solution.py:362
  99.9 10.9 %copy-start.3 = (bf16[96,3072]{1,0:T(8,128)(2,1)}, bf16[96,3072]{1,0:T(8,128)(2,1)S(1)}, u32[]{:S(2)}) copy-start(bf16[96,3072]{1,0:T(8,128)(2,1)S(1)} %get-tuple-element.80.refs_1_) | copy-start | bytes 1769476
  99.9 10.9 %copy-start.4 = (bf16[96,3072]{1,0:T(8,128)(2,1)}, bf16[96,3072]{1,0:T(8,128)(2,1)S(1)}, u32[]{:S(2)}) copy-start(bf16[96,3072]{1,0:T(8,128)(2,1)S(1)} %get-tuple-element.81.refs_0_) | copy-start | bytes 1769476
  99.9 10.8 %copy-start.10 = (bf16[4,48,1536]{2,1,0:T(8,128)(2,1)S(1)}, bf16[4,48,1536]{2,1,0:T(8,128)(2,1)}, u32[]{:S(2)}) copy-start(bf16[4,48,1536]{2,1,0:T(8,128)(2,1)} %get-tuple-element.64) | copy-start | bytes 1769476
  99.9 10.9 %collective-permute-start.11 = (bf16[96,3072]{1,0:T(8,128)(2,1)S(1)}, bf16[96,3072]{1,0:T(8,128)(2,1)S(1)}, u32[]{:S(2)}, u32[]{:S(2)}) collective-permute-start(bf16[96,3072]{1,0:T(8,128)(2,1)S(1)} %get-tuple-element.81.refs_0_), channel_id=1, source_target_pairs={{0,4},{1,5},{2,6},{3,7},{4,0},{5,1},{6,2},{7,3},{8,12},{9,13},{10,... | collective-permute-start | bytes 1769480 | tf_op jit(solution)/shard_map/ppermute | solution.py:362
  100.4 10.5 %collective-permute-start.12 = (bf16[96,3072]{1,0:T(8,128)(2,1)S(1)}, bf16[96,3072]{1,0:T(8,128)(2,1)S(1)}, u32[]{:S(2)}, u32[]{:S(2)}) collective-permute-start(bf16[96,3072]{1,0:T(8,128)(2,1)S(1)} %get-tuple-element.80.refs_1_), channel_id=1, source_target_pairs={{0,4},{1,5},{2,6},{3,7},{4,0},{5,1},{6,2},{7,3},{8,12},{9,13},{10,... | collective-permute-start | bytes 1769480 | tf_op jit(solution)/shard_map/ppermute | solution.py:362
  101.9 19.2 %collective-permute-start.25 = (bf16[48,1536]{1,0:T(8,128)(2,1)S(1)}, bf16[48,1536]{1,0:T(8,128)(2,1)S(1)}, u32[]{:S(2)}, u32[]{:S(2)}) collective-permute-start(bf16[48,1536]{1,0:T(8,128)(2,1)S(1)} %get-tuple-element.78), channel_id=1, source_target_pairs={{0,8},{1,9},{2,10},{3,11},{4,12},{5,13},{6,14},{7,15},{8,16},{9,17... | collective-permute-start | bytes 442376 | tf_op jit(solution)/shard_map/ppermute | solution.py:362
  105.3 17.2 %collective-permute-start.26 = (bf16[48,1536]{1,0:T(8,128)(2,1)S(1)}, bf16[48,1536]{1,0:T(8,128)(2,1)S(1)}, u32[]{:S(2)}, u32[]{:S(2)}) collective-permute-start(bf16[48,1536]{1,0:T(8,128)(2,1)S(1)} %get-tuple-element.77), channel_id=1, source_target_pairs={{0,16},{1,17},{2,18},{3,19},{4,20},{5,21},{6,22},{7,23},{8,24},{9,... | collective-permute-start | bytes 442376 | tf_op jit(solution)/shard_map/ppermute | solution.py:362
  110.4 12.1 %collective-permute-start.27 = (bf16[48,1536]{1,0:T(8,128)(2,1)S(1)}, bf16[48,1536]{1,0:T(8,128)(2,1)S(1)}, u32[]{:S(2)}, u32[]{:S(2)}) collective-permute-start(bf16[48,1536]{1,0:T(8,128)(2,1)S(1)} %get-tuple-element.76), channel_id=1, source_target_pairs={{0,24},{1,25},{2,26},{3,27},{4,28},{5,29},{6,30},{7,31},{8,0},{9,1... | collective-permute-start | bytes 442376 | tf_op jit(solution)/shard_map/ppermute | solution.py:362
  110.8 2.2 %copy-start.8 = (bf16[96,3072]{1,0:T(8,128)(2,1)}, bf16[96,3072]{1,0:T(8,128)(2,1)S(1)}, u32[]{:S(2)}) copy-start(bf16[96,3072]{1,0:T(8,128)(2,1)S(1)} %collective-permute-done.11.refs_2_) | copy-start | bytes 1769476
  110.8 25.3 %collective-permute-start.35 = (bf16[48,1536]{1,0:T(8,128)(2,1)S(1)}, bf16[48,1536]{1,0:T(8,128)(2,1)S(1)}, u32[]{:S(2)}, u32[]{:S(2)}) collective-permute-start(bf16[48,1536]{1,0:T(8,128)(2,1)S(1)} %get-tuple-element.74), channel_id=1, source_target_pairs={{0,1},{1,0},{2,3},{3,2},{4,5},{5,4},{6,7},{7,6},{8,9},{9,8},{10,11... | collective-permute-start | bytes 442376 | tf_op jit(solution)/shard_map/ppermute | solution.py:362
  110.9 2.1 %copy-start.9 = (bf16[96,3072]{1,0:T(8,128)(2,1)}, bf16[96,3072]{1,0:T(8,128)(2,1)S(1)}, u32[]{:S(2)}) copy-start(bf16[96,3072]{1,0:T(8,128)(2,1)S(1)} %collective-permute-done.12.refs_3_) | copy-start | bytes 1769476
  110.9 26.6 %collective-permute-start.36 = (bf16[48,1536]{1,0:T(8,128)(2,1)S(1)}, bf16[48,1536]{1,0:T(8,128)(2,1)S(1)}, u32[]{:S(2)}, u32[]{:S(2)}) collective-permute-start(bf16[48,1536]{1,0:T(8,128)(2,1)S(1)} %get-tuple-element.73), channel_id=1, source_target_pairs={{0,2},{1,3},{2,0},{3,1},{4,6},{5,7},{6,4},{7,5},{8,10},{9,11},{10,... | collective-permute-start | bytes 442376 | tf_op jit(solution)/shard_map/ppermute | solution.py:362
  121.0 17.4 %collective-permute-start.37 = (bf16[48,1536]{1,0:T(8,128)(2,1)S(1)}, bf16[48,1536]{1,0:T(8,128)(2,1)S(1)}, u32[]{:S(2)}, u32[]{:S(2)}) collective-permute-start(bf16[48,1536]{1,0:T(8,128)(2,1)S(1)} %get-tuple-element.72), channel_id=1, source_target_pairs={{0,3},{1,2},{2,1},{3,0},{4,7},{5,6},{6,5},{7,4},{8,11},{9,10},{10,... | collective-permute-start | bytes 442376 | tf_op jit(solution)/shard_map/ppermute | solution.py:362
  122.6 17.2 %collective-permute-start.28 = (bf16[48,1536]{1,0:T(8,128)(2,1)S(1)}, bf16[48,1536]{1,0:T(8,128)(2,1)S(1)}, u32[]{:S(2)}, u32[]{:S(2)}) collective-permute-start(bf16[48,1536]{1,0:T(8,128)(2,1)S(1)} %add_convert_fusion.5), channel_id=1, source_target_pairs={{0,1},{1,0},{2,3},{3,2},{4,5},{5,4},{6,7},{7,6},{8,9},{9,8},{10,11... | collective-permute-start | bytes 442376 | tf_op jit(solution)/shard_map/ppermute | solution.py:362
  123.5 17.2 %collective-permute-start.29 = (bf16[48,1536]{1,0:T(8,128)(2,1)S(1)}, bf16[48,1536]{1,0:T(8,128)(2,1)S(1)}, u32[]{:S(2)}, u32[]{:S(2)}) collective-permute-start(bf16[48,1536]{1,0:T(8,128)(2,1)S(1)} %add_convert_fusion.5), channel_id=1, source_target_pairs={{0,2},{1,3},{2,0},{3,1},{4,6},{5,7},{6,4},{7,5},{8,10},{9,11},{10,... | collective-permute-start | bytes 442376 | tf_op jit(solution)/shard_map/ppermute | solution.py:362
  136.1 11.3 %copy-start.23 = (bf16[3,256,384]{2,1,0:T(8,128)(2,1)S(1)}, bf16[3,256,384]{2,1,0:T(8,128)(2,1)}, u32[]{:S(2)}) copy-start(bf16[3,256,384]{2,1,0:T(8,128)(2,1)} %get-tuple-element.53) | copy-start | bytes 1769476
  136.1 7.7 %collective-permute-start.30 = (bf16[48,1536]{1,0:T(8,128)(2,1)S(1)}, bf16[48,1536]{1,0:T(8,128)(2,1)S(1)}, u32[]{:S(2)}, u32[]{:S(2)}) collective-permute-start(bf16[48,1536]{1,0:T(8,128)(2,1)S(1)} %add_convert_fusion.5), channel_id=1, source_target_pairs={{0,3},{1,2},{2,1},{3,0},{4,7},{5,6},{6,5},{7,4},{8,11},{9,10},{10,... | collective-permute-start | bytes 442376 | tf_op jit(solution)/shard_map/ppermute | solution.py:362
  137.6 40.4 %collective-permute-start.21 = (bf16[3,256,384]{2,1,0:T(8,128)(2,1)}, bf16[3,256,384]{2,1,0:T(8,128)(2,1)S(1)}, u32[]{:S(2)}, u32[]{:S(2)}) collective-permute-start(bf16[3,256,384]{2,1,0:T(8,128)(2,1)} %get-tuple-element.51), channel_id=1, source_target_pairs={{0,1},{1,0},{2,3},{3,2},{4,5},{5,4},{6,7},{7,6},{8,9},{9,8},{10,11... | collective-permute-start | bytes 1769480 | tf_op jit(solution)/shard_map/ppermute | solution.py:362
  138.5 39.5 %collective-permute-start.22 = (bf16[3,256,384]{2,1,0:T(8,128)(2,1)}, bf16[3,256,384]{2,1,0:T(8,128)(2,1)S(1)}, u32[]{:S(2)}, u32[]{:S(2)}) collective-permute-start(bf16[3,256,384]{2,1,0:T(8,128)(2,1)} %get-tuple-element.52), channel_id=1, source_target_pairs={{0,2},{1,3},{2,0},{3,1},{4,6},{5,7},{6,4},{7,5},{8,10},{9,11},{10,... | collective-permute-start | bytes 1769480 | tf_op jit(solution)/shard_map/ppermute | solution.py:362
  139.8 7.6 %collective-permute-start.40 = (bf16[48,1536]{1,0:T(8,128)(2,1)S(1)}, bf16[48,1536]{1,0:T(8,128)(2,1)S(1)}, u32[]{:S(2)}, u32[]{:S(2)}) collective-permute-start(bf16[48,1536]{1,0:T(8,128)(2,1)S(1)} %get-tuple-element.85), channel_id=1, source_target_pairs={{0,24},{1,25},{2,26},{3,27},{4,28},{5,29},{6,30},{7,31},{8,0},{9,1... | collective-permute-start | bytes 442376 | tf_op jit(solution)/shard_map/ppermute | solution.py:362
  140.7 12.8 %collective-permute-start.39 = (bf16[48,1536]{1,0:T(8,128)(2,1)S(1)}, bf16[48,1536]{1,0:T(8,128)(2,1)S(1)}, u32[]{:S(2)}, u32[]{:S(2)}) collective-permute-start(bf16[48,1536]{1,0:T(8,128)(2,1)S(1)} %get-tuple-element.86), channel_id=1, source_target_pairs={{0,16},{1,17},{2,18},{3,19},{4,20},{5,21},{6,22},{7,23},{8,24},{9,... | collective-permute-start | bytes 442376 | tf_op jit(solution)/shard_map/ppermute | solution.py:362
  143.8 10.8 %collective-permute-start.38 = (bf16[48,1536]{1,0:T(8,128)(2,1)S(1)}, bf16[48,1536]{1,0:T(8,128)(2,1)S(1)}, u32[]{:S(2)}, u32[]{:S(2)}) collective-permute-start(bf16[48,1536]{1,0:T(8,128)(2,1)S(1)} %get-tuple-element.84), channel_id=1, source_target_pairs={{0,8},{1,9},{2,10},{3,11},{4,12},{5,13},{6,14},{7,15},{8,16},{9,17... | collective-permute-start | bytes 442376 | tf_op jit(solution)/shard_map/ppermute | solution.py:362
  147.4 30.6 %collective-permute-start.23 = (bf16[3,256,384]{2,1,0:T(8,128)(2,1)S(1)}, bf16[3,256,384]{2,1,0:T(8,128)(2,1)S(1)}, u32[]{:S(2)}, u32[]{:S(2)}) collective-permute-start(bf16[3,256,384]{2,1,0:T(8,128)(2,1)S(1)} %copy-done.23), channel_id=1, source_target_pairs={{0,3},{1,2},{2,1},{3,0},{4,7},{5,6},{6,5},{7,4},{8,11},{9,10},{10,... | collective-permute-start | bytes 1769480 | tf_op jit(solution)/shard_map/ppermute | solution.py:362
  153.5 8.6 %collective-permute-start.31 = (bf16[48,1536]{1,0:T(8,128)(2,1)S(1)}, bf16[48,1536]{1,0:T(8,128)(2,1)S(1)}, u32[]{:S(2)}, u32[]{:S(2)}) collective-permute-start(bf16[48,1536]{1,0:T(8,128)(2,1)S(1)} %get-tuple-element.89), channel_id=1, source_target_pairs={{0,8},{1,9},{2,10},{3,11},{4,12},{5,13},{6,14},{7,15},{8,16},{9,17... | collective-permute-start | bytes 442376 | tf_op jit(solution)/shard_map/ppermute | solution.py:362
  154.6 11.0 %collective-permute-start.32 = (bf16[48,1536]{1,0:T(8,128)(2,1)S(1)}, bf16[48,1536]{1,0:T(8,128)(2,1)S(1)}, u32[]{:S(2)}, u32[]{:S(2)}) collective-permute-start(bf16[48,1536]{1,0:T(8,128)(2,1)S(1)} %get-tuple-element.88), channel_id=1, source_target_pairs={{0,16},{1,17},{2,18},{3,19},{4,20},{5,21},{6,22},{7,23},{8,24},{9,... | collective-permute-start | bytes 442376 | tf_op jit(solution)/shard_map/ppermute | solution.py:362
  155.6 22.4 %copy-start.12 = (bf16[48,1536]{1,0:T(8,128)(2,1)}, bf16[48,1536]{1,0:T(8,128)(2,1)S(1)}, u32[]{:S(2)}) copy-start(bf16[48,1536]{1,0:T(8,128)(2,1)S(1)} %add_convert_fusion.refs_8_) | copy-start | bytes 442372
  162.0 15.9 %copy-start.17 = (bf16[48,1536]{1,0:T(8,128)(2,1)}, bf16[48,1536]{1,0:T(8,128)(2,1)S(1)}, u32[]{:S(2)}) copy-start(bf16[48,1536]{1,0:T(8,128)(2,1)S(1)} %collective-permute-done.31.refs_5_) | copy-start | bytes 442372
  162.0 5.1 %collective-permute-start.33 = (bf16[48,1536]{1,0:T(8,128)(2,1)S(1)}, bf16[48,1536]{1,0:T(8,128)(2,1)S(1)}, u32[]{:S(2)}, u32[]{:S(2)}) collective-permute-start(bf16[48,1536]{1,0:T(8,128)(2,1)S(1)} %get-tuple-element.87), channel_id=1, source_target_pairs={{0,24},{1,25},{2,26},{3,27},{4,28},{5,29},{6,30},{7,31},{8,0},{9,1... | collective-permute-start | bytes 442376 | tf_op jit(solution)/shard_map/ppermute | solution.py:362
  165.6 12.4 %copy-start.18 = (bf16[48,1536]{1,0:T(8,128)(2,1)}, bf16[48,1536]{1,0:T(8,128)(2,1)S(1)}, u32[]{:S(2)}) copy-start(bf16[48,1536]{1,0:T(8,128)(2,1)S(1)} %collective-permute-done.32.refs_6_) | copy-start | bytes 442372
  165.6 5.1 %collective-permute-start.41 = (bf16[48,1536]{1,0:T(8,128)(2,1)S(1)}, bf16[48,1536]{1,0:T(8,128)(2,1)S(1)}, u32[]{:S(2)}, u32[]{:S(2)}) collective-permute-start(bf16[48,1536]{1,0:T(8,128)(2,1)S(1)} %add_convert_fusion.refs_8_), channel_id=1, source_target_pairs={{0,1},{1,0},{2,3},{3,2},{4,5},{5,4},{6,7},{7,6},{8,9},{9,8},{10,11... | collective-permute-start | bytes 442376 | tf_op jit(solution)/shard_map/ppermute | solution.py:362
  167.2 10.8 %copy-start.19 = (bf16[48,1536]{1,0:T(8,128)(2,1)}, bf16[48,1536]{1,0:T(8,128)(2,1)S(1)}, u32[]{:S(2)}) copy-start(bf16[48,1536]{1,0:T(8,128)(2,1)S(1)} %collective-permute-done.33.refs_7_) | copy-start | bytes 442372
  167.2 7.6 %collective-permute-start.42 = (bf16[48,1536]{1,0:T(8,128)(2,1)S(1)}, bf16[48,1536]{1,0:T(8,128)(2,1)S(1)}, u32[]{:S(2)}, u32[]{:S(2)}) collective-permute-start(bf16[48,1536]{1,0:T(8,128)(2,1)S(1)} %add_convert_fusion.refs_8_), channel_id=1, source_target_pairs={{0,2},{1,3},{2,0},{3,1},{4,6},{5,7},{6,4},{7,5},{8,10},{9,11},{10,... | collective-permute-start | bytes 442376 | tf_op jit(solution)/shard_map/ppermute | solution.py:362
  170.8 7.3 %copy-start.20 = (bf16[48,1536]{1,0:T(8,128)(2,1)}, bf16[48,1536]{1,0:T(8,128)(2,1)S(1)}, u32[]{:S(2)}) copy-start(bf16[48,1536]{1,0:T(8,128)(2,1)S(1)} %collective-permute-done.41.refs_9_) | copy-start | bytes 442372
  170.8 7.2 %collective-permute-start.43 = (bf16[48,1536]{1,0:T(8,128)(2,1)S(1)}, bf16[48,1536]{1,0:T(8,128)(2,1)S(1)}, u32[]{:S(2)}, u32[]{:S(2)}) collective-permute-start(bf16[48,1536]{1,0:T(8,128)(2,1)S(1)} %add_convert_fusion.refs_8_), channel_id=1, source_target_pairs={{0,3},{1,2},{2,1},{3,0},{4,7},{5,6},{6,5},{7,4},{8,11},{9,10},{10,... | collective-permute-start | bytes 442376 | tf_op jit(solution)/shard_map/ppermute | solution.py:362
  174.8 3.2 %copy-start.21 = (bf16[48,1536]{1,0:T(8,128)(2,1)}, bf16[48,1536]{1,0:T(8,128)(2,1)S(1)}, u32[]{:S(2)}) copy-start(bf16[48,1536]{1,0:T(8,128)(2,1)S(1)} %collective-permute-done.42.refs_10_) | copy-start | bytes 442372
  178.0 1.2 copy-start.15
  (4 other events, 3.7 us)

commit v8 on v7

--- a/solution.py
+++ b/solution.py
@@ -379,9 +379,9 @@
         cut = chunk.shape[0] // 2
         upper, lower = by_x[:cut], by_y[cut:]
         by_both = [to_row(upper, 2), to_row(lower, 1)]
-        return [chunk, by_x, by_y, *by_both], (upper, lower)
-
-    grads = [gather(grad_flat[:, :wide])[0]]
+        return [chunk, by_x, by_y, *by_both]
+
+    grads = [gather(grad_flat[:, :wide])]
 
     away = jnp.abs(plane - row)
     cut = w_out.shape[0] // 2
@@ -413,11 +413,7 @@
             here = jnp.where(away == hop, stages[hop], here)
         return here
 
-    weights = [mine(first), mine(second)]
-    weights += [to_core(part) for part in weights]
-    block, handed = gather(after(grad_flat[:, wide:], parts), attended)
-    grads.append(block)
-    first[-1], second[-1] = after((first[-1], second[-1]), handed)
+    grads.append(gather(after(grad_flat[:, wide:], parts), attended))
 
     def reduce_cores(at, attended, chunk):
         keep, give = weight_terms(place, attended, chunk, rows, not at)
@@ -448,6 +444,9 @@
 
     early = to_planes(add_cores(*reduce_cores(0, attended, grads[0])))
     late = to_rows(add_cores(*reduce_cores(1, attended, grads[1])))
+    first[-1], second[-1] = after((first[-1], second[-1]), late[0])
+    weights = [mine(first), mine(second)]
+    weights += [to_core(part) for part in weights]
     grad_attn = project(place, weights, grads)
     early = to_rows([added(after(early, grad_attn))] * rows)
     sent = backward(parts, probs, grad_attn, 0, probs.shape[0])

time: 184 us -> 211 us (1.15)
  starting transfers between devices: 60.6 us -> 73.5 us
  waiting for transfers between devices: 59.3 us -> 66.4 us
  other arithmetic: 4.5 us -> 9.41 us
    ppermute x44, starting transfers between devices: 60.6 us -> 73.5 us  [send(): return lax.ppermute(array, ('fsdp', 'rows'), pairs)]
    ppermute x44, waiting for transfers between devices: 59.3 us -> 66.4 us  [send(): return lax.ppermute(array, ('fsdp', 'rows'), pairs)]
    convert_element_type x2, other arithmetic: 1.41 us -> 4.21 us  [add_cores(): (keep[slot].astype(jnp.float32) + got[slot].astype(jnp.float32)).astype(j...]
  transfers between devices with their start and end apart: 44 -> 44, of which waited for: 15 -> 13; matrix products, arithmetic and copies ran while one was open for 5% -> 8% of each run, Pallas kernels for 25% -> 20%
where the time goes in v8:
time: 211 us; the launch traced here: 210 us
  starting transfers between devices  73.5 us (35%)
  waiting for transfers between devices  66.4 us (31%)
  Pallas kernels  50.3 us (24%)
  other arithmetic  9.41 us (4%)
  local copies, waits for them, and re-layouts  9.27 us (4%)
    ppermute x44, starting transfers between devices, send(): return lax.ppermute(array, ('fsdp', 'rows'), pairs)  73.5 us
    ppermute x44, waiting for transfers between devices, send(): return lax.ppermute(array, ('fsdp', 'rows'), pairs)  66.4 us
    pallas_call x1, Pallas kernels, forward(): pl.pallas_call(body, grid=(heads,), in_specs=[part] * rows, out_specs=[pl...  12.6 us
    pallas_call x1, Pallas kernels, backward(): pl.pallas_call(body, grid=(count,), in_specs=[part] * rows + [pl.BlockSpe...  11.4 us
    pallas_call x2, Pallas kernels, weight_terms(): pl.pallas_call(body, grid_spec=pltpu.PrefetchScalarGridSpec(num_scalar_pr...  10.5 us
    pallas_call x1, Pallas kernels, project(): pl.pallas_call(body, grid_spec=pltpu.PrefetchScalarGridSpec(num_scalar_pr...  8.01 us
    slice x4, local copies, waits for them, and re-layouts, gather(): upper, lower = (by_x[:cut], by_y[cut:])  5.59 us
    pallas_call x1, Pallas kernels, finish(): pl.pallas_call(body, grid_spec=pltpu.PrefetchScalarGridSpec(num_scalar_pr...  4.48 us
  transfers between devices with their start and end apart: 44, of which 13 were waited for; matrix products, arithmetic and copies ran while one was open for 8% of the time, Pallas kernels for 20%

profile of v8, /device:TPU:0, one launch (start us, length us, event | category | flops | bytes accessed | tf_op | source)
XLA Modules:
  0.0 210.1 jit_solution(15199062165276443984)
XLA Ops:
  0.7 0.6 pad_add_fusion.place_ref
  1.3 3.3 %pack.1 = (bf16[3,256,384]{2,1,0:T(8,128)(2,1)}, bf16[3,256,384]{2,1,0:T(8,128)(2,1)}, bf16[3,256,384]{2,1,0:T(8,128)(2,1)}, bf16[3,256,384]{2,1,0:T(8,128)(2,1)}) custom-call(s32[3]{0:T(128)} %pad_add_fusion.place_ref, bf16[1,256,1536]{2,1,0:T(8,128)(2,1)} %refs_0_.1, bf16[1,256,1536]{2,1,0:T(8,128)(2,1)} %refs_1_.1, bf16[1,256,1536]{2,1,0:T(8,128)(2,1)} %refs_2_.1), custom_call_target="tpu_custom_call" | custom-call | bytes 4718592 | tf_op jit(solution)/shard_map/pack/pallas_call | solution.py:52
  4.6 3.0 %collective-permute-start = (bf16[3,256,384]{2,1,0:T(8,128)(2,1)}, bf16[3,256,384]{2,1,0:T(8,128)(2,1)}, u32[]{:S(2)}, u32[]{:S(2)}) collective-permute-start(bf16[3,256,384]{2,1,0:T(8,128)(2,1)} %get-tuple-element.40), channel_id=1, source_target_pairs={{0,1},{1,0},{2,3},{3,2},{4,5},{5,4},{6,7},{7,6},{8,9},{9,8},{10,11... | collective-permute-start | bytes 1769480 | tf_op jit(solution)/shard_map/ppermute | solution.py:362
  7.6 1.5 collective-permute-start.1
  9.1 1.0 fusion.9
  10.1 4.8 %collective-permute-start.3 = (bf16[96,3072]{1,0:T(8,128)(2,1)S(1)}, bf16[96,3072]{1,0:T(8,128)(2,1)}, u32[]{:S(2)}, u32[]{:S(2)}) collective-permute-start(bf16[96,3072]{1,0:T(8,128)(2,1)S(1)} %get-tuple-element.87), channel_id=1, source_target_pairs={{0,8},{4,12},{9,17},{13,21},{18,26},{22,30}} | collective-permute-start | bytes 1769480 | tf_op jit(solution)/shard_map/ppermute | solution.py:362
  14.9 1.5 collective-permute-start.4
  16.3 1.5 fusion.8
  17.8 4.2 %collective-permute-done.refs_1_ = bf16[3,256,384]{2,1,0:T(8,128)(2,1)} collective-permute-done((bf16[3,256,384]{2,1,0:T(8,128)(2,1)}, bf16[3,256,384]{2,1,0:T(8,128)(2,1)}, u32[]{:S(2)}, u32[]{:S(2)}) %collective-permute-start) | collective-permute-done | bytes 589856 | tf_op jit(solution)/shard_map/ppermute | solution.py:362
  22.1 13.2 %collective-permute-done.1.refs_2_ = bf16[3,256,384]{2,1,0:T(8,128)(2,1)} collective-permute-done((bf16[3,256,384]{2,1,0:T(8,128)(2,1)}, bf16[3,256,384]{2,1,0:T(8,128)(2,1)}, u32[]{:S(2)}, u32[]{:S(2)}) %collective-permute-start.1) | collective-permute-done | bytes 589856 | tf_op jit(solution)/shard_map/ppermute | solution.py:362
  35.3 1.2 collective-permute-start.11
  36.6 0.8 collective-permute-start.12
  37.4 1.1 broadcast_select_fusion.1
  38.5 4.3 %collective-permute-start.7 = (bf16[96,3072]{1,0:T(8,128)(2,1)}, bf16[96,3072]{1,0:T(8,128)(2,1)}, u32[]{:S(2)}, u32[]{:S(2)}) collective-permute-start(bf16[96,3072]{1,0:T(8,128)(2,1)} %get-tuple-element.44), channel_id=1, source_target_pairs={{0,8},{4,12},{9,17},{13,21},{18,26},{22,30}} | collective-permute-start | bytes 1769480 | tf_op jit(solution)/shard_map/ppermute | solution.py:362
  42.8 1.5 collective-permute-start.8
  44.3 12.6 %forward.1 = (bf16[3,1024,1024]{2,1,0:T(8,128)(2,1)}, bf16[384,1024]{1,0:T(8,128)(2,1)}) custom-call(bf16[3,256,384]{2,1,0:T(8,128)(2,1)} %get-tuple-element.39.refs_0_, bf16[3,256,384]{2,1,0:T(8,128)(2,1)} %collective-permute-done.refs_1_, bf16[3,256,384]{2,1,0:T(8,128)(2,1)} %collective-permute-done.1.refs_2_, ...), custom_call_target="tpu_custom_call" | custom-call | flops 3221225472 | bytes 6291456 | tf_op jit(solution)/shard_map/forward/pallas_call | solution.py:180
  57.4 1.5 collective-permute-start.5
  58.9 1.0 slice.75
  59.9 1.0 slice.76
  61.0 1.5 collective-permute-start.13
  62.4 2.2 %collective-permute-start.14 = (bf16[128,1536]{1,0:T(8,128)(2,1)S(1)}, bf16[128,1536]{1,0:T(8,128)(2,1)}, u32[]{:S(2)}, u32[]{:S(2)}) collective-permute-start(bf16[128,1536]{1,0:T(8,128)(2,1)S(1)} %slice.76), channel_id=1, source_target_pairs={{0,1},{1,0},{2,3},{3,2},{4,5},{5,4},{6,7},{7,6},{8,9},{9,8},{10,11... | collective-permute-start | bytes 1179656 | tf_op jit(solution)/shard_map/ppermute | solution.py:362
  64.7 1.1 broadcast_select_fusion
  65.8 17.0 %collective-permute-done.13.refs_3_.refs_12_ = bf16[128,1536]{1,0:T(8,128)(2,1)} collective-permute-done((bf16[128,1536]{1,0:T(8,128)(2,1)S(1)}, bf16[128,1536]{1,0:T(8,128)(2,1)}, u32[]{:S(2)}, u32[]{:S(2)}) %collective-permute-start.13) | collective-permute-done | bytes 393248 | tf_op jit(solution)/shard_map/ppermute | solution.py:362
  82.8 1.5 collective-permute-start.9
  84.4 5.3 %weight_terms.2 = (bf16[4,48,1536]{2,1,0:T(8,128)(2,1)}, bf16[4,48,1536]{2,1,0:T(8,128)(2,1)}) custom-call(s32[3]{0:T(128)} %pad_add_fusion.place_ref, bf16[384,1024]{1,0:T(8,128)(2,1)} %get-tuple-element.45.attended_ref, bf16[256,1536]{1,0:T(8,128)(2,1)} %copy-done.2, bf16[256,1536]{1,0:T(8,128)(2,1)} %collective-permute-done.11.refs_1_.refs_10_, ...), custom_call_target="tpu_custom_call" | custom-call | flops 1207959552 | bytes 3932160 | tf_op jit(solution)/shard_map/weight_terms/pallas_call | solution.py:323
  89.8 1.8 slice.80
  91.6 1.8 slice.81
  93.4 2.0 collective-permute-start.21
  95.3 1.6 collective-permute-start.6
  97.0 1.5 collective-permute-start.10
  98.5 4.9 %collective-permute-done.20.refs_7_.refs_3_ = bf16[128,1536]{1,0:T(8,128)(2,1)} collective-permute-done((bf16[128,1536]{1,0:T(8,128)(2,1)}, bf16[128,1536]{1,0:T(8,128)(2,1)}, u32[]{:S(2)}, u32[]{:S(2)}) %collective-permute-start.20) | collective-permute-done | bytes 393248 | tf_op jit(solution)/shard_map/ppermute | solution.py:362
  103.3 1.8 collective-permute-done.21.refs_8_.refs_4_
  105.1 5.2 %weight_terms.3 = (bf16[4,48,1536]{2,1,0:T(8,128)(2,1)}, bf16[4,48,1536]{2,1,0:T(8,128)(2,1)}) custom-call(s32[3]{0:T(128)} %pad_add_fusion.place_ref, bf16[384,1024]{1,0:T(8,128)(2,1)} %get-tuple-element.45.attended_ref, bf16[256,1536]{1,0:T(8,128)(2,1)} %copy-done.1, bf16[256,1536]{1,0:T(8,128)(2,1)} %collective-permute-done.18.refs_5_.refs_1_, ...), custom_call_target="tpu_custom_call" | custom-call | flops 1207959552 | bytes 3932160 | tf_op jit(solution)/shard_map/weight_terms/pallas_call | solution.py:323
  110.4 2.0 fusion.7
  112.8 0.5 collective-permute-start.16
  113.4 2.2 %fusion.4 = (bf16[48,1536]{1,0:T(8,128)(2,1)}, bf16[48,1536]{1,0:T(8,128)(2,1)}, bf16[48,1536]{1,0:T(8,128)(2,1)}, bf16[48,1536]{1,0:T(8,128)(2,1)S(1)}) fusion(bf16[4,48,1536]{2,1,0:T(8,128)(2,1)} %collective-permute-done.25, bf16[4,48,1536]{2,1,0:T(8,128)(2,1)} %get-tuple-element.60), kind=kLoop, calls=%fused_computation.18 | loop fusion | flops 1179648 | bytes 1769472 | tf_op jit(solution)/shard_map/convert_element_type | solution.py:424
  115.6 4.8 %collective-permute-start.26 = (bf16[48,1536]{1,0:T(8,128)(2,1)}, bf16[48,1536]{1,0:T(8,128)(2,1)}, u32[]{:S(2)}, u32[]{:S(2)}) collective-permute-start(bf16[48,1536]{1,0:T(8,128)(2,1)} %get-tuple-element.82), channel_id=1, source_target_pairs={{0,8},{1,9},{2,10},{3,11},{4,12},{5,13},{6,14},{7,15},{8,16},{9,17... | collective-permute-start | bytes 442376 | tf_op jit(solution)/shard_map/ppermute | solution.py:362
  120.3 14.2 %collective-permute-start.27 = (bf16[48,1536]{1,0:T(8,128)(2,1)}, bf16[48,1536]{1,0:T(8,128)(2,1)}, u32[]{:S(2)}, u32[]{:S(2)}) collective-permute-start(bf16[48,1536]{1,0:T(8,128)(2,1)} %get-tuple-element.81), channel_id=1, source_target_pairs={{0,16},{1,17},{2,18},{3,19},{4,20},{5,21},{6,22},{7,23},{8,24},{9,... | collective-permute-start | bytes 442376 | tf_op jit(solution)/shard_map/ppermute | solution.py:362
  135.1 3.1 %collective-permute-start.36 = (bf16[48,1536]{1,0:T(8,128)(2,1)S(1)}, bf16[48,1536]{1,0:T(8,128)(2,1)S(1)}, u32[]{:S(2)}, u32[]{:S(2)}) collective-permute-start(bf16[48,1536]{1,0:T(8,128)(2,1)S(1)} %copy-done.14), channel_id=1, source_target_pairs={{0,2},{1,3},{2,0},{3,1},{4,6},{5,7},{6,4},{7,5},{8,10},{9,11},{10,... | collective-permute-start | bytes 442376 | tf_op jit(solution)/shard_map/ppermute | solution.py:362
  138.2 8.0 %project.1.refs_5_ = bf16[384,1024]{1,0:T(8,128)(2,1)} custom-call(s32[3]{0:T(128)} %pad_add_fusion.place_ref, bf16[96,3072]{1,0:T(8,128)(2,1)} %copy-done.4, bf16[96,3072]{1,0:T(8,128)(2,1)} %copy-done.3, bf16[96,3072]{1,0:T(8,128)(2,1)} %copy-done.7, bf16[96,3072]{1,0:T(8,128)(2,1)} %copy-done.8, bf16[256,1536]{1,0:T(8,128)(2,1)} %copy-done.1, ...), custom_call_target="tpu_custom_call" | custom-call | flops 2415919104 | bytes 8650752 | tf_op jit(solution)/shard_map/project/pallas_call | solution.py:284
  146.7 1.1 add_convert_fusion.4
  147.8 1.9 collective-permute-start.29
  149.7 1.3 collective-permute-start.30
  151.0 11.4 %backward.1 = (bf16[3,256,384]{2,1,0:T(8,128)(2,1)}, bf16[3,256,384]{2,1,0:T(8,128)(2,1)}, bf16[3,256,384]{2,1,0:T(8,128)(2,1)}, bf16[3,256,384]{2,1,0:T(8,128)(2,1)}) custom-call(bf16[3,256,384]{2,1,0:T(8,128)(2,1)} %get-tuple-element.39.refs_0_, bf16[3,256,384]{2,1,0:T(8,128)(2,1)} %collective-permute-done.refs_1_, ...), custom_call_target="tpu_custom_call" | custom-call | flops 3221225472 | bytes 6291456 | tf_op jit(solution)/shard_map/backward/pallas_call | solution.py:229
  162.8 1.8 collective-permute-start.22
  164.7 1.3 collective-permute-start.23
  166.0 1.4 collective-permute-start.40
  167.4 1.7 collective-permute-start.39
  169.1 1.0 collective-permute-done.31
  170.1 1.6 collective-permute-start.38
  171.7 0.7 select_select_fusion.5
  172.4 0.8 collective-permute-done.40
  173.2 7.0 %collective-permute-done.39 = bf16[48,1536]{1,0:T(8,128)(2,1)S(1)} collective-permute-done((bf16[48,1536]{1,0:T(8,128)(2,1)S(1)}, bf16[48,1536]{1,0:T(8,128)(2,1)S(1)}, u32[]{:S(2)}, u32[]{:S(2)}) %collective-permute-start.39) | collective-permute-done | bytes 147488 | tf_op jit(solution)/shard_map/ppermute | solution.py:362
  180.1 1.9 collective-permute-start.33
  182.1 6.6 %collective-permute-done.32.refs_5_ = bf16[48,1536]{1,0:T(8,128)(2,1)S(1)} collective-permute-done((bf16[48,1536]{1,0:T(8,128)(2,1)S(1)}, bf16[48,1536]{1,0:T(8,128)(2,1)S(1)}, u32[]{:S(2)}, u32[]{:S(2)}) %collective-permute-start.32) | collective-permute-done | bytes 147488 | tf_op jit(solution)/shard_map/ppermute | solution.py:362
  188.7 3.6 %collective-permute-done.33.refs_6_ = bf16[48,1536]{1,0:T(8,128)(2,1)S(1)} collective-permute-done((bf16[48,1536]{1,0:T(8,128)(2,1)S(1)}, bf16[48,1536]{1,0:T(8,128)(2,1)S(1)}, u32[]{:S(2)}, u32[]{:S(2)}) %collective-permute-start.33) | collective-permute-done | bytes 147488 | tf_op jit(solution)/shard_map/ppermute | solution.py:362
  192.4 0.9 collective-permute-start.41
  193.3 0.6 collective-permute-done.34.refs_7_
  193.9 1.1 collective-permute-start.42
  195.0 2.5 %collective-permute-done.41.refs_9_ = bf16[48,1536]{1,0:T(8,128)(2,1)S(1)} collective-permute-done((bf16[48,1536]{1,0:T(8,128)(2,1)S(1)}, bf16[48,1536]{1,0:T(8,128)(2,1)S(1)}, u32[]{:S(2)}, u32[]{:S(2)}) %collective-permute-start.41) | collective-permute-done | bytes 147488 | tf_op jit(solution)/shard_map/ppermute | solution.py:362
  197.5 3.5 %collective-permute-start.43 = (bf16[48,1536]{1,0:T(8,128)(2,1)S(1)}, bf16[48,1536]{1,0:T(8,128)(2,1)S(1)}, u32[]{:S(2)}, u32[]{:S(2)}) collective-permute-start(bf16[48,1536]{1,0:T(8,128)(2,1)S(1)} %add_convert_fusion.refs_8_), channel_id=1, source_target_pairs={{0,3},{1,2},{2,1},{3,0},{4,7},{5,6},{6,5},{7,4},{8,11},{9,10},{10,... | collective-permute-start | bytes 442376 | tf_op jit(solution)/shard_map/ppermute | solution.py:362
  201.0 3.1 %collective-permute-done.43.refs_11_ = bf16[48,1536]{1,0:T(8,128)(2,1)S(1)} collective-permute-done((bf16[48,1536]{1,0:T(8,128)(2,1)S(1)}, bf16[48,1536]{1,0:T(8,128)(2,1)S(1)}, u32[]{:S(2)}, u32[]{:S(2)}) %collective-permute-start.43) | collective-permute-done | bytes 147488 | tf_op jit(solution)/shard_map/ppermute | solution.py:362
  204.2 0.6 copy-done.21
  205.4 4.5 %finish.1 = (bf16[1,256,1536]{2,1,0:T(8,128)(2,1)}, bf16[1,256,1536]{2,1,0:T(8,128)(2,1)}, bf16[1,256,1536]{2,1,0:T(8,128)(2,1)}, f32[192,3072]{1,0:T(8,128)}) custom-call(s32[3]{0:T(128)} %pad_add_fusion.place_ref, bf16[3,256,384]{2,1,0:T(8,128)(2,1)} %get-tuple-element.56.refs_0_, bf16[3,256,384]{2,1,0:T(8,128)(2,1)} %copy-done.11, ...), custom_call_target="tpu_custom_call" | custom-call | bytes 8257536 | tf_op jit(solution)/shard_map/finish/pallas_call | solution.py:138
  (93 shorter events, 3.4 us)
Async XLA Ops:
  0.6 8.5 %copy-start = (bf16[192,3072]{1,0:T(8,128)(2,1)S(1)}, bf16[192,3072]{1,0:T(8,128)(2,1)}, u32[]{:S(2)}) copy-start(bf16[192,3072]{1,0:T(8,128)(2,1)} %param.9) | copy-start | bytes 3538948
  4.6 17.5 %collective-permute-start = (bf16[3,256,384]{2,1,0:T(8,128)(2,1)}, bf16[3,256,384]{2,1,0:T(8,128)(2,1)}, u32[]{:S(2)}, u32[]{:S(2)}) collective-permute-start(bf16[3,256,384]{2,1,0:T(8,128)(2,1)} %get-tuple-element.40), channel_id=1, source_target_pairs={{0,1},{1,0},{2,3},{3,2},{4,5},{5,4},{6,7},{7,6},{8,9},{9,8},{10,11... | collective-permute-start | bytes 1769480 | tf_op jit(solution)/shard_map/ppermute | solution.py:362
  7.6 27.7 %collective-permute-start.1 = (bf16[3,256,384]{2,1,0:T(8,128)(2,1)}, bf16[3,256,384]{2,1,0:T(8,128)(2,1)}, u32[]{:S(2)}, u32[]{:S(2)}) collective-permute-start(bf16[3,256,384]{2,1,0:T(8,128)(2,1)} %get-tuple-element.41), channel_id=1, source_target_pairs={{0,2},{1,3},{2,0},{3,1},{4,6},{5,7},{6,4},{7,5},{8,10},{9,11},{10,... | collective-permute-start | bytes 1769480 | tf_op jit(solution)/shard_map/ppermute | solution.py:362
  9.1 26.2 %collective-permute-start.2 = (bf16[3,256,384]{2,1,0:T(8,128)(2,1)}, bf16[3,256,384]{2,1,0:T(8,128)(2,1)}, u32[]{:S(2)}, u32[]{:S(2)}) collective-permute-start(bf16[3,256,384]{2,1,0:T(8,128)(2,1)} %get-tuple-element.42), channel_id=1, source_target_pairs={{0,3},{1,2},{2,1},{3,0},{4,7},{5,6},{6,5},{7,4},{8,11},{9,10},{10,... | collective-permute-start | bytes 1769480 | tf_op jit(solution)/shard_map/ppermute | solution.py:362
  10.1 27.3 %collective-permute-start.3 = (bf16[96,3072]{1,0:T(8,128)(2,1)S(1)}, bf16[96,3072]{1,0:T(8,128)(2,1)}, u32[]{:S(2)}, u32[]{:S(2)}) collective-permute-start(bf16[96,3072]{1,0:T(8,128)(2,1)S(1)} %get-tuple-element.87), channel_id=1, source_target_pairs={{0,8},{4,12},{9,17},{13,21},{18,26},{22,30}} | collective-permute-start | bytes 1769480 | tf_op jit(solution)/shard_map/ppermute | solution.py:362
  14.9 22.5 %collective-permute-start.4 = (bf16[96,3072]{1,0:T(8,128)(2,1)S(1)}, bf16[96,3072]{1,0:T(8,128)(2,1)}, u32[]{:S(2)}, u32[]{:S(2)}) collective-permute-start(bf16[96,3072]{1,0:T(8,128)(2,1)S(1)} %get-tuple-element.87), channel_id=1, source_target_pairs={{9,1},{13,5},{18,10},{22,14},{27,19},{31,23}} | collective-permute-start | bytes 1769480 | tf_op jit(solution)/shard_map/ppermute | solution.py:362
  17.8 39.1 %copy-start.2 = (bf16[256,1536]{1,0:T(8,128)(2,1)}, bf16[256,1536]{1,0:T(8,128)(2,1)S(1)}, u32[]{:S(2)}) copy-start(bf16[256,1536]{1,0:T(8,128)(2,1)S(1)} %get-tuple-element.47.refs_0_.refs_9_) | copy-start | bytes 2359300
  17.8 39.1 %copy-start.1 = (bf16[256,1536]{1,0:T(8,128)(2,1)}, bf16[256,1536]{1,0:T(8,128)(2,1)S(1)}, u32[]{:S(2)}) copy-start(bf16[256,1536]{1,0:T(8,128)(2,1)S(1)} %get-tuple-element.74.refs_4_.refs_0_) | copy-start | bytes 2359300
  35.3 21.6 %collective-permute-start.11 = (bf16[256,1536]{1,0:T(8,128)(2,1)S(1)}, bf16[256,1536]{1,0:T(8,128)(2,1)}, u32[]{:S(2)}, u32[]{:S(2)}) collective-permute-start(bf16[256,1536]{1,0:T(8,128)(2,1)S(1)} %get-tuple-element.47.refs_0_.refs_9_), channel_id=1, source_target_pairs={{0,1},{1,0},{2,3},{3,2},{4,5},{5,4},{6,7},{7,6},{8,9},{9,8},{10,11... | collective-permute-start | bytes 2359304 | tf_op jit(solution)/shard_map/ppermute | solution.py:362
  36.6 20.8 %collective-permute-start.12 = (bf16[256,1536]{1,0:T(8,128)(2,1)S(1)}, bf16[256,1536]{1,0:T(8,128)(2,1)}, u32[]{:S(2)}, u32[]{:S(2)}) collective-permute-start(bf16[256,1536]{1,0:T(8,128)(2,1)S(1)} %get-tuple-element.47.refs_0_.refs_9_), channel_id=1, source_target_pairs={{0,2},{1,3},{2,0},{3,1},{4,6},{5,7},{6,4},{7,5},{8,10},{9,11},{10,... | collective-permute-start | bytes 2359304 | tf_op jit(solution)/shard_map/ppermute | solution.py:362
  38.5 22.4 %collective-permute-start.7 = (bf16[96,3072]{1,0:T(8,128)(2,1)}, bf16[96,3072]{1,0:T(8,128)(2,1)}, u32[]{:S(2)}, u32[]{:S(2)}) collective-permute-start(bf16[96,3072]{1,0:T(8,128)(2,1)} %get-tuple-element.44), channel_id=1, source_target_pairs={{0,8},{4,12},{9,17},{13,21},{18,26},{22,30}} | collective-permute-start | bytes 1769480 | tf_op jit(solution)/shard_map/ppermute | solution.py:362
  42.8 19.6 %collective-permute-start.8 = (bf16[96,3072]{1,0:T(8,128)(2,1)}, bf16[96,3072]{1,0:T(8,128)(2,1)}, u32[]{:S(2)}, u32[]{:S(2)}) collective-permute-start(bf16[96,3072]{1,0:T(8,128)(2,1)} %get-tuple-element.44), channel_id=1, source_target_pairs={{9,1},{13,5},{18,10},{22,14},{27,19},{31,23}} | collective-permute-start | bytes 1769480 | tf_op jit(solution)/shard_map/ppermute | solution.py:362
  44.3 45.4 %collective-permute-start.18 = (bf16[256,1536]{1,0:T(8,128)(2,1)S(1)}, bf16[256,1536]{1,0:T(8,128)(2,1)}, u32[]{:S(2)}, u32[]{:S(2)}) collective-permute-start(bf16[256,1536]{1,0:T(8,128)(2,1)S(1)} %get-tuple-element.74.refs_4_.refs_0_), channel_id=1, source_target_pairs={{0,1},{1,0},{2,3},{3,2},{4,5},{5,4},{6,7},{7,6},{8,9},{9,8},{10,11... | collective-permute-start | bytes 2359304 | tf_op jit(solution)/shard_map/ppermute | solution.py:362
  56.9 32.8 %collective-permute-start.19 = (bf16[256,1536]{1,0:T(8,128)(2,1)S(1)}, bf16[256,1536]{1,0:T(8,128)(2,1)}, u32[]{:S(2)}, u32[]{:S(2)}) collective-permute-start(bf16[256,1536]{1,0:T(8,128)(2,1)S(1)} %get-tuple-element.74.refs_4_.refs_0_), channel_id=1, source_target_pairs={{0,2},{1,3},{2,0},{3,1},{4,6},{5,7},{6,4},{7,5},{8,10},{9,11},{10,... | collective-permute-start | bytes 2359304 | tf_op jit(solution)/shard_map/ppermute | solution.py:362
  57.4 38.0 %collective-permute-start.5 = (bf16[96,3072]{1,0:T(8,128)(2,1)S(1)}, bf16[96,3072]{1,0:T(8,128)(2,1)}, u32[]{:S(2)}, u32[]{:S(2)}) collective-permute-start(bf16[96,3072]{1,0:T(8,128)(2,1)S(1)} %broadcast_select_fusion.1), channel_id=1, source_target_pairs={{8,16},{10,2},{12,20},{14,6},{17,25},{19,11},{21,29},{23,15}} | collective-permute-start | bytes 1769480 | tf_op jit(solution)/shard_map/ppermute | solution.py:362
  61.0 21.9 %collective-permute-start.13 = (bf16[128,1536]{1,0:T(8,128)(2,1)S(1)}, bf16[128,1536]{1,0:T(8,128)(2,1)}, u32[]{:S(2)}, u32[]{:S(2)}) collective-permute-start(bf16[128,1536]{1,0:T(8,128)(2,1)S(1)} %slice.75), channel_id=1, source_target_pairs={{0,2},{1,3},{2,0},{3,1},{4,6},{5,7},{6,4},{7,5},{8,10},{9,11},{10,... | collective-permute-start | bytes 1179656 | tf_op jit(solution)/shard_map/ppermute | solution.py:362
  62.4 21.9 %collective-permute-start.14 = (bf16[128,1536]{1,0:T(8,128)(2,1)S(1)}, bf16[128,1536]{1,0:T(8,128)(2,1)}, u32[]{:S(2)}, u32[]{:S(2)}) collective-permute-start(bf16[128,1536]{1,0:T(8,128)(2,1)S(1)} %slice.76), channel_id=1, source_target_pairs={{0,1},{1,0},{2,3},{3,2},{4,5},{5,4},{6,7},{7,6},{8,9},{9,8},{10,11... | collective-permute-start | bytes 1179656 | tf_op jit(solution)/shard_map/ppermute | solution.py:362
  65.8 23.9 %copy-start.5 = (bf16[96,3072]{1,0:T(8,128)(2,1)}, bf16[96,3072]{1,0:T(8,128)(2,1)S(1)}, u32[]{:S(2)}) copy-start(bf16[96,3072]{1,0:T(8,128)(2,1)S(1)} %broadcast_select_fusion) | copy-start | bytes 1769476
  82.8 14.2 %collective-permute-start.9 = (bf16[96,3072]{1,0:T(8,128)(2,1)S(1)}, bf16[96,3072]{1,0:T(8,128)(2,1)}, u32[]{:S(2)}, u32[]{:S(2)}) collective-permute-start(bf16[96,3072]{1,0:T(8,128)(2,1)S(1)} %broadcast_select_fusion), channel_id=1, source_target_pairs={{8,16},{10,2},{12,20},{14,6},{17,25},{19,11},{21,29},{23,15}} | collective-permute-start | bytes 1769480 | tf_op jit(solution)/shard_map/ppermute | solution.py:362
  89.7 20.7 %collective-permute-start.15 = (bf16[4,48,1536]{2,1,0:T(8,128)(2,1)}, bf16[4,48,1536]{2,1,0:T(8,128)(2,1)}, u32[]{:S(2)}, u32[]{:S(2)}) collective-permute-start(bf16[4,48,1536]{2,1,0:T(8,128)(2,1)} %get-tuple-element.51), channel_id=1, source_target_pairs={{0,4},{1,5},{2,6},{3,7},{4,0},{5,1},{6,2},{7,3},{8,12},{9,13},{10,... | collective-permute-start | bytes 1769480 | tf_op jit(solution)/shard_map/ppermute | solution.py:362
  91.5 11.8 %collective-permute-start.20 = (bf16[128,1536]{1,0:T(8,128)(2,1)}, bf16[128,1536]{1,0:T(8,128)(2,1)}, u32[]{:S(2)}, u32[]{:S(2)}) collective-permute-start(bf16[128,1536]{1,0:T(8,128)(2,1)} %slice.80), channel_id=1, source_target_pairs={{0,2},{1,3},{2,0},{3,1},{4,6},{5,7},{6,4},{7,5},{8,10},{9,11},{10,... | collective-permute-start | bytes 1179656 | tf_op jit(solution)/shard_map/ppermute | solution.py:362
  93.4 11.8 %collective-permute-start.21 = (bf16[128,1536]{1,0:T(8,128)(2,1)}, bf16[128,1536]{1,0:T(8,128)(2,1)}, u32[]{:S(2)}, u32[]{:S(2)}) collective-permute-start(bf16[128,1536]{1,0:T(8,128)(2,1)} %slice.81), channel_id=1, source_target_pairs={{0,1},{1,0},{2,3},{3,2},{4,5},{5,4},{6,7},{7,6},{8,9},{9,8},{10,11... | collective-permute-start | bytes 1179656 | tf_op jit(solution)/shard_map/ppermute | solution.py:362
  95.3 15.1 %copy-start.9 = (bf16[4,48,1536]{2,1,0:T(8,128)(2,1)S(1)}, bf16[4,48,1536]{2,1,0:T(8,128)(2,1)}, u32[]{:S(2)}) copy-start(bf16[4,48,1536]{2,1,0:T(8,128)(2,1)} %get-tuple-element.50) | copy-start | bytes 1769476
  95.3 17.1 %collective-permute-start.6 = (bf16[96,3072]{1,0:T(8,128)(2,1)}, bf16[96,3072]{1,0:T(8,128)(2,1)}, u32[]{:S(2)}, u32[]{:S(2)}) collective-permute-start(bf16[96,3072]{1,0:T(8,128)(2,1)} %collective-permute-done.5), channel_id=1, source_target_pairs={{11,3},{15,7},{16,24},{20,28}} | collective-permute-start | bytes 1769480 | tf_op jit(solution)/shard_map/ppermute | solution.py:362
  97.0 15.4 %collective-permute-start.10 = (bf16[96,3072]{1,0:T(8,128)(2,1)}, bf16[96,3072]{1,0:T(8,128)(2,1)}, u32[]{:S(2)}, u32[]{:S(2)}) collective-permute-start(bf16[96,3072]{1,0:T(8,128)(2,1)} %collective-permute-done.9), channel_id=1, source_target_pairs={{11,3},{15,7},{16,24},{20,28}} | collective-permute-start | bytes 1769480 | tf_op jit(solution)/shard_map/ppermute | solution.py:362
  110.3 2.1 copy-start.6
  110.3 3.0 %collective-permute-start.25 = (bf16[4,48,1536]{2,1,0:T(8,128)(2,1)}, bf16[4,48,1536]{2,1,0:T(8,128)(2,1)}, u32[]{:S(2)}, u32[]{:S(2)}) collective-permute-start(bf16[4,48,1536]{2,1,0:T(8,128)(2,1)} %get-tuple-element.61), channel_id=1, source_target_pairs={{0,4},{1,5},{2,6},{3,7},{4,0},{5,1},{6,2},{7,3},{8,12},{9,13},{10,... | collective-permute-start | bytes 1769480 | tf_op jit(solution)/shard_map/ppermute | solution.py:362
  112.7 25.5 %copy-start.3 = (bf16[96,3072]{1,0:T(8,128)(2,1)}, bf16[96,3072]{1,0:T(8,128)(2,1)S(1)}, u32[]{:S(2)}) copy-start(bf16[96,3072]{1,0:T(8,128)(2,1)S(1)} %get-tuple-element.84.refs_1_) | copy-start | bytes 1769476
  112.7 25.5 %copy-start.4 = (bf16[96,3072]{1,0:T(8,128)(2,1)}, bf16[96,3072]{1,0:T(8,128)(2,1)S(1)}, u32[]{:S(2)}) copy-start(bf16[96,3072]{1,0:T(8,128)(2,1)S(1)} %get-tuple-element.85.refs_0_) | copy-start | bytes 1769476
  112.8 22.2 %copy-start.15 = (bf16[48,1536]{1,0:T(8,128)(2,1)S(1)}, bf16[48,1536]{1,0:T(8,128)(2,1)}, u32[]{:S(2)}) copy-start(bf16[48,1536]{1,0:T(8,128)(2,1)} %get-tuple-element.78) | copy-start | bytes 442372
  112.8 22.3 %copy-start.14 = (bf16[48,1536]{1,0:T(8,128)(2,1)S(1)}, bf16[48,1536]{1,0:T(8,128)(2,1)}, u32[]{:S(2)}) copy-start(bf16[48,1536]{1,0:T(8,128)(2,1)} %get-tuple-element.77) | copy-start | bytes 442372
  112.8 22.2 %collective-permute-start.16 = (bf16[96,3072]{1,0:T(8,128)(2,1)S(1)}, bf16[96,3072]{1,0:T(8,128)(2,1)S(1)}, u32[]{:S(2)}, u32[]{:S(2)}) collective-permute-start(bf16[96,3072]{1,0:T(8,128)(2,1)S(1)} %get-tuple-element.85.refs_0_), channel_id=1, source_target_pairs={{0,4},{1,5},{2,6},{3,7},{4,0},{5,1},{6,2},{7,3},{8,12},{9,13},{10,... | collective-permute-start | bytes 1769480 | tf_op jit(solution)/shard_map/ppermute | solution.py:362
  113.3 21.8 %collective-permute-start.17 = (bf16[96,3072]{1,0:T(8,128)(2,1)S(1)}, bf16[96,3072]{1,0:T(8,128)(2,1)S(1)}, u32[]{:S(2)}, u32[]{:S(2)}) collective-permute-start(bf16[96,3072]{1,0:T(8,128)(2,1)S(1)} %get-tuple-element.84.refs_1_), channel_id=1, source_target_pairs={{0,4},{1,5},{2,6},{3,7},{4,0},{5,1},{6,2},{7,3},{8,12},{9,13},{10,... | collective-permute-start | bytes 1769480 | tf_op jit(solution)/shard_map/ppermute | solution.py:362
  115.6 30.7 %collective-permute-start.26 = (bf16[48,1536]{1,0:T(8,128)(2,1)}, bf16[48,1536]{1,0:T(8,128)(2,1)}, u32[]{:S(2)}, u32[]{:S(2)}) collective-permute-start(bf16[48,1536]{1,0:T(8,128)(2,1)} %get-tuple-element.82), channel_id=1, source_target_pairs={{0,8},{1,9},{2,10},{3,11},{4,12},{5,13},{6,14},{7,15},{8,16},{9,17... | collective-permute-start | bytes 442376 | tf_op jit(solution)/shard_map/ppermute | solution.py:362
  120.3 26.4 %collective-permute-start.27 = (bf16[48,1536]{1,0:T(8,128)(2,1)}, bf16[48,1536]{1,0:T(8,128)(2,1)}, u32[]{:S(2)}, u32[]{:S(2)}) collective-permute-start(bf16[48,1536]{1,0:T(8,128)(2,1)} %get-tuple-element.81), channel_id=1, source_target_pairs={{0,16},{1,17},{2,18},{3,19},{4,20},{5,21},{6,22},{7,23},{8,24},{9,... | collective-permute-start | bytes 442376 | tf_op jit(solution)/shard_map/ppermute | solution.py:362
  134.5 12.2 %collective-permute-start.28 = (bf16[48,1536]{1,0:T(8,128)(2,1)}, bf16[48,1536]{1,0:T(8,128)(2,1)}, u32[]{:S(2)}, u32[]{:S(2)}) collective-permute-start(bf16[48,1536]{1,0:T(8,128)(2,1)} %get-tuple-element.80), channel_id=1, source_target_pairs={{0,24},{1,25},{2,26},{3,27},{4,28},{5,29},{6,30},{7,31},{8,0},{9,1... | collective-permute-start | bytes 442376 | tf_op jit(solution)/shard_map/ppermute | solution.py:362
  134.9 3.3 %copy-start.7 = (bf16[96,3072]{1,0:T(8,128)(2,1)}, bf16[96,3072]{1,0:T(8,128)(2,1)S(1)}, u32[]{:S(2)}) copy-start(bf16[96,3072]{1,0:T(8,128)(2,1)S(1)} %collective-permute-done.16.refs_2_) | copy-start | bytes 1769476
  134.9 27.5 %collective-permute-start.35 = (bf16[48,1536]{1,0:T(8,128)(2,1)S(1)}, bf16[48,1536]{1,0:T(8,128)(2,1)S(1)}, u32[]{:S(2)}, u32[]{:S(2)}) collective-permute-start(bf16[48,1536]{1,0:T(8,128)(2,1)S(1)} %copy-done.15), channel_id=1, source_target_pairs={{0,1},{1,0},{2,3},{3,2},{4,5},{5,4},{6,7},{7,6},{8,9},{9,8},{10,11... | collective-permute-start | bytes 442376 | tf_op jit(solution)/shard_map/ppermute | solution.py:362
  135.0 3.2 %copy-start.8 = (bf16[96,3072]{1,0:T(8,128)(2,1)}, bf16[96,3072]{1,0:T(8,128)(2,1)S(1)}, u32[]{:S(2)}) copy-start(bf16[96,3072]{1,0:T(8,128)(2,1)S(1)} %collective-permute-done.17.refs_3_) | copy-start | bytes 1769476
  135.1 27.8 %collective-permute-start.36 = (bf16[48,1536]{1,0:T(8,128)(2,1)S(1)}, bf16[48,1536]{1,0:T(8,128)(2,1)S(1)}, u32[]{:S(2)}, u32[]{:S(2)}) collective-permute-start(bf16[48,1536]{1,0:T(8,128)(2,1)S(1)} %copy-done.14), channel_id=1, source_target_pairs={{0,2},{1,3},{2,0},{3,1},{4,6},{5,7},{6,4},{7,5},{8,10},{9,11},{10,... | collective-permute-start | bytes 442376 | tf_op jit(solution)/shard_map/ppermute | solution.py:362
  146.2 18.4 %collective-permute-start.37 = (bf16[48,1536]{1,0:T(8,128)(2,1)S(1)}, bf16[48,1536]{1,0:T(8,128)(2,1)S(1)}, u32[]{:S(2)}, u32[]{:S(2)}) collective-permute-start(bf16[48,1536]{1,0:T(8,128)(2,1)S(1)} %get-tuple-element.76), channel_id=1, source_target_pairs={{0,3},{1,2},{2,1},{3,0},{4,7},{5,6},{6,5},{7,4},{8,11},{9,10},{10,... | collective-permute-start | bytes 442376 | tf_op jit(solution)/shard_map/ppermute | solution.py:362
  147.8 18.2 %collective-permute-start.29 = (bf16[48,1536]{1,0:T(8,128)(2,1)S(1)}, bf16[48,1536]{1,0:T(8,128)(2,1)S(1)}, u32[]{:S(2)}, u32[]{:S(2)}) collective-permute-start(bf16[48,1536]{1,0:T(8,128)(2,1)S(1)} %add_convert_fusion.4), channel_id=1, source_target_pairs={{0,1},{1,0},{2,3},{3,2},{4,5},{5,4},{6,7},{7,6},{8,9},{9,8},{10,11... | collective-permute-start | bytes 442376 | tf_op jit(solution)/shard_map/ppermute | solution.py:362
  149.7 17.8 %collective-permute-start.30 = (bf16[48,1536]{1,0:T(8,128)(2,1)S(1)}, bf16[48,1536]{1,0:T(8,128)(2,1)S(1)}, u32[]{:S(2)}, u32[]{:S(2)}) collective-permute-start(bf16[48,1536]{1,0:T(8,128)(2,1)S(1)} %add_convert_fusion.4), channel_id=1, source_target_pairs={{0,2},{1,3},{2,0},{3,1},{4,6},{5,7},{6,4},{7,5},{8,10},{9,11},{10,... | collective-permute-start | bytes 442376 | tf_op jit(solution)/shard_map/ppermute | solution.py:362
  162.4 10.8 %copy-start.22 = (bf16[3,256,384]{2,1,0:T(8,128)(2,1)S(1)}, bf16[3,256,384]{2,1,0:T(8,128)(2,1)}, u32[]{:S(2)}) copy-start(bf16[3,256,384]{2,1,0:T(8,128)(2,1)} %get-tuple-element.59) | copy-start | bytes 1769476
  162.4 7.7 %collective-permute-start.31 = (bf16[48,1536]{1,0:T(8,128)(2,1)S(1)}, bf16[48,1536]{1,0:T(8,128)(2,1)S(1)}, u32[]{:S(2)}, u32[]{:S(2)}) collective-permute-start(bf16[48,1536]{1,0:T(8,128)(2,1)S(1)} %add_convert_fusion.4), channel_id=1, source_target_pairs={{0,3},{1,2},{2,1},{3,0},{4,7},{5,6},{6,5},{7,4},{8,11},{9,10},{10,... | collective-permute-start | bytes 442376 | tf_op jit(solution)/shard_map/ppermute | solution.py:362
  162.8 41.3 %collective-permute-start.22 = (bf16[3,256,384]{2,1,0:T(8,128)(2,1)}, bf16[3,256,384]{2,1,0:T(8,128)(2,1)S(1)}, u32[]{:S(2)}, u32[]{:S(2)}) collective-permute-start(bf16[3,256,384]{2,1,0:T(8,128)(2,1)} %get-tuple-element.57), channel_id=1, source_target_pairs={{0,1},{1,0},{2,3},{3,2},{4,5},{5,4},{6,7},{7,6},{8,9},{9,8},{10,11... | collective-permute-start | bytes 1769480 | tf_op jit(solution)/shard_map/ppermute | solution.py:362
  164.7 39.5 %collective-permute-start.23 = (bf16[3,256,384]{2,1,0:T(8,128)(2,1)}, bf16[3,256,384]{2,1,0:T(8,128)(2,1)S(1)}, u32[]{:S(2)}, u32[]{:S(2)}) collective-permute-start(bf16[3,256,384]{2,1,0:T(8,128)(2,1)} %get-tuple-element.58), channel_id=1, source_target_pairs={{0,2},{1,3},{2,0},{3,1},{4,6},{5,7},{6,4},{7,5},{8,10},{9,11},{10,... | collective-permute-start | bytes 1769480 | tf_op jit(solution)/shard_map/ppermute | solution.py:362
  166.0 7.1 %collective-permute-start.40 = (bf16[48,1536]{1,0:T(8,128)(2,1)S(1)}, bf16[48,1536]{1,0:T(8,128)(2,1)S(1)}, u32[]{:S(2)}, u32[]{:S(2)}) collective-permute-start(bf16[48,1536]{1,0:T(8,128)(2,1)S(1)} %get-tuple-element.89), channel_id=1, source_target_pairs={{0,24},{1,25},{2,26},{3,27},{4,28},{5,29},{6,30},{7,31},{8,0},{9,1... | collective-permute-start | bytes 442376 | tf_op jit(solution)/shard_map/ppermute | solution.py:362
  167.4 12.7 %collective-permute-start.39 = (bf16[48,1536]{1,0:T(8,128)(2,1)S(1)}, bf16[48,1536]{1,0:T(8,128)(2,1)S(1)}, u32[]{:S(2)}, u32[]{:S(2)}) collective-permute-start(bf16[48,1536]{1,0:T(8,128)(2,1)S(1)} %get-tuple-element.90), channel_id=1, source_target_pairs={{0,16},{1,17},{2,18},{3,19},{4,20},{5,21},{6,22},{7,23},{8,24},{9,... | collective-permute-start | bytes 442376 | tf_op jit(solution)/shard_map/ppermute | solution.py:362
  170.1 10.0 %collective-permute-start.38 = (bf16[48,1536]{1,0:T(8,128)(2,1)S(1)}, bf16[48,1536]{1,0:T(8,128)(2,1)S(1)}, u32[]{:S(2)}, u32[]{:S(2)}) collective-permute-start(bf16[48,1536]{1,0:T(8,128)(2,1)S(1)} %get-tuple-element.88), channel_id=1, source_target_pairs={{0,8},{1,9},{2,10},{3,11},{4,12},{5,13},{6,14},{7,15},{8,16},{9,17... | collective-permute-start | bytes 442376 | tf_op jit(solution)/shard_map/ppermute | solution.py:362
  173.2 31.0 %collective-permute-start.24 = (bf16[3,256,384]{2,1,0:T(8,128)(2,1)S(1)}, bf16[3,256,384]{2,1,0:T(8,128)(2,1)S(1)}, u32[]{:S(2)}, u32[]{:S(2)}) collective-permute-start(bf16[3,256,384]{2,1,0:T(8,128)(2,1)S(1)} %copy-done.22), channel_id=1, source_target_pairs={{0,3},{1,2},{2,1},{3,0},{4,7},{5,6},{6,5},{7,4},{8,11},{9,10},{10,... | collective-permute-start | bytes 1769480 | tf_op jit(solution)/shard_map/ppermute | solution.py:362
  180.1 8.6 %collective-permute-start.32 = (bf16[48,1536]{1,0:T(8,128)(2,1)S(1)}, bf16[48,1536]{1,0:T(8,128)(2,1)S(1)}, u32[]{:S(2)}, u32[]{:S(2)}) collective-permute-start(bf16[48,1536]{1,0:T(8,128)(2,1)S(1)} %get-tuple-element.93), channel_id=1, source_target_pairs={{0,8},{1,9},{2,10},{3,11},{4,12},{5,13},{6,14},{7,15},{8,16},{9,17... | collective-permute-start | bytes 442376 | tf_op jit(solution)/shard_map/ppermute | solution.py:362
  180.1 12.2 %collective-permute-start.33 = (bf16[48,1536]{1,0:T(8,128)(2,1)S(1)}, bf16[48,1536]{1,0:T(8,128)(2,1)S(1)}, u32[]{:S(2)}, u32[]{:S(2)}) collective-permute-start(bf16[48,1536]{1,0:T(8,128)(2,1)S(1)} %get-tuple-element.92), channel_id=1, source_target_pairs={{0,16},{1,17},{2,18},{3,19},{4,20},{5,21},{6,22},{7,23},{8,24},{9,... | collective-permute-start | bytes 442376 | tf_op jit(solution)/shard_map/ppermute | solution.py:362
  182.1 22.1 %copy-start.10 = (bf16[48,1536]{1,0:T(8,128)(2,1)}, bf16[48,1536]{1,0:T(8,128)(2,1)S(1)}, u32[]{:S(2)}) copy-start(bf16[48,1536]{1,0:T(8,128)(2,1)S(1)} %add_convert_fusion.refs_8_) | copy-start | bytes 442372
  188.7 15.5 %copy-start.16 = (bf16[48,1536]{1,0:T(8,128)(2,1)}, bf16[48,1536]{1,0:T(8,128)(2,1)S(1)}, u32[]{:S(2)}) copy-start(bf16[48,1536]{1,0:T(8,128)(2,1)S(1)} %collective-permute-done.32.refs_5_) | copy-start | bytes 442372
  188.7 5.2 %collective-permute-start.34 = (bf16[48,1536]{1,0:T(8,128)(2,1)S(1)}, bf16[48,1536]{1,0:T(8,128)(2,1)S(1)}, u32[]{:S(2)}, u32[]{:S(2)}) collective-permute-start(bf16[48,1536]{1,0:T(8,128)(2,1)S(1)} %get-tuple-element.91), channel_id=1, source_target_pairs={{0,24},{1,25},{2,26},{3,27},{4,28},{5,29},{6,30},{7,31},{8,0},{9,1... | collective-permute-start | bytes 442376 | tf_op jit(solution)/shard_map/ppermute | solution.py:362
  192.4 11.8 %copy-start.17 = (bf16[48,1536]{1,0:T(8,128)(2,1)}, bf16[48,1536]{1,0:T(8,128)(2,1)S(1)}, u32[]{:S(2)}) copy-start(bf16[48,1536]{1,0:T(8,128)(2,1)S(1)} %collective-permute-done.33.refs_6_) | copy-start | bytes 442372
  192.4 5.1 %collective-permute-start.41 = (bf16[48,1536]{1,0:T(8,128)(2,1)S(1)}, bf16[48,1536]{1,0:T(8,128)(2,1)S(1)}, u32[]{:S(2)}, u32[]{:S(2)}) collective-permute-start(bf16[48,1536]{1,0:T(8,128)(2,1)S(1)} %add_convert_fusion.refs_8_), channel_id=1, source_target_pairs={{0,1},{1,0},{2,3},{3,2},{4,5},{5,4},{6,7},{7,6},{8,9},{9,8},{10,11... | collective-permute-start | bytes 442376 | tf_op jit(solution)/shard_map/ppermute | solution.py:362
  193.9 10.3 %copy-start.18 = (bf16[48,1536]{1,0:T(8,128)(2,1)}, bf16[48,1536]{1,0:T(8,128)(2,1)S(1)}, u32[]{:S(2)}) copy-start(bf16[48,1536]{1,0:T(8,128)(2,1)S(1)} %collective-permute-done.34.refs_7_) | copy-start | bytes 442372
  193.9 7.1 %collective-permute-start.42 = (bf16[48,1536]{1,0:T(8,128)(2,1)S(1)}, bf16[48,1536]{1,0:T(8,128)(2,1)S(1)}, u32[]{:S(2)}, u32[]{:S(2)}) collective-permute-start(bf16[48,1536]{1,0:T(8,128)(2,1)S(1)} %add_convert_fusion.refs_8_), channel_id=1, source_target_pairs={{0,2},{1,3},{2,0},{3,1},{4,6},{5,7},{6,4},{7,5},{8,10},{9,11},{10,... | collective-permute-start | bytes 442376 | tf_op jit(solution)/shard_map/ppermute | solution.py:362
  197.5 6.7 %copy-start.19 = (bf16[48,1536]{1,0:T(8,128)(2,1)}, bf16[48,1536]{1,0:T(8,128)(2,1)S(1)}, u32[]{:S(2)}) copy-start(bf16[48,1536]{1,0:T(8,128)(2,1)S(1)} %collective-permute-done.41.refs_9_) | copy-start | bytes 442372
  197.5 6.6 %collective-permute-start.43 = (bf16[48,1536]{1,0:T(8,128)(2,1)S(1)}, bf16[48,1536]{1,0:T(8,128)(2,1)S(1)}, u32[]{:S(2)}, u32[]{:S(2)}) collective-permute-start(bf16[48,1536]{1,0:T(8,128)(2,1)S(1)} %add_convert_fusion.refs_8_), channel_id=1, source_target_pairs={{0,3},{1,2},{2,1},{3,0},{4,7},{5,6},{6,5},{7,4},{8,11},{9,10},{10,... | collective-permute-start | bytes 442376 | tf_op jit(solution)/shard_map/ppermute | solution.py:362
  201.0 3.2 %copy-start.20 = (bf16[48,1536]{1,0:T(8,128)(2,1)}, bf16[48,1536]{1,0:T(8,128)(2,1)S(1)}, u32[]{:S(2)}) copy-start(bf16[48,1536]{1,0:T(8,128)(2,1)S(1)} %collective-permute-done.42.refs_10_) | copy-start | bytes 442372
  204.2 1.2 copy-start.13
  (3 other events, 2.6 us)
